TPU v7x, 128 devices: a whole 4x4x4 slice. The times are simulated.
128 devices in a mesh: cores: 8 (over y, core), samp: 16 (over z, x).
Axes of the slice: x: 4, y: 4, z: 4, core: 2. Of those that a mesh axis runs over, the one named last changes fastest.
Arguments:
- cores: float32 [8, 512, 2304], P('cores'), may hold values from -0.875 to 0.875
- indices: int32 [16384, 8], P('samp'), may hold values from 0 to 511
- observed: float32 [16384], P('samp'), may hold values from -6 to 6
- step_size: float32 [], replicated, may hold values from 0.2 to 0.6
Outputs:
- new_cores: float32 [8, 512, 2304], P('cores', 'samp')
All inputs are finite; a program needn't handle non-finite values.
Results may differ from a plain program's by a relative error of at most 0.0003.
Values sent between devices are 32-bit elements; how exact they have to be, the bound alone decides.
No kernel may reach another device: no remote copies, remote signals or barrier semaphores. Data moves between devices by JAX's collectives and lax.ppermute only.
A program may use at most 128 MiB of HBM per device.

v0:
```python
import jax
import jax.numpy as jnp
from jax import lax
from jax.sharding import PartitionSpec as P

R = 48
N = 512


HIGH = lax.Precision.HIGHEST


def from_behind(array, axis, by):
    peers = lax.axis_size(axis)
    pairs = [(i, i + by) for i in range(peers) if 0 <= i + by < peers]
    return lax.ppermute(array, axis, pairs)


def cut_along(array, dim, peers):
    lengths = array.shape
    parts = array.reshape(*lengths[:dim], peers, lengths[dim] // peers, *lengths[dim + 1 :])
    return jnp.moveaxis(parts, dim, 0)


def sent_and_summed(array, axis, dim):
    parts = cut_along(array, dim, lax.axis_size(axis))
    arrived = lax.all_to_all(parts, axis, split_axis=0, concat_axis=0, tiled=True)
    return arrived.sum(axis=0)


def sent_to_all(array, axis):
    copies = jnp.broadcast_to(array, (lax.axis_size(axis), *array.shape))
    return lax.all_to_all(copies, axis, split_axis=0, concat_axis=0, tiled=True)


def over_copies(array, axis):
    everything = sent_to_all(array, axis)
    return jnp.sum(everything, axis=0)


def on_device(cores, indices, observed, step_size):
    ncores = lax.axis_size("cores")
    mine = lax.axis_index("cores")
    nsamp = lax.axis_size("samp")
    count = indices.shape[0]
    table = cores[0]
    own_index = lax.dynamic_index_in_dim(indices, mine, 1, keepdims=False)
    mats = jnp.take(table, own_index, axis=0).reshape(count, R, R)
    unit = jnp.broadcast_to((jnp.arange(R) == 0).astype(jnp.float32), (count, R))
    left = unit
    right = unit
    for turn in range(ncores - 1):
        sent = jnp.einsum("sa,sab->sb", left, mats, precision=HIGH)
        moved = from_behind(sent, "cores", 1)
        left = jnp.where(mine == 0, unit, moved)
    for turn in range(ncores - 1):
        sent = jnp.einsum("sab,sb->sa", mats, right, precision=HIGH)
        moved = from_behind(sent, "cores", -1)
        right = jnp.where(mine == ncores - 1, unit, moved)
    predicted = jnp.sum(jnp.einsum("sa,sab->sb", left, mats, precision=HIGH) * right, axis=1)
    residual = predicted - observed
    outer = (left[:, :, None] * (residual[:, None] * right)[:, None, :]).reshape(count, R * R)
    partial_grad = jax.ops.segment_sum(outer, own_index, num_segments=N)
    slab = N // nsamp
    first = lax.axis_index("samp") * slab
    gradient = sent_and_summed(partial_grad, "samp", 0)
    kept = lax.dynamic_slice_in_dim(table, first, slab, 0)
    updated = (kept - step_size * gradient).reshape(slab, R, R)

    def gram_of(product):
        local = jnp.einsum("iab,iac->bc", product, product, precision=HIGH)
        return over_copies(local, "samp") / N

    eye_mat = jnp.eye(R, dtype=jnp.float32)

    def factor(carry):
        product = jnp.einsum("ac,icb->iab", carry, updated, precision=HIGH)
        lower = jnp.linalg.cholesky(gram_of(product))
        return (product, lower)

    carry = eye_mat
    for turn in range(ncores - 1):
        product, lower = factor(carry)
        moved = from_behind(lower.T, "cores", 1)
        carry = jnp.where(mine == 0, eye_mat, moved)
    product, lower = factor(carry)
    rows_here = product.shape[0]
    flat = product.reshape(rows_here * R, R)
    ortho = lax.linalg.triangular_solve(lower, flat, left_side=False, lower=True, transpose_a=True)
    result = jnp.where(mine == ncores - 1, flat, ortho).reshape(rows_here, R * R)
    return result[None]


def solution(mesh):
    in_specs = (P("cores", None, None), P("samp", None), P("samp"), P())
    out_specs = P("cores", "samp", None)
    return jax.shard_map(
        on_device, mesh=mesh, in_specs=in_specs, out_specs=out_specs, check_vma=False
    )
```

profile of v0, /device:TPU:16, one launch (start us, length us, event | category | flops | bytes accessed | tf_op | source)
XLA Modules:
  0.0 471.6 jit_solution(17185432621066835447)
XLA Ops:
  0.8 12.1 %gather_fusion = f32[1024,2304]{1,0:T(8,128)} fusion(f32[512,2304]{1,0:T(8,128)} %bitcast.185, s32[1024]{0:T(1024)S(1)} %broadcast_clamp_fusion), kind=kCustom, calls=%fused_computation | custom fusion | bytes 18878464 | tf_op jit(solution)/shard_map/jit(_take)/gather | solution.py:48
  12.9 9.6 %copy.79 = f32[1024,2304]{0,1:T(8,128)} copy(f32[1024,2304]{1,0:T(8,128)} %gather_fusion) | data formatting | bytes 18874368 | tf_op jit(solution)/shard_map/jit(_take)/gather | solution.py:48
  22.5 5.0 %multiply_reduce_fusion.8 = f32[1024,48]{0,1:T(8,128)S(1)} fusion(f32[48]{0:T(128)S(1)} %compare_convert_fusion, f32[1024,48,48]{0,2,1:T(8,128)} %bitcast.166, pred[1024]{0:T(1024)(128)(4,1)S(1)} %get-tuple-element.6), kind=kLoop, calls=%fused_computation.22 | loop fusion | flops 7028736 | bytes 9635008 | tf_op jit(solution)/shard_map/sa,sab->sb/dot_general | solution.py:53
  29.5 5.1 %collective-permute-done = f32[1024,48]{0,1:T(8,128)S(1)} collective-permute-done((f32[1024,48]{0,1:T(8,128)S(1)}, f32[1024,48]{0,1:T(8,128)S(1)}, u32[]{:S(2)}, u32[]{:S(2)}) %collective-permute-start) | collective-permute-done | bytes 196640 | tf_op jit(solution)/shard_map/ppermute | solution.py:16
  34.6 5.2 %multiply_reduce_fusion.7 = f32[1024,48]{0,1:T(8,128)S(1)} fusion(f32[1024,48]{0,1:T(8,128)S(1)} %broadcast_select_fusion.13, f32[1024,48,48]{0,2,1:T(8,128)} %bitcast.167, pred[1024]{0:T(1024)(128)(4,1)S(1)} %get-tuple-element.6), kind=kLoop, calls=%fused_computation.21 | loop fusion | flops 7028736 | bytes 9831424 | tf_op jit(solution)/shard_map/sa,sab->sb/dot_general | solution.py:53
  41.7 5.1 %collective-permute-done.1 = f32[1024,48]{0,1:T(8,128)S(1)} collective-permute-done((f32[1024,48]{0,1:T(8,128)S(1)}, f32[1024,48]{0,1:T(8,128)S(1)}, u32[]{:S(2)}, u32[]{:S(2)}) %collective-permute-start.1) | collective-permute-done | bytes 196640 | tf_op jit(solution)/shard_map/ppermute | solution.py:16
  46.9 5.1 %multiply_reduce_fusion.6 = f32[1024,48]{0,1:T(8,128)S(1)} fusion(f32[1024,48]{0,1:T(8,128)S(1)} %broadcast_select_fusion.12, f32[1024,48,48]{0,2,1:T(8,128)} %bitcast.168, pred[1024]{0:T(1024)(128)(4,1)S(1)} %get-tuple-element.6), kind=kLoop, calls=%fused_computation.20 | loop fusion | flops 7028736 | bytes 9831424 | tf_op jit(solution)/shard_map/sa,sab->sb/dot_general | solution.py:53
  53.9 5.1 %collective-permute-done.2 = f32[1024,48]{0,1:T(8,128)S(1)} collective-permute-done((f32[1024,48]{0,1:T(8,128)S(1)}, f32[1024,48]{0,1:T(8,128)S(1)}, u32[]{:S(2)}, u32[]{:S(2)}) %collective-permute-start.2) | collective-permute-done | bytes 196640 | tf_op jit(solution)/shard_map/ppermute | solution.py:16
  62.6 5.1 %collective-permute-done.3 = f32[1024,48]{0,1:T(8,128)S(1)} collective-permute-done((f32[1024,48]{0,1:T(8,128)S(1)}, f32[1024,48]{0,1:T(8,128)S(1)}, u32[]{:S(2)}, u32[]{:S(2)}) %collective-permute-start.3) | collective-permute-done | bytes 196640 | tf_op jit(solution)/shard_map/ppermute | solution.py:16
  80.2 5.0 %collective-permute-done.5 = f32[1024,48]{0,1:T(8,128)S(1)} collective-permute-done((f32[1024,48]{0,1:T(8,128)S(1)}, f32[1024,48]{0,1:T(8,128)S(1)}, u32[]{:S(2)}, u32[]{:S(2)}) %collective-permute-start.5) | collective-permute-done | bytes 196640 | tf_op jit(solution)/shard_map/ppermute | solution.py:16
  85.4 5.4 %fusion.4 = f32[1024,48]{0,1:T(8,128)S(1)} fusion(f32[1024,48]{0,1:T(8,128)S(1)} %get-tuple-element.12, f32[1024,48,48]{0,2,1:T(8,128)} %bitcast.169, pred[1024]{0:T(1024)(128)(4,1)S(1)} %get-tuple-element.6), kind=kLoop, calls=%fused_computation.13 | loop fusion | flops 7028736 | bytes 9831424 | tf_op jit(solution)/shard_map/sab,sb->sa/dot_general | solution.py:57
  96.0 5.3 %fusion.3 = f32[1024,48]{0,1:T(8,128)S(1)} fusion(f32[1024,48]{0,1:T(8,128)S(1)} %broadcast_select_fusion.4, f32[1024,48,48]{0,2,1:T(8,128)} %bitcast.170, pred[1024]{0:T(1024)(128)(4,1)S(1)} %get-tuple-element.6), kind=kLoop, calls=%fused_computation.12 | loop fusion | flops 7028736 | bytes 9831424 | tf_op jit(solution)/shard_map/sab,sb->sa/dot_general | solution.py:57
  143.1 4.9 %broadcast_multiply_fusion = f32[1024,48,48]{0,2,1:T(8,128)} fusion(f32[1024,48]{0,1:T(8,128)S(1)} %select_multiply_fusion, f32[1024,48]{0,1:T(8,128)S(1)} %get-tuple-element.9), kind=kLoop, calls=%fused_computation.23 | loop fusion | flops 2359296 | bytes 9830400 | tf_op jit(solution)/shard_map/mul | solution.py:62
  148.0 9.7 %copy.80 = f32[1024,2304]{1,0:T(8,128)} copy(f32[1024,2304]{0,1:T(8,128)} %bitcast.186) | data formatting | bytes 18874368 | tf_op jit(solution)/shard_map/mul | solution.py:62
  157.7 17.9 %scatter_custom_fusion = f32[512,2304]{1,0:T(8,128)} fusion(s32[1024]{0:T(1024)S(1)} %bitcast.189, f32[1024,2304]{1,0:T(8,128)} %copy.80, f32[]{:T(128)} %constant.76.clone.1), kind=kCustom, calls=%fused_computation.26 | custom fusion | flops 2359296 | bytes 4719104 | tf_op jit(solution)/shard_map/scatter-add | solution.py:63
  175.5 8.1 %all-to-all-start = ((f32[16,32,2304]{2,1,0:T(8,128)}), f32[16,32,2304]{2,1,0:T(8,128)}, u32[]{:S(2)}, u32[]{:S(2)}) async-start(f32[16,32,2304]{2,1,0:T(8,128)} %bitcast.187), calls=%async_computation | async-start | bytes 9437184 | tf_op jit(solution)/shard_map/all_to_all | solution.py:27
  185.8 71.7 %all-to-all-done = f32[16,32,2304]{2,1,0:T(8,128)} async-done(((f32[16,32,2304]{2,1,0:T(8,128)}), f32[16,32,2304]{2,1,0:T(8,128)}, u32[]{:S(2)}, u32[]{:S(2)}) %all-to-all-start) | async-done | bytes 4718624 | tf_op jit(solution)/shard_map/all_to_all | solution.py:27
  262.7 11.4 %all_to_all.45 = f32[16,1,2304]{2,1,0:T(1,128)S(1)} all-to-all(f32[16,1,2304]{2,1,0:T(1,128)S(1)} %reshape.105), channel_id=1, replica_groups=mesh['cores'=8,'samp'=16] {'samp'}, dimensions={0} | all-to-all | bytes 294912 | tf_op jit(solution)/shard_map/all_to_all | solution.py:33
  276.2 4.4 cholesky.134
  289.7 11.1 %all_to_all.46 = f32[16,1,2304]{2,1,0:T(1,128)S(1)} all-to-all(f32[16,1,2304]{2,1,0:T(1,128)S(1)} %reshape.107), channel_id=1, replica_groups=mesh['cores'=8,'samp'=16] {'samp'}, dimensions={0} | all-to-all | bytes 294912 | tf_op jit(solution)/shard_map/all_to_all | solution.py:33
  302.3 4.4 cholesky.145
  315.8 11.1 %all_to_all.47 = f32[16,1,2304]{2,1,0:T(1,128)S(1)} all-to-all(f32[16,1,2304]{2,1,0:T(1,128)S(1)} %reshape.109), channel_id=1, replica_groups=mesh['cores'=8,'samp'=16] {'samp'}, dimensions={0} | all-to-all | bytes 294912 | tf_op jit(solution)/shard_map/all_to_all | solution.py:33
  328.4 4.4 cholesky.156
  341.8 11.1 %all_to_all.48 = f32[16,1,2304]{2,1,0:T(1,128)S(1)} all-to-all(f32[16,1,2304]{2,1,0:T(1,128)S(1)} %reshape.111), channel_id=1, replica_groups=mesh['cores'=8,'samp'=16] {'samp'}, dimensions={0} | all-to-all | bytes 294912 | tf_op jit(solution)/shard_map/all_to_all | solution.py:33
  354.4 4.4 cholesky.167
  367.9 11.1 %all_to_all.49 = f32[16,1,2304]{2,1,0:T(1,128)S(1)} all-to-all(f32[16,1,2304]{2,1,0:T(1,128)S(1)} %reshape.113), channel_id=1, replica_groups=mesh['cores'=8,'samp'=16] {'samp'}, dimensions={0} | all-to-all | bytes 294912 | tf_op jit(solution)/shard_map/all_to_all | solution.py:33
  380.5 4.4 cholesky.178
  394.0 11.1 %all_to_all.50 = f32[16,1,2304]{2,1,0:T(1,128)S(1)} all-to-all(f32[16,1,2304]{2,1,0:T(1,128)S(1)} %reshape.115), channel_id=1, replica_groups=mesh['cores'=8,'samp'=16] {'samp'}, dimensions={0} | all-to-all | bytes 294912 | tf_op jit(solution)/shard_map/all_to_all | solution.py:33
  406.6 4.4 cholesky.189
  420.0 11.1 %all_to_all.51 = f32[16,1,2304]{2,1,0:T(1,128)S(1)} all-to-all(f32[16,1,2304]{2,1,0:T(1,128)S(1)} %reshape.117), channel_id=1, replica_groups=mesh['cores'=8,'samp'=16] {'samp'}, dimensions={0} | all-to-all | bytes 294912 | tf_op jit(solution)/shard_map/all_to_all | solution.py:33
  451.5 7.3 %all-to-all-done.8 = f32[16,1,2304]{2,1,0:T(1,128)S(1)} async-done(((f32[16,1,2304]{2,1,0:T(1,128)}), f32[16,1,2304]{2,1,0:T(1,128)S(1)}, u32[]{:S(2)}, u32[]{:S(2)}) %all-to-all-start.8) | async-done | bytes 147488 | tf_op jit(solution)/shard_map/all_to_all | solution.py:33
  460.3 4.4 cholesky.211
  (207 shorter events, 168.1 us)
Async XLA Ops:
  27.5 7.0 %collective-permute-start = (f32[1024,48]{0,1:T(8,128)S(1)}, f32[1024,48]{0,1:T(8,128)S(1)}, u32[]{:S(2)}, u32[]{:S(2)}) collective-permute-start(f32[1024,48]{0,1:T(8,128)S(1)} %multiply_reduce_fusion.8), channel_id=1, source_target_pairs={{0,16},{16,32},{32,48},{48,64},{64,80},{80,96},{96,112},{1,17},{17... | collective-permute-start | bytes 589832 | tf_op jit(solution)/shard_map/ppermute | solution.py:16
  34.6 24.5 %slice-start = ((s8[9437184]{0:T(1024)(128)(4,1)}), s8[4194304]{0:T(1024)(128)(4,1)S(1)}, s32[]{:S(2)}) async-start(s8[9437184]{0:T(1024)(128)(4,1)} %bitcast.171), calls=%async_computation.9 | async-start | bytes 8388608
  34.6 24.5 %slice-start.1 = ((s8[9437184]{0:T(1024)(128)(4,1)}), s8[4194304]{0:T(1024)(128)(4,1)S(1)}, s32[]{:S(2)}) async-start(s8[9437184]{0:T(1024)(128)(4,1)} %bitcast.171), calls=%async_computation.10 | async-start | bytes 8388608
  39.8 7.0 %collective-permute-start.1 = (f32[1024,48]{0,1:T(8,128)S(1)}, f32[1024,48]{0,1:T(8,128)S(1)}, u32[]{:S(2)}, u32[]{:S(2)}) collective-permute-start(f32[1024,48]{0,1:T(8,128)S(1)} %multiply_reduce_fusion.7), channel_id=1, source_target_pairs={{0,16},{16,32},{32,48},{48,64},{64,80},{80,96},{96,112},{1,17},{17... | collective-permute-start | bytes 589832 | tf_op jit(solution)/shard_map/ppermute | solution.py:16
  46.9 12.2 %slice-start.2 = ((s8[9437184]{0:T(1024)(128)(4,1)}), s8[1048576]{0:T(1024)(128)(4,1)S(1)}, s32[]{:S(2)}) async-start(s8[9437184]{0:T(1024)(128)(4,1)} %bitcast.171), calls=%async_computation.11 | async-start | bytes 2097152
  52.0 7.0 %collective-permute-start.2 = (f32[1024,48]{0,1:T(8,128)S(1)}, f32[1024,48]{0,1:T(8,128)S(1)}, u32[]{:S(2)}, u32[]{:S(2)}) collective-permute-start(f32[1024,48]{0,1:T(8,128)S(1)} %multiply_reduce_fusion.6), channel_id=1, source_target_pairs={{0,16},{16,32},{32,48},{48,64},{64,80},{80,96},{96,112},{1,17},{17... | collective-permute-start | bytes 589832 | tf_op jit(solution)/shard_map/ppermute | solution.py:16
  60.6 7.0 %collective-permute-start.3 = (f32[1024,48]{0,1:T(8,128)S(1)}, f32[1024,48]{0,1:T(8,128)S(1)}, u32[]{:S(2)}, u32[]{:S(2)}) collective-permute-start(f32[1024,48]{0,1:T(8,128)S(1)} %multiply_reduce_fusion.5), channel_id=1, source_target_pairs={{0,16},{16,32},{32,48},{48,64},{64,80},{80,96},{96,112},{1,17},{17... | collective-permute-start | bytes 589832 | tf_op jit(solution)/shard_map/ppermute | solution.py:16
  69.2 7.5 %collective-permute-start.4 = (f32[1024,48]{0,1:T(8,128)S(1)}, f32[1024,48]{0,1:T(8,128)S(1)}, u32[]{:S(2)}, u32[]{:S(2)}) collective-permute-start(f32[1024,48]{0,1:T(8,128)S(1)} %multiply_reduce_fusion.4), channel_id=1, source_target_pairs={{0,16},{16,32},{32,48},{48,64},{64,80},{80,96},{96,112},{1,17},{17... | collective-permute-start | bytes 589832 | tf_op jit(solution)/shard_map/ppermute | solution.py:16
  72.8 7.5 %collective-permute-start.7 = (f32[1024,48]{0,1:T(8,128)S(1)}, f32[1024,48]{0,1:T(8,128)S(1)}, u32[]{:S(2)}, u32[]{:S(2)}) collective-permute-start(f32[1024,48]{0,1:T(8,128)S(1)} %fusion.5), channel_id=1, source_target_pairs={{16,0},{32,16},{48,32},{64,48},{80,64},{96,80},{112,96},{17,1},{33... | collective-permute-start | bytes 589832 | tf_op jit(solution)/shard_map/ppermute | solution.py:16
  78.3 7.0 %collective-permute-start.5 = (f32[1024,48]{0,1:T(8,128)S(1)}, f32[1024,48]{0,1:T(8,128)S(1)}, u32[]{:S(2)}, u32[]{:S(2)}) collective-permute-start(f32[1024,48]{0,1:T(8,128)S(1)} %multiply_reduce_fusion.3), channel_id=1, source_target_pairs={{0,16},{16,32},{32,48},{48,64},{64,80},{80,96},{96,112},{1,17},{17... | collective-permute-start | bytes 589832 | tf_op jit(solution)/shard_map/ppermute | solution.py:16
  85.4 23.0 %slice-start.3 = ((s8[9437184]{0:T(1024)(128)(4,1)}), s8[4194304]{0:T(1024)(128)(4,1)S(1)}, s32[]{:S(2)}) async-start(s8[9437184]{0:T(1024)(128)(4,1)} %bitcast.177), calls=%async_computation.12 | async-start | bytes 8388608
  85.4 23.0 %slice-start.4 = ((s8[9437184]{0:T(1024)(128)(4,1)}), s8[4194304]{0:T(1024)(128)(4,1)S(1)}, s32[]{:S(2)}) async-start(s8[9437184]{0:T(1024)(128)(4,1)} %bitcast.177), calls=%async_computation.13 | async-start | bytes 8388608
  90.8 5.1 %collective-permute-start.8 = (f32[1024,48]{0,1:T(8,128)S(1)}, f32[1024,48]{0,1:T(8,128)S(1)}, u32[]{:S(2)}, u32[]{:S(2)}) collective-permute-start(f32[1024,48]{0,1:T(8,128)S(1)} %fusion.4), channel_id=1, source_target_pairs={{16,0},{32,16},{48,32},{64,48},{80,64},{96,80},{112,96},{17,1},{33... | collective-permute-start | bytes 589832 | tf_op jit(solution)/shard_map/ppermute | solution.py:16
  96.0 12.4 %slice-start.5 = ((s8[9437184]{0:T(1024)(128)(4,1)}), s8[1048576]{0:T(1024)(128)(4,1)S(1)}, s32[]{:S(2)}) async-start(s8[9437184]{0:T(1024)(128)(4,1)} %bitcast.177), calls=%async_computation.14 | async-start | bytes 2097152
  101.3 7.0 %collective-permute-start.9 = (f32[1024,48]{0,1:T(8,128)S(1)}, f32[1024,48]{0,1:T(8,128)S(1)}, u32[]{:S(2)}, u32[]{:S(2)}) collective-permute-start(f32[1024,48]{0,1:T(8,128)S(1)} %fusion.3), channel_id=1, source_target_pairs={{16,0},{32,16},{48,32},{64,48},{80,64},{96,80},{112,96},{17,1},{33... | collective-permute-start | bytes 589832 | tf_op jit(solution)/shard_map/ppermute | solution.py:16
  110.0 7.0 %collective-permute-start.10 = (f32[1024,48]{0,1:T(8,128)S(1)}, f32[1024,48]{0,1:T(8,128)S(1)}, u32[]{:S(2)}, u32[]{:S(2)}) collective-permute-start(f32[1024,48]{0,1:T(8,128)S(1)} %fusion.2), channel_id=1, source_target_pairs={{16,0},{32,16},{48,32},{64,48},{80,64},{96,80},{112,96},{17,1},{33... | collective-permute-start | bytes 589832 | tf_op jit(solution)/shard_map/ppermute | solution.py:16
  118.6 7.3 %collective-permute-start.11 = (f32[1024,48]{0,1:T(8,128)S(1)}, f32[1024,48]{0,1:T(8,128)S(1)}, u32[]{:S(2)}, u32[]{:S(2)}) collective-permute-start(f32[1024,48]{0,1:T(8,128)S(1)} %fusion.1), channel_id=1, source_target_pairs={{16,0},{32,16},{48,32},{64,48},{80,64},{96,80},{112,96},{17,1},{33... | collective-permute-start | bytes 589832 | tf_op jit(solution)/shard_map/ppermute | solution.py:16
  123.9 7.7 %collective-permute-start.6 = (f32[1024,48]{0,1:T(8,128)S(1)}, f32[1024,48]{0,1:T(8,128)S(1)}, u32[]{:S(2)}, u32[]{:S(2)}) collective-permute-start(f32[1024,48]{0,1:T(8,128)S(1)} %multiply_reduce_fusion.2), channel_id=1, source_target_pairs={{0,16},{16,32},{32,48},{48,64},{64,80},{80,96},{96,112},{1,17},{17... | collective-permute-start | bytes 589832 | tf_op jit(solution)/shard_map/ppermute | solution.py:16
  127.5 6.8 %collective-permute-start.12 = (f32[1024,48]{0,1:T(8,128)S(1)}, f32[1024,48]{0,1:T(8,128)S(1)}, u32[]{:S(2)}, u32[]{:S(2)}) collective-permute-start(f32[1024,48]{0,1:T(8,128)S(1)} %fusion), channel_id=1, source_target_pairs={{16,0},{32,16},{48,32},{64,48},{80,64},{96,80},{112,96},{17,1},{33... | collective-permute-start | bytes 589832 | tf_op jit(solution)/shard_map/ppermute | solution.py:16
  134.4 8.6 %copy-start = (f32[1024]{0:T(1024)S(1)}, f32[1024]{0:T(1024)}, u32[]{:S(2)}) copy-start(f32[1024]{0:T(1024)} %param.7) | copy-start | bytes 12292
  135.9 7.0 %collective-permute-start.13 = (f32[1024,48]{0,1:T(8,128)S(1)}, f32[1024,48]{0,1:T(8,128)S(1)}, u32[]{:S(2)}, u32[]{:S(2)}) collective-permute-start(f32[1024,48]{0,1:T(8,128)S(1)} %multiply_reduce_fusion), channel_id=1, source_target_pairs={{16,0},{32,16},{48,32},{64,48},{80,64},{96,80},{112,96},{17,1},{33... | collective-permute-start | bytes 589832 | tf_op jit(solution)/shard_map/ppermute | solution.py:16
  175.5 82.0 %all-to-all-start = ((f32[16,32,2304]{2,1,0:T(8,128)}), f32[16,32,2304]{2,1,0:T(8,128)}, u32[]{:S(2)}, u32[]{:S(2)}) async-start(f32[16,32,2304]{2,1,0:T(8,128)} %bitcast.187), calls=%async_computation | async-start | bytes 9437184 | tf_op jit(solution)/shard_map/all_to_all | solution.py:27
  281.9 5.1 %collective-permute-start.14 = (f32[48,48]{0,1:T(8,128)S(1)}, f32[48,48]{0,1:T(8,128)S(1)}, u32[]{:S(2)}, u32[]{:S(2)}) collective-permute-start(f32[48,48]{0,1:T(8,128)S(1)} %fusion.55), channel_id=1, source_target_pairs={{0,16},{16,32},{32,48},{48,64},{64,80},{80,96},{96,112},{1,17},{17... | collective-permute-start | bytes 27656 | tf_op jit(solution)/shard_map/ppermute | solution.py:16
  308.0 5.1 %collective-permute-start.15 = (f32[48,48]{0,1:T(8,128)S(1)}, f32[48,48]{0,1:T(8,128)S(1)}, u32[]{:S(2)}, u32[]{:S(2)}) collective-permute-start(f32[48,48]{0,1:T(8,128)S(1)} %fusion.54), channel_id=1, source_target_pairs={{0,16},{16,32},{32,48},{48,64},{64,80},{80,96},{96,112},{1,17},{17... | collective-permute-start | bytes 27656 | tf_op jit(solution)/shard_map/ppermute | solution.py:16
  334.1 5.1 %collective-permute-start.16 = (f32[48,48]{0,1:T(8,128)S(1)}, f32[48,48]{0,1:T(8,128)S(1)}, u32[]{:S(2)}, u32[]{:S(2)}) collective-permute-start(f32[48,48]{0,1:T(8,128)S(1)} %fusion.53), channel_id=1, source_target_pairs={{0,16},{16,32},{32,48},{48,64},{64,80},{80,96},{96,112},{1,17},{17... | collective-permute-start | bytes 27656 | tf_op jit(solution)/shard_map/ppermute | solution.py:16
  360.2 5.1 %collective-permute-start.17 = (f32[48,48]{0,1:T(8,128)S(1)}, f32[48,48]{0,1:T(8,128)S(1)}, u32[]{:S(2)}, u32[]{:S(2)}) collective-permute-start(f32[48,48]{0,1:T(8,128)S(1)} %fusion.52), channel_id=1, source_target_pairs={{0,16},{16,32},{32,48},{48,64},{64,80},{80,96},{96,112},{1,17},{17... | collective-permute-start | bytes 27656 | tf_op jit(solution)/shard_map/ppermute | solution.py:16
  386.2 5.1 %collective-permute-start.18 = (f32[48,48]{0,1:T(8,128)S(1)}, f32[48,48]{0,1:T(8,128)S(1)}, u32[]{:S(2)}, u32[]{:S(2)}) collective-permute-start(f32[48,48]{0,1:T(8,128)S(1)} %fusion.51), channel_id=1, source_target_pairs={{0,16},{16,32},{32,48},{48,64},{64,80},{80,96},{96,112},{1,17},{17... | collective-permute-start | bytes 27656 | tf_op jit(solution)/shard_map/ppermute | solution.py:16
  412.3 5.1 %collective-permute-start.19 = (f32[48,48]{0,1:T(8,128)S(1)}, f32[48,48]{0,1:T(8,128)S(1)}, u32[]{:S(2)}, u32[]{:S(2)}) collective-permute-start(f32[48,48]{0,1:T(8,128)S(1)} %fusion.50), channel_id=1, source_target_pairs={{0,16},{16,32},{32,48},{48,64},{64,80},{80,96},{96,112},{1,17},{17... | collective-permute-start | bytes 27656 | tf_op jit(solution)/shard_map/ppermute | solution.py:16
  438.4 5.1 %collective-permute-start.20 = (f32[48,48]{0,1:T(8,128)S(1)}, f32[48,48]{0,1:T(8,128)S(1)}, u32[]{:S(2)}, u32[]{:S(2)}) collective-permute-start(f32[48,48]{0,1:T(8,128)S(1)} %select_bitcast_fusion), channel_id=1, source_target_pairs={{0,16},{16,32},{32,48},{48,64},{64,80},{80,96},{96,112},{1,17},{17... | collective-permute-start | bytes 27656 | tf_op jit(solution)/shard_map/ppermute | solution.py:16
  446.8 12.0 %all-to-all-start.8 = ((f32[16,1,2304]{2,1,0:T(1,128)}), f32[16,1,2304]{2,1,0:T(1,128)S(1)}, u32[]{:S(2)}, u32[]{:S(2)}) async-start(f32[16,1,2304]{2,1,0:T(1,128)} %reshape.119), calls=%async_computation.8 | async-start | bytes 294912 | tf_op jit(solution)/shard_map/all_to_all | solution.py:33
where the time goes:
time: 481 us; the launch traced here: 472 us
  waiting for transfers between devices  140 us (29%)
  other arithmetic  127 us (26%)
  blocking collectives  78.2 us (16%)
  starting transfers between devices  64.4 us (13%)
  local copies, waits for them, and re-layouts  42.7 us (9%)
  matrix products  17.2 us (4%)
    all_to_all x7, blocking collectives, sent_to_all(): return lax.all_to_all(copies, axis, split_axis=0, concat_axis=0, tiled=True)  78.2 us
    all_to_all x1, waiting for transfers between devices, sent_and_summed(): lax.all_to_all(parts, axis, split_axis=0, concat_axis=0, tiled=True)  71.7 us
    ppermute x21, waiting for transfers between devices, from_behind(): return lax.ppermute(array, axis, pairs)  61.4 us
    ppermute x21, starting transfers between devices, from_behind(): return lax.ppermute(array, axis, pairs)  52.3 us
    another operation x24, other arithmetic, factor(): lower = jnp.linalg.cholesky(gram_of(product))  40.4 us
    gather x2, local copies, waits for them, and re-layouts, on_device(): mats = jnp.take(table, own_index, axis=0).reshape(count, R, R)  21.7 us
    dot_general x7, other arithmetic, on_device(): sent = jnp.einsum('sa,sab->sb', left, mats, precision=HIGH)  21.3 us
    dot_general x7, other arithmetic, on_device(): sent = jnp.einsum('sab,sb->sa', mats, right, precision=HIGH)  18.4 us
  transfers between devices with their start and end apart: 23, of which 19 were waited for; matrix products, arithmetic and copies ran while one was open for 2% of the time, Pallas kernels for 0%

commit v1 on v0

v1 whole, which is shorter than its diff:
```python
import functools

import jax
import jax.numpy as jnp
from jax import lax
from jax.experimental import pallas as pl
from jax.experimental.pallas import tpu as pltpu
from jax.sharding import PartitionSpec as P

R = 48
N = 512
MODES = 8
RR = R * R
GROUPS = 8
WIDE = 4
ROWS = GROUPS * R
LANES = WIDE * 64
FEATS = 104
SLOTS = 128
HIGH = lax.Precision.HIGHEST
F32 = jnp.float32
BF16 = jnp.bfloat16
COLS = 384
BIG = 48 << 20


def dot_rows(a, b):
    return lax.dot_general(a, b, (((0,), (0,)), ((), ())), preferred_element_type=F32)


def dot_lanes(a, b, precision=None):
    return lax.dot_general(
        a, b, (((1,), (1,)), ((), ())), preferred_element_type=F32, precision=precision
    )


def halves(x):
    hi = x.astype(BF16)
    return hi, (x - hi.astype(F32)).astype(BF16)


def iota(shape, dim):
    return lax.broadcasted_iota(jnp.int32, shape, dim)


def ranks(row, peers, slab):
    count = row.shape[1]
    chunks = count // 128
    dest = row // slab
    hit = (iota((peers, count), 0) == dest).astype(F32)
    stacked = jnp.concatenate([hit[:, c * 128 : (c + 1) * 128] for c in range(chunks)], axis=0)
    upper = (iota((128, 128), 0) <= iota((128, 128), 1)).astype(BF16)
    inside = jnp.dot(stacked.astype(BF16), upper, preferred_element_type=F32)
    before = jnp.zeros((peers, 1), F32)
    out = []
    for c in range(chunks):
        part = inside[c * peers : (c + 1) * peers]
        mine = hit[:, c * 128 : (c + 1) * 128]
        out.append(jnp.sum(mine * (part + before), axis=0, keepdims=True))
        before = before + part[:, 127:128]
    return jnp.concatenate(out, axis=1).astype(jnp.int32) - 1, dest


def gather_kernel(idx_ref, table_ref, mats_ref, sent_ref, slot_ref, most_ref, hot_ref, *, peers):
    step = pl.program_id(0)
    mode = lax.axis_index("cores")
    leftward = mode < MODES // 2
    slab = N // peers

    @pl.when(step == 0)
    def _():
        row = idx_ref[pl.ds(mode, 1), :]
        count = row.shape[1]
        hot_ref[...] = (iota((N, count), 0) == row).astype(BF16)
        place, dest = ranks(row, peers, slab)
        slot_ref[0:1, :] = place
        slot_ref[1:2, :] = dest
        slot_ref[2:3, :] = row - dest * slab
        slot_ref[3:8, :] = jnp.zeros((5, count), jnp.int32)
        every = idx_ref[...] // slab
        most = jnp.zeros((MODES, 1), F32)
        for j in range(peers):
            most = jnp.maximum(most, jnp.sum((every == j).astype(F32), axis=1, keepdims=True))
        most_ref[...] = jnp.broadcast_to(jnp.max(most, axis=0, keepdims=True), (8, 128))

    hot = hot_ref[...]
    hi, lo = halves(table_ref[...])
    out = dot_rows(hi, hot) + dot_rows(lo, hot)
    mats_ref[...] = out

    @pl.when(jnp.logical_and(leftward, step == 0))
    def _():
        sent_ref[...] = out[0:R]

    @pl.when(jnp.logical_not(leftward))
    def _():
        per = COLS // R
        rows = jnp.concatenate([out[i * R : i * R + 1] for i in range(per)], axis=0)
        sent_ref[pl.ds(pl.multiple_of(step * per, per), per), :] = rows


def times_left(mats_ref, vec_ref, out_ref):
    count = vec_ref.shape[1]

    def chunk(c, _):
        lanes = pl.ds(pl.multiple_of(c * 128, 128), 128)
        acc = [jnp.zeros((R, 128), F32) for _ in range(2)]
        for a in range(R):
            acc[a % 2] = acc[a % 2] + mats_ref[a * R : (a + 1) * R, lanes] * vec_ref[a : a + 1, lanes]
        out_ref[:, lanes] = acc[0] + acc[1]
        return 0

    lax.fori_loop(0, count // 128, chunk, 0)


def times_right(mats_ref, vec_ref, out_ref):
    count = vec_ref.shape[1]

    def chunk(c, _):
        lanes = pl.ds(pl.multiple_of(c * 128, 128), 128)
        vec = vec_ref[:, lanes]
        for a in range(0, R, 8):
            rows = [
                jnp.sum(mats_ref[(a + i) * R : (a + i + 1) * R, lanes] * vec, axis=0, keepdims=True)
                for i in range(8)
            ]
            out_ref[a : a + 8, lanes] = jnp.concatenate(rows, axis=0)
        return 0

    lax.fori_loop(0, count // 128, chunk, 0)


def apply(left, mats_ref, vec_ref, out_ref):
    @pl.when(left)
    def _():
        times_left(mats_ref, vec_ref, out_ref)

    @pl.when(jnp.logical_not(left))
    def _():
        times_right(mats_ref, vec_ref, out_ref)


def hop_kernel(mats_ref, vec_ref, out_ref, *, second):
    mode = lax.axis_index("cores")
    left = (mode >= MODES // 2) if second else (mode < MODES // 2)
    apply(left, mats_ref, vec_ref, out_ref)


def spread(values, slot_ref, most_ref, turn, pay_ref):
    place = slot_ref[0:1, :] - turn * SLOTS
    fits = jnp.logical_and(place >= 0, place < SLOTS)
    key = jnp.where(fits, slot_ref[1:2, :] * SLOTS + place, -1)
    hi, lo = halves(values)
    both = jnp.concatenate([hi, lo], axis=0)
    peers = pay_ref.shape[0]
    count = values.shape[1]
    for pair in range(peers // 2):
        base = pair * 2 * SLOTS
        hot = (iota((2 * SLOTS, count), 0) + base == key).astype(BF16)
        out = dot_lanes(both, hot)
        out = out[:FEATS] + out[FEATS:]
        pay_ref[2 * pair] = out[:, :SLOTS]
        pay_ref[2 * pair + 1] = out[:, SLOTS:]
    for peer in range(peers):
        pay_ref[peer, 97:98, :] = most_ref[0:1, :]


def route_kernel(mats_ref, one_ref, two_ref, obs_ref, slot_ref, most_ref, pay_ref, val_ref, tmp_ref):
    mode = lax.axis_index("cores")
    early = mode < MODES // 2
    apply(jnp.logical_not(early), mats_ref, two_ref, tmp_ref)
    one = one_ref[...]
    two = two_ref[...]
    predicted = jnp.sum(tmp_ref[...] * one, axis=0, keepdims=True)
    residual = predicted - obs_ref[...]
    flag = jnp.where(early, 1.0, 0.0)
    left = jnp.where(flag > 0.5, one, two)
    right = jnp.where(flag > 0.5, two, one) * residual
    count = one.shape[1]
    values = jnp.concatenate(
        [left, right, slot_ref[2:3, :].astype(F32), jnp.zeros((FEATS - 97, count), F32)], axis=0
    )
    val_ref[...] = values
    spread(values, slot_ref, most_ref, 0, pay_ref)


def again_kernel(turn_ref, val_ref, slot_ref, most_ref, pay_ref):
    spread(val_ref[...], slot_ref, most_ref, turn_ref[0], pay_ref)


def collect_kernel(step_ref, recv_ref, base_ref, out_ref, turns_ref):
    peers = recv_ref.shape[0]
    left = jnp.concatenate([recv_ref[s, 0:R, :] for s in range(peers)], axis=1)
    right = jnp.concatenate([recv_ref[s, R : 2 * R, :] for s in range(peers)], axis=1)
    loc = jnp.concatenate([recv_ref[s, 96:97, :] for s in range(peers)], axis=1).astype(jnp.int32)
    row_of = loc // WIDE
    lane_of = loc - row_of * WIDE
    count = loc.shape[1]

    def picked(x, key, n, pad):
        hi = x.astype(BF16).astype(F32)
        lo = x - hi
        tail = [jnp.zeros((pad, count), BF16)] if pad else []
        his, los = [], []
        for i in range(n):
            here = key == i
            his += [jnp.where(here, hi, 0.0).astype(BF16)] + tail
            los += [jnp.where(here, lo, 0.0).astype(BF16)] + tail
        return jnp.concatenate(his, axis=0), jnp.concatenate(los, axis=0)

    xh, xl = picked(left, row_of, GROUPS, 0)
    yh, yl = picked(right, lane_of, WIDE, 16)
    grad = dot_lanes(xh, yh) + (dot_lanes(xh, yl) + dot_lanes(xl, yh))
    out_ref[...] = base_ref[...] - step_ref[0] * grad
    most = jnp.max(recv_ref[:, 97, :]).astype(jnp.int32)
    turns_ref[0] = (most + SLOTS - 1) // SLOTS


def unpacked(packed):
    return jnp.concatenate([packed, pltpu.roll(packed, 64, 1)], axis=0)[:, :R]


def gram_kernel(*refs, turn):
    if turn == 0:
        own_ref, other_ref, out_ref, prod_ref = refs
    else:
        recv_ref, own_ref, other_ref, out_ref, sum_ref, prod_ref = refs
    mode = lax.axis_index("cores")
    mine = jnp.where(mode % 2 == turn % 2, 1.0, 0.0)
    core = jnp.where(mine > 0.5, own_ref[...], other_ref[...])
    if turn == 0:
        prod = core
    else:
        packed = jnp.sum(recv_ref[...], axis=0)
        sum_ref[...] = packed
        before = unpacked(packed)
        for g in range(GROUPS):
            prod_ref[g * R : (g + 1) * R, :] = jnp.dot(
                before, core[g * R : (g + 1) * R], preferred_element_type=F32, precision=HIGH
            )
        prod = prod_ref[...]
    even = jnp.zeros((64, 128), F32)
    odd = jnp.zeros((64, 128), F32)
    for part in range(2):
        z = lax.dot_general(
            core[:, part * 128 : (part + 1) * 128],
            prod[:, part * 128 : (part + 1) * 128],
            (((0,), (0,)), ((), ())),
            preferred_element_type=F32,
            precision=HIGH,
        )
        even = even + z[0:64]
        odd = odd + z[64:128]
    low = even + pltpu.roll(odd, 64, 1)
    high = pltpu.roll(even, 64, 1) + odd
    packed = jnp.where(iota((24, 128), 1) < 64, low[0:24], high[24:48])
    live = jnp.where(mode // 2 == turn // 2, 1.0 / N, 0.0)
    packed = packed * live
    for peer in range(out_ref.shape[0]):
        out_ref[peer] = packed


def final_kernel(*refs):
    sums = refs[: MODES - 2]
    recv_ref, own_ref, out_ref, prod_ref, block_ref = refs[MODES - 2 :]
    mode = lax.axis_index("cores")
    every = [s[...] for s in sums] + [jnp.sum(recv_ref[...], axis=0)]
    own = jnp.zeros((24, 128), F32)
    prev = jnp.zeros((24, 128), F32)
    for t in range(MODES - 1):
        own = own + every[t] * jnp.where(mode == t, 1.0, 0.0)
        prev = prev + every[t] * jnp.where(mode == t + 1, 1.0, 0.0)
    row = iota((R, 128), 0)
    lane = iota((R, 128), 1)
    eye = jnp.where(lane == row, 1.0, 0.0)
    side = jnp.where(lane == row + 64, 1.0, 0.0)

    def start(packed, absent):
        full = jnp.concatenate([packed, pltpu.roll(packed, 64, 1)], axis=0)
        full = jnp.where(lane < R, full, 0.0)
        return full + eye * absent + side

    mats = [
        start(own, jnp.where(mode == MODES - 1, 1.0, 0.0)),
        start(prev, jnp.where(mode == 0, 1.0, 0.0)),
    ]
    for j in range(R):
        for w in range(2):
            m = mats[w]
            pivot = m[j : j + 1, :]
            scale = 1.0 / m[j : j + 1, j : j + 1]
            col = jnp.where(row[:, 0:1] > j, m[:, j : j + 1] * scale, 0.0)
            mats[w] = m - col * pivot
    tri = []
    for w in range(2):
        diag = jnp.sum(jnp.where(lane == row, mats[w], 0.0), axis=1, keepdims=True)
        tri.append(mats[w] * (1.0 / jnp.sqrt(diag)))
    carry = tri[1][:, :R]
    inv = jnp.where(lane >= 64, tri[0], 0.0)
    turned = pltpu.roll(inv, 64, 1)
    block_ref[...] = jnp.zeros((LANES, LANES), F32)
    for h in range(WIDE):
        block_ref[h * 64 : h * 64 + R, (h // 2) * 128 : (h // 2 + 1) * 128] = inv if h % 2 else turned
    for g in range(GROUPS):
        prod_ref[g * R : (g + 1) * R, :] = jnp.dot(
            carry, own_ref[g * R : (g + 1) * R, :], preferred_element_type=F32, precision=HIGH
        )
    out_ref[...] = dot_lanes(prod_ref[...], block_ref[...], HIGH)


def vmem():
    return pl.BlockSpec(memory_space=pltpu.VMEM)


def smem():
    return pl.BlockSpec(memory_space=pltpu.SMEM)


def call(kernel, outs, ins, scratch=(), name=None):
    return pl.pallas_call(
        kernel,
        out_shape=outs,
        in_specs=ins,
        out_specs=jax.tree.map(lambda o: smem() if o.dtype == jnp.int32 and o.size == 1 else vmem(), outs),
        scratch_shapes=list(scratch),
        compiler_params=pltpu.CompilerParams(vmem_limit_bytes=BIG),
        name=name,
    )


def shape(*dims, dtype=F32):
    return jax.ShapeDtypeStruct(dims, dtype)


def on_device(cores, indices, observed, step_size):
    peers = lax.axis_size("samp")
    count = indices.shape[0]
    slab = N // peers
    table = cores[0]
    idx = indices.T
    step = step_size.reshape(1)

    mats, sent, slot, most = pl.pallas_call(
        functools.partial(gather_kernel, peers=peers),
        grid=(RR // COLS,),
        in_specs=[
            pl.BlockSpec((MODES, count), lambda i: (0, 0)),
            pl.BlockSpec((N, COLS), lambda i: (0, i)),
        ],
        out_specs=[
            pl.BlockSpec((COLS, count), lambda i: (i, 0)),
            pl.BlockSpec((R, count), lambda i: (0, 0)),
            pl.BlockSpec((8, count), lambda i: (0, 0)),
            pl.BlockSpec((8, 128), lambda i: (0, 0)),
        ],
        out_shape=[shape(RR, count), shape(R, count), shape(8, count, dtype=jnp.int32), shape(8, 128)],
        scratch_shapes=[pltpu.VMEM((N, count), BF16)],
        compiler_params=pltpu.CompilerParams(vmem_limit_bytes=BIG),
        name="gather",
    )(idx, table)

    first = lax.axis_index("samp") * slab
    kept = lax.dynamic_slice_in_dim(table, first, slab, 0)
    base = kept.reshape(GROUPS, WIDE, R, R).transpose(0, 2, 1, 3)
    base = jnp.pad(base, ((0, 0), (0, 0), (0, 0), (0, 64 - R))).reshape(ROWS, LANES)

    mode = lax.axis_index("cores")
    edge = jnp.logical_or(mode == 0, mode == MODES - 1)
    unit = jnp.broadcast_to((jnp.arange(R) == 0).astype(F32)[:, None], (R, count))
    one = jnp.where(edge, unit, 0.0)
    two = jnp.zeros((R, count), F32)
    for turn in range(MODES - 1):
        if turn > 0:
            sent = call(
                functools.partial(hop_kernel, second=turn >= MODES // 2),
                shape(R, count),
                [vmem(), vmem()],
                name=f"hop{turn}",
            )(mats, moved)
        moved = lax.ppermute(sent, "cores", [(turn, turn + 1), (7 - turn, 6 - turn)])
        if turn < 3:
            one = one + moved
        else:
            two = two + moved

    pay, values = call(
        route_kernel,
        (shape(peers, FEATS, SLOTS), shape(FEATS, count)),
        [vmem()] * 6,
        [pltpu.VMEM((R, count), F32)],
        name="route",
    )(mats, one, two, observed.reshape(1, count), slot, most)

    def exchanged(block):
        return lax.all_to_all(block, "samp", 0, 0, tiled=True)

    def collected(recv, so_far):
        return call(
            collect_kernel,
            (shape(ROWS, LANES), shape(1, dtype=jnp.int32)),
            [smem(), vmem(), vmem()],
            name="collect",
        )(step, recv, so_far)

    updated, turns = collected(exchanged(pay), base)

    def more(state):
        return state[0] < turns[0]

    def another(state):
        turn, so_far = state
        pay = call(
            again_kernel,
            shape(peers, FEATS, SLOTS),
            [smem(), vmem(), vmem(), vmem()],
            name="again",
        )(turn.reshape(1), values, slot, most)
        return turn + 1, collected(exchanged(pay), so_far)[0]

    _, updated = lax.while_loop(more, another, (jnp.int32(1), updated))

    other = lax.ppermute(updated, "cores", [(i, i ^ 1) for i in range(MODES)])

    sums = []
    recv = None
    for turn in range(MODES - 1):
        odd = turn % 2 == 1
        size = 2 * peers if odd else peers
        outs = [shape(size, 24, 128)] + ([shape(24, 128)] if turn else [])
        res = call(
            functools.partial(gram_kernel, turn=turn),
            outs,
            [vmem()] * (2 if turn == 0 else 3),
            [pltpu.VMEM((ROWS, LANES), F32)],
            name=f"gram{turn}",
        )(*([] if turn == 0 else [recv]), updated, other)
        if turn:
            sums.append(res[1])
        if odd:
            here = turn // 2
            groups = []
            for c in (here, here + 2):
                for h in range(2):
                    pair = [(2 * (c % 4) + h), (2 * ((c + 1) % 4) + h)]
                    groups.append([m * peers + j for m in pair for j in range(peers)])
            recv = lax.all_to_all(
                res[0], ("cores", "samp"), 0, 0, axis_index_groups=groups, tiled=True
            )
        else:
            recv = lax.all_to_all(res[0], "samp", 0, 0, tiled=True)

    out = call(
        final_kernel,
        shape(ROWS, LANES),
        [vmem()] * (MODES),
        [pltpu.VMEM((ROWS, LANES), F32), pltpu.VMEM((LANES, LANES), F32)],
        name="final",
    )(*sums, recv, updated)
    out = out.reshape(GROUPS, R, WIDE, 64)[..., :R].transpose(0, 2, 1, 3)
    return out.reshape(1, slab, RR)


def solution(mesh):
    in_specs = (P("cores", None, None), P("samp", None), P("samp"), P())
    out_specs = P("cores", "samp", None)
    return jax.shard_map(
        on_device, mesh=mesh, in_specs=in_specs, out_specs=out_specs, check_vma=False
    )
```

time: 481 us -> 210 us (0.44); the launches traced: 472 us -> 208 us
  other arithmetic: 127 us -> 0.14 us
  waiting for transfers between devices: 140 us -> 27.6 us
  Pallas kernels: 0 us -> 60.6 us
  starting transfers between devices: 64.4 us -> 17.4 us
  local copies, waits for them, and re-layouts: 42.7 us -> 6.98 us
  matrix products: 17.2 us -> 0 us
  blocking collectives: 78.2 us -> 93.4 us
    all_to_all x2 -> x1, waiting for transfers between devices: 79.1 us -> 11.3 us  [exchanged(): return lax.all_to_all(block, 'samp', 0, 0, tiled=True)]
    pallas_call x0 -> x17, Pallas kernels: none -> 60.6 us  [the longest x6 30.6 us: on_device(): call(functools.partial(hop_kernel, second=turn >= MODES // 2), shape(R, c...]
    ppermute x21 -> x8, waiting for transfers between devices: 61.4 us -> 16.4 us  [the longest x7 15 us: on_device(): lax.ppermute(sent, 'cores', [(turn, turn + 1), (7 - turn, 6 - turn)])]
    another operation x26 -> x0, other arithmetic: 44.7 us -> none  [the longest x24 40.4 us: factor(): lower = jnp.linalg.cholesky(gram_of(product))]
    ppermute x21 -> x8, starting transfers between devices: 52.3 us -> 9.5 us  [the longest x7 7.19 us: on_device(): lax.ppermute(sent, 'cores', [(turn, turn + 1), (7 - turn, 6 - turn)])]
    dot_general x15 -> x0, other arithmetic: 41.3 us -> none  [the longest x7 21.3 us: on_device(): sent = jnp.einsum('sa,sab->sb', left, mats, precision=HIGH)]
    gather x2 -> x0, local copies, waits for them, and re-layouts: 21.7 us -> none  [on_device(): mats = jnp.take(table, own_index, axis=0).reshape(count, R, R)]
    scatter-add x1 -> x0, other arithmetic: 17.9 us -> none  [on_device(): partial_grad = jax.ops.segment_sum(outer, own_index, num_segments=N)]
  transfers between devices with their start and end apart: 23 -> 9, of which waited for: 19 -> 5; matrix products, arithmetic and copies ran while one was open for 2% -> 1% of each run, Pallas kernels for 0% -> 0%
where the time goes in v1:
time: 210 us; the launch traced here: 208 us
  blocking collectives  93.4 us (44%)
  Pallas kernels  60.6 us (29%)
  waiting for transfers between devices  27.6 us (13%)
  starting transfers between devices  17.4 us (8%)
  local copies, waits for them, and re-layouts  6.98 us (3%)
    all_to_all x4, blocking collectives, on_device(): recv = lax.all_to_all(res[0], 'samp', 0, 0, tiled=True)  47.6 us
    all_to_all x3, blocking collectives, on_device(): lax.all_to_all(res[0], ('cores', 'samp'), 0, 0, axis_index_groups=groups,...  45.8 us
    pallas_call x6, Pallas kernels, on_device(): call(functools.partial(hop_kernel, second=turn >= MODES // 2), shape(R, c...  30.6 us
    ppermute x7, waiting for transfers between devices, on_device(): lax.ppermute(sent, 'cores', [(turn, turn + 1), (7 - turn, 6 - turn)])  15 us
    all_to_all x1, waiting for transfers between devices, exchanged(): return lax.all_to_all(block, 'samp', 0, 0, tiled=True)  11.3 us
    pallas_call x1, Pallas kernels, on_device(): pl.pallas_call(functools.partial(gather_kernel, peers=peers), grid=(RR //...  8.68 us
    all_to_all x1, starting transfers between devices, exchanged(): return lax.all_to_all(block, 'samp', 0, 0, tiled=True)  7.89 us
    pallas_call x1, Pallas kernels, on_device(): call(route_kernel, (shape(peers, FEATS, SLOTS), shape(FEATS, count)), [vm...  7.5 us
  transfers between devices with their start and end apart: 9, of which 5 were waited for; matrix products, arithmetic and copies ran while one was open for 1% of the time, Pallas kernels for 0%

profile of v1, /device:TPU:16, one launch (start us, length us, event | category | flops | bytes accessed | tf_op | source)
XLA Modules:
  0.0 207.7 jit_solution(18227699190237872364)
XLA Ops:
  0.0 2.3 %copy-done = f32[1,512,2304]{2,1,0:T(8,128)S(1)} copy-done((f32[1,512,2304]{2,1,0:T(8,128)S(1)}, f32[1,512,2304]{2,1,0:T(8,128)}, u32[]{:S(2)}) %copy-start) | copy-done | bytes 4718616
  3.1 8.7 %gather.1 = (f32[2304,1024]{1,0:T(8,128)}, f32[48,1024]{1,0:T(8,128)S(1)}, s32[8,1024]{1,0:T(8,128)S(1)}, f32[8,128]{1,0:T(8,128)S(1)}) custom-call(s32[8,1024]{1,0:T(8,128)S(1)} %bitcast.16, f32[512,2304]{1,0:T(8,128)S(1)} %bitcast.15), custom_call_target="tpu_custom_call" | custom-call | tf_op jit(solution)/shard_map/gather/pallas_call | solution.py:343
  12.5 5.1 %hop1.1 = f32[48,1024]{1,0:T(8,128)S(1)} custom-call(f32[2304,1024]{1,0:T(8,128)} %get-tuple-element.64.mats_ref, f32[48,1024]{1,0:T(8,128)S(1)} %collective-permute-done.vec_ref), custom_call_target="tpu_custom_call" | custom-call | tf_op jit(solution)/shard_map/hop1/pallas_call | solution.py:374
  18.2 5.1 %hop2.1 = f32[48,1024]{1,0:T(8,128)S(1)} custom-call(f32[2304,1024]{1,0:T(8,128)} %get-tuple-element.64.mats_ref, f32[48,1024]{1,0:T(8,128)S(1)} %collective-permute-done.1.vec_ref), custom_call_target="tpu_custom_call" | custom-call | tf_op jit(solution)/shard_map/hop2/pallas_call | solution.py:374
  23.3 1.3 collective-permute-start.2
  24.6 8.9 %collective-permute-done.2.vec_ref = f32[48,1024]{1,0:T(8,128)S(1)} collective-permute-done((f32[48,1024]{1,0:T(8,128)S(1)}, f32[48,1024]{1,0:T(8,128)S(1)}, u32[]{:S(2)}, u32[]{:S(2)}) %collective-permute-start.2) | collective-permute-done | bytes 196640 | tf_op jit(solution)/shard_map/ppermute | solution.py:380
  33.5 5.1 %hop3.1 = f32[48,1024]{1,0:T(8,128)S(1)} custom-call(f32[2304,1024]{1,0:T(8,128)} %get-tuple-element.64.mats_ref, f32[48,1024]{1,0:T(8,128)S(1)} %collective-permute-done.2.vec_ref), custom_call_target="tpu_custom_call" | custom-call | tf_op jit(solution)/shard_map/hop3/pallas_call | solution.py:374
  38.5 1.9 collective-permute-start.3
  40.5 5.1 %collective-permute-done.3.vec_ref = f32[48,1024]{1,0:T(8,128)S(1)} collective-permute-done((f32[48,1024]{1,0:T(8,128)S(1)}, f32[48,1024]{1,0:T(8,128)S(1)}, u32[]{:S(2)}, u32[]{:S(2)}) %collective-permute-start.3) | collective-permute-done | bytes 196640 | tf_op jit(solution)/shard_map/ppermute | solution.py:380
  45.5 5.1 %hop4.1 = f32[48,1024]{1,0:T(8,128)S(1)} custom-call(f32[2304,1024]{1,0:T(8,128)} %get-tuple-element.64.mats_ref, f32[48,1024]{1,0:T(8,128)S(1)} %collective-permute-done.3.vec_ref), custom_call_target="tpu_custom_call" | custom-call | tf_op jit(solution)/shard_map/hop4/pallas_call | solution.py:374
  50.7 1.3 collective-permute-start.4
  52.0 1.0 collective-permute-done.4.vec_ref
  53.0 5.1 %hop5.1 = f32[48,1024]{1,0:T(8,128)S(1)} custom-call(f32[2304,1024]{1,0:T(8,128)} %get-tuple-element.64.mats_ref, f32[48,1024]{1,0:T(8,128)S(1)} %collective-permute-done.4.vec_ref), custom_call_target="tpu_custom_call" | custom-call | tf_op jit(solution)/shard_map/hop5/pallas_call | solution.py:374
  58.9 5.1 %hop6.1 = f32[48,1024]{1,0:T(8,128)S(1)} custom-call(f32[2304,1024]{1,0:T(8,128)} %get-tuple-element.64.mats_ref, f32[48,1024]{1,0:T(8,128)S(1)} %collective-permute-done.5.vec_ref), custom_call_target="tpu_custom_call" | custom-call | tf_op jit(solution)/shard_map/hop6/pallas_call | solution.py:374
  64.9 7.5 %route.1 = (f32[16,104,128]{2,1,0:T(8,128)}, f32[104,1024]{1,0:T(8,128)S(1)}) custom-call(f32[2304,1024]{1,0:T(8,128)} %get-tuple-element.64.mats_ref, f32[48,1024]{1,0:T(8,128)S(1)} %add_add_fusion.1.one_ref, f32[48,1024]{1,0:T(8,128)S(1)} %add_add_fusion.two_ref, f32[1,1024]{1,0:T(1,128)S(1)} %bitcast.17, s32[8,1024]{1,0:T(8,128)S(1)} %get-tuple-element.149.slot_ref, ...), custom_call_target="tpu_custom_call" | custom-call | tf_op jit(solution)/shard_map/route/pallas_call | solution.py:386
  72.4 7.9 %all-to-all-start.1 = ((f32[16,104,128]{2,1,0:T(8,128)}), f32[16,104,128]{2,1,0:T(8,128)S(1)}, u32[]{:S(2)}, u32[]{:S(2)}) async-start(f32[16,104,128]{2,1,0:T(8,128)} %get-tuple-element.68), calls=%async_computation.1 | async-start | bytes 1703936 | tf_op jit(solution)/shard_map/all_to_all | solution.py:395
  83.3 11.3 %all-to-all-done.1.recv_ref = f32[16,104,128]{2,1,0:T(8,128)S(1)} async-done(((f32[16,104,128]{2,1,0:T(8,128)}), f32[16,104,128]{2,1,0:T(8,128)S(1)}, u32[]{:S(2)}, u32[]{:S(2)}) %all-to-all-start.1) | async-done | bytes 852000 | tf_op jit(solution)/shard_map/all_to_all | solution.py:395
  94.6 1.9 collect.2
  97.1 2.3 %collective-permute-start.7 = (f32[384,256]{1,0:T(8,128)S(1)}, f32[384,256]{1,0:T(8,128)S(1)}, u32[]{:S(2)}, u32[]{:S(2)}) collective-permute-start(f32[384,256]{1,0:T(8,128)S(1)} %get-tuple-element.72.refs_0_.refs_1_.refs_7_), channel_id=1, source_target_pairs={{0,16},{16,0},{32,48},{48,32},{64,80},{80,64},{96,112},{112,96},{1... | collective-permute-start | bytes 1179656 | tf_op jit(solution)/shard_map/ppermute | solution.py:422
  99.4 1.3 collective-permute-done.7.refs_1_.refs_2_
  101.4 11.6 %all_to_all.46.refs_0_ = f32[16,24,128]{2,1,0:T(8,128)S(1)} all-to-all(f32[16,24,128]{2,1,0:T(8,128)S(1)} %gram0.1), channel_id=1, replica_groups=mesh['cores'=8,'samp'=16] {'samp'}, dimensions={0} | all-to-all | bytes 393216 | tf_op jit(solution)/shard_map/all_to_all | solution.py:450
  114.0 18.9 %all_to_all.47.refs_0_ = f32[32,24,128]{2,1,0:T(8,128)S(1)} all-to-all(f32[32,24,128]{2,1,0:T(8,128)S(1)} %get-tuple-element.74), channel_id=1, replica_groups={{0,1,2,3,4,5,6,7,8,9,10,11,12,13,14,15,32,33,34,35,36,37,38,39,40,41,42..., dimensions={0} | all-to-all | bytes 786432 | tf_op jit(solution)/shard_map/all_to_all | solution.py:446
  132.9 1.0 gram2.1
  133.9 12.2 %all_to_all.48.refs_0_ = f32[16,24,128]{2,1,0:T(8,128)S(1)} all-to-all(f32[16,24,128]{2,1,0:T(8,128)S(1)} %get-tuple-element.76), channel_id=1, replica_groups=mesh['cores'=8,'samp'=16] {'samp'}, dimensions={0} | all-to-all | bytes 393216 | tf_op jit(solution)/shard_map/all_to_all | solution.py:450
  146.1 1.0 gram3.1
  147.1 13.1 %all_to_all.49.refs_0_ = f32[32,24,128]{2,1,0:T(8,128)S(1)} all-to-all(f32[32,24,128]{2,1,0:T(8,128)S(1)} %get-tuple-element.78), channel_id=1, replica_groups={{32,33,34,35,36,37,38,39,40,41,42,43,44,45,46,47,64,65,66,67,68,69,70,7..., dimensions={0} | all-to-all | bytes 786432 | tf_op jit(solution)/shard_map/all_to_all | solution.py:446
  161.3 11.6 %all_to_all.50.refs_0_ = f32[16,24,128]{2,1,0:T(8,128)S(1)} all-to-all(f32[16,24,128]{2,1,0:T(8,128)S(1)} %get-tuple-element.80), channel_id=1, replica_groups=mesh['cores'=8,'samp'=16] {'samp'}, dimensions={0} | all-to-all | bytes 393216 | tf_op jit(solution)/shard_map/all_to_all | solution.py:450
  173.0 1.0 gram5.1
  174.0 13.8 %all_to_all.51.refs_0_ = f32[32,24,128]{2,1,0:T(8,128)S(1)} all-to-all(f32[32,24,128]{2,1,0:T(8,128)S(1)} %get-tuple-element.82), channel_id=1, replica_groups={{64,65,66,67,68,69,70,71,72,73,74,75,76,77,78,79,96,97,98,99,100,101,10..., dimensions={0} | all-to-all | bytes 786432 | tf_op jit(solution)/shard_map/all_to_all | solution.py:446
  187.8 1.0 gram6.1
  188.9 12.2 %all_to_all.52.refs_6_ = f32[16,24,128]{2,1,0:T(8,128)S(1)} all-to-all(f32[16,24,128]{2,1,0:T(8,128)S(1)} %get-tuple-element.84), channel_id=1, replica_groups=mesh['cores'=8,'samp'=16] {'samp'}, dimensions={0} | all-to-all | bytes 393216 | tf_op jit(solution)/shard_map/all_to_all | solution.py:450
  201.1 5.1 %final.1 = f32[384,256]{1,0:T(8,128)S(1)} custom-call(f32[24,128]{1,0:T(8,128)S(1)} %get-tuple-element.73.refs_0_, f32[24,128]{1,0:T(8,128)S(1)} %get-tuple-element.75.refs_1_, f32[24,128]{1,0:T(8,128)S(1)} %get-tuple-element.77.refs_2_, f32[24,128]{1,0:T(8,128)S(1)} %get-tuple-element.79.refs_3_, f32[24,128]{1,0:T(8,128)S(1)} %get-tuple-element.81.refs_4_, ...), custom_call_target="tpu_custom_call" | custom-call | tf_op jit(solution)/shard_map/final/pallas_call | solution.py:452
  (29 shorter events, 10.8 us)
Async XLA Ops:
  0.0 2.3 %copy-start = (f32[1,512,2304]{2,1,0:T(8,128)S(1)}, f32[1,512,2304]{2,1,0:T(8,128)}, u32[]{:S(2)}) copy-start(f32[1,512,2304]{2,1,0:T(8,128)} %param.6) | copy-start | bytes 14155780
  2.3 0.8 copy-start.1
  11.8 0.7 collective-permute-start
  17.5 0.7 collective-permute-start.1
  23.3 10.2 %collective-permute-start.2 = (f32[48,1024]{1,0:T(8,128)S(1)}, f32[48,1024]{1,0:T(8,128)S(1)}, u32[]{:S(2)}, u32[]{:S(2)}) collective-permute-start(f32[48,1024]{1,0:T(8,128)S(1)} %hop2.1), channel_id=1, source_target_pairs={{32,48},{80,64},{33,49},{81,65},{34,50},{82,66},{35,51},{83,67},{3... | collective-permute-start | bytes 589832 | tf_op jit(solution)/shard_map/ppermute | solution.py:380
  38.5 7.0 %collective-permute-start.3 = (f32[48,1024]{1,0:T(8,128)S(1)}, f32[48,1024]{1,0:T(8,128)S(1)}, u32[]{:S(2)}, u32[]{:S(2)}) collective-permute-start(f32[48,1024]{1,0:T(8,128)S(1)} %hop3.1), channel_id=1, source_target_pairs={{48,64},{64,48},{49,65},{65,49},{50,66},{66,50},{51,67},{67,51},{5... | collective-permute-start | bytes 589832 | tf_op jit(solution)/shard_map/ppermute | solution.py:380
  50.7 2.4 %collective-permute-start.4 = (f32[48,1024]{1,0:T(8,128)S(1)}, f32[48,1024]{1,0:T(8,128)S(1)}, u32[]{:S(2)}, u32[]{:S(2)}) collective-permute-start(f32[48,1024]{1,0:T(8,128)S(1)} %hop4.1), channel_id=1, source_target_pairs={{64,80},{48,32},{65,81},{49,33},{66,82},{50,34},{67,83},{51,35},{6... | collective-permute-start | bytes 589832 | tf_op jit(solution)/shard_map/ppermute | solution.py:380
  58.2 0.7 collective-permute-start.5
  58.9 6.0 %copy-start.2 = (f32[1024]{0:T(1024)S(1)}, f32[1024]{0:T(1024)}, u32[]{:S(2)}) copy-start(f32[1024]{0:T(1024)} %param.8) | copy-start | bytes 12292
  64.0 0.8 collective-permute-start.6
  72.4 22.3 %all-to-all-start.1 = ((f32[16,104,128]{2,1,0:T(8,128)}), f32[16,104,128]{2,1,0:T(8,128)S(1)}, u32[]{:S(2)}, u32[]{:S(2)}) async-start(f32[16,104,128]{2,1,0:T(8,128)} %get-tuple-element.68), calls=%async_computation.1 | async-start | bytes 1703936 | tf_op jit(solution)/shard_map/all_to_all | solution.py:395
  97.1 3.7 %collective-permute-start.7 = (f32[384,256]{1,0:T(8,128)S(1)}, f32[384,256]{1,0:T(8,128)S(1)}, u32[]{:S(2)}, u32[]{:S(2)}) collective-permute-start(f32[384,256]{1,0:T(8,128)S(1)} %get-tuple-element.72.refs_0_.refs_1_.refs_7_), channel_id=1, source_target_pairs={{0,16},{16,0},{32,48},{48,32},{64,80},{80,64},{96,112},{112,96},{1... | collective-permute-start | bytes 1179656 | tf_op jit(solution)/shard_map/ppermute | solution.py:422

commit v2 on v1

--- a/solution.py
+++ b/solution.py
@@ -21,7 +21,7 @@
 F32 = jnp.float32
 BF16 = jnp.bfloat16
 COLS = 384
-BIG = 48 << 20
+BIG = 14 << 20
 
 
 def dot_rows(a, b):
@@ -165,9 +165,15 @@
         pay_ref[peer, 97:98, :] = most_ref[0:1, :]
 
 
-def route_kernel(mats_ref, one_ref, two_ref, obs_ref, slot_ref, most_ref, pay_ref, val_ref, tmp_ref):
+def route_kernel(mats_ref, *refs):
+    moved = refs[: MODES - 1]
+    obs_ref, slot_ref, most_ref, pay_ref, val_ref, one_ref, two_ref, tmp_ref = refs[MODES - 1 :]
     mode = lax.axis_index("cores")
     early = mode < MODES // 2
+    edge = jnp.where(jnp.logical_or(mode == 0, mode == MODES - 1), 1.0, 0.0)
+    one = jnp.where(iota(one_ref.shape, 0) == 0, edge, 0.0)
+    one_ref[...] = one + ((moved[0][...] + moved[1][...]) + moved[2][...])
+    two_ref[...] = (moved[3][...] + moved[4][...]) + (moved[5][...] + moved[6][...])
     apply(jnp.logical_not(early), mats_ref, two_ref, tmp_ref)
     one = one_ref[...]
     two = two_ref[...]
@@ -216,24 +222,52 @@
     turns_ref[0] = (most + SLOTS - 1) // SLOTS
 
 
-def unpacked(packed):
-    return jnp.concatenate([packed, pltpu.roll(packed, 64, 1)], axis=0)[:, :R]
+def halved(full, parity):
+    lane = iota((8, 128), 1)
+    even = jnp.where(lane < 80, pltpu.roll(full[16:24], 32, 1), pltpu.roll(full[32:40], 48, 1))
+    even = jnp.where(lane < 48, full[0:8], jnp.where(lane < 96, even, 0.0))
+    odd = jnp.where(lane < 64, pltpu.roll(full[24:32], 16, 1), pltpu.roll(full[40:48], 24, 1))
+    odd = jnp.where(lane < 40, pltpu.roll(full[8:16], 120, 1), jnp.where(lane < 72, odd, 0.0))
+    return jnp.where(parity == 0, even, odd)
+
+
+def whole(even, odd):
+    rows = [
+        even,
+        pltpu.roll(odd, 8, 1),
+        pltpu.roll(even, 96, 1),
+        pltpu.roll(odd, 112, 1),
+        pltpu.roll(even, 80, 1),
+        pltpu.roll(odd, 104, 1),
+    ]
+    full = jnp.concatenate(rows, axis=0)
+    block = iota((R, 128), 0) // 8
+    lane = iota((R, 128), 1)
+    upper = jnp.where(jnp.logical_and(lane >= 8 * block, lane < R), full, 0.0)
+    above = jnp.where(lane // 8 > block, upper, 0.0)
+    square = jnp.concatenate([above, jnp.zeros((128 - R, 128), F32)], axis=0)
+    return upper + square.T[:R]
 
 
 def gram_kernel(*refs, turn):
+    mode = lax.axis_index("cores")
+    parity = mode % 2
     if turn == 0:
         own_ref, other_ref, out_ref, prod_ref = refs
     else:
-        recv_ref, own_ref, other_ref, out_ref, sum_ref, prod_ref = refs
-    mode = lax.axis_index("cores")
-    mine = jnp.where(mode % 2 == turn % 2, 1.0, 0.0)
+        recv_ref, swap_ref, own_ref, other_ref, out_ref, sum_ref, prod_ref = refs
+    mine = jnp.where(parity == turn % 2, 1.0, 0.0)
     core = jnp.where(mine > 0.5, own_ref[...], other_ref[...])
     if turn == 0:
         prod = core
     else:
-        packed = jnp.sum(recv_ref[...], axis=0)
-        sum_ref[...] = packed
-        before = unpacked(packed)
+        one = jnp.sum(recv_ref[...], axis=0)
+        two = jnp.sum(swap_ref[...], axis=0)
+        even = jnp.where(parity == 0, one, two)
+        odd = jnp.where(parity == 0, two, one)
+        sum_ref[0:8] = even
+        sum_ref[8:16] = odd
+        before = whole(even, odd)[:, :R]
         for g in range(GROUPS):
             prod_ref[g * R : (g + 1) * R, :] = jnp.dot(
                 before, core[g * R : (g + 1) * R], preferred_element_type=F32, precision=HIGH
@@ -251,22 +285,23 @@
         )
         even = even + z[0:64]
         odd = odd + z[64:128]
-    low = even + pltpu.roll(odd, 64, 1)
-    high = pltpu.roll(even, 64, 1) + odd
-    packed = jnp.where(iota((24, 128), 1) < 64, low[0:24], high[24:48])
     live = jnp.where(mode // 2 == turn // 2, 1.0 / N, 0.0)
-    packed = packed * live
+    half = halved((even + pltpu.roll(odd, 64, 1)) * live, parity)
     for peer in range(out_ref.shape[0]):
-        out_ref[peer] = packed
+        out_ref[peer] = half
 
 
 def final_kernel(*refs):
     sums = refs[: MODES - 2]
-    recv_ref, own_ref, out_ref, prod_ref, block_ref = refs[MODES - 2 :]
+    recv_ref, swap_ref, own_ref, out_ref, prod_ref, block_ref = refs[MODES - 2 :]
     mode = lax.axis_index("cores")
-    every = [s[...] for s in sums] + [jnp.sum(recv_ref[...], axis=0)]
-    own = jnp.zeros((24, 128), F32)
-    prev = jnp.zeros((24, 128), F32)
+    parity = mode % 2
+    one = jnp.sum(recv_ref[...], axis=0)
+    two = jnp.sum(swap_ref[...], axis=0)
+    last = jnp.concatenate([jnp.where(parity == 0, one, two), jnp.where(parity == 0, two, one)], axis=0)
+    every = [s[...] for s in sums] + [last]
+    own = jnp.zeros((16, 128), F32)
+    prev = jnp.zeros((16, 128), F32)
     for t in range(MODES - 1):
         own = own + every[t] * jnp.where(mode == t, 1.0, 0.0)
         prev = prev + every[t] * jnp.where(mode == t + 1, 1.0, 0.0)
@@ -276,9 +311,7 @@
     side = jnp.where(lane == row + 64, 1.0, 0.0)
 
     def start(packed, absent):
-        full = jnp.concatenate([packed, pltpu.roll(packed, 64, 1)], axis=0)
-        full = jnp.where(lane < R, full, 0.0)
-        return full + eye * absent + side
+        return whole(packed[0:8], packed[8:16]) + eye * absent + side
 
     mats = [
         start(own, jnp.where(mode == MODES - 1, 1.0, 0.0)),
@@ -357,18 +390,14 @@
         scratch_shapes=[pltpu.VMEM((N, count), BF16)],
         compiler_params=pltpu.CompilerParams(vmem_limit_bytes=BIG),
         name="gather",
-    )(idx, table)
+    )(idx, pltpu.with_memory_space_constraint(table, pltpu.HBM))
 
     first = lax.axis_index("samp") * slab
     kept = lax.dynamic_slice_in_dim(table, first, slab, 0)
     base = kept.reshape(GROUPS, WIDE, R, R).transpose(0, 2, 1, 3)
     base = jnp.pad(base, ((0, 0), (0, 0), (0, 0), (0, 64 - R))).reshape(ROWS, LANES)
 
-    mode = lax.axis_index("cores")
-    edge = jnp.logical_or(mode == 0, mode == MODES - 1)
-    unit = jnp.broadcast_to((jnp.arange(R) == 0).astype(F32)[:, None], (R, count))
-    one = jnp.where(edge, unit, 0.0)
-    two = jnp.zeros((R, count), F32)
+    every = []
     for turn in range(MODES - 1):
         if turn > 0:
             sent = call(
@@ -378,18 +407,15 @@
                 name=f"hop{turn}",
             )(mats, moved)
         moved = lax.ppermute(sent, "cores", [(turn, turn + 1), (7 - turn, 6 - turn)])
-        if turn < 3:
-            one = one + moved
-        else:
-            two = two + moved
+        every.append(moved)
 
     pay, values = call(
         route_kernel,
         (shape(peers, FEATS, SLOTS), shape(FEATS, count)),
-        [vmem()] * 6,
-        [pltpu.VMEM((R, count), F32)],
+        [vmem()] * (MODES + 3),
+        [pltpu.VMEM((R, count), F32)] * 3,
         name="route",
-    )(mats, one, two, observed.reshape(1, count), slot, most)
+    )(mats, *every, observed.reshape(1, count), slot, most)
 
     def exchanged(block):
         return lax.all_to_all(block, "samp", 0, 0, tiled=True)
@@ -419,21 +445,22 @@
 
     _, updated = lax.while_loop(more, another, (jnp.int32(1), updated))
 
-    other = lax.ppermute(updated, "cores", [(i, i ^ 1) for i in range(MODES)])
+    siblings = [(i, i ^ 1) for i in range(MODES)]
+    other = lax.ppermute(updated, "cores", siblings)
 
     sums = []
     recv = None
     for turn in range(MODES - 1):
         odd = turn % 2 == 1
         size = 2 * peers if odd else peers
-        outs = [shape(size, 24, 128)] + ([shape(24, 128)] if turn else [])
+        outs = [shape(size, 8, 128)] + ([shape(16, 128)] if turn else [])
         res = call(
             functools.partial(gram_kernel, turn=turn),
             outs,
-            [vmem()] * (2 if turn == 0 else 3),
+            [vmem()] * (2 if turn == 0 else 4),
             [pltpu.VMEM((ROWS, LANES), F32)],
             name=f"gram{turn}",
-        )(*([] if turn == 0 else [recv]), updated, other)
+        )(*([] if turn == 0 else [recv, swap]), updated, other)
         if turn:
             sums.append(res[1])
         if odd:
@@ -448,14 +475,15 @@
             )
         else:
             recv = lax.all_to_all(res[0], "samp", 0, 0, tiled=True)
+        swap = lax.ppermute(recv, "cores", siblings)
 
     out = call(
         final_kernel,
         shape(ROWS, LANES),
-        [vmem()] * (MODES),
+        [vmem()] * (MODES + 1),
         [pltpu.VMEM((ROWS, LANES), F32), pltpu.VMEM((LANES, LANES), F32)],
         name="final",
-    )(*sums, recv, updated)
+    )(*sums, recv, swap, updated)
     out = out.reshape(GROUPS, R, WIDE, 64)[..., :R].transpose(0, 2, 1, 3)
     return out.reshape(1, slab, RR)
 

time: 210 us -> 186 us (0.89)
  Pallas kernels: 60.6 us -> 35.7 us
  waiting for transfers between devices: 27.6 us -> 36.6 us
  blocking collectives: 93.4 us -> 87.3 us
  local copies, waits for them, and re-layouts: 6.98 us -> 4.64 us
    pallas_call x6, Pallas kernels: 30.6 us -> 8.56 us  [on_device(): call(functools.partial(hop_kernel, second=turn >= MODES // 2), shape(R, c...]
    ppermute x1 -> x8, waiting for transfers between devices: 1.35 us -> 10.4 us  [the longest x7 9.04 us: on_device(): swap = lax.ppermute(recv, 'cores', siblings)]
    all_to_all x4, blocking collectives: 47.6 us -> 43.8 us  [on_device(): recv = lax.all_to_all(res[0], 'samp', 0, 0, tiled=True)]
    pallas_call x1, Pallas kernels: 7.5 us -> 3.92 us  [on_device(): call(route_kernel, (shape(peers, FEATS, SLOTS), shape(FEATS, count)), [vm...]
    unnamed x7 -> x5, local copies, waits for them, and re-layouts: 3.41 us -> 1.07 us
    all_to_all x3, blocking collectives: 45.8 us -> 43.5 us  [on_device(): lax.all_to_all(res[0], ('cores', 'samp'), 0, 0, axis_index_groups=groups,...]
  transfers between devices with their start and end apart: 9 -> 16, of which waited for: 5 -> 12; matrix products, arithmetic and copies ran while one was open for 1% -> 1% of each run, Pallas kernels for 0% -> 0%
where the time goes in v2:
time: 186 us; the launch traced here: 183 us
  blocking collectives  87.3 us (47%)
  waiting for transfers between devices  36.6 us (20%)
  Pallas kernels  35.7 us (19%)
  starting transfers between devices  17.2 us (9%)
  local copies, waits for them, and re-layouts  4.64 us (2%)
    all_to_all x4, blocking collectives, on_device(): recv = lax.all_to_all(res[0], 'samp', 0, 0, tiled=True)  43.8 us
    all_to_all x3, blocking collectives, on_device(): lax.all_to_all(res[0], ('cores', 'samp'), 0, 0, axis_index_groups=groups,...  43.5 us
    ppermute x7, waiting for transfers between devices, on_device(): lax.ppermute(sent, 'cores', [(turn, turn + 1), (7 - turn, 6 - turn)])  15 us
    all_to_all x1, waiting for transfers between devices, exchanged(): return lax.all_to_all(block, 'samp', 0, 0, tiled=True)  11.3 us
    ppermute x7, waiting for transfers between devices, on_device(): swap = lax.ppermute(recv, 'cores', siblings)  9.04 us
    pallas_call x6, Pallas kernels, on_device(): call(functools.partial(hop_kernel, second=turn >= MODES // 2), shape(R, c...  8.56 us
    pallas_call x1, Pallas kernels, on_device(): pl.pallas_call(functools.partial(gather_kernel, peers=peers), grid=(RR //...  8.27 us
    all_to_all x1, starting transfers between devices, exchanged(): return lax.all_to_all(block, 'samp', 0, 0, tiled=True)  7.88 us
  transfers between devices with their start and end apart: 16, of which 12 were waited for; matrix products, arithmetic and copies ran while one was open for 1% of the time, Pallas kernels for 0%

profile of v2, /device:TPU:16, one launch (start us, length us, event | category | flops | bytes accessed | tf_op | source)
XLA Modules:
  0.0 183.1 jit_solution(7657014591010066824)
XLA Ops:
  0.8 8.3 %gather.1 = (f32[2304,1024]{1,0:T(8,128)S(1)}, f32[48,1024]{1,0:T(8,128)S(1)}, s32[8,1024]{1,0:T(8,128)S(1)}, f32[8,128]{1,0:T(8,128)S(1)}) custom-call(s32[8,1024]{1,0:T(8,128)S(1)} %bitcast.15, f32[512,2304]{1,0:T(8,128)} %bitcast.17), custom_call_target="tpu_custom_call" | custom-call | tf_op jit(solution)/shard_map/gather/pallas_call | solution.py:376
  9.7 1.4 hop1.1
  11.8 1.4 hop2.1
  13.2 1.3 collective-permute-start.2
  14.5 8.9 %collective-permute-done.2.vec_ref.refs_2_ = f32[48,1024]{1,0:T(8,128)S(1)} collective-permute-done((f32[48,1024]{1,0:T(8,128)S(1)}, f32[48,1024]{1,0:T(8,128)S(1)}, u32[]{:S(2)}, u32[]{:S(2)}) %collective-permute-start.2) | collective-permute-done | bytes 196640 | tf_op jit(solution)/shard_map/ppermute | solution.py:409
  23.4 1.4 hop3.1
  24.8 1.9 %collective-permute-start.3 = (f32[48,1024]{1,0:T(8,128)S(1)}, f32[48,1024]{1,0:T(8,128)S(1)}, u32[]{:S(2)}, u32[]{:S(2)}) collective-permute-start(f32[48,1024]{1,0:T(8,128)S(1)} %hop3.1), channel_id=1, source_target_pairs={{48,64},{64,48},{49,65},{65,49},{50,66},{66,50},{51,67},{67,51},{5... | collective-permute-start | bytes 589832 | tf_op jit(solution)/shard_map/ppermute | solution.py:409
  26.7 5.1 %collective-permute-done.3.vec_ref.refs_3_ = f32[48,1024]{1,0:T(8,128)S(1)} collective-permute-done((f32[48,1024]{1,0:T(8,128)S(1)}, f32[48,1024]{1,0:T(8,128)S(1)}, u32[]{:S(2)}, u32[]{:S(2)}) %collective-permute-start.3) | collective-permute-done | bytes 196640 | tf_op jit(solution)/shard_map/ppermute | solution.py:409
  31.8 1.4 hop4.1
  33.2 1.3 collective-permute-start.4
  35.6 1.4 hop5.1
  37.7 1.5 hop6.1
  39.9 3.9 %route.1 = (f32[16,104,128]{2,1,0:T(8,128)}, f32[104,1024]{1,0:T(8,128)S(1)}) custom-call(f32[2304,1024]{1,0:T(8,128)S(1)} %get-tuple-element.64.mats_ref, f32[48,1024]{1,0:T(8,128)S(1)} %collective-permute-done.vec_ref.refs_0_, f32[48,1024]{1,0:T(8,128)S(1)} %collective-permute-done.1.vec_ref.refs_1_, ...), custom_call_target="tpu_custom_call" | custom-call | tf_op jit(solution)/shard_map/route/pallas_call | solution.py:412
  43.8 7.9 %all-to-all-start.1 = ((f32[16,104,128]{2,1,0:T(8,128)}), f32[16,104,128]{2,1,0:T(8,128)S(1)}, u32[]{:S(2)}, u32[]{:S(2)}) async-start(f32[16,104,128]{2,1,0:T(8,128)} %get-tuple-element.68), calls=%async_computation.1 | async-start | bytes 1703936 | tf_op jit(solution)/shard_map/all_to_all | solution.py:421
  54.8 11.3 %all-to-all-done.1.recv_ref = f32[16,104,128]{2,1,0:T(8,128)S(1)} async-done(((f32[16,104,128]{2,1,0:T(8,128)}), f32[16,104,128]{2,1,0:T(8,128)S(1)}, u32[]{:S(2)}, u32[]{:S(2)}) %all-to-all-start.1) | async-done | bytes 852000 | tf_op jit(solution)/shard_map/all_to_all | solution.py:421
  66.1 1.9 %collect.2 = (f32[384,256]{1,0:T(8,128)S(1)}, s32[1]{0:T(128)}) custom-call(f32[1]{0:T(128)} %bitcast.14.step_ref, f32[16,104,128]{2,1,0:T(8,128)S(1)} %all-to-all-done.1.recv_ref, f32[384,256]{1,0:T(8,128)S(1)} %reshape.26.base_ref), custom_call_target="tpu_custom_call" | custom-call | tf_op jit(solution)/shard_map/collect/pallas_call | solution.py:424
  68.6 2.1 %collective-permute-start.7 = (f32[384,256]{1,0:T(8,128)S(1)}, f32[384,256]{1,0:T(8,128)S(1)}, u32[]{:S(2)}, u32[]{:S(2)}) collective-permute-start(f32[384,256]{1,0:T(8,128)S(1)} %get-tuple-element.72.refs_0_.refs_2_.refs_8_), channel_id=1, source_target_pairs={{0,16},{16,0},{32,48},{48,32},{64,80},{80,64},{96,112},{112,96},{1... | collective-permute-start | bytes 1179656 | tf_op jit(solution)/shard_map/ppermute | solution.py:449
  70.7 1.3 collective-permute-done.7.refs_1_.refs_3_
  72.8 10.7 %all_to_all.46.refs_0_ = f32[16,8,128]{2,1,0:T(8,128)S(1)} all-to-all(f32[16,8,128]{2,1,0:T(8,128)S(1)} %gram0.1), channel_id=1, replica_groups=mesh['cores'=8,'samp'=16] {'samp'}, dimensions={0} | all-to-all | bytes 131072 | tf_op jit(solution)/shard_map/all_to_all | solution.py:477
  83.5 1.3 collective-permute-done.8.refs_1_
  86.0 18.4 %all_to_all.47.refs_0_ = f32[32,8,128]{2,1,0:T(8,128)S(1)} all-to-all(f32[32,8,128]{2,1,0:T(8,128)S(1)} %get-tuple-element.74), channel_id=1, replica_groups={{0,1,2,3,4,5,6,7,8,9,10,11,12,13,14,15,32,33,34,35,36,37,38,39,40,41,42..., dimensions={0} | all-to-all | bytes 262144 | tf_op jit(solution)/shard_map/all_to_all | solution.py:473
  104.4 1.3 collective-permute-done.9.refs_1_
  106.9 11.1 %all_to_all.48.refs_0_ = f32[16,8,128]{2,1,0:T(8,128)S(1)} all-to-all(f32[16,8,128]{2,1,0:T(8,128)S(1)} %get-tuple-element.76), channel_id=1, replica_groups=mesh['cores'=8,'samp'=16] {'samp'}, dimensions={0} | all-to-all | bytes 131072 | tf_op jit(solution)/shard_map/all_to_all | solution.py:477
  118.0 1.3 collective-permute-done.10.refs_1_
  120.4 12.0 %all_to_all.49.refs_0_ = f32[32,8,128]{2,1,0:T(8,128)S(1)} all-to-all(f32[32,8,128]{2,1,0:T(8,128)S(1)} %get-tuple-element.78), channel_id=1, replica_groups={{32,33,34,35,36,37,38,39,40,41,42,43,44,45,46,47,64,65,66,67,68,69,70,7..., dimensions={0} | all-to-all | bytes 262144 | tf_op jit(solution)/shard_map/all_to_all | solution.py:473
  132.5 1.3 collective-permute-done.11.refs_1_
  135.0 10.9 %all_to_all.50.refs_0_ = f32[16,8,128]{2,1,0:T(8,128)S(1)} all-to-all(f32[16,8,128]{2,1,0:T(8,128)S(1)} %get-tuple-element.80), channel_id=1, replica_groups=mesh['cores'=8,'samp'=16] {'samp'}, dimensions={0} | all-to-all | bytes 131072 | tf_op jit(solution)/shard_map/all_to_all | solution.py:477
  148.3 13.1 %all_to_all.51.refs_0_ = f32[32,8,128]{2,1,0:T(8,128)S(1)} all-to-all(f32[32,8,128]{2,1,0:T(8,128)S(1)} %get-tuple-element.82), channel_id=1, replica_groups={{64,65,66,67,68,69,70,71,72,73,74,75,76,77,78,79,96,97,98,99,100,101,10..., dimensions={0} | all-to-all | bytes 262144 | tf_op jit(solution)/shard_map/all_to_all | solution.py:473
  161.5 1.3 collective-permute-done.13.refs_1_
  164.0 11.1 %all_to_all.52.refs_6_ = f32[16,8,128]{2,1,0:T(8,128)S(1)} all-to-all(f32[16,8,128]{2,1,0:T(8,128)S(1)} %get-tuple-element.84), channel_id=1, replica_groups=mesh['cores'=8,'samp'=16] {'samp'}, dimensions={0} | all-to-all | bytes 131072 | tf_op jit(solution)/shard_map/all_to_all | solution.py:477
  175.1 1.3 collective-permute-done.14.refs_7_
  176.3 5.3 %final.1 = f32[384,256]{1,0:T(8,128)S(1)} custom-call(f32[16,128]{1,0:T(8,128)S(1)} %get-tuple-element.73.refs_0_, f32[16,128]{1,0:T(8,128)S(1)} %get-tuple-element.75.refs_1_, f32[16,128]{1,0:T(8,128)S(1)} %get-tuple-element.77.refs_2_, f32[16,128]{1,0:T(8,128)S(1)} %get-tuple-element.79.refs_3_, f32[16,128]{1,0:T(8,128)S(1)} %get-tuple-element.81.refs_4_, ...), custom_call_target="tpu_custom_call" | custom-call | tf_op jit(solution)/shard_map/final/pallas_call | solution.py:480
  (38 shorter events, 18.1 us)
Async XLA Ops:
  0.0 0.8 copy-start
  9.0 0.7 collective-permute-start
  11.1 0.7 collective-permute-start.1
  13.2 10.2 %collective-permute-start.2 = (f32[48,1024]{1,0:T(8,128)S(1)}, f32[48,1024]{1,0:T(8,128)S(1)}, u32[]{:S(2)}, u32[]{:S(2)}) collective-permute-start(f32[48,1024]{1,0:T(8,128)S(1)} %hop2.1), channel_id=1, source_target_pairs={{32,48},{80,64},{33,49},{81,65},{34,50},{82,66},{35,51},{83,67},{3... | collective-permute-start | bytes 589832 | tf_op jit(solution)/shard_map/ppermute | solution.py:409
  24.8 7.0 %collective-permute-start.3 = (f32[48,1024]{1,0:T(8,128)S(1)}, f32[48,1024]{1,0:T(8,128)S(1)}, u32[]{:S(2)}, u32[]{:S(2)}) collective-permute-start(f32[48,1024]{1,0:T(8,128)S(1)} %hop3.1), channel_id=1, source_target_pairs={{48,64},{64,48},{49,65},{65,49},{50,66},{66,50},{51,67},{67,51},{5... | collective-permute-start | bytes 589832 | tf_op jit(solution)/shard_map/ppermute | solution.py:409
  33.2 2.4 %collective-permute-start.4 = (f32[48,1024]{1,0:T(8,128)S(1)}, f32[48,1024]{1,0:T(8,128)S(1)}, u32[]{:S(2)}, u32[]{:S(2)}) collective-permute-start(f32[48,1024]{1,0:T(8,128)S(1)} %hop4.1), channel_id=1, source_target_pairs={{64,80},{48,32},{65,81},{49,33},{66,82},{50,34},{67,83},{51,35},{6... | collective-permute-start | bytes 589832 | tf_op jit(solution)/shard_map/ppermute | solution.py:409
  37.0 2.9 %copy-start.1 = (f32[1024]{0:T(1024)S(1)}, f32[1024]{0:T(1024)}, u32[]{:S(2)}) copy-start(f32[1024]{0:T(1024)} %param.8) | copy-start | bytes 12292
  37.0 0.7 collective-permute-start.5
  39.2 0.7 collective-permute-start.6
  43.8 22.3 %all-to-all-start.1 = ((f32[16,104,128]{2,1,0:T(8,128)}), f32[16,104,128]{2,1,0:T(8,128)S(1)}, u32[]{:S(2)}, u32[]{:S(2)}) async-start(f32[16,104,128]{2,1,0:T(8,128)} %get-tuple-element.68), calls=%async_computation.1 | async-start | bytes 1703936 | tf_op jit(solution)/shard_map/all_to_all | solution.py:421
  68.6 3.5 %collective-permute-start.7 = (f32[384,256]{1,0:T(8,128)S(1)}, f32[384,256]{1,0:T(8,128)S(1)}, u32[]{:S(2)}, u32[]{:S(2)}) collective-permute-start(f32[384,256]{1,0:T(8,128)S(1)} %get-tuple-element.72.refs_0_.refs_2_.refs_8_), channel_id=1, source_target_pairs={{0,16},{16,0},{32,48},{48,32},{64,80},{80,64},{96,112},{112,96},{1... | collective-permute-start | bytes 1179656 | tf_op jit(solution)/shard_map/ppermute | solution.py:449
  83.5 1.3 collective-permute-start.8
  104.4 1.3 collective-permute-start.9
  118.0 1.3 collective-permute-start.10
  132.5 1.3 collective-permute-start.11
  145.9 1.3 collective-permute-start.12
  161.5 1.3 collective-permute-start.13
  175.1 1.3 collective-permute-start.14

commit v3 on v2

--- a/solution.py
+++ b/solution.py
@@ -11,12 +11,13 @@
 N = 512
 MODES = 8
 RR = R * R
-GROUPS = 8
-WIDE = 4
+GROUPS = 4
+WIDE = 8
 ROWS = GROUPS * R
-LANES = WIDE * 64
+LANES = WIDE * R
 FEATS = 104
 SLOTS = 128
+WAYS = 4
 HIGH = lax.Precision.HIGHEST
 F32 = jnp.float32
 BF16 = jnp.bfloat16
@@ -203,115 +204,130 @@
     lane_of = loc - row_of * WIDE
     count = loc.shape[1]
 
-    def picked(x, key, n, pad):
+    def picked(x, key, n):
         hi = x.astype(BF16).astype(F32)
         lo = x - hi
-        tail = [jnp.zeros((pad, count), BF16)] if pad else []
         his, los = [], []
         for i in range(n):
             here = key == i
-            his += [jnp.where(here, hi, 0.0).astype(BF16)] + tail
-            los += [jnp.where(here, lo, 0.0).astype(BF16)] + tail
+            his += [jnp.where(here, hi, 0.0).astype(BF16)]
+            los += [jnp.where(here, lo, 0.0).astype(BF16)]
         return jnp.concatenate(his, axis=0), jnp.concatenate(los, axis=0)
 
-    xh, xl = picked(left, row_of, GROUPS, 0)
-    yh, yl = picked(right, lane_of, WIDE, 16)
+    xh, xl = picked(left, row_of, GROUPS)
+    yh, yl = picked(right, lane_of, WIDE)
     grad = dot_lanes(xh, yh) + (dot_lanes(xh, yl) + dot_lanes(xl, yh))
     out_ref[...] = base_ref[...] - step_ref[0] * grad
     most = jnp.max(recv_ref[:, 97, :]).astype(jnp.int32)
     turns_ref[0] = (most + SLOTS - 1) // SLOTS
 
 
-def halved(full, parity):
-    lane = iota((8, 128), 1)
-    even = jnp.where(lane < 80, pltpu.roll(full[16:24], 32, 1), pltpu.roll(full[32:40], 48, 1))
-    even = jnp.where(lane < 48, full[0:8], jnp.where(lane < 96, even, 0.0))
-    odd = jnp.where(lane < 64, pltpu.roll(full[24:32], 16, 1), pltpu.roll(full[40:48], 24, 1))
-    odd = jnp.where(lane < 40, pltpu.roll(full[8:16], 120, 1), jnp.where(lane < 72, odd, 0.0))
-    return jnp.where(parity == 0, even, odd)
-
-
-def whole(even, odd):
-    rows = [
-        even,
-        pltpu.roll(odd, 8, 1),
-        pltpu.roll(even, 96, 1),
-        pltpu.roll(odd, 112, 1),
-        pltpu.roll(even, 80, 1),
-        pltpu.roll(odd, 104, 1),
-    ]
-    full = jnp.concatenate(rows, axis=0)
-    block = iota((R, 128), 0) // 8
-    lane = iota((R, 128), 1)
-    upper = jnp.where(jnp.logical_and(lane >= 8 * block, lane < R), full, 0.0)
-    above = jnp.where(lane // 8 > block, upper, 0.0)
-    square = jnp.concatenate([above, jnp.zeros((128 - R, 128), F32)], axis=0)
-    return upper + square.T[:R]
-
-
-def gram_kernel(*refs, turn):
+def arrange_kernel(*refs):
+    own = refs[:WAYS]
+    other = refs[WAYS : 2 * WAYS]
+    outs = refs[2 * WAYS :]
+    even_first = jnp.where(lax.axis_index("cores") % 2 == 0, 1.0, 0.0)
+    for w in range(WAYS):
+        rows = slice(w * ROWS, (w + 1) * ROWS)
+        mine = own[w][...]
+        theirs = other[w][...]
+        for k in range(2):
+            flag = even_first if k == 0 else 1.0 - even_first
+            core = jnp.where(flag > 0.5, mine, theirs)
+            outs[4 * k][rows, :], outs[4 * k + 1][rows, :] = halves(core)
+            outs[4 * k + 2][:, rows], outs[4 * k + 3][:, rows] = halves(core.T)
+
+
+def three(a, b):
+    (ah, al), (bh, bl) = a, b
+    mul = functools.partial(jnp.dot, preferred_element_type=F32)
+    return mul(ah, bh) + (mul(ah, bl) + mul(al, bh))
+
+
+def packed_of(full):
+    lane = iota((24, 128), 1)
+    return jnp.where(lane < 64, full[0:24], pltpu.roll(full[24:48], 64, 1))
+
+
+def whole(packed):
+    both = jnp.concatenate([packed, pltpu.roll(packed, 64, 1)], axis=0)
+    return jnp.where(iota((R, 128), 1) < R, both, 0.0)
+
+
+def pulled(before, core, prod_ref):
+    high, low, high_t, low_t = core
+    if before is None:
+        prod = (high[...], low[...])
+    else:
+        weights = halves(before[:, :R])
+        for g in range(WAYS * GROUPS):
+            rows = slice(g * R, (g + 1) * R)
+            prod_ref[rows, :] = three(weights, (high[rows, :], low[rows, :]))
+        prod = halves(prod_ref[...])
+    total = jnp.zeros((R, 256), F32)
+    for part, slices in ((0, range(5)), (128, range(5, WIDE))):
+        cols = slice(part, part + 256)
+        z = three((high_t[cols, :], low_t[cols, :]), (prod[0][:, cols], prod[1][:, cols]))
+        for h in slices:
+            at = h * R - part
+            block = z[at : at + R]
+            total = total + (pltpu.roll(block, 256 - at, 1) if at else block)
+    return jnp.where(iota((R, 128), 1) < R, total[:, :128], 0.0) * (1.0 / N)
+
+
+def pair_kernel(*refs, pair):
+    last = pair == MODES // 2 - 1
+    refs = list(refs)
+    recv_ref = refs.pop(0) if pair else None
+    saved = [refs.pop(0) for _ in range(pair)] if last else []
+    even = [refs.pop(0) for _ in range(4)]
+    odd = None if last else [refs.pop(0) for _ in range(4)]
+    prod_ref = refs.pop()
+    if pair:
+        sum_ref = refs.pop()
+        arrived = jnp.sum(recv_ref[...], axis=0)
+        sum_ref[...] = arrived
+        before = whole(arrived)
+    else:
+        before = None
+    chip = lax.axis_index("cores") // 2
+    live = jnp.where(chip == pair, 1.0, 0.0)
+    middle = pulled(before, even, prod_ref) * live
+    kept = packed_of(middle)
+    if last:
+        for s in saved:
+            kept = kept + s[...]
+        refs[0][...] = kept
+        return
+    out_ref, save_ref = refs
+    save_ref[...] = kept
+    packed = packed_of(pulled(middle, odd, prod_ref))
+    for peer in range(out_ref.shape[0]):
+        out_ref[peer] = packed
+
+
+def final_kernel(*refs):
+    pairs = MODES // 2 - 1
+    sums = refs[:pairs]
+    parts = refs[pairs : pairs + WAYS]
+    own_ref, out_ref, prod_ref, block_ref = refs[pairs + WAYS :]
     mode = lax.axis_index("cores")
-    parity = mode % 2
-    if turn == 0:
-        own_ref, other_ref, out_ref, prod_ref = refs
-    else:
-        recv_ref, swap_ref, own_ref, other_ref, out_ref, sum_ref, prod_ref = refs
-    mine = jnp.where(parity == turn % 2, 1.0, 0.0)
-    core = jnp.where(mine > 0.5, own_ref[...], other_ref[...])
-    if turn == 0:
-        prod = core
-    else:
-        one = jnp.sum(recv_ref[...], axis=0)
-        two = jnp.sum(swap_ref[...], axis=0)
-        even = jnp.where(parity == 0, one, two)
-        odd = jnp.where(parity == 0, two, one)
-        sum_ref[0:8] = even
-        sum_ref[8:16] = odd
-        before = whole(even, odd)[:, :R]
-        for g in range(GROUPS):
-            prod_ref[g * R : (g + 1) * R, :] = jnp.dot(
-                before, core[g * R : (g + 1) * R], preferred_element_type=F32, precision=HIGH
-            )
-        prod = prod_ref[...]
-    even = jnp.zeros((64, 128), F32)
-    odd = jnp.zeros((64, 128), F32)
-    for part in range(2):
-        z = lax.dot_general(
-            core[:, part * 128 : (part + 1) * 128],
-            prod[:, part * 128 : (part + 1) * 128],
-            (((0,), (0,)), ((), ())),
-            preferred_element_type=F32,
-            precision=HIGH,
-        )
-        even = even + z[0:64]
-        odd = odd + z[64:128]
-    live = jnp.where(mode // 2 == turn // 2, 1.0 / N, 0.0)
-    half = halved((even + pltpu.roll(odd, 64, 1)) * live, parity)
-    for peer in range(out_ref.shape[0]):
-        out_ref[peer] = half
-
-
-def final_kernel(*refs):
-    sums = refs[: MODES - 2]
-    recv_ref, swap_ref, own_ref, out_ref, prod_ref, block_ref = refs[MODES - 2 :]
-    mode = lax.axis_index("cores")
-    parity = mode % 2
-    one = jnp.sum(recv_ref[...], axis=0)
-    two = jnp.sum(swap_ref[...], axis=0)
-    last = jnp.concatenate([jnp.where(parity == 0, one, two), jnp.where(parity == 0, two, one)], axis=0)
-    every = [s[...] for s in sums] + [last]
-    own = jnp.zeros((16, 128), F32)
-    prev = jnp.zeros((16, 128), F32)
-    for t in range(MODES - 1):
-        own = own + every[t] * jnp.where(mode == t, 1.0, 0.0)
-        prev = prev + every[t] * jnp.where(mode == t + 1, 1.0, 0.0)
+    chip = mode // 2
+    first = jnp.where(mode % 2 == 0, 1.0, 0.0)
+    second = 1.0 - first
+    level = (parts[0][...] + parts[1][...]) + (parts[2][...] + parts[3][...])
+    own = level * first
+    prev = level * second
+    for p in range(pairs):
+        own = own + sums[p][...] * jnp.where(chip == p, second, 0.0)
+        prev = prev + sums[p][...] * jnp.where(chip == p + 1, first, 0.0)
     row = iota((R, 128), 0)
     lane = iota((R, 128), 1)
     eye = jnp.where(lane == row, 1.0, 0.0)
     side = jnp.where(lane == row + 64, 1.0, 0.0)
 
     def start(packed, absent):
-        return whole(packed[0:8], packed[8:16]) + eye * absent + side
+        return whole(packed) + eye * absent + side
 
     mats = [
         start(own, jnp.where(mode == MODES - 1, 1.0, 0.0)),
@@ -331,9 +347,9 @@
     carry = tri[1][:, :R]
     inv = jnp.where(lane >= 64, tri[0], 0.0)
     turned = pltpu.roll(inv, 64, 1)
-    block_ref[...] = jnp.zeros((LANES, LANES), F32)
+    wide = jnp.concatenate([jnp.where(lane < R, turned, 0.0), jnp.zeros((R, LANES - 128), F32)], axis=1)
     for h in range(WIDE):
-        block_ref[h * 64 : h * 64 + R, (h // 2) * 128 : (h // 2 + 1) * 128] = inv if h % 2 else turned
+        block_ref[h * R : (h + 1) * R, :] = pltpu.roll(wide, h * R, 1) if h else wide
     for g in range(GROUPS):
         prod_ref[g * R : (g + 1) * R, :] = jnp.dot(
             carry, own_ref[g * R : (g + 1) * R, :], preferred_element_type=F32, precision=HIGH
@@ -395,7 +411,7 @@
     first = lax.axis_index("samp") * slab
     kept = lax.dynamic_slice_in_dim(table, first, slab, 0)
     base = kept.reshape(GROUPS, WIDE, R, R).transpose(0, 2, 1, 3)
-    base = jnp.pad(base, ((0, 0), (0, 0), (0, 0), (0, 64 - R))).reshape(ROWS, LANES)
+    base = base.reshape(ROWS, LANES)
 
     every = []
     for turn in range(MODES - 1):
@@ -445,46 +461,63 @@
 
     _, updated = lax.while_loop(more, another, (jnp.int32(1), updated))
 
-    siblings = [(i, i ^ 1) for i in range(MODES)]
-    other = lax.ppermute(updated, "cores", siblings)
-
-    sums = []
+    side = int(peers**0.5)
+
+    def along(mode, peer, by):
+        z, x = peer // side, peer % side
+        return z * side + (x + by) % side if mode % 2 == 0 else (z + by) % side * side + x
+
+    ring = [
+        [(m * peers + p, m * peers + along(m, p, by)) for m in range(MODES) for p in range(peers)]
+        for by in range(1, side)
+    ]
+    level = [[(p, along(1, p, by)) for p in range(peers)] for by in range(1, side)]
+    siblings = [(m, m ^ 1) for m in range(MODES)]
+    own = [updated] + [lax.ppermute(updated, ("cores", "samp"), pairs) for pairs in ring]
+    other = [lax.ppermute(o, "cores", siblings) for o in own]
+    tall = shape(WAYS * ROWS, LANES, dtype=BF16)
+    flat = shape(LANES, WAYS * ROWS, dtype=BF16)
+    arranged = call(arrange_kernel, [tall, tall, flat, flat] * 2, [vmem()] * 8, name="arrange")(*own, *other)
+    even, odd = list(arranged[:4]), list(arranged[4:])
+
+    saved, sums = [], []
     recv = None
-    for turn in range(MODES - 1):
-        odd = turn % 2 == 1
-        size = 2 * peers if odd else peers
-        outs = [shape(size, 8, 128)] + ([shape(16, 128)] if turn else [])
+    for pair in range(MODES // 2):
+        last = pair == MODES // 2 - 1
+        ins = ([recv] if pair else []) + (saved if last else []) + even + ([] if last else odd)
+        outs = [shape(24, 128)] if last else [shape(2 * peers, 24, 128), shape(24, 128)]
+        if pair:
+            outs.append(shape(24, 128))
         res = call(
-            functools.partial(gram_kernel, turn=turn),
+            functools.partial(pair_kernel, pair=pair),
             outs,
-            [vmem()] * (2 if turn == 0 else 4),
-            [pltpu.VMEM((ROWS, LANES), F32)],
-            name=f"gram{turn}",
-        )(*([] if turn == 0 else [recv, swap]), updated, other)
-        if turn:
-            sums.append(res[1])
-        if odd:
-            here = turn // 2
+            [vmem()] * len(ins),
+            [pltpu.VMEM((WAYS * ROWS, LANES), F32)],
+            name=f"pair{pair}",
+        )(*ins)
+        if pair:
+            sums.append(res[-1])
+        if last:
+            parts = [res[0]] + [lax.ppermute(res[0], "samp", pairs) for pairs in level]
+        else:
+            saved.append(res[1])
             groups = []
-            for c in (here, here + 2):
+            for c in (pair, pair + 2):
                 for h in range(2):
-                    pair = [(2 * (c % 4) + h), (2 * ((c + 1) % 4) + h)]
-                    groups.append([m * peers + j for m in pair for j in range(peers)])
+                    both = [2 * (c % 4) + h, 2 * ((c + 1) % 4) + h]
+                    groups.append([m * peers + j for m in both for j in range(peers)])
             recv = lax.all_to_all(
                 res[0], ("cores", "samp"), 0, 0, axis_index_groups=groups, tiled=True
             )
-        else:
-            recv = lax.all_to_all(res[0], "samp", 0, 0, tiled=True)
-        swap = lax.ppermute(recv, "cores", siblings)
 
     out = call(
         final_kernel,
         shape(ROWS, LANES),
-        [vmem()] * (MODES + 1),
+        [vmem()] * (MODES // 2 - 1 + WAYS + 1),
         [pltpu.VMEM((ROWS, LANES), F32), pltpu.VMEM((LANES, LANES), F32)],
         name="final",
-    )(*sums, recv, swap, updated)
-    out = out.reshape(GROUPS, R, WIDE, 64)[..., :R].transpose(0, 2, 1, 3)
+    )(*sums, *parts, updated)
+    out = out.reshape(GROUPS, R, WIDE, R).transpose(0, 2, 1, 3)
     return out.reshape(1, slab, RR)
 
 

time: 186 us -> 161 us (0.87)
  blocking collectives: 87.3 us -> 50.6 us
  starting transfers between devices: 17.2 us -> 25.6 us
  Pallas kernels: 35.7 us -> 40 us
    all_to_all x4 -> x0, blocking collectives: 43.8 us -> none  [on_device(): recv = lax.all_to_all(res[0], 'samp', 0, 0, tiled=True)]
    ppermute x8 -> x10, starting transfers between devices: 2.15 us -> 10.6 us  [the longest x3 4.26 us: on_device(): parts = [res[0]] + [lax.ppermute(res[0], 'samp', pairs) for pairs in level]]
    all_to_all x3, blocking collectives: 43.5 us -> 50.6 us  [on_device(): lax.all_to_all(res[0], ('cores', 'samp'), 0, 0, axis_index_groups=groups,...]
    pallas_call x8 -> x6, Pallas kernels: 13.1 us -> 17.1 us  [the longest x4 10.4 us: on_device(): call(functools.partial(pair_kernel, pair=pair), outs, [vmem()] * len(ins)...]
    ppermute x8 -> x10, waiting for transfers between devices: 10.4 us -> 10.4 us  [the longest x3 6.38 us: on_device(): lax.ppermute(updated, ('cores', 'samp'), pairs)]
  transfers between devices with their start and end apart: 16 -> 18, of which waited for: 12 -> 11; matrix products, arithmetic and copies ran while one was open for 1% -> 1% of each run, Pallas kernels for 0% -> 0%
where the time goes in v3:
time: 161 us; the launch traced here: 159 us
  blocking collectives  50.6 us (31%)
  Pallas kernels  40 us (25%)
  waiting for transfers between devices  37 us (23%)
  starting transfers between devices  25.6 us (16%)
  local copies, waits for them, and re-layouts  4.21 us (3%)
    all_to_all x3, blocking collectives, on_device(): lax.all_to_all(res[0], ('cores', 'samp'), 0, 0, axis_index_groups=groups,...  50.6 us
    ppermute x7, waiting for transfers between devices, on_device(): lax.ppermute(sent, 'cores', [(turn, turn + 1), (7 - turn, 6 - turn)])  15 us
    all_to_all x1, waiting for transfers between devices, exchanged(): return lax.all_to_all(block, 'samp', 0, 0, tiled=True)  11.7 us
    pallas_call x4, Pallas kernels, on_device(): call(functools.partial(pair_kernel, pair=pair), outs, [vmem()] * len(ins)...  10.4 us
    pallas_call x6, Pallas kernels, on_device(): call(functools.partial(hop_kernel, second=turn >= MODES // 2), shape(R, c...  8.56 us
    pallas_call x1, Pallas kernels, on_device(): pl.pallas_call(functools.partial(gather_kernel, peers=peers), grid=(RR //...  8.27 us
    all_to_all x1, starting transfers between devices, exchanged(): return lax.all_to_all(block, 'samp', 0, 0, tiled=True)  7.88 us
    ppermute x7, starting transfers between devices, on_device(): lax.ppermute(sent, 'cores', [(turn, turn + 1), (7 - turn, 6 - turn)])  7.21 us
  transfers between devices with their start and end apart: 18, of which 11 were waited for; matrix products, arithmetic and copies ran while one was open for 1% of the time, Pallas kernels for 0%

profile of v3, /device:TPU:16, one launch (start us, length us, event | category | flops | bytes accessed | tf_op | source)
XLA Modules:
  0.0 159.0 jit_solution(579093669018282452)
XLA Ops:
  0.8 8.3 %gather.1 = (f32[2304,1024]{1,0:T(8,128)S(1)}, f32[48,1024]{1,0:T(8,128)S(1)}, s32[8,1024]{1,0:T(8,128)S(1)}, f32[8,128]{1,0:T(8,128)S(1)}) custom-call(s32[8,1024]{1,0:T(8,128)S(1)} %bitcast.16, f32[512,2304]{1,0:T(8,128)} %bitcast.18), custom_call_target="tpu_custom_call" | custom-call | tf_op jit(solution)/shard_map/gather/pallas_call | solution.py:392
  9.7 1.4 hop1.1
  11.8 1.4 hop2.1
  13.2 1.3 collective-permute-start.2
  14.5 8.9 %collective-permute-done.2.vec_ref.refs_2_ = f32[48,1024]{1,0:T(8,128)S(1)} collective-permute-done((f32[48,1024]{1,0:T(8,128)S(1)}, f32[48,1024]{1,0:T(8,128)S(1)}, u32[]{:S(2)}, u32[]{:S(2)}) %collective-permute-start.2) | collective-permute-done | bytes 196640 | tf_op jit(solution)/shard_map/ppermute | solution.py:425
  23.4 1.4 hop3.1
  24.8 1.9 %collective-permute-start.3 = (f32[48,1024]{1,0:T(8,128)S(1)}, f32[48,1024]{1,0:T(8,128)S(1)}, u32[]{:S(2)}, u32[]{:S(2)}) collective-permute-start(f32[48,1024]{1,0:T(8,128)S(1)} %hop3.1), channel_id=1, source_target_pairs={{48,64},{64,48},{49,65},{65,49},{50,66},{66,50},{51,67},{67,51},{5... | collective-permute-start | bytes 589832 | tf_op jit(solution)/shard_map/ppermute | solution.py:425
  26.7 5.1 %collective-permute-done.3.vec_ref.refs_3_ = f32[48,1024]{1,0:T(8,128)S(1)} collective-permute-done((f32[48,1024]{1,0:T(8,128)S(1)}, f32[48,1024]{1,0:T(8,128)S(1)}, u32[]{:S(2)}, u32[]{:S(2)}) %collective-permute-start.3) | collective-permute-done | bytes 196640 | tf_op jit(solution)/shard_map/ppermute | solution.py:425
  31.8 1.4 hop4.1
  33.2 1.3 collective-permute-start.4
  34.5 1.0 collective-permute-done.4.vec_ref.refs_4_
  35.6 1.4 hop5.1
  37.7 1.5 hop6.1
  39.9 3.9 %route.1 = (f32[16,104,128]{2,1,0:T(8,128)}, f32[104,1024]{1,0:T(8,128)S(1)}) custom-call(f32[2304,1024]{1,0:T(8,128)S(1)} %get-tuple-element.70.mats_ref, f32[48,1024]{1,0:T(8,128)S(1)} %collective-permute-done.vec_ref.refs_0_, f32[48,1024]{1,0:T(8,128)S(1)} %collective-permute-done.1.vec_ref.refs_1_, ...), custom_call_target="tpu_custom_call" | custom-call | tf_op jit(solution)/shard_map/route/pallas_call | solution.py:428
  43.8 7.9 %all-to-all-start.1 = ((f32[16,104,128]{2,1,0:T(8,128)}), f32[16,104,128]{2,1,0:T(8,128)S(1)}, u32[]{:S(2)}, u32[]{:S(2)}) async-start(f32[16,104,128]{2,1,0:T(8,128)} %get-tuple-element.74), calls=%async_computation.1 | async-start | bytes 1703936 | tf_op jit(solution)/shard_map/all_to_all | solution.py:437
  54.4 11.7 %all-to-all-done.1.recv_ref = f32[16,104,128]{2,1,0:T(8,128)S(1)} async-done(((f32[16,104,128]{2,1,0:T(8,128)}), f32[16,104,128]{2,1,0:T(8,128)S(1)}, u32[]{:S(2)}, u32[]{:S(2)}) %all-to-all-start.1) | async-done | bytes 852000 | tf_op jit(solution)/shard_map/all_to_all | solution.py:437
  66.1 2.1 %collect.2 = (f32[192,384]{1,0:T(8,128)S(1)}, s32[1]{0:T(128)}) custom-call(f32[1]{0:T(128)} %bitcast.15.step_ref, f32[16,104,128]{2,1,0:T(8,128)S(1)} %all-to-all-done.1.recv_ref, f32[192,384]{1,0:T(8,128)S(1)} %reshape.26.base_ref), custom_call_target="tpu_custom_call" | custom-call | tf_op jit(solution)/shard_map/collect/pallas_call | solution.py:440
  70.4 1.9 %collective-permute-start.9 = (f32[192,384]{1,0:T(8,128)S(1)}, f32[192,384]{1,0:T(8,128)S(1)}, u32[]{:S(2)}, u32[]{:S(2)}) collective-permute-start(f32[192,384]{1,0:T(8,128)S(1)} %get-tuple-element.78.refs_0_.refs_7_), channel_id=1, source_target_pairs={{0,3},{1,0},{2,1},{3,2},{4,7},{5,4},{6,5},{7,6},{8,11},{9,8},{10,9... | collective-permute-start | bytes 884744 | tf_op jit(solution)/shard_map/ppermute | solution.py:476
  72.4 1.3 collective-permute-start.10
  73.7 6.4 %collective-permute-done.7.refs_1_ = f32[192,384]{1,0:T(8,128)S(1)} collective-permute-done((f32[192,384]{1,0:T(8,128)S(1)}, f32[192,384]{1,0:T(8,128)S(1)}, u32[]{:S(2)}, u32[]{:S(2)}) %collective-permute-start.7) | collective-permute-done | bytes 294944 | tf_op jit(solution)/shard_map/ppermute | solution.py:476
  83.0 1.4 arrange.1
  84.4 2.4 %pair0.1 = (f32[32,24,128]{2,1,0:T(8,128)S(1)}, f32[24,128]{1,0:T(8,128)S(1)}) custom-call(bf16[768,384]{1,0:T(8,128)(2,1)S(1)} %get-tuple-element.79.refs_0_.refs_1_.refs_4_, bf16[768,384]{1,0:T(8,128)(2,1)S(1)} %get-tuple-element.80.refs_1_.refs_2_.refs_5_, bf16[384,768]{1,0:T(8,128)(2,1)S(1)} %get-tuple-element.81.refs_2_.refs_3_.refs_6_, ...), custom_call_target="tpu_custom_call" | custom-call | tf_op jit(solution)/shard_map/pair0/pallas_call | solution.py:491
  86.8 22.5 %all_to_all.26.refs_0_ = f32[32,24,128]{2,1,0:T(8,128)S(1)} all-to-all(f32[32,24,128]{2,1,0:T(8,128)S(1)} %get-tuple-element.87), channel_id=1, replica_groups={{0,1,2,3,4,5,6,7,8,9,10,11,12,13,14,15,32,33,34,35,36,37,38,39,40,41,42..., dimensions={0} | all-to-all | bytes 786432 | tf_op jit(solution)/shard_map/all_to_all | solution.py:509
  109.3 3.2 %pair1.1 = (f32[32,24,128]{2,1,0:T(8,128)S(1)}, f32[24,128]{1,0:T(8,128)S(1)}, f32[24,128]{1,0:T(8,128)S(1)}) custom-call(f32[32,24,128]{2,1,0:T(8,128)S(1)} %all_to_all.26.refs_0_, bf16[768,384]{1,0:T(8,128)(2,1)S(1)} %get-tuple-element.79.refs_0_.refs_1_.refs_4_, bf16[768,384]{1,0:T(8,128)(2,1)S(1)} %get-tuple-element.80.refs_1_.refs_2_.refs_5_, ...), custom_call_target="tpu_custom_call" | custom-call | tf_op jit(solution)/shard_map/pair1/pallas_call | solution.py:491
  112.5 14.0 %all_to_all.27.refs_0_ = f32[32,24,128]{2,1,0:T(8,128)S(1)} all-to-all(f32[32,24,128]{2,1,0:T(8,128)S(1)} %get-tuple-element.89), channel_id=1, replica_groups={{32,33,34,35,36,37,38,39,40,41,42,43,44,45,46,47,64,65,66,67,68,69,70,7..., dimensions={0} | all-to-all | bytes 786432 | tf_op jit(solution)/shard_map/all_to_all | solution.py:509
  126.5 3.2 %pair2.1 = (f32[32,24,128]{2,1,0:T(8,128)S(1)}, f32[24,128]{1,0:T(8,128)S(1)}, f32[24,128]{1,0:T(8,128)S(1)}) custom-call(f32[32,24,128]{2,1,0:T(8,128)S(1)} %all_to_all.27.refs_0_, bf16[768,384]{1,0:T(8,128)(2,1)S(1)} %get-tuple-element.79.refs_0_.refs_1_.refs_4_, bf16[768,384]{1,0:T(8,128)(2,1)S(1)} %get-tuple-element.80.refs_1_.refs_2_.refs_5_, ...), custom_call_target="tpu_custom_call" | custom-call | tf_op jit(solution)/shard_map/pair2/pallas_call | solution.py:491
  129.7 14.1 %all_to_all.28.refs_0_ = f32[32,24,128]{2,1,0:T(8,128)S(1)} all-to-all(f32[32,24,128]{2,1,0:T(8,128)S(1)} %get-tuple-element.91), channel_id=1, replica_groups={{64,65,66,67,68,69,70,71,72,73,74,75,76,77,78,79,96,97,98,99,100,101,10..., dimensions={0} | all-to-all | bytes 786432 | tf_op jit(solution)/shard_map/all_to_all | solution.py:509
  143.8 1.7 %pair3.1 = (f32[24,128]{1,0:T(8,128)S(1)}, f32[24,128]{1,0:T(8,128)S(1)}) custom-call(f32[32,24,128]{2,1,0:T(8,128)S(1)} %all_to_all.28.refs_0_, f32[24,128]{1,0:T(8,128)S(1)} %get-tuple-element.92.refs_1_, f32[24,128]{1,0:T(8,128)S(1)} %get-tuple-element.93.refs_2_, f32[24,128]{1,0:T(8,128)S(1)} %get-tuple-element.94.refs_3_, ...), custom_call_target="tpu_custom_call" | custom-call | tf_op jit(solution)/shard_map/pair3/pallas_call | solution.py:491
  146.0 2.6 %collective-permute-start.15 = (f32[24,128]{1,0:T(8,128)S(1)}, f32[24,128]{1,0:T(8,128)S(1)}, u32[]{:S(2)}, u32[]{:S(2)}) collective-permute-start(f32[24,128]{1,0:T(8,128)S(1)} %get-tuple-element.96.refs_3_), channel_id=1, source_target_pairs={{0,8},{1,9},{2,10},{3,11},{4,12},{5,13},{6,14},{7,15},{8,0},{9,1},... | collective-permute-start | bytes 36872 | tf_op jit(solution)/shard_map/ppermute | solution.py:501
  148.6 1.1 collective-permute-start.16
  151.2 1.1 collective-permute-done.16.refs_6_
  152.3 5.3 %final.1 = f32[192,384]{1,0:T(8,128)S(1)} custom-call(f32[24,128]{1,0:T(8,128)S(1)} %get-tuple-element.88.refs_0_, f32[24,128]{1,0:T(8,128)S(1)} %get-tuple-element.90.refs_1_, f32[24,128]{1,0:T(8,128)S(1)} %get-tuple-element.95.refs_2_, f32[24,128]{1,0:T(8,128)S(1)} %get-tuple-element.96.refs_3_, f32[24,128]{1,0:T(8,128)S(1)} %collective-permute-done.14.refs_4_, ...), custom_call_target="tpu_custom_call" | custom-call | tf_op jit(solution)/shard_map/final/pallas_call | solution.py:513
  (34 shorter events, 14.0 us)
Async XLA Ops:
  0.0 0.8 copy-start
  9.0 0.7 collective-permute-start
  11.1 0.7 collective-permute-start.1
  13.2 10.2 %collective-permute-start.2 = (f32[48,1024]{1,0:T(8,128)S(1)}, f32[48,1024]{1,0:T(8,128)S(1)}, u32[]{:S(2)}, u32[]{:S(2)}) collective-permute-start(f32[48,1024]{1,0:T(8,128)S(1)} %hop2.1), channel_id=1, source_target_pairs={{32,48},{80,64},{33,49},{81,65},{34,50},{82,66},{35,51},{83,67},{3... | collective-permute-start | bytes 589832 | tf_op jit(solution)/shard_map/ppermute | solution.py:425
  24.8 7.0 %collective-permute-start.3 = (f32[48,1024]{1,0:T(8,128)S(1)}, f32[48,1024]{1,0:T(8,128)S(1)}, u32[]{:S(2)}, u32[]{:S(2)}) collective-permute-start(f32[48,1024]{1,0:T(8,128)S(1)} %hop3.1), channel_id=1, source_target_pairs={{48,64},{64,48},{49,65},{65,49},{50,66},{66,50},{51,67},{67,51},{5... | collective-permute-start | bytes 589832 | tf_op jit(solution)/shard_map/ppermute | solution.py:425
  33.2 2.4 %collective-permute-start.4 = (f32[48,1024]{1,0:T(8,128)S(1)}, f32[48,1024]{1,0:T(8,128)S(1)}, u32[]{:S(2)}, u32[]{:S(2)}) collective-permute-start(f32[48,1024]{1,0:T(8,128)S(1)} %hop4.1), channel_id=1, source_target_pairs={{64,80},{48,32},{65,81},{49,33},{66,82},{50,34},{67,83},{51,35},{6... | collective-permute-start | bytes 589832 | tf_op jit(solution)/shard_map/ppermute | solution.py:425
  37.0 2.9 %copy-start.1 = (f32[1024]{0:T(1024)S(1)}, f32[1024]{0:T(1024)}, u32[]{:S(2)}) copy-start(f32[1024]{0:T(1024)} %param.8) | copy-start | bytes 12292
  37.0 0.7 collective-permute-start.5
  39.2 0.7 collective-permute-start.6
  43.8 22.3 %all-to-all-start.1 = ((f32[16,104,128]{2,1,0:T(8,128)}), f32[16,104,128]{2,1,0:T(8,128)S(1)}, u32[]{:S(2)}, u32[]{:S(2)}) async-start(f32[16,104,128]{2,1,0:T(8,128)} %get-tuple-element.74), calls=%async_computation.1 | async-start | bytes 1703936 | tf_op jit(solution)/shard_map/all_to_all | solution.py:437
  68.9 11.2 %collective-permute-start.7 = (f32[192,384]{1,0:T(8,128)S(1)}, f32[192,384]{1,0:T(8,128)S(1)}, u32[]{:S(2)}, u32[]{:S(2)}) collective-permute-start(f32[192,384]{1,0:T(8,128)S(1)} %get-tuple-element.78.refs_0_.refs_7_), channel_id=1, source_target_pairs={{0,1},{1,2},{2,3},{3,0},{4,5},{5,6},{6,7},{7,4},{8,9},{9,10},{10,1... | collective-permute-start | bytes 884744 | tf_op jit(solution)/shard_map/ppermute | solution.py:476
  69.6 11.4 %collective-permute-start.8 = (f32[192,384]{1,0:T(8,128)S(1)}, f32[192,384]{1,0:T(8,128)S(1)}, u32[]{:S(2)}, u32[]{:S(2)}) collective-permute-start(f32[192,384]{1,0:T(8,128)S(1)} %get-tuple-element.78.refs_0_.refs_7_), channel_id=1, source_target_pairs={{0,2},{1,3},{2,0},{3,1},{4,6},{5,7},{6,4},{7,5},{8,10},{9,11},{10,... | collective-permute-start | bytes 884744 | tf_op jit(solution)/shard_map/ppermute | solution.py:476
  70.4 10.5 %collective-permute-start.9 = (f32[192,384]{1,0:T(8,128)S(1)}, f32[192,384]{1,0:T(8,128)S(1)}, u32[]{:S(2)}, u32[]{:S(2)}) collective-permute-start(f32[192,384]{1,0:T(8,128)S(1)} %get-tuple-element.78.refs_0_.refs_7_), channel_id=1, source_target_pairs={{0,3},{1,0},{2,1},{3,2},{4,7},{5,4},{6,5},{7,6},{8,11},{9,8},{10,9... | collective-permute-start | bytes 884744 | tf_op jit(solution)/shard_map/ppermute | solution.py:476
  72.4 9.2 %collective-permute-start.10 = (f32[192,384]{1,0:T(8,128)S(1)}, f32[192,384]{1,0:T(8,128)S(1)}, u32[]{:S(2)}, u32[]{:S(2)}) collective-permute-start(f32[192,384]{1,0:T(8,128)S(1)} %get-tuple-element.78.refs_0_.refs_7_), channel_id=1, source_target_pairs={{0,16},{16,0},{32,48},{48,32},{64,80},{80,64},{96,112},{112,96},{1... | collective-permute-start | bytes 884744 | tf_op jit(solution)/shard_map/ppermute | solution.py:477
  80.0 2.1 %collective-permute-start.11 = (f32[192,384]{1,0:T(8,128)S(1)}, f32[192,384]{1,0:T(8,128)S(1)}, u32[]{:S(2)}, u32[]{:S(2)}) collective-permute-start(f32[192,384]{1,0:T(8,128)S(1)} %collective-permute-done.7.refs_1_), channel_id=1, source_target_pairs={{0,16},{16,0},{32,48},{48,32},{64,80},{80,64},{96,112},{112,96},{1... | collective-permute-start | bytes 884744 | tf_op jit(solution)/shard_map/ppermute | solution.py:477
  80.9 1.6 %collective-permute-start.12 = (f32[192,384]{1,0:T(8,128)S(1)}, f32[192,384]{1,0:T(8,128)S(1)}, u32[]{:S(2)}, u32[]{:S(2)}) collective-permute-start(f32[192,384]{1,0:T(8,128)S(1)} %collective-permute-done.8.refs_2_), channel_id=1, source_target_pairs={{0,16},{16,0},{32,48},{48,32},{64,80},{80,64},{96,112},{112,96},{1... | collective-permute-start | bytes 884744 | tf_op jit(solution)/shard_map/ppermute | solution.py:477
  81.0 2.0 %collective-permute-start.13 = (f32[192,384]{1,0:T(8,128)S(1)}, f32[192,384]{1,0:T(8,128)S(1)}, u32[]{:S(2)}, u32[]{:S(2)}) collective-permute-start(f32[192,384]{1,0:T(8,128)S(1)} %collective-permute-done.9.refs_3_), channel_id=1, source_target_pairs={{0,16},{16,0},{32,48},{48,32},{64,80},{80,64},{96,112},{112,96},{1... | collective-permute-start | bytes 884744 | tf_op jit(solution)/shard_map/ppermute | solution.py:477
  145.5 5.0 %collective-permute-start.14 = (f32[24,128]{1,0:T(8,128)S(1)}, f32[24,128]{1,0:T(8,128)S(1)}, u32[]{:S(2)}, u32[]{:S(2)}) collective-permute-start(f32[24,128]{1,0:T(8,128)S(1)} %get-tuple-element.96.refs_3_), channel_id=1, source_target_pairs={{0,4},{1,5},{2,6},{3,7},{4,8},{5,9},{6,10},{7,11},{8,12},{9,13},{1... | collective-permute-start | bytes 36872 | tf_op jit(solution)/shard_map/ppermute | solution.py:501
  146.0 5.2 %collective-permute-start.15 = (f32[24,128]{1,0:T(8,128)S(1)}, f32[24,128]{1,0:T(8,128)S(1)}, u32[]{:S(2)}, u32[]{:S(2)}) collective-permute-start(f32[24,128]{1,0:T(8,128)S(1)} %get-tuple-element.96.refs_3_), channel_id=1, source_target_pairs={{0,8},{1,9},{2,10},{3,11},{4,12},{5,13},{6,14},{7,15},{8,0},{9,1},... | collective-permute-start | bytes 36872 | tf_op jit(solution)/shard_map/ppermute | solution.py:501
  148.6 3.7 %collective-permute-start.16 = (f32[24,128]{1,0:T(8,128)S(1)}, f32[24,128]{1,0:T(8,128)S(1)}, u32[]{:S(2)}, u32[]{:S(2)}) collective-permute-start(f32[24,128]{1,0:T(8,128)S(1)} %get-tuple-element.96.refs_3_), channel_id=1, source_target_pairs={{0,12},{1,13},{2,14},{3,15},{4,0},{5,1},{6,2},{7,3},{8,4},{9,5},{1... | collective-permute-start | bytes 36872 | tf_op jit(solution)/shard_map/ppermute | solution.py:501

commit v4 on v3

--- a/solution.py
+++ b/solution.py
@@ -254,20 +254,11 @@
     return jnp.where(iota((R, 128), 1) < R, both, 0.0)
 
 
-def pulled(before, core, prod_ref):
-    high, low, high_t, low_t = core
-    if before is None:
-        prod = (high[...], low[...])
-    else:
-        weights = halves(before[:, :R])
-        for g in range(WAYS * GROUPS):
-            rows = slice(g * R, (g + 1) * R)
-            prod_ref[rows, :] = three(weights, (high[rows, :], low[rows, :]))
-        prod = halves(prod_ref[...])
+def folded(turned, prod):
     total = jnp.zeros((R, 256), F32)
     for part, slices in ((0, range(5)), (128, range(5, WIDE))):
         cols = slice(part, part + 256)
-        z = three((high_t[cols, :], low_t[cols, :]), (prod[0][:, cols], prod[1][:, cols]))
+        z = three([t[cols, :] for t in turned], [p[:, cols] for p in prod])
         for h in slices:
             at = h * R - part
             block = z[at : at + R]
@@ -275,24 +266,42 @@
     return jnp.where(iota((R, 128), 1) < R, total[:, :128], 0.0) * (1.0 / N)
 
 
+def pulled(before, core, prod_ref):
+    high, low, high_t, low_t = core
+    weights = halves(before[:, :R])
+    for g in range(WAYS * GROUPS):
+        rows = slice(g * R, (g + 1) * R)
+        prod_ref[rows, :] = three(weights, (high[rows, :], low[rows, :]))
+    return folded((high_t, low_t), halves(prod_ref[...]))
+
+
+def first_kernel(own_ref, out_ref):
+    parts = halves(own_ref[...])
+    turned = halves(own_ref[...].T)
+    packed = packed_of(folded(turned, parts))
+    for peer in range(out_ref.shape[0]):
+        out_ref[peer] = packed
+
+
 def pair_kernel(*refs, pair):
     last = pair == MODES // 2 - 1
     refs = list(refs)
-    recv_ref = refs.pop(0) if pair else None
+    recv_ref = refs.pop(0)
+    swap_ref = None if pair else refs.pop(0)
     saved = [refs.pop(0) for _ in range(pair)] if last else []
-    even = [refs.pop(0) for _ in range(4)]
+    even = [refs.pop(0) for _ in range(4)] if pair else None
     odd = None if last else [refs.pop(0) for _ in range(4)]
     prod_ref = refs.pop()
+    mode = lax.axis_index("cores")
+    live = jnp.where(mode // 2 == pair, 1.0, 0.0)
+    arrived = jnp.sum(recv_ref[...], axis=0)
     if pair:
         sum_ref = refs.pop()
-        arrived = jnp.sum(recv_ref[...], axis=0)
         sum_ref[...] = arrived
-        before = whole(arrived)
+        middle = pulled(whole(arrived), even, prod_ref) * live
     else:
-        before = None
-    chip = lax.axis_index("cores") // 2
-    live = jnp.where(chip == pair, 1.0, 0.0)
-    middle = pulled(before, even, prod_ref) * live
+        arrived = jnp.where(mode % 2 == 0, arrived, jnp.sum(swap_ref[...], axis=0))
+        middle = whole(arrived) * (live / WAYS)
     kept = packed_of(middle)
     if last:
         for s in saved:
@@ -475,16 +484,18 @@
     siblings = [(m, m ^ 1) for m in range(MODES)]
     own = [updated] + [lax.ppermute(updated, ("cores", "samp"), pairs) for pairs in ring]
     other = [lax.ppermute(o, "cores", siblings) for o in own]
+    first = call(first_kernel, shape(peers, 24, 128), [vmem()], name="first")(updated)
+    recv = lax.all_to_all(first, "samp", 0, 0, tiled=True)
+    swap = lax.ppermute(recv, "cores", siblings)
     tall = shape(WAYS * ROWS, LANES, dtype=BF16)
     flat = shape(LANES, WAYS * ROWS, dtype=BF16)
     arranged = call(arrange_kernel, [tall, tall, flat, flat] * 2, [vmem()] * 8, name="arrange")(*own, *other)
     even, odd = list(arranged[:4]), list(arranged[4:])
 
     saved, sums = [], []
-    recv = None
     for pair in range(MODES // 2):
         last = pair == MODES // 2 - 1
-        ins = ([recv] if pair else []) + (saved if last else []) + even + ([] if last else odd)
+        ins = [recv] + (saved + even if last else even + odd if pair else [swap] + odd)
         outs = [shape(24, 128)] if last else [shape(2 * peers, 24, 128), shape(24, 128)]
         if pair:
             outs.append(shape(24, 128))

time: 161 us -> 163 us (1.012)
  starting transfers between devices: 25.6 us -> 29.6 us
    all_to_all x0 -> x1, waiting for transfers between devices: none -> 5.66 us  [on_device(): recv = lax.all_to_all(first, 'samp', 0, 0, tiled=True)]
    ppermute x3, waiting for transfers between devices: 6.38 us -> 1.17 us  [on_device(): lax.ppermute(updated, ('cores', 'samp'), pairs)]
    all_to_all x0 -> x1, starting transfers between devices: none -> 4.95 us  [on_device(): recv = lax.all_to_all(first, 'samp', 0, 0, tiled=True)]
  transfers between devices with their start and end apart: 18 -> 20, of which waited for: 11 -> 9; matrix products, arithmetic and copies ran while one was open for 1% -> 1% of each run, Pallas kernels for 0% -> 2%
where the time goes in v4:
time: 163 us; the launch traced here: 161 us
  blocking collectives  49.6 us (30%)
  Pallas kernels  40.4 us (25%)
  waiting for transfers between devices  36.1 us (22%)
  starting transfers between devices  29.6 us (18%)
  local copies, waits for them, and re-layouts  4.21 us (3%)
    all_to_all x3, blocking collectives, on_device(): lax.all_to_all(res[0], ('cores', 'samp'), 0, 0, axis_index_groups=groups,...  49.6 us
    ppermute x7, waiting for transfers between devices, on_device(): lax.ppermute(sent, 'cores', [(turn, turn + 1), (7 - turn, 6 - turn)])  15 us
    all_to_all x1, waiting for transfers between devices, exchanged(): return lax.all_to_all(block, 'samp', 0, 0, tiled=True)  11.7 us
    pallas_call x4, Pallas kernels, on_device(): call(functools.partial(pair_kernel, pair=pair), outs, [vmem()] * len(ins)...  9.64 us
    pallas_call x6, Pallas kernels, on_device(): call(functools.partial(hop_kernel, second=turn >= MODES // 2), shape(R, c...  8.56 us
    pallas_call x1, Pallas kernels, on_device(): pl.pallas_call(functools.partial(gather_kernel, peers=peers), grid=(RR //...  8.27 us
    all_to_all x1, starting transfers between devices, exchanged(): return lax.all_to_all(block, 'samp', 0, 0, tiled=True)  7.88 us
    ppermute x7, starting transfers between devices, on_device(): lax.ppermute(sent, 'cores', [(turn, turn + 1), (7 - turn, 6 - turn)])  7.21 us
  transfers between devices with their start and end apart: 20, of which 9 were waited for; matrix products, arithmetic and copies ran while one was open for 1% of the time, Pallas kernels for 2%

profile of v4, /device:TPU:16, one launch (start us, length us, event | category | flops | bytes accessed | tf_op | source)
XLA Modules:
  0.0 161.5 jit_solution(7657852030893345438)
XLA Ops:
  0.8 8.3 %gather.1 = (f32[2304,1024]{1,0:T(8,128)S(1)}, f32[48,1024]{1,0:T(8,128)S(1)}, s32[8,1024]{1,0:T(8,128)S(1)}, f32[8,128]{1,0:T(8,128)S(1)}) custom-call(s32[8,1024]{1,0:T(8,128)S(1)} %bitcast.16, f32[512,2304]{1,0:T(8,128)} %bitcast.18), custom_call_target="tpu_custom_call" | custom-call | tf_op jit(solution)/shard_map/gather/pallas_call | solution.py:401
  9.7 1.4 hop1.1
  11.8 1.4 hop2.1
  13.2 1.3 collective-permute-start.2
  14.5 8.9 %collective-permute-done.2.vec_ref.refs_2_ = f32[48,1024]{1,0:T(8,128)S(1)} collective-permute-done((f32[48,1024]{1,0:T(8,128)S(1)}, f32[48,1024]{1,0:T(8,128)S(1)}, u32[]{:S(2)}, u32[]{:S(2)}) %collective-permute-start.2) | collective-permute-done | bytes 196640 | tf_op jit(solution)/shard_map/ppermute | solution.py:434
  23.4 1.4 hop3.1
  24.8 1.9 %collective-permute-start.3 = (f32[48,1024]{1,0:T(8,128)S(1)}, f32[48,1024]{1,0:T(8,128)S(1)}, u32[]{:S(2)}, u32[]{:S(2)}) collective-permute-start(f32[48,1024]{1,0:T(8,128)S(1)} %hop3.1), channel_id=1, source_target_pairs={{48,64},{64,48},{49,65},{65,49},{50,66},{66,50},{51,67},{67,51},{5... | collective-permute-start | bytes 589832 | tf_op jit(solution)/shard_map/ppermute | solution.py:434
  26.7 5.1 %collective-permute-done.3.vec_ref.refs_3_ = f32[48,1024]{1,0:T(8,128)S(1)} collective-permute-done((f32[48,1024]{1,0:T(8,128)S(1)}, f32[48,1024]{1,0:T(8,128)S(1)}, u32[]{:S(2)}, u32[]{:S(2)}) %collective-permute-start.3) | collective-permute-done | bytes 196640 | tf_op jit(solution)/shard_map/ppermute | solution.py:434
  31.8 1.4 hop4.1
  33.2 1.3 collective-permute-start.4
  35.6 1.4 hop5.1
  37.7 1.5 hop6.1
  39.9 3.9 %route.1 = (f32[16,104,128]{2,1,0:T(8,128)}, f32[104,1024]{1,0:T(8,128)S(1)}) custom-call(f32[2304,1024]{1,0:T(8,128)S(1)} %get-tuple-element.70.mats_ref, f32[48,1024]{1,0:T(8,128)S(1)} %collective-permute-done.vec_ref.refs_0_, f32[48,1024]{1,0:T(8,128)S(1)} %collective-permute-done.1.vec_ref.refs_1_, ...), custom_call_target="tpu_custom_call" | custom-call | tf_op jit(solution)/shard_map/route/pallas_call | solution.py:437
  43.8 7.9 %all-to-all-start.1 = ((f32[16,104,128]{2,1,0:T(8,128)}), f32[16,104,128]{2,1,0:T(8,128)S(1)}, u32[]{:S(2)}, u32[]{:S(2)}) async-start(f32[16,104,128]{2,1,0:T(8,128)} %get-tuple-element.74), calls=%async_computation.1 | async-start | bytes 1703936 | tf_op jit(solution)/shard_map/all_to_all | solution.py:446
  54.4 11.7 %all-to-all-done.1.recv_ref = f32[16,104,128]{2,1,0:T(8,128)S(1)} async-done(((f32[16,104,128]{2,1,0:T(8,128)}), f32[16,104,128]{2,1,0:T(8,128)S(1)}, u32[]{:S(2)}, u32[]{:S(2)}) %all-to-all-start.1) | async-done | bytes 852000 | tf_op jit(solution)/shard_map/all_to_all | solution.py:446
  66.1 2.1 %collect.2 = (f32[192,384]{1,0:T(8,128)S(1)}, s32[1]{0:T(128)}) custom-call(f32[1]{0:T(128)} %bitcast.15.step_ref, f32[16,104,128]{2,1,0:T(8,128)S(1)} %all-to-all-done.1.recv_ref, f32[192,384]{1,0:T(8,128)S(1)} %reshape.26.base_ref), custom_call_target="tpu_custom_call" | custom-call | tf_op jit(solution)/shard_map/collect/pallas_call | solution.py:449
  70.4 1.9 %collective-permute-start.10 = (f32[192,384]{1,0:T(8,128)S(1)}, f32[192,384]{1,0:T(8,128)S(1)}, u32[]{:S(2)}, u32[]{:S(2)}) collective-permute-start(f32[192,384]{1,0:T(8,128)S(1)} %get-tuple-element.78.own_ref.refs_0_.refs_7_), channel_id=1, source_target_pairs={{0,3},{1,0},{2,1},{3,2},{4,7},{5,4},{6,5},{7,6},{8,11},{9,8},{10,9... | collective-permute-start | bytes 884744 | tf_op jit(solution)/shard_map/ppermute | solution.py:485
  72.3 1.3 first.1
  73.6 4.9 %all-to-all-start.2 = ((f32[16,24,128]{2,1,0:T(8,128)}), f32[16,24,128]{2,1,0:T(8,128)S(1)}, u32[]{:S(2)}, u32[]{:S(2)}) async-start(f32[16,24,128]{2,1,0:T(8,128)} %first.1), calls=%async_computation.2 | async-start | bytes 393216 | tf_op jit(solution)/shard_map/all_to_all | solution.py:488
  78.9 1.2 collective-permute-done.8.refs_1_
  81.5 5.7 %all-to-all-done.2.refs_0_ = f32[16,24,128]{2,1,0:T(8,128)S(1)} async-done(((f32[16,24,128]{2,1,0:T(8,128)}), f32[16,24,128]{2,1,0:T(8,128)S(1)}, u32[]{:S(2)}, u32[]{:S(2)}) %all-to-all-start.2) | async-done | bytes 196640 | tf_op jit(solution)/shard_map/all_to_all | solution.py:488
  87.2 1.4 arrange.1
  88.7 1.7 %pair0.1 = (f32[32,24,128]{2,1,0:T(8,128)S(1)}, f32[24,128]{1,0:T(8,128)S(1)}) custom-call(f32[16,24,128]{2,1,0:T(8,128)S(1)} %all-to-all-done.2.refs_0_, f32[16,24,128]{2,1,0:T(8,128)S(1)} %collective-permute-done.7.refs_1_, bf16[768,384]{1,0:T(8,128)(2,1)S(1)} %get-tuple-element.79.refs_2_.refs_5_, bf16[768,384]{1,0:T(8,128)(2,1)S(1)} %get-tuple-element.80.refs_3_.refs_6_, ...), custom_call_target="tpu_custom_call" | custom-call | tf_op jit(solution)/shard_map/pair0/pallas_call | solution.py:502
  90.3 21.3 %all_to_all.31.refs_0_ = f32[32,24,128]{2,1,0:T(8,128)S(1)} all-to-all(f32[32,24,128]{2,1,0:T(8,128)S(1)} %get-tuple-element.83), channel_id=1, replica_groups={{0,1,2,3,4,5,6,7,8,9,10,11,12,13,14,15,32,33,34,35,36,37,38,39,40,41,42..., dimensions={0} | all-to-all | bytes 786432 | tf_op jit(solution)/shard_map/all_to_all | solution.py:520
  111.7 3.2 %pair1.1 = (f32[32,24,128]{2,1,0:T(8,128)S(1)}, f32[24,128]{1,0:T(8,128)S(1)}, f32[24,128]{1,0:T(8,128)S(1)}) custom-call(f32[32,24,128]{2,1,0:T(8,128)S(1)} %all_to_all.31.refs_0_, bf16[768,384]{1,0:T(8,128)(2,1)S(1)} %get-tuple-element.84.refs_1_.refs_4_, bf16[768,384]{1,0:T(8,128)(2,1)S(1)} %get-tuple-element.85.refs_2_.refs_5_, ...), custom_call_target="tpu_custom_call" | custom-call | tf_op jit(solution)/shard_map/pair1/pallas_call | solution.py:502
  114.8 14.0 %all_to_all.32.refs_0_ = f32[32,24,128]{2,1,0:T(8,128)S(1)} all-to-all(f32[32,24,128]{2,1,0:T(8,128)S(1)} %get-tuple-element.89), channel_id=1, replica_groups={{32,33,34,35,36,37,38,39,40,41,42,43,44,45,46,47,64,65,66,67,68,69,70,7..., dimensions={0} | all-to-all | bytes 786432 | tf_op jit(solution)/shard_map/all_to_all | solution.py:520
  128.9 3.2 %pair2.1 = (f32[32,24,128]{2,1,0:T(8,128)S(1)}, f32[24,128]{1,0:T(8,128)S(1)}, f32[24,128]{1,0:T(8,128)S(1)}) custom-call(f32[32,24,128]{2,1,0:T(8,128)S(1)} %all_to_all.32.refs_0_, bf16[768,384]{1,0:T(8,128)(2,1)S(1)} %get-tuple-element.84.refs_1_.refs_4_, bf16[768,384]{1,0:T(8,128)(2,1)S(1)} %get-tuple-element.85.refs_2_.refs_5_, ...), custom_call_target="tpu_custom_call" | custom-call | tf_op jit(solution)/shard_map/pair2/pallas_call | solution.py:502
  132.0 14.2 %all_to_all.33.refs_0_ = f32[32,24,128]{2,1,0:T(8,128)S(1)} all-to-all(f32[32,24,128]{2,1,0:T(8,128)S(1)} %get-tuple-element.91), channel_id=1, replica_groups={{64,65,66,67,68,69,70,71,72,73,74,75,76,77,78,79,96,97,98,99,100,101,10..., dimensions={0} | all-to-all | bytes 786432 | tf_op jit(solution)/shard_map/all_to_all | solution.py:520
  146.2 1.6 %pair3.1 = (f32[24,128]{1,0:T(8,128)S(1)}, f32[24,128]{1,0:T(8,128)S(1)}) custom-call(f32[32,24,128]{2,1,0:T(8,128)S(1)} %all_to_all.33.refs_0_, f32[24,128]{1,0:T(8,128)S(1)} %get-tuple-element.92.refs_1_, f32[24,128]{1,0:T(8,128)S(1)} %get-tuple-element.93.refs_2_, f32[24,128]{1,0:T(8,128)S(1)} %get-tuple-element.94.refs_3_, ...), custom_call_target="tpu_custom_call" | custom-call | tf_op jit(solution)/shard_map/pair3/pallas_call | solution.py:502
  148.4 2.6 %collective-permute-start.16 = (f32[24,128]{1,0:T(8,128)S(1)}, f32[24,128]{1,0:T(8,128)S(1)}, u32[]{:S(2)}, u32[]{:S(2)}) collective-permute-start(f32[24,128]{1,0:T(8,128)S(1)} %get-tuple-element.96.refs_3_), channel_id=1, source_target_pairs={{0,8},{1,9},{2,10},{3,11},{4,12},{5,13},{6,14},{7,15},{8,0},{9,1},... | collective-permute-start | bytes 36872 | tf_op jit(solution)/shard_map/ppermute | solution.py:512
  151.0 1.2 collective-permute-start.17
  154.7 5.3 %final.1 = f32[192,384]{1,0:T(8,128)S(1)} custom-call(f32[24,128]{1,0:T(8,128)S(1)} %get-tuple-element.88.refs_0_, f32[24,128]{1,0:T(8,128)S(1)} %get-tuple-element.90.refs_1_, f32[24,128]{1,0:T(8,128)S(1)} %get-tuple-element.95.refs_2_, f32[24,128]{1,0:T(8,128)S(1)} %get-tuple-element.96.refs_3_, f32[24,128]{1,0:T(8,128)S(1)} %collective-permute-done.15.refs_4_, ...), custom_call_target="tpu_custom_call" | custom-call | tf_op jit(solution)/shard_map/final/pallas_call | solution.py:524
  (39 shorter events, 15.1 us)
Async XLA Ops:
  0.0 0.8 copy-start
  9.0 0.7 collective-permute-start
  11.1 0.7 collective-permute-start.1
  13.2 10.2 %collective-permute-start.2 = (f32[48,1024]{1,0:T(8,128)S(1)}, f32[48,1024]{1,0:T(8,128)S(1)}, u32[]{:S(2)}, u32[]{:S(2)}) collective-permute-start(f32[48,1024]{1,0:T(8,128)S(1)} %hop2.1), channel_id=1, source_target_pairs={{32,48},{80,64},{33,49},{81,65},{34,50},{82,66},{35,51},{83,67},{3... | collective-permute-start | bytes 589832 | tf_op jit(solution)/shard_map/ppermute | solution.py:434
  24.8 7.0 %collective-permute-start.3 = (f32[48,1024]{1,0:T(8,128)S(1)}, f32[48,1024]{1,0:T(8,128)S(1)}, u32[]{:S(2)}, u32[]{:S(2)}) collective-permute-start(f32[48,1024]{1,0:T(8,128)S(1)} %hop3.1), channel_id=1, source_target_pairs={{48,64},{64,48},{49,65},{65,49},{50,66},{66,50},{51,67},{67,51},{5... | collective-permute-start | bytes 589832 | tf_op jit(solution)/shard_map/ppermute | solution.py:434
  33.2 2.4 %collective-permute-start.4 = (f32[48,1024]{1,0:T(8,128)S(1)}, f32[48,1024]{1,0:T(8,128)S(1)}, u32[]{:S(2)}, u32[]{:S(2)}) collective-permute-start(f32[48,1024]{1,0:T(8,128)S(1)} %hop4.1), channel_id=1, source_target_pairs={{64,80},{48,32},{65,81},{49,33},{66,82},{50,34},{67,83},{51,35},{6... | collective-permute-start | bytes 589832 | tf_op jit(solution)/shard_map/ppermute | solution.py:434
  37.0 2.9 %copy-start.1 = (f32[1024]{0:T(1024)S(1)}, f32[1024]{0:T(1024)}, u32[]{:S(2)}) copy-start(f32[1024]{0:T(1024)} %param.8) | copy-start | bytes 12292
  37.0 0.7 collective-permute-start.5
  39.2 0.7 collective-permute-start.6
  43.8 22.3 %all-to-all-start.1 = ((f32[16,104,128]{2,1,0:T(8,128)}), f32[16,104,128]{2,1,0:T(8,128)S(1)}, u32[]{:S(2)}, u32[]{:S(2)}) async-start(f32[16,104,128]{2,1,0:T(8,128)} %get-tuple-element.74), calls=%async_computation.1 | async-start | bytes 1703936 | tf_op jit(solution)/shard_map/all_to_all | solution.py:446
  68.9 11.2 %collective-permute-start.8 = (f32[192,384]{1,0:T(8,128)S(1)}, f32[192,384]{1,0:T(8,128)S(1)}, u32[]{:S(2)}, u32[]{:S(2)}) collective-permute-start(f32[192,384]{1,0:T(8,128)S(1)} %get-tuple-element.78.own_ref.refs_0_.refs_7_), channel_id=1, source_target_pairs={{0,1},{1,2},{2,3},{3,0},{4,5},{5,6},{6,7},{7,4},{8,9},{9,10},{10,1... | collective-permute-start | bytes 884744 | tf_op jit(solution)/shard_map/ppermute | solution.py:485
  69.6 11.3 %collective-permute-start.9 = (f32[192,384]{1,0:T(8,128)S(1)}, f32[192,384]{1,0:T(8,128)S(1)}, u32[]{:S(2)}, u32[]{:S(2)}) collective-permute-start(f32[192,384]{1,0:T(8,128)S(1)} %get-tuple-element.78.own_ref.refs_0_.refs_7_), channel_id=1, source_target_pairs={{0,2},{1,3},{2,0},{3,1},{4,6},{5,7},{6,4},{7,5},{8,10},{9,11},{10,... | collective-permute-start | bytes 884744 | tf_op jit(solution)/shard_map/ppermute | solution.py:485
  70.4 10.5 %collective-permute-start.10 = (f32[192,384]{1,0:T(8,128)S(1)}, f32[192,384]{1,0:T(8,128)S(1)}, u32[]{:S(2)}, u32[]{:S(2)}) collective-permute-start(f32[192,384]{1,0:T(8,128)S(1)} %get-tuple-element.78.own_ref.refs_0_.refs_7_), channel_id=1, source_target_pairs={{0,3},{1,0},{2,1},{3,2},{4,7},{5,4},{6,5},{7,6},{8,11},{9,8},{10,9... | collective-permute-start | bytes 884744 | tf_op jit(solution)/shard_map/ppermute | solution.py:485
  73.6 13.6 %all-to-all-start.2 = ((f32[16,24,128]{2,1,0:T(8,128)}), f32[16,24,128]{2,1,0:T(8,128)S(1)}, u32[]{:S(2)}, u32[]{:S(2)}) async-start(f32[16,24,128]{2,1,0:T(8,128)} %first.1), calls=%async_computation.2 | async-start | bytes 393216 | tf_op jit(solution)/shard_map/all_to_all | solution.py:488
  78.6 8.7 %collective-permute-start.11 = (f32[192,384]{1,0:T(8,128)S(1)}, f32[192,384]{1,0:T(8,128)S(1)}, u32[]{:S(2)}, u32[]{:S(2)}) collective-permute-start(f32[192,384]{1,0:T(8,128)S(1)} %get-tuple-element.78.own_ref.refs_0_.refs_7_), channel_id=1, source_target_pairs={{0,16},{16,0},{32,48},{48,32},{64,80},{80,64},{96,112},{112,96},{1... | collective-permute-start | bytes 884744 | tf_op jit(solution)/shard_map/ppermute | solution.py:486
  80.0 7.2 %collective-permute-start.12 = (f32[192,384]{1,0:T(8,128)S(1)}, f32[192,384]{1,0:T(8,128)S(1)}, u32[]{:S(2)}, u32[]{:S(2)}) collective-permute-start(f32[192,384]{1,0:T(8,128)S(1)} %collective-permute-done.8.refs_1_), channel_id=1, source_target_pairs={{0,16},{16,0},{32,48},{48,32},{64,80},{80,64},{96,112},{112,96},{1... | collective-permute-start | bytes 884744 | tf_op jit(solution)/shard_map/ppermute | solution.py:486
  80.9 6.3 %collective-permute-start.13 = (f32[192,384]{1,0:T(8,128)S(1)}, f32[192,384]{1,0:T(8,128)S(1)}, u32[]{:S(2)}, u32[]{:S(2)}) collective-permute-start(f32[192,384]{1,0:T(8,128)S(1)} %collective-permute-done.9.refs_2_), channel_id=1, source_target_pairs={{0,16},{16,0},{32,48},{48,32},{64,80},{80,64},{96,112},{112,96},{1... | collective-permute-start | bytes 884744 | tf_op jit(solution)/shard_map/ppermute | solution.py:486
  80.9 6.3 %collective-permute-start.14 = (f32[192,384]{1,0:T(8,128)S(1)}, f32[192,384]{1,0:T(8,128)S(1)}, u32[]{:S(2)}, u32[]{:S(2)}) collective-permute-start(f32[192,384]{1,0:T(8,128)S(1)} %collective-permute-done.10.refs_3_), channel_id=1, source_target_pairs={{0,16},{16,0},{32,48},{48,32},{64,80},{80,64},{96,112},{112,96},{1... | collective-permute-start | bytes 884744 | tf_op jit(solution)/shard_map/ppermute | solution.py:486
  87.2 1.4 collective-permute-start.7
  147.9 5.0 %collective-permute-start.15 = (f32[24,128]{1,0:T(8,128)S(1)}, f32[24,128]{1,0:T(8,128)S(1)}, u32[]{:S(2)}, u32[]{:S(2)}) collective-permute-start(f32[24,128]{1,0:T(8,128)S(1)} %get-tuple-element.96.refs_3_), channel_id=1, source_target_pairs={{0,4},{1,5},{2,6},{3,7},{4,8},{5,9},{6,10},{7,11},{8,12},{9,13},{1... | collective-permute-start | bytes 36872 | tf_op jit(solution)/shard_map/ppermute | solution.py:512
  148.4 5.2 %collective-permute-start.16 = (f32[24,128]{1,0:T(8,128)S(1)}, f32[24,128]{1,0:T(8,128)S(1)}, u32[]{:S(2)}, u32[]{:S(2)}) collective-permute-start(f32[24,128]{1,0:T(8,128)S(1)} %get-tuple-element.96.refs_3_), channel_id=1, source_target_pairs={{0,8},{1,9},{2,10},{3,11},{4,12},{5,13},{6,14},{7,15},{8,0},{9,1},... | collective-permute-start | bytes 36872 | tf_op jit(solution)/shard_map/ppermute | solution.py:512
  151.0 3.7 %collective-permute-start.17 = (f32[24,128]{1,0:T(8,128)S(1)}, f32[24,128]{1,0:T(8,128)S(1)}, u32[]{:S(2)}, u32[]{:S(2)}) collective-permute-start(f32[24,128]{1,0:T(8,128)S(1)} %get-tuple-element.96.refs_3_), channel_id=1, source_target_pairs={{0,12},{1,13},{2,14},{3,15},{4,0},{5,1},{6,2},{7,3},{8,4},{9,5},{1... | collective-permute-start | bytes 36872 | tf_op jit(solution)/shard_map/ppermute | solution.py:512

commit v5 on v3

--- a/solution.py
+++ b/solution.py
@@ -18,6 +18,7 @@
 FEATS = 104
 SLOTS = 128
 WAYS = 4
+PARTS = 2
 HIGH = lax.Precision.HIGHEST
 F32 = jnp.float32
 BF16 = jnp.bfloat16
@@ -62,7 +63,10 @@
     return jnp.concatenate(out, axis=1).astype(jnp.int32) - 1, dest
 
 
-def gather_kernel(idx_ref, table_ref, mats_ref, sent_ref, slot_ref, most_ref, hot_ref, *, peers):
+def gather_kernel(idx_ref, table_ref, mats_ref, *refs, peers):
+    sent_refs = refs[:PARTS]
+    slot_ref, most_ref, hot_ref = refs[PARTS:]
+    width = sent_refs[0].shape[1]
     step = pl.program_id(0)
     mode = lax.axis_index("cores")
     leftward = mode < MODES // 2
@@ -91,38 +95,42 @@
 
     @pl.when(jnp.logical_and(leftward, step == 0))
     def _():
-        sent_ref[...] = out[0:R]
+        for p in range(PARTS):
+            sent_refs[p][...] = out[0:R, p * width : (p + 1) * width]
 
     @pl.when(jnp.logical_not(leftward))
     def _():
         per = COLS // R
         rows = jnp.concatenate([out[i * R : i * R + 1] for i in range(per)], axis=0)
-        sent_ref[pl.ds(pl.multiple_of(step * per, per), per), :] = rows
-
-
-def times_left(mats_ref, vec_ref, out_ref):
+        for p in range(PARTS):
+            sent_refs[p][pl.ds(pl.multiple_of(step * per, per), per), :] = rows[:, p * width : (p + 1) * width]
+
+
+def times_left(mats_ref, vec_ref, out_ref, first):
     count = vec_ref.shape[1]
 
     def chunk(c, _):
         lanes = pl.ds(pl.multiple_of(c * 128, 128), 128)
+        from_ = pl.ds(pl.multiple_of(c * 128 + first, 128), 128)
         acc = [jnp.zeros((R, 128), F32) for _ in range(2)]
         for a in range(R):
-            acc[a % 2] = acc[a % 2] + mats_ref[a * R : (a + 1) * R, lanes] * vec_ref[a : a + 1, lanes]
+            acc[a % 2] = acc[a % 2] + mats_ref[a * R : (a + 1) * R, from_] * vec_ref[a : a + 1, lanes]
         out_ref[:, lanes] = acc[0] + acc[1]
         return 0
 
     lax.fori_loop(0, count // 128, chunk, 0)
 
 
-def times_right(mats_ref, vec_ref, out_ref):
+def times_right(mats_ref, vec_ref, out_ref, first):
     count = vec_ref.shape[1]
 
     def chunk(c, _):
         lanes = pl.ds(pl.multiple_of(c * 128, 128), 128)
+        from_ = pl.ds(pl.multiple_of(c * 128 + first, 128), 128)
         vec = vec_ref[:, lanes]
         for a in range(0, R, 8):
             rows = [
-                jnp.sum(mats_ref[(a + i) * R : (a + i + 1) * R, lanes] * vec, axis=0, keepdims=True)
+                jnp.sum(mats_ref[(a + i) * R : (a + i + 1) * R, from_] * vec, axis=0, keepdims=True)
                 for i in range(8)
             ]
             out_ref[a : a + 8, lanes] = jnp.concatenate(rows, axis=0)
@@ -131,20 +139,20 @@
     lax.fori_loop(0, count // 128, chunk, 0)
 
 
-def apply(left, mats_ref, vec_ref, out_ref):
+def apply(left, mats_ref, vec_ref, out_ref, first=0):
     @pl.when(left)
     def _():
-        times_left(mats_ref, vec_ref, out_ref)
+        times_left(mats_ref, vec_ref, out_ref, first)
 
     @pl.when(jnp.logical_not(left))
     def _():
-        times_right(mats_ref, vec_ref, out_ref)
-
-
-def hop_kernel(mats_ref, vec_ref, out_ref, *, second):
+        times_right(mats_ref, vec_ref, out_ref, first)
+
+
+def hop_kernel(mats_ref, vec_ref, out_ref, *, second, part):
     mode = lax.axis_index("cores")
     left = (mode >= MODES // 2) if second else (mode < MODES // 2)
-    apply(left, mats_ref, vec_ref, out_ref)
+    apply(left, mats_ref, vec_ref, out_ref, part * vec_ref.shape[1])
 
 
 def spread(values, slot_ref, most_ref, turn, pay_ref):
@@ -167,14 +175,18 @@
 
 
 def route_kernel(mats_ref, *refs):
-    moved = refs[: MODES - 1]
-    obs_ref, slot_ref, most_ref, pay_ref, val_ref, one_ref, two_ref, tmp_ref = refs[MODES - 1 :]
+    turns = MODES - 1
+    obs_ref, slot_ref, most_ref, pay_ref, val_ref, one_ref, two_ref, tmp_ref = refs[turns * PARTS :]
+    width = refs[0].shape[1]
     mode = lax.axis_index("cores")
     early = mode < MODES // 2
     edge = jnp.where(jnp.logical_or(mode == 0, mode == MODES - 1), 1.0, 0.0)
-    one = jnp.where(iota(one_ref.shape, 0) == 0, edge, 0.0)
-    one_ref[...] = one + ((moved[0][...] + moved[1][...]) + moved[2][...])
-    two_ref[...] = (moved[3][...] + moved[4][...]) + (moved[5][...] + moved[6][...])
+    for p in range(PARTS):
+        moved = refs[p * turns : (p + 1) * turns]
+        lanes = slice(p * width, (p + 1) * width)
+        one = jnp.where(iota((R, width), 0) == 0, edge, 0.0)
+        one_ref[:, lanes] = one + ((moved[0][...] + moved[1][...]) + moved[2][...])
+        two_ref[:, lanes] = (moved[3][...] + moved[4][...]) + (moved[5][...] + moved[6][...])
     apply(jnp.logical_not(early), mats_ref, two_ref, tmp_ref)
     one = one_ref[...]
     two = two_ref[...]
@@ -389,7 +401,8 @@
     idx = indices.T
     step = step_size.reshape(1)
 
-    mats, sent, slot, most = pl.pallas_call(
+    width = count // PARTS
+    mats, *sent, slot, most = pl.pallas_call(
         functools.partial(gather_kernel, peers=peers),
         grid=(RR // COLS,),
         in_specs=[
@@ -398,40 +411,46 @@
         ],
         out_specs=[
             pl.BlockSpec((COLS, count), lambda i: (i, 0)),
-            pl.BlockSpec((R, count), lambda i: (0, 0)),
+            *[pl.BlockSpec((R, width), lambda i: (0, 0))] * PARTS,
             pl.BlockSpec((8, count), lambda i: (0, 0)),
             pl.BlockSpec((8, 128), lambda i: (0, 0)),
         ],
-        out_shape=[shape(RR, count), shape(R, count), shape(8, count, dtype=jnp.int32), shape(8, 128)],
+        out_shape=[
+            shape(RR, count),
+            *[shape(R, width)] * PARTS,
+            shape(8, count, dtype=jnp.int32),
+            shape(8, 128),
+        ],
         scratch_shapes=[pltpu.VMEM((N, count), BF16)],
         compiler_params=pltpu.CompilerParams(vmem_limit_bytes=BIG),
         name="gather",
-    )(idx, pltpu.with_memory_space_constraint(table, pltpu.HBM))
+    )(*[pltpu.with_memory_space_constraint(a, pltpu.HBM) for a in (idx, table)])
 
     first = lax.axis_index("samp") * slab
     kept = lax.dynamic_slice_in_dim(table, first, slab, 0)
     base = kept.reshape(GROUPS, WIDE, R, R).transpose(0, 2, 1, 3)
     base = base.reshape(ROWS, LANES)
 
-    every = []
+    every = [[] for _ in range(PARTS)]
     for turn in range(MODES - 1):
-        if turn > 0:
-            sent = call(
-                functools.partial(hop_kernel, second=turn >= MODES // 2),
-                shape(R, count),
-                [vmem(), vmem()],
-                name=f"hop{turn}",
-            )(mats, moved)
-        moved = lax.ppermute(sent, "cores", [(turn, turn + 1), (7 - turn, 6 - turn)])
-        every.append(moved)
+        for p in range(PARTS):
+            if turn > 0:
+                sent[p] = call(
+                    functools.partial(hop_kernel, second=turn >= MODES // 2, part=p),
+                    shape(R, width),
+                    [vmem(), vmem()],
+                    name=f"hop{turn}_{p}",
+                )(mats, every[p][-1])
+            pairs = [(turn, turn + 1), (7 - turn, 6 - turn)]
+            every[p].append(lax.ppermute(sent[p], "cores", pairs))
 
     pay, values = call(
         route_kernel,
         (shape(peers, FEATS, SLOTS), shape(FEATS, count)),
-        [vmem()] * (MODES + 3),
+        [vmem()] * (PARTS * (MODES - 1) + 4),
         [pltpu.VMEM((R, count), F32)] * 3,
         name="route",
-    )(mats, *every, observed.reshape(1, count), slot, most)
+    )(mats, *sum(every, []), observed.reshape(1, count), slot, most)
 
     def exchanged(block):
         return lax.all_to_all(block, "samp", 0, 0, tiled=True)

time: 161 us -> 155 us (0.963); the launches traced: 159 us -> 155 us
  waiting for transfers between devices: 37 us -> 29.5 us
  starting transfers between devices: 25.6 us -> 32.1 us
  blocking collectives: 50.6 us -> 47.9 us
    ppermute x7 -> x14, waiting for transfers between devices: 15 us -> 3.68 us  [on_device(): every[p].append(lax.ppermute(sent[p], 'cores', pairs))]
    ppermute x7 -> x14, starting transfers between devices: 7.21 us -> 16.1 us  [on_device(): every[p].append(lax.ppermute(sent[p], 'cores', pairs))]
    all_to_all x3, blocking collectives: 50.6 us -> 47.9 us  [on_device(): lax.all_to_all(res[0], ('cores', 'samp'), 0, 0, axis_index_groups=groups,...]
    ppermute x4, starting transfers between devices: 2.82 us -> 0.52 us  [on_device(): other = [lax.ppermute(o, 'cores', siblings) for o in own]]
    ppermute x3, waiting for transfers between devices: 6.38 us -> 8.24 us  [on_device(): lax.ppermute(updated, ('cores', 'samp'), pairs)]
    all_to_all x1, waiting for transfers between devices: 11.7 us -> 13.4 us  [exchanged(): return lax.all_to_all(block, 'samp', 0, 0, tiled=True)]
    pallas_call x6 -> x12, Pallas kernels: 8.56 us -> 8.7 us  [on_device(): call(functools.partial(hop_kernel, second=turn >= MODES // 2, part=p), sh...]
  transfers between devices with their start and end apart: 18 -> 25, of which waited for: 11 -> 11; matrix products, arithmetic and copies ran while one was open for 1% -> 1% of each run, Pallas kernels for 0% -> 6%
where the time goes in v5:
time: 155 us
  blocking collectives  47.9 us (31%)
  Pallas kernels  40.1 us (26%)
  starting transfers between devices  32.1 us (21%)
  waiting for transfers between devices  29.5 us (19%)
  local copies, waits for them, and re-layouts  3.45 us (2%)
    all_to_all x3, blocking collectives, on_device(): lax.all_to_all(res[0], ('cores', 'samp'), 0, 0, axis_index_groups=groups,...  47.9 us
    ppermute x14, starting transfers between devices, on_device(): every[p].append(lax.ppermute(sent[p], 'cores', pairs))  16.1 us
    all_to_all x1, waiting for transfers between devices, exchanged(): return lax.all_to_all(block, 'samp', 0, 0, tiled=True)  13.4 us
    pallas_call x4, Pallas kernels, on_device(): call(functools.partial(pair_kernel, pair=pair), outs, [vmem()] * len(ins)...  10.4 us
    pallas_call x12, Pallas kernels, on_device(): call(functools.partial(hop_kernel, second=turn >= MODES // 2, part=p), sh...  8.7 us
    pallas_call x1, Pallas kernels, on_device(): pl.pallas_call(functools.partial(gather_kernel, peers=peers), grid=(RR //...  8.28 us
    ppermute x3, waiting for transfers between devices, on_device(): lax.ppermute(updated, ('cores', 'samp'), pairs)  8.24 us
    all_to_all x1, starting transfers between devices, exchanged(): return lax.all_to_all(block, 'samp', 0, 0, tiled=True)  7.88 us
  transfers between devices with their start and end apart: 25, of which 11 were waited for; matrix products, arithmetic and copies ran while one was open for 1% of the time, Pallas kernels for 6%

profile of v5, /device:TPU:16, one launch (start us, length us, event | category | flops | bytes accessed | tf_op | source)
XLA Modules:
  0.0 154.9 jit_solution(3023873428567286217)
XLA Ops:
  0.0 8.3 %gather.1 = (f32[2304,1024]{1,0:T(8,128)S(1)}, f32[48,512]{1,0:T(8,128)S(1)}, f32[48,512]{1,0:T(8,128)S(1)}, s32[8,1024]{1,0:T(8,128)S(1)}, f32[8,128]{1,0:T(8,128)S(1)}) custom-call(s32[8,1024]{1,0:T(8,128)} %bitcast.20, f32[512,2304]{1,0:T(8,128)} %bitcast.17), custom_call_target="tpu_custom_call" | custom-call | tf_op jit(solution)/shard_map/gather/pallas_call | solution.py:405
  13.2 1.3 collective-permute-start.9
  15.2 1.3 collective-permute-start.2
  16.5 3.4 %collective-permute-done.9.vec_ref.refs_9_ = f32[48,512]{1,0:T(8,128)S(1)} collective-permute-done((f32[48,512]{1,0:T(8,128)S(1)}, f32[48,512]{1,0:T(8,128)S(1)}, u32[]{:S(2)}, u32[]{:S(2)}) %collective-permute-start.9) | collective-permute-done | bytes 98336 | tf_op jit(solution)/shard_map/ppermute | solution.py:445
  20.6 1.9 %collective-permute-start.10 = (f32[48,512]{1,0:T(8,128)S(1)}, f32[48,512]{1,0:T(8,128)S(1)}, u32[]{:S(2)}, u32[]{:S(2)}) collective-permute-start(f32[48,512]{1,0:T(8,128)S(1)} %hop3_1.1), channel_id=1, source_target_pairs={{48,64},{64,48},{49,65},{65,49},{50,66},{66,50},{51,67},{67,51},{5... | collective-permute-start | bytes 294920 | tf_op jit(solution)/shard_map/ppermute | solution.py:445
  23.3 3.7 %collective-permute-start.3 = (f32[48,512]{1,0:T(8,128)S(1)}, f32[48,512]{1,0:T(8,128)S(1)}, u32[]{:S(2)}, u32[]{:S(2)}) collective-permute-start(f32[48,512]{1,0:T(8,128)S(1)} %hop3_0.1), channel_id=1, source_target_pairs={{48,64},{64,48},{49,65},{65,49},{50,66},{66,50},{51,67},{67,51},{5... | collective-permute-start | bytes 294920 | tf_op jit(solution)/shard_map/ppermute | solution.py:445
  27.7 1.3 collective-permute-start.11
  30.0 1.3 collective-permute-start.4
  31.3 0.7 hop5_1.1
  37.1 3.9 %route.1 = (f32[16,104,128]{2,1,0:T(8,128)}, f32[104,1024]{1,0:T(8,128)S(1)}) custom-call(f32[2304,1024]{1,0:T(8,128)S(1)} %get-tuple-element.71.mats_ref, f32[48,512]{1,0:T(8,128)S(1)} %collective-permute-done.vec_ref.refs_0_, f32[48,512]{1,0:T(8,128)S(1)} %collective-permute-done.1.vec_ref.refs_1_, f32[48,512]{1,0:T(8,128)S(1)} %collective-permute-done.2.vec_ref.refs_2_, ...), custom_call_target="tpu_custom_call" | custom-call | tf_op jit(solution)/shard_map/route/pallas_call | solution.py:447
  41.0 7.9 %all-to-all-start.1 = ((f32[16,104,128]{2,1,0:T(8,128)}), f32[16,104,128]{2,1,0:T(8,128)S(1)}, u32[]{:S(2)}, u32[]{:S(2)}) async-start(f32[16,104,128]{2,1,0:T(8,128)} %get-tuple-element.76), calls=%async_computation.1 | async-start | bytes 1703936 | tf_op jit(solution)/shard_map/all_to_all | solution.py:456
  48.9 1.0 constant_dynamic-slice_fusion
  51.5 13.4 %all-to-all-done.1.recv_ref = f32[16,104,128]{2,1,0:T(8,128)S(1)} async-done(((f32[16,104,128]{2,1,0:T(8,128)}), f32[16,104,128]{2,1,0:T(8,128)S(1)}, u32[]{:S(2)}, u32[]{:S(2)}) %all-to-all-start.1) | async-done | bytes 852000 | tf_op jit(solution)/shard_map/all_to_all | solution.py:456
  64.9 2.1 %collect.2 = (f32[192,384]{1,0:T(8,128)S(1)}, s32[1]{0:T(128)}) custom-call(f32[1]{0:T(128)} %bitcast.15.step_ref, f32[16,104,128]{2,1,0:T(8,128)S(1)} %all-to-all-done.1.recv_ref, f32[192,384]{1,0:T(8,128)S(1)} %reshape.26.base_ref), custom_call_target="tpu_custom_call" | custom-call | tf_op jit(solution)/shard_map/collect/pallas_call | solution.py:459
  67.1 0.8 while.10
  68.4 1.4 collective-permute-start.15
  69.7 1.5 collective-permute-start.16
  71.2 7.8 %collective-permute-done.14.refs_1_ = f32[192,384]{1,0:T(8,128)S(1)} collective-permute-done((f32[192,384]{1,0:T(8,128)S(1)}, f32[192,384]{1,0:T(8,128)S(1)}, u32[]{:S(2)}, u32[]{:S(2)}) %collective-permute-start.14) | collective-permute-done | bytes 294944 | tf_op jit(solution)/shard_map/ppermute | solution.py:495
  81.6 1.4 arrange.1
  82.9 2.4 %pair0.1 = (f32[32,24,128]{2,1,0:T(8,128)S(1)}, f32[24,128]{1,0:T(8,128)S(1)}) custom-call(bf16[768,384]{1,0:T(8,128)(2,1)S(1)} %get-tuple-element.81.refs_0_.refs_1_.refs_4_, bf16[768,384]{1,0:T(8,128)(2,1)S(1)} %get-tuple-element.82.refs_1_.refs_2_.refs_5_, bf16[384,768]{1,0:T(8,128)(2,1)S(1)} %get-tuple-element.83.refs_2_.refs_3_.refs_6_, ...), custom_call_target="tpu_custom_call" | custom-call | tf_op jit(solution)/shard_map/pair0/pallas_call | solution.py:510
  85.4 18.1 %all_to_all.26.refs_0_ = f32[32,24,128]{2,1,0:T(8,128)S(1)} all-to-all(f32[32,24,128]{2,1,0:T(8,128)S(1)} %get-tuple-element.89), channel_id=1, replica_groups={{0,1,2,3,4,5,6,7,8,9,10,11,12,13,14,15,32,33,34,35,36,37,38,39,40,41,42..., dimensions={0} | all-to-all | bytes 786432 | tf_op jit(solution)/shard_map/all_to_all | solution.py:528
  103.5 3.2 %pair1.1 = (f32[32,24,128]{2,1,0:T(8,128)S(1)}, f32[24,128]{1,0:T(8,128)S(1)}, f32[24,128]{1,0:T(8,128)S(1)}) custom-call(f32[32,24,128]{2,1,0:T(8,128)S(1)} %all_to_all.26.refs_0_, bf16[768,384]{1,0:T(8,128)(2,1)S(1)} %get-tuple-element.81.refs_0_.refs_1_.refs_4_, bf16[768,384]{1,0:T(8,128)(2,1)S(1)} %get-tuple-element.82.refs_1_.refs_2_.refs_5_, ...), custom_call_target="tpu_custom_call" | custom-call | tf_op jit(solution)/shard_map/pair1/pallas_call | solution.py:510
  106.6 14.0 %all_to_all.27.refs_0_ = f32[32,24,128]{2,1,0:T(8,128)S(1)} all-to-all(f32[32,24,128]{2,1,0:T(8,128)S(1)} %get-tuple-element.91), channel_id=1, replica_groups={{32,33,34,35,36,37,38,39,40,41,42,43,44,45,46,47,64,65,66,67,68,69,70,7..., dimensions={0} | all-to-all | bytes 786432 | tf_op jit(solution)/shard_map/all_to_all | solution.py:528
  120.6 3.2 %pair2.1 = (f32[32,24,128]{2,1,0:T(8,128)S(1)}, f32[24,128]{1,0:T(8,128)S(1)}, f32[24,128]{1,0:T(8,128)S(1)}) custom-call(f32[32,24,128]{2,1,0:T(8,128)S(1)} %all_to_all.27.refs_0_, bf16[768,384]{1,0:T(8,128)(2,1)S(1)} %get-tuple-element.81.refs_0_.refs_1_.refs_4_, bf16[768,384]{1,0:T(8,128)(2,1)S(1)} %get-tuple-element.82.refs_1_.refs_2_.refs_5_, ...), custom_call_target="tpu_custom_call" | custom-call | tf_op jit(solution)/shard_map/pair2/pallas_call | solution.py:510
  123.8 15.8 %all_to_all.28.refs_0_ = f32[32,24,128]{2,1,0:T(8,128)S(1)} all-to-all(f32[32,24,128]{2,1,0:T(8,128)S(1)} %get-tuple-element.93), channel_id=1, replica_groups={{64,65,66,67,68,69,70,71,72,73,74,75,76,77,78,79,96,97,98,99,100,101,10..., dimensions={0} | all-to-all | bytes 786432 | tf_op jit(solution)/shard_map/all_to_all | solution.py:528
  139.6 1.6 %pair3.1 = (f32[24,128]{1,0:T(8,128)S(1)}, f32[24,128]{1,0:T(8,128)S(1)}) custom-call(f32[32,24,128]{2,1,0:T(8,128)S(1)} %all_to_all.28.refs_0_, f32[24,128]{1,0:T(8,128)S(1)} %get-tuple-element.94.refs_1_, f32[24,128]{1,0:T(8,128)S(1)} %get-tuple-element.95.refs_2_, f32[24,128]{1,0:T(8,128)S(1)} %get-tuple-element.96.refs_3_, ...), custom_call_target="tpu_custom_call" | custom-call | tf_op jit(solution)/shard_map/pair3/pallas_call | solution.py:510
  141.8 2.6 %collective-permute-start.22 = (f32[24,128]{1,0:T(8,128)S(1)}, f32[24,128]{1,0:T(8,128)S(1)}, u32[]{:S(2)}, u32[]{:S(2)}) collective-permute-start(f32[24,128]{1,0:T(8,128)S(1)} %get-tuple-element.98.refs_3_), channel_id=1, source_target_pairs={{0,8},{1,9},{2,10},{3,11},{4,12},{5,13},{6,14},{7,15},{8,0},{9,1},... | collective-permute-start | bytes 36872 | tf_op jit(solution)/shard_map/ppermute | solution.py:520
  144.4 1.1 collective-permute-start.23
  146.2 0.8 collective-permute-done.22.refs_5_
  147.0 1.1 collective-permute-done.23.refs_6_
  148.1 5.3 %final.1 = f32[192,384]{1,0:T(8,128)S(1)} custom-call(f32[24,128]{1,0:T(8,128)S(1)} %get-tuple-element.90.refs_0_, f32[24,128]{1,0:T(8,128)S(1)} %get-tuple-element.92.refs_1_, f32[24,128]{1,0:T(8,128)S(1)} %get-tuple-element.97.refs_2_, f32[24,128]{1,0:T(8,128)S(1)} %get-tuple-element.98.refs_3_, f32[24,128]{1,0:T(8,128)S(1)} %collective-permute-done.21.refs_4_, ...), custom_call_target="tpu_custom_call" | custom-call | tf_op jit(solution)/shard_map/final/pallas_call | solution.py:532
  153.8 1.0 reshape.28
  (52 shorter events, 19.1 us)
Async XLA Ops:
  8.3 1.4 collective-permute-start.7
  9.0 2.1 %collective-permute-start = (f32[48,512]{1,0:T(8,128)S(1)}, f32[48,512]{1,0:T(8,128)S(1)}, u32[]{:S(2)}, u32[]{:S(2)}) collective-permute-start(f32[48,512]{1,0:T(8,128)S(1)} %get-tuple-element.72), channel_id=1, source_target_pairs={{0,16},{112,96},{1,17},{113,97},{2,18},{114,98},{3,19},{115,99},{4... | collective-permute-start | bytes 294920 | tf_op jit(solution)/shard_map/ppermute | solution.py:445
  10.4 2.1 %collective-permute-start.8 = (f32[48,512]{1,0:T(8,128)S(1)}, f32[48,512]{1,0:T(8,128)S(1)}, u32[]{:S(2)}, u32[]{:S(2)}) collective-permute-start(f32[48,512]{1,0:T(8,128)S(1)} %hop1_1.1), channel_id=1, source_target_pairs={{16,32},{96,80},{17,33},{97,81},{18,34},{98,82},{19,35},{99,83},{2... | collective-permute-start | bytes 294920 | tf_op jit(solution)/shard_map/ppermute | solution.py:445
  11.8 2.7 %collective-permute-start.1 = (f32[48,512]{1,0:T(8,128)S(1)}, f32[48,512]{1,0:T(8,128)S(1)}, u32[]{:S(2)}, u32[]{:S(2)}) collective-permute-start(f32[48,512]{1,0:T(8,128)S(1)} %hop1_0.1), channel_id=1, source_target_pairs={{16,32},{96,80},{17,33},{97,81},{18,34},{98,82},{19,35},{99,83},{2... | collective-permute-start | bytes 294920 | tf_op jit(solution)/shard_map/ppermute | solution.py:445
  13.2 6.8 %collective-permute-start.9 = (f32[48,512]{1,0:T(8,128)S(1)}, f32[48,512]{1,0:T(8,128)S(1)}, u32[]{:S(2)}, u32[]{:S(2)}) collective-permute-start(f32[48,512]{1,0:T(8,128)S(1)} %hop2_1.1), channel_id=1, source_target_pairs={{32,48},{80,64},{33,49},{81,65},{34,50},{82,66},{35,51},{83,67},{3... | collective-permute-start | bytes 294920 | tf_op jit(solution)/shard_map/ppermute | solution.py:445
  15.2 7.4 %collective-permute-start.2 = (f32[48,512]{1,0:T(8,128)S(1)}, f32[48,512]{1,0:T(8,128)S(1)}, u32[]{:S(2)}, u32[]{:S(2)}) collective-permute-start(f32[48,512]{1,0:T(8,128)S(1)} %hop2_0.1), channel_id=1, source_target_pairs={{32,48},{80,64},{33,49},{81,65},{34,50},{82,66},{35,51},{83,67},{3... | collective-permute-start | bytes 294920 | tf_op jit(solution)/shard_map/ppermute | solution.py:445
  20.6 6.3 %collective-permute-start.10 = (f32[48,512]{1,0:T(8,128)S(1)}, f32[48,512]{1,0:T(8,128)S(1)}, u32[]{:S(2)}, u32[]{:S(2)}) collective-permute-start(f32[48,512]{1,0:T(8,128)S(1)} %hop3_1.1), channel_id=1, source_target_pairs={{48,64},{64,48},{49,65},{65,49},{50,66},{66,50},{51,67},{67,51},{5... | collective-permute-start | bytes 294920 | tf_op jit(solution)/shard_map/ppermute | solution.py:445
  23.3 6.0 %collective-permute-start.3 = (f32[48,512]{1,0:T(8,128)S(1)}, f32[48,512]{1,0:T(8,128)S(1)}, u32[]{:S(2)}, u32[]{:S(2)}) collective-permute-start(f32[48,512]{1,0:T(8,128)S(1)} %hop3_0.1), channel_id=1, source_target_pairs={{48,64},{64,48},{49,65},{65,49},{50,66},{66,50},{51,67},{67,51},{5... | collective-permute-start | bytes 294920 | tf_op jit(solution)/shard_map/ppermute | solution.py:445
  27.7 3.6 %collective-permute-start.11 = (f32[48,512]{1,0:T(8,128)S(1)}, f32[48,512]{1,0:T(8,128)S(1)}, u32[]{:S(2)}, u32[]{:S(2)}) collective-permute-start(f32[48,512]{1,0:T(8,128)S(1)} %hop4_1.1), channel_id=1, source_target_pairs={{64,80},{48,32},{65,81},{49,33},{66,82},{50,34},{67,83},{51,35},{6... | collective-permute-start | bytes 294920 | tf_op jit(solution)/shard_map/ppermute | solution.py:445
  30.0 2.7 %collective-permute-start.4 = (f32[48,512]{1,0:T(8,128)S(1)}, f32[48,512]{1,0:T(8,128)S(1)}, u32[]{:S(2)}, u32[]{:S(2)}) collective-permute-start(f32[48,512]{1,0:T(8,128)S(1)} %hop4_0.1), channel_id=1, source_target_pairs={{64,80},{48,32},{65,81},{49,33},{66,82},{50,34},{67,83},{51,35},{6... | collective-permute-start | bytes 294920 | tf_op jit(solution)/shard_map/ppermute | solution.py:445
  32.0 2.1 %collective-permute-start.12 = (f32[48,512]{1,0:T(8,128)S(1)}, f32[48,512]{1,0:T(8,128)S(1)}, u32[]{:S(2)}, u32[]{:S(2)}) collective-permute-start(f32[48,512]{1,0:T(8,128)S(1)} %hop5_1.1), channel_id=1, source_target_pairs={{80,96},{32,16},{81,97},{33,17},{82,98},{34,18},{83,99},{35,19},{8... | collective-permute-start | bytes 294920 | tf_op jit(solution)/shard_map/ppermute | solution.py:445
  33.5 2.1 %collective-permute-start.5 = (f32[48,512]{1,0:T(8,128)S(1)}, f32[48,512]{1,0:T(8,128)S(1)}, u32[]{:S(2)}, u32[]{:S(2)}) collective-permute-start(f32[48,512]{1,0:T(8,128)S(1)} %hop5_0.1), channel_id=1, source_target_pairs={{80,96},{32,16},{81,97},{33,17},{82,98},{34,18},{83,99},{35,19},{8... | collective-permute-start | bytes 294920 | tf_op jit(solution)/shard_map/ppermute | solution.py:445
  34.9 2.1 %copy-start = (f32[1024]{0:T(1024)S(1)}, f32[1024]{0:T(1024)}, u32[]{:S(2)}) copy-start(f32[1024]{0:T(1024)} %param.8) | copy-start | bytes 12292
  34.9 2.1 %collective-permute-start.13 = (f32[48,512]{1,0:T(8,128)S(1)}, f32[48,512]{1,0:T(8,128)S(1)}, u32[]{:S(2)}, u32[]{:S(2)}) collective-permute-start(f32[48,512]{1,0:T(8,128)S(1)} %hop6_1.1), channel_id=1, source_target_pairs={{96,112},{16,0},{97,113},{17,1},{98,114},{18,2},{99,115},{19,3},{1... | collective-permute-start | bytes 294920 | tf_op jit(solution)/shard_map/ppermute | solution.py:445
  36.4 0.7 collective-permute-start.6
  41.0 23.9 %all-to-all-start.1 = ((f32[16,104,128]{2,1,0:T(8,128)}), f32[16,104,128]{2,1,0:T(8,128)S(1)}, u32[]{:S(2)}, u32[]{:S(2)}) async-start(f32[16,104,128]{2,1,0:T(8,128)} %get-tuple-element.76), calls=%async_computation.1 | async-start | bytes 1703936 | tf_op jit(solution)/shard_map/all_to_all | solution.py:456
  67.9 11.2 %collective-permute-start.14 = (f32[192,384]{1,0:T(8,128)S(1)}, f32[192,384]{1,0:T(8,128)S(1)}, u32[]{:S(2)}, u32[]{:S(2)}) collective-permute-start(f32[192,384]{1,0:T(8,128)S(1)} %get-tuple-element.80.refs_0_.refs_7_), channel_id=1, source_target_pairs={{0,1},{1,2},{2,3},{3,0},{4,5},{5,6},{6,7},{7,4},{8,9},{9,10},{10,1... | collective-permute-start | bytes 884744 | tf_op jit(solution)/shard_map/ppermute | solution.py:495
  68.4 10.7 %collective-permute-start.15 = (f32[192,384]{1,0:T(8,128)S(1)}, f32[192,384]{1,0:T(8,128)S(1)}, u32[]{:S(2)}, u32[]{:S(2)}) collective-permute-start(f32[192,384]{1,0:T(8,128)S(1)} %get-tuple-element.80.refs_0_.refs_7_), channel_id=1, source_target_pairs={{0,2},{1,3},{2,0},{3,1},{4,6},{5,7},{6,4},{7,5},{8,10},{9,11},{10,... | collective-permute-start | bytes 884744 | tf_op jit(solution)/shard_map/ppermute | solution.py:495
  69.7 10.3 %collective-permute-start.16 = (f32[192,384]{1,0:T(8,128)S(1)}, f32[192,384]{1,0:T(8,128)S(1)}, u32[]{:S(2)}, u32[]{:S(2)}) collective-permute-start(f32[192,384]{1,0:T(8,128)S(1)} %get-tuple-element.80.refs_0_.refs_7_), channel_id=1, source_target_pairs={{0,3},{1,0},{2,1},{3,2},{4,7},{5,4},{6,5},{7,6},{8,11},{9,8},{10,9... | collective-permute-start | bytes 884744 | tf_op jit(solution)/shard_map/ppermute | solution.py:495
  71.2 8.8 %collective-permute-start.17 = (f32[192,384]{1,0:T(8,128)S(1)}, f32[192,384]{1,0:T(8,128)S(1)}, u32[]{:S(2)}, u32[]{:S(2)}) collective-permute-start(f32[192,384]{1,0:T(8,128)S(1)} %get-tuple-element.80.refs_0_.refs_7_), channel_id=1, source_target_pairs={{0,16},{16,0},{32,48},{48,32},{64,80},{80,64},{96,112},{112,96},{1... | collective-permute-start | bytes 884744 | tf_op jit(solution)/shard_map/ppermute | solution.py:496
  79.1 1.6 %collective-permute-start.18 = (f32[192,384]{1,0:T(8,128)S(1)}, f32[192,384]{1,0:T(8,128)S(1)}, u32[]{:S(2)}, u32[]{:S(2)}) collective-permute-start(f32[192,384]{1,0:T(8,128)S(1)} %collective-permute-done.14.refs_1_), channel_id=1, source_target_pairs={{0,16},{16,0},{32,48},{48,32},{64,80},{80,64},{96,112},{112,96},{1... | collective-permute-start | bytes 884744 | tf_op jit(solution)/shard_map/ppermute | solution.py:496
  79.1 2.0 %collective-permute-start.19 = (f32[192,384]{1,0:T(8,128)S(1)}, f32[192,384]{1,0:T(8,128)S(1)}, u32[]{:S(2)}, u32[]{:S(2)}) collective-permute-start(f32[192,384]{1,0:T(8,128)S(1)} %collective-permute-done.15.refs_2_), channel_id=1, source_target_pairs={{0,16},{16,0},{32,48},{48,32},{64,80},{80,64},{96,112},{112,96},{1... | collective-permute-start | bytes 884744 | tf_op jit(solution)/shard_map/ppermute | solution.py:496
  80.0 1.6 %collective-permute-start.20 = (f32[192,384]{1,0:T(8,128)S(1)}, f32[192,384]{1,0:T(8,128)S(1)}, u32[]{:S(2)}, u32[]{:S(2)}) collective-permute-start(f32[192,384]{1,0:T(8,128)S(1)} %collective-permute-done.16.refs_3_), channel_id=1, source_target_pairs={{0,16},{16,0},{32,48},{48,32},{64,80},{80,64},{96,112},{112,96},{1... | collective-permute-start | bytes 884744 | tf_op jit(solution)/shard_map/ppermute | solution.py:496
  141.3 5.0 %collective-permute-start.21 = (f32[24,128]{1,0:T(8,128)S(1)}, f32[24,128]{1,0:T(8,128)S(1)}, u32[]{:S(2)}, u32[]{:S(2)}) collective-permute-start(f32[24,128]{1,0:T(8,128)S(1)} %get-tuple-element.98.refs_3_), channel_id=1, source_target_pairs={{0,4},{1,5},{2,6},{3,7},{4,8},{5,9},{6,10},{7,11},{8,12},{9,13},{1... | collective-permute-start | bytes 36872 | tf_op jit(solution)/shard_map/ppermute | solution.py:520
  141.8 5.2 %collective-permute-start.22 = (f32[24,128]{1,0:T(8,128)S(1)}, f32[24,128]{1,0:T(8,128)S(1)}, u32[]{:S(2)}, u32[]{:S(2)}) collective-permute-start(f32[24,128]{1,0:T(8,128)S(1)} %get-tuple-element.98.refs_3_), channel_id=1, source_target_pairs={{0,8},{1,9},{2,10},{3,11},{4,12},{5,13},{6,14},{7,15},{8,0},{9,1},... | collective-permute-start | bytes 36872 | tf_op jit(solution)/shard_map/ppermute | solution.py:520
  144.4 3.7 %collective-permute-start.23 = (f32[24,128]{1,0:T(8,128)S(1)}, f32[24,128]{1,0:T(8,128)S(1)}, u32[]{:S(2)}, u32[]{:S(2)}) collective-permute-start(f32[24,128]{1,0:T(8,128)S(1)} %get-tuple-element.98.refs_3_), channel_id=1, source_target_pairs={{0,12},{1,13},{2,14},{3,15},{4,0},{5,1},{6,2},{7,3},{8,4},{9,5},{1... | collective-permute-start | bytes 36872 | tf_op jit(solution)/shard_map/ppermute | solution.py:520

commit v6 on v3

--- a/solution.py
+++ b/solution.py
@@ -21,7 +21,7 @@
 HIGH = lax.Precision.HIGHEST
 F32 = jnp.float32
 BF16 = jnp.bfloat16
-COLS = 384
+COLS = 768
 BIG = 14 << 20
 
 
@@ -62,89 +62,118 @@
     return jnp.concatenate(out, axis=1).astype(jnp.int32) - 1, dest
 
 
-def gather_kernel(idx_ref, table_ref, mats_ref, sent_ref, slot_ref, most_ref, hot_ref, *, peers):
+def half_of(row, second):
+    half = row.shape[1] // 2
+    flag = jnp.where(second, 1.0, 0.0)
+    return jnp.where(flag > 0.5, row[:, half:], row[:, :half])
+
+
+def gather_kernel(idx_ref, table_ref, *refs, peers):
+    own = peers is not None
+    mats_ref, *outs, hot_ref = refs if own else refs[1:]
     step = pl.program_id(0)
     mode = lax.axis_index("cores")
-    leftward = mode < MODES // 2
-    slab = N // peers
 
     @pl.when(step == 0)
     def _():
-        row = idx_ref[pl.ds(mode, 1), :]
-        count = row.shape[1]
-        hot_ref[...] = (iota((N, count), 0) == row).astype(BF16)
-        place, dest = ranks(row, peers, slab)
-        slot_ref[0:1, :] = place
-        slot_ref[1:2, :] = dest
-        slot_ref[2:3, :] = row - dest * slab
-        slot_ref[3:8, :] = jnp.zeros((5, count), jnp.int32)
-        every = idx_ref[...] // slab
-        most = jnp.zeros((MODES, 1), F32)
-        for j in range(peers):
-            most = jnp.maximum(most, jnp.sum((every == j).astype(F32), axis=1, keepdims=True))
-        most_ref[...] = jnp.broadcast_to(jnp.max(most, axis=0, keepdims=True), (8, 128))
+        which = mode if own else mode + 1 - 2 * (mode % 2)
+        row = idx_ref[pl.ds(which, 1), :]
+        half = half_of(row, mode % 2 == 1)
+        hot_ref[...] = (iota(hot_ref.shape, 0) == half).astype(BF16)
+        if own:
+            slot_ref, most_ref = outs
+            slab = N // peers
+            place, dest = ranks(row, peers, slab)
+            slot_ref[0:1, :] = place
+            slot_ref[1:2, :] = dest
+            slot_ref[2:3, :] = row - dest * slab
+            slot_ref[3:8, :] = jnp.zeros((5, row.shape[1]), jnp.int32)
+            every = idx_ref[...] // slab
+            most = jnp.zeros((MODES, 1), F32)
+            for j in range(peers):
+                most = jnp.maximum(most, jnp.sum((every == j).astype(F32), axis=1, keepdims=True))
+            most_ref[...] = jnp.broadcast_to(jnp.max(most, axis=0, keepdims=True), (8, 128))
 
     hot = hot_ref[...]
     hi, lo = halves(table_ref[...])
-    out = dot_rows(hi, hot) + dot_rows(lo, hot)
-    mats_ref[...] = out
-
-    @pl.when(jnp.logical_and(leftward, step == 0))
-    def _():
-        sent_ref[...] = out[0:R]
-
-    @pl.when(jnp.logical_not(leftward))
-    def _():
-        per = COLS // R
-        rows = jnp.concatenate([out[i * R : i * R + 1] for i in range(per)], axis=0)
-        sent_ref[pl.ds(pl.multiple_of(step * per, per), per), :] = rows
-
-
-def times_left(mats_ref, vec_ref, out_ref):
+    mats_ref[...] = dot_rows(hi, hot) + dot_rows(lo, hot)
+
+
+def times(left, mats_ref, base, vec_ref, out_ref):
     count = vec_ref.shape[1]
 
-    def chunk(c, _):
-        lanes = pl.ds(pl.multiple_of(c * 128, 128), 128)
-        acc = [jnp.zeros((R, 128), F32) for _ in range(2)]
-        for a in range(R):
-            acc[a % 2] = acc[a % 2] + mats_ref[a * R : (a + 1) * R, lanes] * vec_ref[a : a + 1, lanes]
-        out_ref[:, lanes] = acc[0] + acc[1]
-        return 0
-
-    lax.fori_loop(0, count // 128, chunk, 0)
-
-
-def times_right(mats_ref, vec_ref, out_ref):
-    count = vec_ref.shape[1]
-
-    def chunk(c, _):
-        lanes = pl.ds(pl.multiple_of(c * 128, 128), 128)
-        vec = vec_ref[:, lanes]
-        for a in range(0, R, 8):
-            rows = [
-                jnp.sum(mats_ref[(a + i) * R : (a + i + 1) * R, lanes] * vec, axis=0, keepdims=True)
-                for i in range(8)
-            ]
-            out_ref[a : a + 8, lanes] = jnp.concatenate(rows, axis=0)
-        return 0
-
-    lax.fori_loop(0, count // 128, chunk, 0)
-
-
-def apply(left, mats_ref, vec_ref, out_ref):
+    def rows(a):
+        return pl.ds(pl.multiple_of(base + a * R, 8), R)
+
     @pl.when(left)
     def _():
-        times_left(mats_ref, vec_ref, out_ref)
+        def chunk(c, _):
+            lanes = pl.ds(pl.multiple_of(c * 128, 128), 128)
+            acc = [jnp.zeros((R, 128), F32) for _ in range(2)]
+            for a in range(R):
+                acc[a % 2] = acc[a % 2] + mats_ref[rows(a), lanes] * vec_ref[a : a + 1, lanes]
+            out_ref[:, lanes] = acc[0] + acc[1]
+            return 0
+
+        lax.fori_loop(0, count // 128, chunk, 0)
 
     @pl.when(jnp.logical_not(left))
     def _():
-        times_right(mats_ref, vec_ref, out_ref)
-
-
-def hop_kernel(mats_ref, vec_ref, out_ref, *, second):
+        def chunk(c, _):
+            lanes = pl.ds(pl.multiple_of(c * 128, 128), 128)
+            vec = vec_ref[:, lanes]
+            for a in range(0, R, 8):
+                sums = [
+                    jnp.sum(mats_ref[rows(a + i), lanes] * vec, axis=0, keepdims=True) for i in range(8)
+                ]
+                out_ref[a : a + 8, lanes] = jnp.concatenate(sums, axis=0)
+            return 0
+
+        lax.fori_loop(0, count // 128, chunk, 0)
+
+
+def both_modes(turn, mats_ref, vec_ref, mid_ref, out_ref):
     mode = lax.axis_index("cores")
-    left = (mode >= MODES // 2) if second else (mode < MODES // 2)
-    apply(left, mats_ref, vec_ref, out_ref)
+    chips = MODES // 2
+    left = (mode // 2 < chips // 2) if turn < chips // 2 else (mode // 2 >= chips // 2)
+    even = (mode % 2) * RR
+    base = jnp.where(left, even, RR - even)
+    times(left, mats_ref, base, vec_ref, mid_ref)
+    times(left, mats_ref, RR - base, mid_ref, out_ref)
+
+
+def unit_at_ends(shape_):
+    chip = lax.axis_index("cores") // 2
+    edge = jnp.where(jnp.logical_or(chip == 0, chip == MODES // 2 - 1), 1.0, 0.0)
+    return jnp.where(iota(shape_, 0) == 0, edge, 0.0)
+
+
+def hop_kernel(mats_ref, *refs, turn):
+    vec_ref, mid_ref, out_ref = refs if turn else (refs[2], refs[0], refs[1])
+    if turn == 0:
+        vec_ref[...] = unit_at_ends(vec_ref.shape)
+    both_modes(turn, mats_ref, vec_ref, mid_ref, out_ref)
+
+
+def finish_kernel(mats_ref, *refs):
+    recv, mids = refs[0:3], refs[3:6]
+    out2_ref, obs_ref, own_ref, other_ref, mid_ref, out_ref = refs[6:]
+    mode = lax.axis_index("cores")
+    both_modes(3, mats_ref, recv[2], mid_ref, out_ref)
+    end1 = unit_at_ends(mid_ref.shape) + recv[0][...]
+    mid1 = mids[0][...] + mids[1][...]
+    end2 = recv[1][...] + recv[2][...]
+    mid2 = mids[2][...] + mid_ref[...]
+    predicted = jnp.sum((out2_ref[...] + out_ref[...]) * end1, axis=0, keepdims=True)
+    residual = predicted - half_of(obs_ref[...], mode % 2 == 1)
+    early = jnp.where(mode // 2 < MODES // 4, 1.0, 0.0) > 0.5
+    even = (jnp.where(early, end1, end2), jnp.where(early, mid2, mid1) * residual)
+    odd = (jnp.where(early, mid1, mid2), jnp.where(early, end2, end1) * residual)
+    second = jnp.where(mode % 2 == 1, 1.0, 0.0) > 0.5
+    for k in range(2):
+        rows = slice(k * R, (k + 1) * R)
+        own_ref[rows, :] = jnp.where(second, odd[k], even[k])
+        other_ref[rows, :] = jnp.where(second, even[k], odd[k])
 
 
 def spread(values, slot_ref, most_ref, turn, pay_ref):
@@ -166,27 +195,13 @@
         pay_ref[peer, 97:98, :] = most_ref[0:1, :]
 
 
-def route_kernel(mats_ref, *refs):
-    moved = refs[: MODES - 1]
-    obs_ref, slot_ref, most_ref, pay_ref, val_ref, one_ref, two_ref, tmp_ref = refs[MODES - 1 :]
-    mode = lax.axis_index("cores")
-    early = mode < MODES // 2
-    edge = jnp.where(jnp.logical_or(mode == 0, mode == MODES - 1), 1.0, 0.0)
-    one = jnp.where(iota(one_ref.shape, 0) == 0, edge, 0.0)
-    one_ref[...] = one + ((moved[0][...] + moved[1][...]) + moved[2][...])
-    two_ref[...] = (moved[3][...] + moved[4][...]) + (moved[5][...] + moved[6][...])
-    apply(jnp.logical_not(early), mats_ref, two_ref, tmp_ref)
-    one = one_ref[...]
-    two = two_ref[...]
-    predicted = jnp.sum(tmp_ref[...] * one, axis=0, keepdims=True)
-    residual = predicted - obs_ref[...]
-    flag = jnp.where(early, 1.0, 0.0)
-    left = jnp.where(flag > 0.5, one, two)
-    right = jnp.where(flag > 0.5, two, one) * residual
-    count = one.shape[1]
-    values = jnp.concatenate(
-        [left, right, slot_ref[2:3, :].astype(F32), jnp.zeros((FEATS - 97, count), F32)], axis=0
-    )
+def route_kernel(own_ref, got_ref, slot_ref, most_ref, pay_ref, val_ref):
+    second = jnp.where(lax.axis_index("cores") % 2 == 1, 1.0, 0.0) > 0.5
+    own = own_ref[...]
+    got = got_ref[...]
+    vecs = jnp.concatenate([jnp.where(second, got, own), jnp.where(second, own, got)], axis=1)
+    loc = slot_ref[2:3, :].astype(F32)
+    values = jnp.concatenate([vecs, loc, jnp.zeros((FEATS - 97, vecs.shape[1]), F32)], axis=0)
     val_ref[...] = values
     spread(values, slot_ref, most_ref, 0, pay_ref)
 
@@ -389,49 +404,75 @@
     idx = indices.T
     step = step_size.reshape(1)
 
-    mats, sent, slot, most = pl.pallas_call(
+    half = count // 2
+    siblings = [(m, m ^ 1) for m in range(MODES)]
+    other_table = lax.ppermute(table, "cores", siblings)
+    steps = RR // COLS
+    params = pltpu.CompilerParams(vmem_limit_bytes=BIG)
+    in_specs = [
+        pl.BlockSpec((MODES, count), lambda i: (0, 0)),
+        pl.BlockSpec((N, COLS), lambda i: (0, i)),
+    ]
+    hot = [pltpu.VMEM((N, half), BF16)]
+    idx, table_in = [pltpu.with_memory_space_constraint(a, pltpu.HBM) for a in (idx, table)]
+    mats, slot, most = pl.pallas_call(
         functools.partial(gather_kernel, peers=peers),
-        grid=(RR // COLS,),
-        in_specs=[
-            pl.BlockSpec((MODES, count), lambda i: (0, 0)),
-            pl.BlockSpec((N, COLS), lambda i: (0, i)),
-        ],
+        grid=(steps,),
+        in_specs=in_specs,
         out_specs=[
-            pl.BlockSpec((COLS, count), lambda i: (i, 0)),
-            pl.BlockSpec((R, count), lambda i: (0, 0)),
+            pl.BlockSpec((COLS, half), lambda i: (i, 0)),
             pl.BlockSpec((8, count), lambda i: (0, 0)),
             pl.BlockSpec((8, 128), lambda i: (0, 0)),
         ],
-        out_shape=[shape(RR, count), shape(R, count), shape(8, count, dtype=jnp.int32), shape(8, 128)],
-        scratch_shapes=[pltpu.VMEM((N, count), BF16)],
-        compiler_params=pltpu.CompilerParams(vmem_limit_bytes=BIG),
+        out_shape=[shape(2 * RR, half), shape(8, count, dtype=jnp.int32), shape(8, 128)],
+        scratch_shapes=hot,
+        compiler_params=params,
         name="gather",
-    )(idx, pltpu.with_memory_space_constraint(table, pltpu.HBM))
+    )(idx, table_in)
+    mats = pl.pallas_call(
+        functools.partial(gather_kernel, peers=None),
+        grid=(steps,),
+        in_specs=in_specs + [pl.BlockSpec(memory_space=pl.ANY)],
+        out_specs=pl.BlockSpec((COLS, half), lambda i: (i + steps, 0)),
+        out_shape=shape(2 * RR, half),
+        scratch_shapes=hot,
+        input_output_aliases={2: 0},
+        compiler_params=params,
+        name="gather_other",
+    )(idx, other_table, mats)
 
     first = lax.axis_index("samp") * slab
     kept = lax.dynamic_slice_in_dim(table, first, slab, 0)
     base = kept.reshape(GROUPS, WIDE, R, R).transpose(0, 2, 1, 3)
     base = base.reshape(ROWS, LANES)
 
-    every = []
-    for turn in range(MODES - 1):
-        if turn > 0:
-            sent = call(
-                functools.partial(hop_kernel, second=turn >= MODES // 2),
-                shape(R, count),
-                [vmem(), vmem()],
-                name=f"hop{turn}",
-            )(mats, moved)
-        moved = lax.ppermute(sent, "cores", [(turn, turn + 1), (7 - turn, 6 - turn)])
-        every.append(moved)
-
+    vec = shape(R, half)
+    recv, mids = [], []
+    for turn in range(3):
+        mid, out = call(
+            functools.partial(hop_kernel, turn=turn),
+            [vec, vec],
+            [vmem()] * (2 if turn else 1),
+            [] if turn else [pltpu.VMEM((R, half), F32)],
+            name=f"hop{turn}",
+        )(mats, *recv[-1:])
+        pairs = [(2 * a + h, 2 * b + h) for a, b in ((turn, turn + 1), (3 - turn, 2 - turn)) for h in range(2)]
+        recv.append(lax.ppermute(out, "cores", pairs))
+        mids.append(mid)
+    own_vecs, other_vecs = call(
+        finish_kernel,
+        [shape(2 * R, half)] * 2,
+        [vmem()] * 9,
+        [pltpu.VMEM((R, half), F32)] * 2,
+        name="finish",
+    )(mats, *recv, *mids, out, observed.reshape(1, count))
+    got_vecs = lax.ppermute(other_vecs, "cores", siblings)
     pay, values = call(
         route_kernel,
         (shape(peers, FEATS, SLOTS), shape(FEATS, count)),
-        [vmem()] * (MODES + 3),
-        [pltpu.VMEM((R, count), F32)] * 3,
+        [vmem()] * 4,
         name="route",
-    )(mats, *every, observed.reshape(1, count), slot, most)
+    )(own_vecs, got_vecs, slot, most)
 
     def exchanged(block):
         return lax.all_to_all(block, "samp", 0, 0, tiled=True)
@@ -472,7 +513,6 @@
         for by in range(1, side)
     ]
     level = [[(p, along(1, p, by)) for p in range(peers)] for by in range(1, side)]
-    siblings = [(m, m ^ 1) for m in range(MODES)]
     own = [updated] + [lax.ppermute(updated, ("cores", "samp"), pairs) for pairs in ring]
     other = [lax.ppermute(o, "cores", siblings) for o in own]
     tall = shape(WAYS * ROWS, LANES, dtype=BF16)

time: 161 us -> 149 us (0.925)
  blocking collectives: 50.6 us -> 44.2 us
  starting transfers between devices: 25.6 us -> 20.7 us
  waiting for transfers between devices: 37 us -> 41 us
  Pallas kernels: 40 us -> 36.9 us
    all_to_all x3, blocking collectives: 50.6 us -> 44.2 us  [on_device(): lax.all_to_all(res[0], ('cores', 'samp'), 0, 0, axis_index_groups=groups,...]
    ppermute x4, starting transfers between devices: 2.82 us -> 0.01 us  [on_device(): other = [lax.ppermute(o, 'cores', siblings) for o in own]]
    ppermute x7 -> x5, starting transfers between devices: 7.21 us -> 5.06 us  [the longest x3 4.97 us: on_device(): recv.append(lax.ppermute(out, 'cores', pairs))]
    ppermute x3, waiting for transfers between devices: 6.38 us -> 8.15 us  [on_device(): lax.ppermute(updated, ('cores', 'samp'), pairs)]
    pallas_call x7 -> x6, Pallas kernels: 16.8 us -> 15.3 us  [the longest x1 5.34 us: on_device(): pl.pallas_call(functools.partial(gather_kernel, peers=peers), grid=(steps...]
    ppermute x7 -> x5, waiting for transfers between devices: 15 us -> 15.9 us  [the longest x3 11.7 us: on_device(): recv.append(lax.ppermute(out, 'cores', pairs))]
  transfers between devices with their start and end apart: 18 -> 16, of which waited for: 11 -> 13; matrix products, arithmetic and copies ran while one was open for 1% -> 1% of each run, Pallas kernels for 0% -> 4%
where the time goes in v6:
time: 149 us; the launch traced here: 148 us
  blocking collectives  44.2 us (30%)
  waiting for transfers between devices  41 us (28%)
  Pallas kernels  36.9 us (25%)
  starting transfers between devices  20.7 us (14%)
  local copies, waits for them, and re-layouts  3.45 us (2%)
    all_to_all x3, blocking collectives, on_device(): lax.all_to_all(res[0], ('cores', 'samp'), 0, 0, axis_index_groups=groups,...  44.2 us
    all_to_all x1, waiting for transfers between devices, exchanged(): return lax.all_to_all(block, 'samp', 0, 0, tiled=True)  12.8 us
    ppermute x3, waiting for transfers between devices, on_device(): recv.append(lax.ppermute(out, 'cores', pairs))  11.7 us
    pallas_call x4, Pallas kernels, on_device(): call(functools.partial(pair_kernel, pair=pair), outs, [vmem()] * len(ins)...  10.4 us
    ppermute x3, waiting for transfers between devices, on_device(): lax.ppermute(updated, ('cores', 'samp'), pairs)  8.15 us
    all_to_all x1, starting transfers between devices, exchanged(): return lax.all_to_all(block, 'samp', 0, 0, tiled=True)  7.88 us
    pallas_call x1, Pallas kernels, on_device(): pl.pallas_call(functools.partial(gather_kernel, peers=peers), grid=(steps...  5.34 us
    pallas_call x1, Pallas kernels, on_device(): call(final_kernel, shape(ROWS, LANES), [vmem()] * (MODES // 2 - 1 + WAYS...  5.27 us
  transfers between devices with their start and end apart: 16, of which 13 were waited for; matrix products, arithmetic and copies ran while one was open for 1% of the time, Pallas kernels for 4%

profile of v6, /device:TPU:16, one launch (start us, length us, event | category | flops | bytes accessed | tf_op | source)
XLA Modules:
  0.0 147.7 jit_solution(13993156247775608448)
XLA Ops:
  0.0 5.3 %gather.1 = (f32[4608,512]{1,0:T(8,128)S(1)}, s32[8,1024]{1,0:T(8,128)S(1)}, f32[8,128]{1,0:T(8,128)S(1)}) custom-call(s32[8,1024]{1,0:T(8,128)} %bitcast.21, f32[512,2304]{1,0:T(8,128)} %bitcast.18), custom_call_target="tpu_custom_call" | custom-call | tf_op jit(solution)/shard_map/gather/pallas_call | solution.py:418
  5.3 2.8 %collective-permute-done.table_ref = f32[512,2304]{1,0:T(8,128)S(1)} collective-permute-done((f32[512,2304]{1,0:T(8,128)}, f32[512,2304]{1,0:T(8,128)S(1)}, u32[]{:S(2)}, u32[]{:S(2)}) %collective-permute-start) | collective-permute-done | bytes 4718624 | tf_op jit(solution)/shard_map/ppermute | solution.py:409
  8.1 4.2 %gather_other.1.mats_ref = f32[4608,512]{1,0:T(8,128)S(1)} custom-call(s32[8,1024]{1,0:T(8,128)} %bitcast.22, f32[512,2304]{1,0:T(8,128)S(1)} %collective-permute-done.table_ref, f32[4608,512]{1,0:T(8,128)S(1)} %get-tuple-element.77.refs_0_), custom_call_target="tpu_custom_call", output_to_operand_aliasing={{}: (2, {})} | custom-call | tf_op jit(solution)/shard_map/gather_other/pallas_call | solution.py:432
  12.3 1.4 hop0.1
  13.7 1.3 collective-permute-start.1
  15.0 5.4 %collective-permute-done.1.refs_0_ = f32[48,512]{1,0:T(8,128)S(1)} collective-permute-done((f32[48,512]{1,0:T(8,128)S(1)}, f32[48,512]{1,0:T(8,128)S(1)}, u32[]{:S(2)}, u32[]{:S(2)}) %collective-permute-start.1) | collective-permute-done | bytes 98336 | tf_op jit(solution)/shard_map/ppermute | solution.py:460
  20.5 1.4 hop1.1
  21.9 2.4 %collective-permute-start.2 = (f32[48,512]{1,0:T(8,128)S(1)}, f32[48,512]{1,0:T(8,128)S(1)}, u32[]{:S(2)}, u32[]{:S(2)}) collective-permute-start(f32[48,512]{1,0:T(8,128)S(1)} %get-tuple-element.79), channel_id=1, source_target_pairs={{32,64},{48,80},{64,32},{80,48},{33,65},{49,81},{65,33},{81,49},{3... | collective-permute-start | bytes 294920 | tf_op jit(solution)/shard_map/ppermute | solution.py:460
  24.3 4.1 %collective-permute-done.2.refs_0_.refs_1_ = f32[48,512]{1,0:T(8,128)S(1)} collective-permute-done((f32[48,512]{1,0:T(8,128)S(1)}, f32[48,512]{1,0:T(8,128)S(1)}, u32[]{:S(2)}, u32[]{:S(2)}) %collective-permute-start.2) | collective-permute-done | bytes 98336 | tf_op jit(solution)/shard_map/ppermute | solution.py:460
  28.4 1.4 hop2.1
  29.8 1.3 collective-permute-start.3
  31.1 2.2 %collective-permute-done.3.refs_2_ = f32[48,512]{1,0:T(8,128)S(1)} collective-permute-done((f32[48,512]{1,0:T(8,128)S(1)}, f32[48,512]{1,0:T(8,128)S(1)}, u32[]{:S(2)}, u32[]{:S(2)}) %collective-permute-start.3) | collective-permute-done | bytes 98336 | tf_op jit(solution)/shard_map/ppermute | solution.py:460
  33.3 1.5 %finish.1 = (f32[96,512]{1,0:T(8,128)S(1)}, f32[96,512]{1,0:T(8,128)S(1)}) custom-call(f32[4608,512]{1,0:T(8,128)S(1)} %gather_other.1.mats_ref, f32[48,512]{1,0:T(8,128)S(1)} %collective-permute-done.1.refs_0_, f32[48,512]{1,0:T(8,128)S(1)} %collective-permute-done.2.refs_0_.refs_1_, f32[48,512]{1,0:T(8,128)S(1)} %collective-permute-done.3.refs_2_, ...), custom_call_target="tpu_custom_call" | custom-call | tf_op jit(solution)/shard_map/finish/pallas_call | solution.py:462
  34.9 1.4 collective-permute-done.4.got_ref
  36.4 2.4 %route.1 = (f32[16,104,128]{2,1,0:T(8,128)}, f32[104,1024]{1,0:T(8,128)S(1)}) custom-call(f32[96,512]{1,0:T(8,128)S(1)} %get-tuple-element.84.own_ref, f32[96,512]{1,0:T(8,128)S(1)} %collective-permute-done.4.got_ref, s32[8,1024]{1,0:T(8,128)S(1)} %get-tuple-element.175.slot_ref, f32[8,128]{1,0:T(8,128)S(1)} %get-tuple-element.176.most_ref), custom_call_target="tpu_custom_call" | custom-call | tf_op jit(solution)/shard_map/route/pallas_call | solution.py:470
  38.8 7.9 %all-to-all-start.1 = ((f32[16,104,128]{2,1,0:T(8,128)}), f32[16,104,128]{2,1,0:T(8,128)S(1)}, u32[]{:S(2)}, u32[]{:S(2)}) async-start(f32[16,104,128]{2,1,0:T(8,128)} %get-tuple-element.88), calls=%async_computation.1 | async-start | bytes 1703936 | tf_op jit(solution)/shard_map/all_to_all | solution.py:478
  49.3 12.8 %all-to-all-done.1.recv_ref = f32[16,104,128]{2,1,0:T(8,128)S(1)} async-done(((f32[16,104,128]{2,1,0:T(8,128)}), f32[16,104,128]{2,1,0:T(8,128)S(1)}, u32[]{:S(2)}, u32[]{:S(2)}) %all-to-all-start.1) | async-done | bytes 852000 | tf_op jit(solution)/shard_map/all_to_all | solution.py:478
  62.1 2.1 %collect.2 = (f32[192,384]{1,0:T(8,128)S(1)}, s32[1]{0:T(128)}) custom-call(f32[1]{0:T(128)} %bitcast.15.step_ref, f32[16,104,128]{2,1,0:T(8,128)S(1)} %all-to-all-done.1.recv_ref, f32[192,384]{1,0:T(8,128)S(1)} %reshape.26.base_ref), custom_call_target="tpu_custom_call" | custom-call | tf_op jit(solution)/shard_map/collect/pallas_call | solution.py:481
  65.8 2.5 %collective-permute-start.7 = (f32[192,384]{1,0:T(8,128)S(1)}, f32[192,384]{1,0:T(8,128)S(1)}, u32[]{:S(2)}, u32[]{:S(2)}) collective-permute-start(f32[192,384]{1,0:T(8,128)S(1)} %get-tuple-element.92.refs_0_.refs_7_), channel_id=1, source_target_pairs={{0,3},{1,0},{2,1},{3,2},{4,7},{5,4},{6,5},{7,6},{8,11},{9,8},{10,9... | collective-permute-start | bytes 884744 | tf_op jit(solution)/shard_map/ppermute | solution.py:516
  68.3 5.0 %collective-permute-done.6.refs_2_ = f32[192,384]{1,0:T(8,128)S(1)} collective-permute-done((f32[192,384]{1,0:T(8,128)S(1)}, f32[192,384]{1,0:T(8,128)S(1)}, u32[]{:S(2)}, u32[]{:S(2)}) %collective-permute-start.6) | collective-permute-done | bytes 294944 | tf_op jit(solution)/shard_map/ppermute | solution.py:516
  74.2 2.2 %collective-permute-done.5.refs_1_ = f32[192,384]{1,0:T(8,128)S(1)} collective-permute-done((f32[192,384]{1,0:T(8,128)S(1)}, f32[192,384]{1,0:T(8,128)S(1)}, u32[]{:S(2)}, u32[]{:S(2)}) %collective-permute-start.5) | collective-permute-done | bytes 294944 | tf_op jit(solution)/shard_map/ppermute | solution.py:516
  76.4 1.6 %collective-permute-done.9.refs_5_ = f32[192,384]{1,0:T(8,128)S(1)} collective-permute-done((f32[192,384]{1,0:T(8,128)S(1)}, f32[192,384]{1,0:T(8,128)S(1)}, u32[]{:S(2)}, u32[]{:S(2)}) %collective-permute-start.9) | collective-permute-done | bytes 294944 | tf_op jit(solution)/shard_map/ppermute | solution.py:517
  78.0 1.4 arrange.1
  79.4 2.4 %pair0.1 = (f32[32,24,128]{2,1,0:T(8,128)S(1)}, f32[24,128]{1,0:T(8,128)S(1)}) custom-call(bf16[768,384]{1,0:T(8,128)(2,1)S(1)} %get-tuple-element.93.refs_0_.refs_1_.refs_4_, bf16[768,384]{1,0:T(8,128)(2,1)S(1)} %get-tuple-element.94.refs_1_.refs_2_.refs_5_, bf16[384,768]{1,0:T(8,128)(2,1)S(1)} %get-tuple-element.95.refs_2_.refs_3_.refs_6_, ...), custom_call_target="tpu_custom_call" | custom-call | tf_op jit(solution)/shard_map/pair0/pallas_call | solution.py:531
  81.8 15.5 %all_to_all.26.refs_0_ = f32[32,24,128]{2,1,0:T(8,128)S(1)} all-to-all(f32[32,24,128]{2,1,0:T(8,128)S(1)} %get-tuple-element.101), channel_id=1, replica_groups={{0,1,2,3,4,5,6,7,8,9,10,11,12,13,14,15,32,33,34,35,36,37,38,39,40,41,42..., dimensions={0} | all-to-all | bytes 786432 | tf_op jit(solution)/shard_map/all_to_all | solution.py:549
  97.4 3.2 %pair1.1 = (f32[32,24,128]{2,1,0:T(8,128)S(1)}, f32[24,128]{1,0:T(8,128)S(1)}, f32[24,128]{1,0:T(8,128)S(1)}) custom-call(f32[32,24,128]{2,1,0:T(8,128)S(1)} %all_to_all.26.refs_0_, bf16[768,384]{1,0:T(8,128)(2,1)S(1)} %get-tuple-element.93.refs_0_.refs_1_.refs_4_, bf16[768,384]{1,0:T(8,128)(2,1)S(1)} %get-tuple-element.94.refs_1_.refs_2_.refs_5_, ...), custom_call_target="tpu_custom_call" | custom-call | tf_op jit(solution)/shard_map/pair1/pallas_call | solution.py:531
  100.5 14.0 %all_to_all.27.refs_0_ = f32[32,24,128]{2,1,0:T(8,128)S(1)} all-to-all(f32[32,24,128]{2,1,0:T(8,128)S(1)} %get-tuple-element.103), channel_id=1, replica_groups={{32,33,34,35,36,37,38,39,40,41,42,43,44,45,46,47,64,65,66,67,68,69,70,7..., dimensions={0} | all-to-all | bytes 786432 | tf_op jit(solution)/shard_map/all_to_all | solution.py:549
  114.5 3.2 %pair2.1 = (f32[32,24,128]{2,1,0:T(8,128)S(1)}, f32[24,128]{1,0:T(8,128)S(1)}, f32[24,128]{1,0:T(8,128)S(1)}) custom-call(f32[32,24,128]{2,1,0:T(8,128)S(1)} %all_to_all.27.refs_0_, bf16[768,384]{1,0:T(8,128)(2,1)S(1)} %get-tuple-element.93.refs_0_.refs_1_.refs_4_, bf16[768,384]{1,0:T(8,128)(2,1)S(1)} %get-tuple-element.94.refs_1_.refs_2_.refs_5_, ...), custom_call_target="tpu_custom_call" | custom-call | tf_op jit(solution)/shard_map/pair2/pallas_call | solution.py:531
  117.7 14.7 %all_to_all.28.refs_0_ = f32[32,24,128]{2,1,0:T(8,128)S(1)} all-to-all(f32[32,24,128]{2,1,0:T(8,128)S(1)} %get-tuple-element.105), channel_id=1, replica_groups={{64,65,66,67,68,69,70,71,72,73,74,75,76,77,78,79,96,97,98,99,100,101,10..., dimensions={0} | all-to-all | bytes 786432 | tf_op jit(solution)/shard_map/all_to_all | solution.py:549
  132.4 1.6 %pair3.1 = (f32[24,128]{1,0:T(8,128)S(1)}, f32[24,128]{1,0:T(8,128)S(1)}) custom-call(f32[32,24,128]{2,1,0:T(8,128)S(1)} %all_to_all.28.refs_0_, f32[24,128]{1,0:T(8,128)S(1)} %get-tuple-element.106.refs_1_, f32[24,128]{1,0:T(8,128)S(1)} %get-tuple-element.107.refs_2_, f32[24,128]{1,0:T(8,128)S(1)} %get-tuple-element.108.refs_3_, ...), custom_call_target="tpu_custom_call" | custom-call | tf_op jit(solution)/shard_map/pair3/pallas_call | solution.py:531
  134.6 2.7 %collective-permute-start.13 = (f32[24,128]{1,0:T(8,128)S(1)}, f32[24,128]{1,0:T(8,128)S(1)}, u32[]{:S(2)}, u32[]{:S(2)}) collective-permute-start(f32[24,128]{1,0:T(8,128)S(1)} %get-tuple-element.110.refs_3_), channel_id=1, source_target_pairs={{0,8},{1,9},{2,10},{3,11},{4,12},{5,13},{6,14},{7,15},{8,0},{9,1},... | collective-permute-start | bytes 36872 | tf_op jit(solution)/shard_map/ppermute | solution.py:541
  140.9 5.3 %final.1 = f32[192,384]{1,0:T(8,128)S(1)} custom-call(f32[24,128]{1,0:T(8,128)S(1)} %get-tuple-element.102.refs_0_, f32[24,128]{1,0:T(8,128)S(1)} %get-tuple-element.104.refs_1_, f32[24,128]{1,0:T(8,128)S(1)} %get-tuple-element.109.refs_2_, f32[24,128]{1,0:T(8,128)S(1)} %get-tuple-element.110.refs_3_, f32[24,128]{1,0:T(8,128)S(1)} %collective-permute-done.12.refs_4_, ...), custom_call_target="tpu_custom_call" | custom-call | tf_op jit(solution)/shard_map/final/pallas_call | solution.py:553
  (27 shorter events, 10.2 us)
Async XLA Ops:
  0.0 8.1 %collective-permute-start = (f32[512,2304]{1,0:T(8,128)}, f32[512,2304]{1,0:T(8,128)S(1)}, u32[]{:S(2)}, u32[]{:S(2)}) collective-permute-start(f32[512,2304]{1,0:T(8,128)} %bitcast.17), channel_id=1, source_target_pairs={{0,16},{16,0},{32,48},{48,32},{64,80},{80,64},{96,112},{112,96},{1... | collective-permute-start | bytes 14155784 | tf_op jit(solution)/shard_map/ppermute | solution.py:409
  13.7 6.7 %collective-permute-start.1 = (f32[48,512]{1,0:T(8,128)S(1)}, f32[48,512]{1,0:T(8,128)S(1)}, u32[]{:S(2)}, u32[]{:S(2)}) collective-permute-start(f32[48,512]{1,0:T(8,128)S(1)} %get-tuple-element.78), channel_id=1, source_target_pairs={{0,32},{16,48},{96,64},{112,80},{1,33},{17,49},{97,65},{113,81},{2... | collective-permute-start | bytes 294920 | tf_op jit(solution)/shard_map/ppermute | solution.py:460
  21.9 11.4 %copy-start = (f32[1024]{0:T(1024)S(1)}, f32[1024]{0:T(1024)}, u32[]{:S(2)}) copy-start(f32[1024]{0:T(1024)} %param.8) | copy-start | bytes 12292
  21.9 6.5 %collective-permute-start.2 = (f32[48,512]{1,0:T(8,128)S(1)}, f32[48,512]{1,0:T(8,128)S(1)}, u32[]{:S(2)}, u32[]{:S(2)}) collective-permute-start(f32[48,512]{1,0:T(8,128)S(1)} %get-tuple-element.79), channel_id=1, source_target_pairs={{32,64},{48,80},{64,32},{80,48},{33,65},{49,81},{65,33},{81,49},{3... | collective-permute-start | bytes 294920 | tf_op jit(solution)/shard_map/ppermute | solution.py:460
  29.8 3.5 %collective-permute-start.3 = (f32[48,512]{1,0:T(8,128)S(1)}, f32[48,512]{1,0:T(8,128)S(1)}, u32[]{:S(2)}, u32[]{:S(2)}) collective-permute-start(f32[48,512]{1,0:T(8,128)S(1)} %get-tuple-element.80.refs_6_), channel_id=1, source_target_pairs={{64,96},{80,112},{32,0},{48,16},{65,97},{81,113},{33,1},{49,17},{6... | collective-permute-start | bytes 294920 | tf_op jit(solution)/shard_map/ppermute | solution.py:460
  34.8 1.5 %collective-permute-start.4 = (f32[96,512]{1,0:T(8,128)S(1)}, f32[96,512]{1,0:T(8,128)S(1)}, u32[]{:S(2)}, u32[]{:S(2)}) collective-permute-start(f32[96,512]{1,0:T(8,128)S(1)} %get-tuple-element.85), channel_id=1, source_target_pairs={{0,16},{16,0},{32,48},{48,32},{64,80},{80,64},{96,112},{112,96},{1... | collective-permute-start | bytes 589832 | tf_op jit(solution)/shard_map/ppermute | solution.py:469
  38.8 23.3 %all-to-all-start.1 = ((f32[16,104,128]{2,1,0:T(8,128)}), f32[16,104,128]{2,1,0:T(8,128)S(1)}, u32[]{:S(2)}, u32[]{:S(2)}) async-start(f32[16,104,128]{2,1,0:T(8,128)} %get-tuple-element.88), calls=%async_computation.1 | async-start | bytes 1703936 | tf_op jit(solution)/shard_map/all_to_all | solution.py:478
  64.8 8.5 %collective-permute-start.6 = (f32[192,384]{1,0:T(8,128)S(1)}, f32[192,384]{1,0:T(8,128)S(1)}, u32[]{:S(2)}, u32[]{:S(2)}) collective-permute-start(f32[192,384]{1,0:T(8,128)S(1)} %get-tuple-element.92.refs_0_.refs_7_), channel_id=1, source_target_pairs={{0,2},{1,3},{2,0},{3,1},{4,6},{5,7},{6,4},{7,5},{8,10},{9,11},{10,... | collective-permute-start | bytes 884744 | tf_op jit(solution)/shard_map/ppermute | solution.py:516
  65.8 8.4 %collective-permute-start.7 = (f32[192,384]{1,0:T(8,128)S(1)}, f32[192,384]{1,0:T(8,128)S(1)}, u32[]{:S(2)}, u32[]{:S(2)}) collective-permute-start(f32[192,384]{1,0:T(8,128)S(1)} %get-tuple-element.92.refs_0_.refs_7_), channel_id=1, source_target_pairs={{0,3},{1,0},{2,1},{3,2},{4,7},{5,4},{6,5},{7,6},{8,11},{9,8},{10,9... | collective-permute-start | bytes 884744 | tf_op jit(solution)/shard_map/ppermute | solution.py:516
  68.3 8.2 %collective-permute-start.5 = (f32[192,384]{1,0:T(8,128)S(1)}, f32[192,384]{1,0:T(8,128)S(1)}, u32[]{:S(2)}, u32[]{:S(2)}) collective-permute-start(f32[192,384]{1,0:T(8,128)S(1)} %get-tuple-element.92.refs_0_.refs_7_), channel_id=1, source_target_pairs={{0,1},{1,2},{2,3},{3,0},{4,5},{5,6},{6,7},{7,4},{8,9},{9,10},{10,1... | collective-permute-start | bytes 884744 | tf_op jit(solution)/shard_map/ppermute | solution.py:516
  68.3 8.2 %collective-permute-start.8 = (f32[192,384]{1,0:T(8,128)S(1)}, f32[192,384]{1,0:T(8,128)S(1)}, u32[]{:S(2)}, u32[]{:S(2)}) collective-permute-start(f32[192,384]{1,0:T(8,128)S(1)} %get-tuple-element.92.refs_0_.refs_7_), channel_id=1, source_target_pairs={{0,16},{16,0},{32,48},{48,32},{64,80},{80,64},{96,112},{112,96},{1... | collective-permute-start | bytes 884744 | tf_op jit(solution)/shard_map/ppermute | solution.py:517
  73.3 3.1 %collective-permute-start.10 = (f32[192,384]{1,0:T(8,128)S(1)}, f32[192,384]{1,0:T(8,128)S(1)}, u32[]{:S(2)}, u32[]{:S(2)}) collective-permute-start(f32[192,384]{1,0:T(8,128)S(1)} %collective-permute-done.6.refs_2_), channel_id=1, source_target_pairs={{0,16},{16,0},{32,48},{48,32},{64,80},{80,64},{96,112},{112,96},{1... | collective-permute-start | bytes 884744 | tf_op jit(solution)/shard_map/ppermute | solution.py:517
  74.2 2.2 %collective-permute-start.11 = (f32[192,384]{1,0:T(8,128)S(1)}, f32[192,384]{1,0:T(8,128)S(1)}, u32[]{:S(2)}, u32[]{:S(2)}) collective-permute-start(f32[192,384]{1,0:T(8,128)S(1)} %collective-permute-done.7.refs_3_), channel_id=1, source_target_pairs={{0,16},{16,0},{32,48},{48,32},{64,80},{80,64},{96,112},{112,96},{1... | collective-permute-start | bytes 884744 | tf_op jit(solution)/shard_map/ppermute | solution.py:517
  76.4 1.6 %collective-permute-start.9 = (f32[192,384]{1,0:T(8,128)S(1)}, f32[192,384]{1,0:T(8,128)S(1)}, u32[]{:S(2)}, u32[]{:S(2)}) collective-permute-start(f32[192,384]{1,0:T(8,128)S(1)} %collective-permute-done.5.refs_1_), channel_id=1, source_target_pairs={{0,16},{16,0},{32,48},{48,32},{64,80},{80,64},{96,112},{112,96},{1... | collective-permute-start | bytes 884744 | tf_op jit(solution)/shard_map/ppermute | solution.py:517
  134.0 5.0 %collective-permute-start.12 = (f32[24,128]{1,0:T(8,128)S(1)}, f32[24,128]{1,0:T(8,128)S(1)}, u32[]{:S(2)}, u32[]{:S(2)}) collective-permute-start(f32[24,128]{1,0:T(8,128)S(1)} %get-tuple-element.110.refs_3_), channel_id=1, source_target_pairs={{0,4},{1,5},{2,6},{3,7},{4,8},{5,9},{6,10},{7,11},{8,12},{9,13},{1... | collective-permute-start | bytes 36872 | tf_op jit(solution)/shard_map/ppermute | solution.py:541
  134.6 5.2 %collective-permute-start.13 = (f32[24,128]{1,0:T(8,128)S(1)}, f32[24,128]{1,0:T(8,128)S(1)}, u32[]{:S(2)}, u32[]{:S(2)}) collective-permute-start(f32[24,128]{1,0:T(8,128)S(1)} %get-tuple-element.110.refs_3_), channel_id=1, source_target_pairs={{0,8},{1,9},{2,10},{3,11},{4,12},{5,13},{6,14},{7,15},{8,0},{9,1},... | collective-permute-start | bytes 36872 | tf_op jit(solution)/shard_map/ppermute | solution.py:541
  137.2 3.7 %collective-permute-start.14 = (f32[24,128]{1,0:T(8,128)S(1)}, f32[24,128]{1,0:T(8,128)S(1)}, u32[]{:S(2)}, u32[]{:S(2)}) collective-permute-start(f32[24,128]{1,0:T(8,128)S(1)} %get-tuple-element.110.refs_3_), channel_id=1, source_target_pairs={{0,12},{1,13},{2,14},{3,15},{4,0},{5,1},{6,2},{7,3},{8,4},{9,5},{1... | collective-permute-start | bytes 36872 | tf_op jit(solution)/shard_map/ppermute | solution.py:541

commit v7 on v6

--- a/solution.py
+++ b/solution.py
@@ -247,10 +247,24 @@
         mine = own[w][...]
         theirs = other[w][...]
         for k in range(2):
+            stack_ref, high_ref, low_ref = outs[3 * k : 3 * k + 3]
             flag = even_first if k == 0 else 1.0 - even_first
             core = jnp.where(flag > 0.5, mine, theirs)
-            outs[4 * k][rows, :], outs[4 * k + 1][rows, :] = halves(core)
-            outs[4 * k + 2][:, rows], outs[4 * k + 3][:, rows] = halves(core.T)
+            hi, lo = halves(core)
+            for g in range(GROUPS):
+                at = 3 * (w * GROUPS + g) * R
+                here = slice(g * R, (g + 1) * R)
+                stack_ref[at : at + R, :] = hi[here]
+                stack_ref[at + R : at + 2 * R, :] = hi[here]
+                stack_ref[at + 2 * R : at + 3 * R, :] = lo[here]
+            high_ref[:, rows], low_ref[:, rows] = halves(core.T)
+
+
+def stacked(square):
+    wide = jnp.concatenate([square, jnp.zeros((R, 128), F32)], axis=1)
+    hi = wide.astype(BF16).astype(F32)
+    lo = wide - hi
+    return (hi + (pltpu.roll(lo, R, 1) + pltpu.roll(hi, 2 * R, 1)))[:, : 3 * R].astype(BF16)
 
 
 def three(a, b):
@@ -270,14 +284,17 @@
 
 
 def pulled(before, core, prod_ref):
-    high, low, high_t, low_t = core
+    stack, high_t, low_t = core
     if before is None:
-        prod = (high[...], low[...])
+        first = [stack[3 * g * R : 3 * g * R + R, :] for g in range(WAYS * GROUPS)]
+        second = [stack[3 * g * R + 2 * R : 3 * g * R + 3 * R, :] for g in range(WAYS * GROUPS)]
+        prod = (jnp.concatenate(first, axis=0), jnp.concatenate(second, axis=0))
     else:
-        weights = halves(before[:, :R])
+        weights = stacked(before)
         for g in range(WAYS * GROUPS):
-            rows = slice(g * R, (g + 1) * R)
-            prod_ref[rows, :] = three(weights, (high[rows, :], low[rows, :]))
+            prod_ref[g * R : (g + 1) * R, :] = jnp.dot(
+                weights, stack[3 * g * R : 3 * (g + 1) * R, :], preferred_element_type=F32
+            )
         prod = halves(prod_ref[...])
     total = jnp.zeros((R, 256), F32)
     for part, slices in ((0, range(5)), (128, range(5, WIDE))):
@@ -295,8 +312,8 @@
     refs = list(refs)
     recv_ref = refs.pop(0) if pair else None
     saved = [refs.pop(0) for _ in range(pair)] if last else []
-    even = [refs.pop(0) for _ in range(4)]
-    odd = None if last else [refs.pop(0) for _ in range(4)]
+    even = [refs.pop(0) for _ in range(3)]
+    odd = None if last else [refs.pop(0) for _ in range(3)]
     prod_ref = refs.pop()
     if pair:
         sum_ref = refs.pop()
@@ -348,13 +365,29 @@
         start(own, jnp.where(mode == MODES - 1, 1.0, 0.0)),
         start(prev, jnp.where(mode == 0, 1.0, 0.0)),
     ]
-    for j in range(R):
-        for w in range(2):
-            m = mats[w]
-            pivot = m[j : j + 1, :]
-            scale = 1.0 / m[j : j + 1, j : j + 1]
-            col = jnp.where(row[:, 0:1] > j, m[:, j : j + 1] * scale, 0.0)
-            mats[w] = m - col * pivot
+    mats = [[m[8 * t : 8 * t + 8] for t in range(R // 8)] for m in mats]
+    for start_ in range(0, R, 4):
+        top = start_ // 8
+        below = range(top, R // 8)
+        cols = [
+            [{t: jnp.broadcast_to(m[t][:, start_ + k : start_ + k + 1], (8, 128)) for t in below} for k in range(4)]
+            for m in mats
+        ]
+        for k in range(4):
+            at = start_ + k - 8 * top
+            for w in range(2):
+                m, col = mats[w], cols[w]
+                scale = 1.0 / col[k][top][at : at + 1]
+                fact = {t: col[k][t] * scale for t in below}
+                fact[top] = jnp.where(iota((8, 128), 0) > at, fact[top], 0.0)
+                pivot = m[top][at : at + 1]
+                for q in range(k + 1, 4):
+                    lead = col[q][top][at : at + 1]
+                    for t in below:
+                        col[q][t] = col[q][t] - fact[t] * lead
+                for t in below:
+                    m[t] = m[t] - fact[t] * pivot
+    mats = [jnp.concatenate(m, axis=0) for m in mats]
     tri = []
     for w in range(2):
         diag = jnp.sum(jnp.where(lane == row, mats[w], 0.0), axis=1, keepdims=True)
@@ -515,10 +548,10 @@
     level = [[(p, along(1, p, by)) for p in range(peers)] for by in range(1, side)]
     own = [updated] + [lax.ppermute(updated, ("cores", "samp"), pairs) for pairs in ring]
     other = [lax.ppermute(o, "cores", siblings) for o in own]
-    tall = shape(WAYS * ROWS, LANES, dtype=BF16)
+    stack = shape(3 * WAYS * ROWS, LANES, dtype=BF16)
     flat = shape(LANES, WAYS * ROWS, dtype=BF16)
-    arranged = call(arrange_kernel, [tall, tall, flat, flat] * 2, [vmem()] * 8, name="arrange")(*own, *other)
-    even, odd = list(arranged[:4]), list(arranged[4:])
+    arranged = call(arrange_kernel, [stack, flat, flat] * 2, [vmem()] * 8, name="arrange")(*own, *other)
+    even, odd = list(arranged[:3]), list(arranged[3:])
 
     saved, sums = [], []
     recv = None

time: 149 us -> 145 us (0.973)
  Pallas kernels: 36.9 us -> 33.5 us
    pallas_call x1, Pallas kernels: 5.27 us -> 3.3 us  [on_device(): call(final_kernel, shape(ROWS, LANES), [vmem()] * (MODES // 2 - 1 + WAYS...]
where the time goes in v7:
time: 145 us; the launch traced here: 144 us
  blocking collectives  44.2 us (30%)
  waiting for transfers between devices  41 us (28%)
  Pallas kernels  33.5 us (23%)
  starting transfers between devices  20.7 us (14%)
  local copies, waits for them, and re-layouts  3.45 us (2%)
    all_to_all x3, blocking collectives, on_device(): lax.all_to_all(res[0], ('cores', 'samp'), 0, 0, axis_index_groups=groups,...  44.2 us
    all_to_all x1, waiting for transfers between devices, exchanged(): return lax.all_to_all(block, 'samp', 0, 0, tiled=True)  12.8 us
    ppermute x3, waiting for transfers between devices, on_device(): recv.append(lax.ppermute(out, 'cores', pairs))  11.7 us
    pallas_call x4, Pallas kernels, on_device(): call(functools.partial(pair_kernel, pair=pair), outs, [vmem()] * len(ins)...  8.99 us
    ppermute x3, waiting for transfers between devices, on_device(): lax.ppermute(updated, ('cores', 'samp'), pairs)  8.15 us
    all_to_all x1, starting transfers between devices, exchanged(): return lax.all_to_all(block, 'samp', 0, 0, tiled=True)  7.88 us
    pallas_call x1, Pallas kernels, on_device(): pl.pallas_call(functools.partial(gather_kernel, peers=peers), grid=(steps...  5.34 us
    ppermute x3, starting transfers between devices, on_device(): recv.append(lax.ppermute(out, 'cores', pairs))  4.97 us
  transfers between devices with their start and end apart: 16, of which 13 were waited for; matrix products, arithmetic and copies ran while one was open for 1% of the time, Pallas kernels for 4%

profile of v7, /device:TPU:16, one launch (start us, length us, event | category | flops | bytes accessed | tf_op | source)
XLA Modules:
  0.0 144.3 jit_solution(16278315767020149632)
XLA Ops:
  0.0 5.3 %gather.1 = (f32[4608,512]{1,0:T(8,128)S(1)}, s32[8,1024]{1,0:T(8,128)S(1)}, f32[8,128]{1,0:T(8,128)S(1)}) custom-call(s32[8,1024]{1,0:T(8,128)} %bitcast.21, f32[512,2304]{1,0:T(8,128)} %bitcast.18), custom_call_target="tpu_custom_call" | custom-call | tf_op jit(solution)/shard_map/gather/pallas_call | solution.py:451
  5.3 2.8 %collective-permute-done.table_ref = f32[512,2304]{1,0:T(8,128)S(1)} collective-permute-done((f32[512,2304]{1,0:T(8,128)}, f32[512,2304]{1,0:T(8,128)S(1)}, u32[]{:S(2)}, u32[]{:S(2)}) %collective-permute-start) | collective-permute-done | bytes 4718624 | tf_op jit(solution)/shard_map/ppermute | solution.py:442
  8.1 4.2 %gather_other.1.mats_ref = f32[4608,512]{1,0:T(8,128)S(1)} custom-call(s32[8,1024]{1,0:T(8,128)} %bitcast.22, f32[512,2304]{1,0:T(8,128)S(1)} %collective-permute-done.table_ref, f32[4608,512]{1,0:T(8,128)S(1)} %get-tuple-element.75.refs_0_), custom_call_target="tpu_custom_call", output_to_operand_aliasing={{}: (2, {})} | custom-call | tf_op jit(solution)/shard_map/gather_other/pallas_call | solution.py:465
  12.3 1.4 hop0.1
  13.7 1.3 collective-permute-start.1
  15.0 5.4 %collective-permute-done.1.refs_0_ = f32[48,512]{1,0:T(8,128)S(1)} collective-permute-done((f32[48,512]{1,0:T(8,128)S(1)}, f32[48,512]{1,0:T(8,128)S(1)}, u32[]{:S(2)}, u32[]{:S(2)}) %collective-permute-start.1) | collective-permute-done | bytes 98336 | tf_op jit(solution)/shard_map/ppermute | solution.py:493
  20.5 1.4 hop1.1
  21.9 2.4 %collective-permute-start.2 = (f32[48,512]{1,0:T(8,128)S(1)}, f32[48,512]{1,0:T(8,128)S(1)}, u32[]{:S(2)}, u32[]{:S(2)}) collective-permute-start(f32[48,512]{1,0:T(8,128)S(1)} %get-tuple-element.77), channel_id=1, source_target_pairs={{32,64},{48,80},{64,32},{80,48},{33,65},{49,81},{65,33},{81,49},{3... | collective-permute-start | bytes 294920 | tf_op jit(solution)/shard_map/ppermute | solution.py:493
  24.3 4.1 %collective-permute-done.2.refs_0_.refs_1_ = f32[48,512]{1,0:T(8,128)S(1)} collective-permute-done((f32[48,512]{1,0:T(8,128)S(1)}, f32[48,512]{1,0:T(8,128)S(1)}, u32[]{:S(2)}, u32[]{:S(2)}) %collective-permute-start.2) | collective-permute-done | bytes 98336 | tf_op jit(solution)/shard_map/ppermute | solution.py:493
  28.4 1.4 hop2.1
  29.8 1.3 collective-permute-start.3
  31.1 2.2 %collective-permute-done.3.refs_2_ = f32[48,512]{1,0:T(8,128)S(1)} collective-permute-done((f32[48,512]{1,0:T(8,128)S(1)}, f32[48,512]{1,0:T(8,128)S(1)}, u32[]{:S(2)}, u32[]{:S(2)}) %collective-permute-start.3) | collective-permute-done | bytes 98336 | tf_op jit(solution)/shard_map/ppermute | solution.py:493
  33.3 1.5 %finish.1 = (f32[96,512]{1,0:T(8,128)S(1)}, f32[96,512]{1,0:T(8,128)S(1)}) custom-call(f32[4608,512]{1,0:T(8,128)S(1)} %gather_other.1.mats_ref, f32[48,512]{1,0:T(8,128)S(1)} %collective-permute-done.1.refs_0_, f32[48,512]{1,0:T(8,128)S(1)} %collective-permute-done.2.refs_0_.refs_1_, f32[48,512]{1,0:T(8,128)S(1)} %collective-permute-done.3.refs_2_, ...), custom_call_target="tpu_custom_call" | custom-call | tf_op jit(solution)/shard_map/finish/pallas_call | solution.py:495
  34.9 1.4 collective-permute-done.4.got_ref
  36.4 2.4 %route.1 = (f32[16,104,128]{2,1,0:T(8,128)}, f32[104,1024]{1,0:T(8,128)S(1)}) custom-call(f32[96,512]{1,0:T(8,128)S(1)} %get-tuple-element.82.own_ref, f32[96,512]{1,0:T(8,128)S(1)} %collective-permute-done.4.got_ref, s32[8,1024]{1,0:T(8,128)S(1)} %get-tuple-element.171.slot_ref, f32[8,128]{1,0:T(8,128)S(1)} %get-tuple-element.172.most_ref), custom_call_target="tpu_custom_call" | custom-call | tf_op jit(solution)/shard_map/route/pallas_call | solution.py:503
  38.8 7.9 %all-to-all-start.1 = ((f32[16,104,128]{2,1,0:T(8,128)}), f32[16,104,128]{2,1,0:T(8,128)S(1)}, u32[]{:S(2)}, u32[]{:S(2)}) async-start(f32[16,104,128]{2,1,0:T(8,128)} %get-tuple-element.86), calls=%async_computation.1 | async-start | bytes 1703936 | tf_op jit(solution)/shard_map/all_to_all | solution.py:511
  49.3 12.8 %all-to-all-done.1.recv_ref = f32[16,104,128]{2,1,0:T(8,128)S(1)} async-done(((f32[16,104,128]{2,1,0:T(8,128)}), f32[16,104,128]{2,1,0:T(8,128)S(1)}, u32[]{:S(2)}, u32[]{:S(2)}) %all-to-all-start.1) | async-done | bytes 852000 | tf_op jit(solution)/shard_map/all_to_all | solution.py:511
  62.1 2.1 %collect.2 = (f32[192,384]{1,0:T(8,128)S(1)}, s32[1]{0:T(128)}) custom-call(f32[1]{0:T(128)} %bitcast.15.step_ref, f32[16,104,128]{2,1,0:T(8,128)S(1)} %all-to-all-done.1.recv_ref, f32[192,384]{1,0:T(8,128)S(1)} %reshape.26.base_ref), custom_call_target="tpu_custom_call" | custom-call | tf_op jit(solution)/shard_map/collect/pallas_call | solution.py:514
  65.8 2.5 %collective-permute-start.7 = (f32[192,384]{1,0:T(8,128)S(1)}, f32[192,384]{1,0:T(8,128)S(1)}, u32[]{:S(2)}, u32[]{:S(2)}) collective-permute-start(f32[192,384]{1,0:T(8,128)S(1)} %get-tuple-element.90.refs_0_.refs_7_), channel_id=1, source_target_pairs={{0,3},{1,0},{2,1},{3,2},{4,7},{5,4},{6,5},{7,6},{8,11},{9,8},{10,9... | collective-permute-start | bytes 884744 | tf_op jit(solution)/shard_map/ppermute | solution.py:549
  68.3 5.0 %collective-permute-done.6.refs_2_ = f32[192,384]{1,0:T(8,128)S(1)} collective-permute-done((f32[192,384]{1,0:T(8,128)S(1)}, f32[192,384]{1,0:T(8,128)S(1)}, u32[]{:S(2)}, u32[]{:S(2)}) %collective-permute-start.6) | collective-permute-done | bytes 294944 | tf_op jit(solution)/shard_map/ppermute | solution.py:549
  74.2 2.2 %collective-permute-done.5.refs_1_ = f32[192,384]{1,0:T(8,128)S(1)} collective-permute-done((f32[192,384]{1,0:T(8,128)S(1)}, f32[192,384]{1,0:T(8,128)S(1)}, u32[]{:S(2)}, u32[]{:S(2)}) %collective-permute-start.5) | collective-permute-done | bytes 294944 | tf_op jit(solution)/shard_map/ppermute | solution.py:549
  76.4 1.6 %collective-permute-done.9.refs_5_ = f32[192,384]{1,0:T(8,128)S(1)} collective-permute-done((f32[192,384]{1,0:T(8,128)S(1)}, f32[192,384]{1,0:T(8,128)S(1)}, u32[]{:S(2)}, u32[]{:S(2)}) %collective-permute-start.9) | collective-permute-done | bytes 294944 | tf_op jit(solution)/shard_map/ppermute | solution.py:550
  78.0 1.4 arrange.1
  79.4 2.2 %pair0.1 = (f32[32,24,128]{2,1,0:T(8,128)S(1)}, f32[24,128]{1,0:T(8,128)S(1)}) custom-call(bf16[2304,384]{1,0:T(8,128)(2,1)S(1)} %get-tuple-element.91.refs_0_.refs_1_.refs_4_, bf16[384,768]{1,0:T(8,128)(2,1)S(1)} %get-tuple-element.92.refs_1_.refs_2_.refs_5_, bf16[384,768]{1,0:T(8,128)(2,1)S(1)} %get-tuple-element.93.refs_2_.refs_3_.refs_6_, ...), custom_call_target="tpu_custom_call" | custom-call | tf_op jit(solution)/shard_map/pair0/pallas_call | solution.py:564
  81.6 15.6 %all_to_all.26.refs_0_ = f32[32,24,128]{2,1,0:T(8,128)S(1)} all-to-all(f32[32,24,128]{2,1,0:T(8,128)S(1)} %get-tuple-element.97), channel_id=1, replica_groups={{0,1,2,3,4,5,6,7,8,9,10,11,12,13,14,15,32,33,34,35,36,37,38,39,40,41,42..., dimensions={0} | all-to-all | bytes 786432 | tf_op jit(solution)/shard_map/all_to_all | solution.py:582
  97.2 2.7 %pair1.1 = (f32[32,24,128]{2,1,0:T(8,128)S(1)}, f32[24,128]{1,0:T(8,128)S(1)}, f32[24,128]{1,0:T(8,128)S(1)}) custom-call(f32[32,24,128]{2,1,0:T(8,128)S(1)} %all_to_all.26.refs_0_, bf16[2304,384]{1,0:T(8,128)(2,1)S(1)} %get-tuple-element.91.refs_0_.refs_1_.refs_4_, bf16[384,768]{1,0:T(8,128)(2,1)S(1)} %get-tuple-element.92.refs_1_.refs_2_.refs_5_, ...), custom_call_target="tpu_custom_call" | custom-call | tf_op jit(solution)/shard_map/pair1/pallas_call | solution.py:564
  99.9 14.0 %all_to_all.27.refs_0_ = f32[32,24,128]{2,1,0:T(8,128)S(1)} all-to-all(f32[32,24,128]{2,1,0:T(8,128)S(1)} %get-tuple-element.99), channel_id=1, replica_groups={{32,33,34,35,36,37,38,39,40,41,42,43,44,45,46,47,64,65,66,67,68,69,70,7..., dimensions={0} | all-to-all | bytes 786432 | tf_op jit(solution)/shard_map/all_to_all | solution.py:582
  113.9 2.7 %pair2.1 = (f32[32,24,128]{2,1,0:T(8,128)S(1)}, f32[24,128]{1,0:T(8,128)S(1)}, f32[24,128]{1,0:T(8,128)S(1)}) custom-call(f32[32,24,128]{2,1,0:T(8,128)S(1)} %all_to_all.27.refs_0_, bf16[2304,384]{1,0:T(8,128)(2,1)S(1)} %get-tuple-element.91.refs_0_.refs_1_.refs_4_, bf16[384,768]{1,0:T(8,128)(2,1)S(1)} %get-tuple-element.92.refs_1_.refs_2_.refs_5_, ...), custom_call_target="tpu_custom_call" | custom-call | tf_op jit(solution)/shard_map/pair2/pallas_call | solution.py:564
  116.6 14.7 %all_to_all.28.refs_0_ = f32[32,24,128]{2,1,0:T(8,128)S(1)} all-to-all(f32[32,24,128]{2,1,0:T(8,128)S(1)} %get-tuple-element.101), channel_id=1, replica_groups={{64,65,66,67,68,69,70,71,72,73,74,75,76,77,78,79,96,97,98,99,100,101,10..., dimensions={0} | all-to-all | bytes 786432 | tf_op jit(solution)/shard_map/all_to_all | solution.py:582
  131.2 1.4 pair3.1
  133.2 2.6 %collective-permute-start.13 = (f32[24,128]{1,0:T(8,128)S(1)}, f32[24,128]{1,0:T(8,128)S(1)}, u32[]{:S(2)}, u32[]{:S(2)}) collective-permute-start(f32[24,128]{1,0:T(8,128)S(1)} %get-tuple-element.106.refs_3_), channel_id=1, source_target_pairs={{0,8},{1,9},{2,10},{3,11},{4,12},{5,13},{6,14},{7,15},{8,0},{9,1},... | collective-permute-start | bytes 36872 | tf_op jit(solution)/shard_map/ppermute | solution.py:574
  139.5 3.3 %final.1 = f32[192,384]{1,0:T(8,128)S(1)} custom-call(f32[24,128]{1,0:T(8,128)S(1)} %get-tuple-element.98.refs_0_, f32[24,128]{1,0:T(8,128)S(1)} %get-tuple-element.100.refs_1_, f32[24,128]{1,0:T(8,128)S(1)} %get-tuple-element.105.refs_2_, f32[24,128]{1,0:T(8,128)S(1)} %get-tuple-element.106.refs_3_, f32[24,128]{1,0:T(8,128)S(1)} %collective-permute-done.12.refs_4_, ...), custom_call_target="tpu_custom_call" | custom-call | tf_op jit(solution)/shard_map/final/pallas_call | solution.py:586
  (27 shorter events, 10.2 us)
Async XLA Ops:
  0.0 8.1 %collective-permute-start = (f32[512,2304]{1,0:T(8,128)}, f32[512,2304]{1,0:T(8,128)S(1)}, u32[]{:S(2)}, u32[]{:S(2)}) collective-permute-start(f32[512,2304]{1,0:T(8,128)} %bitcast.17), channel_id=1, source_target_pairs={{0,16},{16,0},{32,48},{48,32},{64,80},{80,64},{96,112},{112,96},{1... | collective-permute-start | bytes 14155784 | tf_op jit(solution)/shard_map/ppermute | solution.py:442
  13.7 6.7 %collective-permute-start.1 = (f32[48,512]{1,0:T(8,128)S(1)}, f32[48,512]{1,0:T(8,128)S(1)}, u32[]{:S(2)}, u32[]{:S(2)}) collective-permute-start(f32[48,512]{1,0:T(8,128)S(1)} %get-tuple-element.76), channel_id=1, source_target_pairs={{0,32},{16,48},{96,64},{112,80},{1,33},{17,49},{97,65},{113,81},{2... | collective-permute-start | bytes 294920 | tf_op jit(solution)/shard_map/ppermute | solution.py:493
  21.9 11.4 %copy-start = (f32[1024]{0:T(1024)S(1)}, f32[1024]{0:T(1024)}, u32[]{:S(2)}) copy-start(f32[1024]{0:T(1024)} %param.8) | copy-start | bytes 12292
  21.9 6.5 %collective-permute-start.2 = (f32[48,512]{1,0:T(8,128)S(1)}, f32[48,512]{1,0:T(8,128)S(1)}, u32[]{:S(2)}, u32[]{:S(2)}) collective-permute-start(f32[48,512]{1,0:T(8,128)S(1)} %get-tuple-element.77), channel_id=1, source_target_pairs={{32,64},{48,80},{64,32},{80,48},{33,65},{49,81},{65,33},{81,49},{3... | collective-permute-start | bytes 294920 | tf_op jit(solution)/shard_map/ppermute | solution.py:493
  29.8 3.5 %collective-permute-start.3 = (f32[48,512]{1,0:T(8,128)S(1)}, f32[48,512]{1,0:T(8,128)S(1)}, u32[]{:S(2)}, u32[]{:S(2)}) collective-permute-start(f32[48,512]{1,0:T(8,128)S(1)} %get-tuple-element.78.refs_6_), channel_id=1, source_target_pairs={{64,96},{80,112},{32,0},{48,16},{65,97},{81,113},{33,1},{49,17},{6... | collective-permute-start | bytes 294920 | tf_op jit(solution)/shard_map/ppermute | solution.py:493
  34.8 1.5 %collective-permute-start.4 = (f32[96,512]{1,0:T(8,128)S(1)}, f32[96,512]{1,0:T(8,128)S(1)}, u32[]{:S(2)}, u32[]{:S(2)}) collective-permute-start(f32[96,512]{1,0:T(8,128)S(1)} %get-tuple-element.83), channel_id=1, source_target_pairs={{0,16},{16,0},{32,48},{48,32},{64,80},{80,64},{96,112},{112,96},{1... | collective-permute-start | bytes 589832 | tf_op jit(solution)/shard_map/ppermute | solution.py:502
  38.8 23.3 %all-to-all-start.1 = ((f32[16,104,128]{2,1,0:T(8,128)}), f32[16,104,128]{2,1,0:T(8,128)S(1)}, u32[]{:S(2)}, u32[]{:S(2)}) async-start(f32[16,104,128]{2,1,0:T(8,128)} %get-tuple-element.86), calls=%async_computation.1 | async-start | bytes 1703936 | tf_op jit(solution)/shard_map/all_to_all | solution.py:511
  64.8 8.5 %collective-permute-start.6 = (f32[192,384]{1,0:T(8,128)S(1)}, f32[192,384]{1,0:T(8,128)S(1)}, u32[]{:S(2)}, u32[]{:S(2)}) collective-permute-start(f32[192,384]{1,0:T(8,128)S(1)} %get-tuple-element.90.refs_0_.refs_7_), channel_id=1, source_target_pairs={{0,2},{1,3},{2,0},{3,1},{4,6},{5,7},{6,4},{7,5},{8,10},{9,11},{10,... | collective-permute-start | bytes 884744 | tf_op jit(solution)/shard_map/ppermute | solution.py:549
  65.8 8.4 %collective-permute-start.7 = (f32[192,384]{1,0:T(8,128)S(1)}, f32[192,384]{1,0:T(8,128)S(1)}, u32[]{:S(2)}, u32[]{:S(2)}) collective-permute-start(f32[192,384]{1,0:T(8,128)S(1)} %get-tuple-element.90.refs_0_.refs_7_), channel_id=1, source_target_pairs={{0,3},{1,0},{2,1},{3,2},{4,7},{5,4},{6,5},{7,6},{8,11},{9,8},{10,9... | collective-permute-start | bytes 884744 | tf_op jit(solution)/shard_map/ppermute | solution.py:549
  68.3 8.2 %collective-permute-start.5 = (f32[192,384]{1,0:T(8,128)S(1)}, f32[192,384]{1,0:T(8,128)S(1)}, u32[]{:S(2)}, u32[]{:S(2)}) collective-permute-start(f32[192,384]{1,0:T(8,128)S(1)} %get-tuple-element.90.refs_0_.refs_7_), channel_id=1, source_target_pairs={{0,1},{1,2},{2,3},{3,0},{4,5},{5,6},{6,7},{7,4},{8,9},{9,10},{10,1... | collective-permute-start | bytes 884744 | tf_op jit(solution)/shard_map/ppermute | solution.py:549
  68.3 8.2 %collective-permute-start.8 = (f32[192,384]{1,0:T(8,128)S(1)}, f32[192,384]{1,0:T(8,128)S(1)}, u32[]{:S(2)}, u32[]{:S(2)}) collective-permute-start(f32[192,384]{1,0:T(8,128)S(1)} %get-tuple-element.90.refs_0_.refs_7_), channel_id=1, source_target_pairs={{0,16},{16,0},{32,48},{48,32},{64,80},{80,64},{96,112},{112,96},{1... | collective-permute-start | bytes 884744 | tf_op jit(solution)/shard_map/ppermute | solution.py:550
  73.3 3.1 %collective-permute-start.10 = (f32[192,384]{1,0:T(8,128)S(1)}, f32[192,384]{1,0:T(8,128)S(1)}, u32[]{:S(2)}, u32[]{:S(2)}) collective-permute-start(f32[192,384]{1,0:T(8,128)S(1)} %collective-permute-done.6.refs_2_), channel_id=1, source_target_pairs={{0,16},{16,0},{32,48},{48,32},{64,80},{80,64},{96,112},{112,96},{1... | collective-permute-start | bytes 884744 | tf_op jit(solution)/shard_map/ppermute | solution.py:550
  74.2 2.2 %collective-permute-start.11 = (f32[192,384]{1,0:T(8,128)S(1)}, f32[192,384]{1,0:T(8,128)S(1)}, u32[]{:S(2)}, u32[]{:S(2)}) collective-permute-start(f32[192,384]{1,0:T(8,128)S(1)} %collective-permute-done.7.refs_3_), channel_id=1, source_target_pairs={{0,16},{16,0},{32,48},{48,32},{64,80},{80,64},{96,112},{112,96},{1... | collective-permute-start | bytes 884744 | tf_op jit(solution)/shard_map/ppermute | solution.py:550
  76.4 1.6 %collective-permute-start.9 = (f32[192,384]{1,0:T(8,128)S(1)}, f32[192,384]{1,0:T(8,128)S(1)}, u32[]{:S(2)}, u32[]{:S(2)}) collective-permute-start(f32[192,384]{1,0:T(8,128)S(1)} %collective-permute-done.5.refs_1_), channel_id=1, source_target_pairs={{0,16},{16,0},{32,48},{48,32},{64,80},{80,64},{96,112},{112,96},{1... | collective-permute-start | bytes 884744 | tf_op jit(solution)/shard_map/ppermute | solution.py:550
  132.6 5.0 %collective-permute-start.12 = (f32[24,128]{1,0:T(8,128)S(1)}, f32[24,128]{1,0:T(8,128)S(1)}, u32[]{:S(2)}, u32[]{:S(2)}) collective-permute-start(f32[24,128]{1,0:T(8,128)S(1)} %get-tuple-element.106.refs_3_), channel_id=1, source_target_pairs={{0,4},{1,5},{2,6},{3,7},{4,8},{5,9},{6,10},{7,11},{8,12},{9,13},{1... | collective-permute-start | bytes 36872 | tf_op jit(solution)/shard_map/ppermute | solution.py:574
  133.2 5.2 %collective-permute-start.13 = (f32[24,128]{1,0:T(8,128)S(1)}, f32[24,128]{1,0:T(8,128)S(1)}, u32[]{:S(2)}, u32[]{:S(2)}) collective-permute-start(f32[24,128]{1,0:T(8,128)S(1)} %get-tuple-element.106.refs_3_), channel_id=1, source_target_pairs={{0,8},{1,9},{2,10},{3,11},{4,12},{5,13},{6,14},{7,15},{8,0},{9,1},... | collective-permute-start | bytes 36872 | tf_op jit(solution)/shard_map/ppermute | solution.py:574
  135.8 3.7 %collective-permute-start.14 = (f32[24,128]{1,0:T(8,128)S(1)}, f32[24,128]{1,0:T(8,128)S(1)}, u32[]{:S(2)}, u32[]{:S(2)}) collective-permute-start(f32[24,128]{1,0:T(8,128)S(1)} %get-tuple-element.106.refs_3_), channel_id=1, source_target_pairs={{0,12},{1,13},{2,14},{3,15},{4,0},{5,1},{6,2},{7,3},{8,4},{9,5},{1... | collective-permute-start | bytes 36872 | tf_op jit(solution)/shard_map/ppermute | solution.py:574

commit v8 on v7

--- a/solution.py
+++ b/solution.py
@@ -18,6 +18,7 @@
 FEATS = 104
 SLOTS = 128
 WAYS = 4
+PARTS = 2
 HIGH = lax.Precision.HIGHEST
 F32 = jnp.float32
 BF16 = jnp.bfloat16
@@ -99,7 +100,7 @@
     mats_ref[...] = dot_rows(hi, hot) + dot_rows(lo, hot)
 
 
-def times(left, mats_ref, base, vec_ref, out_ref):
+def times(left, mats_ref, base, first, vec_ref, out_ref):
     count = vec_ref.shape[1]
 
     def rows(a):
@@ -109,9 +110,10 @@
     def _():
         def chunk(c, _):
             lanes = pl.ds(pl.multiple_of(c * 128, 128), 128)
+            theirs = pl.ds(pl.multiple_of(c * 128 + first, 128), 128)
             acc = [jnp.zeros((R, 128), F32) for _ in range(2)]
             for a in range(R):
-                acc[a % 2] = acc[a % 2] + mats_ref[rows(a), lanes] * vec_ref[a : a + 1, lanes]
+                acc[a % 2] = acc[a % 2] + mats_ref[rows(a), theirs] * vec_ref[a : a + 1, lanes]
             out_ref[:, lanes] = acc[0] + acc[1]
             return 0
 
@@ -121,10 +123,11 @@
     def _():
         def chunk(c, _):
             lanes = pl.ds(pl.multiple_of(c * 128, 128), 128)
+            theirs = pl.ds(pl.multiple_of(c * 128 + first, 128), 128)
             vec = vec_ref[:, lanes]
             for a in range(0, R, 8):
                 sums = [
-                    jnp.sum(mats_ref[rows(a + i), lanes] * vec, axis=0, keepdims=True) for i in range(8)
+                    jnp.sum(mats_ref[rows(a + i), theirs] * vec, axis=0, keepdims=True) for i in range(8)
                 ]
                 out_ref[a : a + 8, lanes] = jnp.concatenate(sums, axis=0)
             return 0
@@ -132,14 +135,15 @@
         lax.fori_loop(0, count // 128, chunk, 0)
 
 
-def both_modes(turn, mats_ref, vec_ref, mid_ref, out_ref):
+def both_modes(turn, part, mats_ref, vec_ref, mid_ref, out_ref):
     mode = lax.axis_index("cores")
     chips = MODES // 2
     left = (mode // 2 < chips // 2) if turn < chips // 2 else (mode // 2 >= chips // 2)
     even = (mode % 2) * RR
     base = jnp.where(left, even, RR - even)
-    times(left, mats_ref, base, vec_ref, mid_ref)
-    times(left, mats_ref, RR - base, mid_ref, out_ref)
+    first = part * vec_ref.shape[1]
+    times(left, mats_ref, base, first, vec_ref, mid_ref)
+    times(left, mats_ref, RR - base, first, mid_ref, out_ref)
 
 
 def unit_at_ends(shape_):
@@ -148,23 +152,32 @@
     return jnp.where(iota(shape_, 0) == 0, edge, 0.0)
 
 
-def hop_kernel(mats_ref, *refs, turn):
+def hop_kernel(mats_ref, *refs, turn, part):
     vec_ref, mid_ref, out_ref = refs if turn else (refs[2], refs[0], refs[1])
     if turn == 0:
         vec_ref[...] = unit_at_ends(vec_ref.shape)
-    both_modes(turn, mats_ref, vec_ref, mid_ref, out_ref)
+    both_modes(turn, part, mats_ref, vec_ref, mid_ref, out_ref)
 
 
 def finish_kernel(mats_ref, *refs):
-    recv, mids = refs[0:3], refs[3:6]
-    out2_ref, obs_ref, own_ref, other_ref, mid_ref, out_ref = refs[6:]
+    refs = list(refs)
+
+    def taken():
+        parts = [refs.pop(0) for _ in range(PARTS)]
+        return jnp.concatenate([p[...] for p in parts], axis=1)
+
+    recv = [taken() for _ in range(3)]
+    mids = [taken() for _ in range(3)]
+    out2 = taken()
+    obs_ref, own_ref, other_ref, vec_ref, mid_ref, out_ref = refs
     mode = lax.axis_index("cores")
-    both_modes(3, mats_ref, recv[2], mid_ref, out_ref)
-    end1 = unit_at_ends(mid_ref.shape) + recv[0][...]
-    mid1 = mids[0][...] + mids[1][...]
-    end2 = recv[1][...] + recv[2][...]
-    mid2 = mids[2][...] + mid_ref[...]
-    predicted = jnp.sum((out2_ref[...] + out_ref[...]) * end1, axis=0, keepdims=True)
+    vec_ref[...] = recv[2]
+    both_modes(3, 0, mats_ref, vec_ref, mid_ref, out_ref)
+    end1 = unit_at_ends(mid_ref.shape) + recv[0]
+    mid1 = mids[0] + mids[1]
+    end2 = recv[1] + recv[2]
+    mid2 = mids[2] + mid_ref[...]
+    predicted = jnp.sum((out2 + out_ref[...]) * end1, axis=0, keepdims=True)
     residual = predicted - half_of(obs_ref[...], mode % 2 == 1)
     early = jnp.where(mode // 2 < MODES // 4, 1.0, 0.0) > 0.5
     even = (jnp.where(early, end1, end2), jnp.where(early, mid2, mid1) * residual)
@@ -479,26 +492,30 @@
     base = kept.reshape(GROUPS, WIDE, R, R).transpose(0, 2, 1, 3)
     base = base.reshape(ROWS, LANES)
 
-    vec = shape(R, half)
-    recv, mids = [], []
+    vec = shape(R, half // PARTS)
+    recv, mids, outs = [], [], [None] * PARTS
     for turn in range(3):
-        mid, out = call(
-            functools.partial(hop_kernel, turn=turn),
-            [vec, vec],
-            [vmem()] * (2 if turn else 1),
-            [] if turn else [pltpu.VMEM((R, half), F32)],
-            name=f"hop{turn}",
-        )(mats, *recv[-1:])
         pairs = [(2 * a + h, 2 * b + h) for a, b in ((turn, turn + 1), (3 - turn, 2 - turn)) for h in range(2)]
-        recv.append(lax.ppermute(out, "cores", pairs))
-        mids.append(mid)
+        arrived = []
+        for part in range(PARTS):
+            mid, out = call(
+                functools.partial(hop_kernel, turn=turn, part=part),
+                [vec, vec],
+                [vmem()] * (2 if turn else 1),
+                [] if turn else [pltpu.VMEM(vec.shape, F32)],
+                name=f"hop{turn}_{part}",
+            )(mats, *([recv[-PARTS + part]] if turn else []))
+            arrived.append(lax.ppermute(out, "cores", pairs))
+            mids.append(mid)
+            outs[part] = out
+        recv += arrived
     own_vecs, other_vecs = call(
         finish_kernel,
         [shape(2 * R, half)] * 2,
-        [vmem()] * 9,
-        [pltpu.VMEM((R, half), F32)] * 2,
+        [vmem()] * (7 * PARTS + 2),
+        [pltpu.VMEM((R, half), F32)] * 3,
         name="finish",
-    )(mats, *recv, *mids, out, observed.reshape(1, count))
+    )(mats, *recv, *mids, *outs, observed.reshape(1, count))
     got_vecs = lax.ppermute(other_vecs, "cores", siblings)
     pay, values = call(
         route_kernel,

time: 145 us -> 147 us (1.014)
  waiting for transfers between devices: 41 us -> 34.1 us
  starting transfers between devices: 20.7 us -> 27.2 us
  blocking collectives: 44.2 us -> 46.1 us
    ppermute x3 -> x6, waiting for transfers between devices: 11.7 us -> 4.89 us  [on_device(): arrived.append(lax.ppermute(out, 'cores', pairs))]
    ppermute x3 -> x6, starting transfers between devices: 4.97 us -> 11 us  [on_device(): arrived.append(lax.ppermute(out, 'cores', pairs))]
    all_to_all x3, blocking collectives: 44.2 us -> 46.1 us  [on_device(): lax.all_to_all(res[0], ('cores', 'samp'), 0, 0, axis_index_groups=groups,...]
    pallas_call x4 -> x7, Pallas kernels: 5.76 us -> 5.84 us  [the longest x6 4.29 us: on_device(): call(functools.partial(hop_kernel, turn=turn, part=part), [vec, vec], [vm...]
  transfers between devices with their start and end apart: 16 -> 19, of which waited for: 13 -> 14; matrix products, arithmetic and copies ran while one was open for 1% -> 1% of each run, Pallas kernels for 4% -> 6%
where the time goes in v8:
time: 147 us; the launch traced here: 146 us
  blocking collectives  46.1 us (31%)
  waiting for transfers between devices  34.1 us (23%)
  Pallas kernels  33.6 us (23%)
  starting transfers between devices  27.2 us (19%)
  local copies, waits for them, and re-layouts  3.45 us (2%)
    all_to_all x3, blocking collectives, on_device(): lax.all_to_all(res[0], ('cores', 'samp'), 0, 0, axis_index_groups=groups,...  46.1 us
    all_to_all x1, waiting for transfers between devices, exchanged(): return lax.all_to_all(block, 'samp', 0, 0, tiled=True)  12.8 us
    ppermute x6, starting transfers between devices, on_device(): arrived.append(lax.ppermute(out, 'cores', pairs))  11 us
    pallas_call x4, Pallas kernels, on_device(): call(functools.partial(pair_kernel, pair=pair), outs, [vmem()] * len(ins)...  9.01 us
    ppermute x3, waiting for transfers between devices, on_device(): lax.ppermute(updated, ('cores', 'samp'), pairs)  8.1 us
    all_to_all x1, starting transfers between devices, exchanged(): return lax.all_to_all(block, 'samp', 0, 0, tiled=True)  7.88 us
    pallas_call x1, Pallas kernels, on_device(): pl.pallas_call(functools.partial(gather_kernel, peers=peers), grid=(steps...  5.34 us
    ppermute x6, waiting for transfers between devices, on_device(): arrived.append(lax.ppermute(out, 'cores', pairs))  4.89 us
  transfers between devices with their start and end apart: 19, of which 14 were waited for; matrix products, arithmetic and copies ran while one was open for 1% of the time, Pallas kernels for 6%

profile of v8, /device:TPU:16, one launch (start us, length us, event | category | flops | bytes accessed | tf_op | source)
XLA Modules:
  0.0 146.2 jit_solution(17337916310032945020)
XLA Ops:
  0.0 5.3 %gather.1 = (f32[4608,512]{1,0:T(8,128)S(1)}, s32[8,1024]{1,0:T(8,128)S(1)}, f32[8,128]{1,0:T(8,128)S(1)}) custom-call(s32[8,1024]{1,0:T(8,128)} %bitcast.21, f32[512,2304]{1,0:T(8,128)} %bitcast.18), custom_call_target="tpu_custom_call" | custom-call | tf_op jit(solution)/shard_map/gather/pallas_call | solution.py:464
  5.3 2.8 %collective-permute-done.table_ref = f32[512,2304]{1,0:T(8,128)S(1)} collective-permute-done((f32[512,2304]{1,0:T(8,128)}, f32[512,2304]{1,0:T(8,128)S(1)}, u32[]{:S(2)}, u32[]{:S(2)}) %collective-permute-start) | collective-permute-done | bytes 4718624 | tf_op jit(solution)/shard_map/ppermute | solution.py:455
  8.1 4.2 %gather_other.1.mats_ref = f32[4608,512]{1,0:T(8,128)S(1)} custom-call(s32[8,1024]{1,0:T(8,128)} %bitcast.22, f32[512,2304]{1,0:T(8,128)S(1)} %collective-permute-done.table_ref, f32[4608,512]{1,0:T(8,128)S(1)} %get-tuple-element.81.refs_0_), custom_call_target="tpu_custom_call", output_to_operand_aliasing={{}: (2, {})} | custom-call | tf_op jit(solution)/shard_map/gather_other/pallas_call | solution.py:478
  13.0 1.3 collective-permute-start.2
  15.0 1.3 collective-permute-start.1
  16.3 2.7 %collective-permute-done.2.refs_0_.refs_1_ = f32[48,256]{1,0:T(8,128)S(1)} collective-permute-done((f32[48,256]{1,0:T(8,128)S(1)}, f32[48,256]{1,0:T(8,128)S(1)}, u32[]{:S(2)}, u32[]{:S(2)}) %collective-permute-start.2) | collective-permute-done | bytes 49184 | tf_op jit(solution)/shard_map/ppermute | solution.py:508
  19.7 2.5 %collective-permute-start.4 = (f32[48,256]{1,0:T(8,128)S(1)}, f32[48,256]{1,0:T(8,128)S(1)}, u32[]{:S(2)}, u32[]{:S(2)}) collective-permute-start(f32[48,256]{1,0:T(8,128)S(1)} %get-tuple-element.85), channel_id=1, source_target_pairs={{32,64},{48,80},{64,32},{80,48},{33,65},{49,81},{65,33},{81,49},{3... | collective-permute-start | bytes 147464 | tf_op jit(solution)/shard_map/ppermute | solution.py:508
  22.9 3.4 %collective-permute-start.3 = (f32[48,256]{1,0:T(8,128)S(1)}, f32[48,256]{1,0:T(8,128)S(1)}, u32[]{:S(2)}, u32[]{:S(2)}) collective-permute-start(f32[48,256]{1,0:T(8,128)S(1)} %get-tuple-element.84), channel_id=1, source_target_pairs={{32,64},{48,80},{64,32},{80,48},{33,65},{49,81},{65,33},{81,49},{3... | collective-permute-start | bytes 147464 | tf_op jit(solution)/shard_map/ppermute | solution.py:508
  27.1 1.3 collective-permute-start.6
  29.6 1.3 collective-permute-start.5
  30.9 1.7 %collective-permute-done.5.refs_4_ = f32[48,256]{1,0:T(8,128)S(1)} collective-permute-done((f32[48,256]{1,0:T(8,128)S(1)}, f32[48,256]{1,0:T(8,128)S(1)}, u32[]{:S(2)}, u32[]{:S(2)}) %collective-permute-start.5) | collective-permute-done | bytes 49184 | tf_op jit(solution)/shard_map/ppermute | solution.py:508
  32.6 1.6 %finish.1 = (f32[96,512]{1,0:T(8,128)S(1)}, f32[96,512]{1,0:T(8,128)S(1)}) custom-call(f32[4608,512]{1,0:T(8,128)S(1)} %gather_other.1.mats_ref, f32[48,256]{1,0:T(8,128)S(1)} %collective-permute-done.1.refs_0_, f32[48,256]{1,0:T(8,128)S(1)} %collective-permute-done.2.refs_0_.refs_1_, f32[48,256]{1,0:T(8,128)S(1)} %collective-permute-done.3.refs_0_.refs_2_, ...), custom_call_target="tpu_custom_call" | custom-call | tf_op jit(solution)/shard_map/finish/pallas_call | solution.py:512
  34.3 1.4 collective-permute-done.7.got_ref
  35.7 2.4 %route.1 = (f32[16,104,128]{2,1,0:T(8,128)}, f32[104,1024]{1,0:T(8,128)S(1)}) custom-call(f32[96,512]{1,0:T(8,128)S(1)} %get-tuple-element.94.own_ref, f32[96,512]{1,0:T(8,128)S(1)} %collective-permute-done.7.got_ref, s32[8,1024]{1,0:T(8,128)S(1)} %get-tuple-element.183.slot_ref, f32[8,128]{1,0:T(8,128)S(1)} %get-tuple-element.184.most_ref), custom_call_target="tpu_custom_call" | custom-call | tf_op jit(solution)/shard_map/route/pallas_call | solution.py:520
  38.1 7.9 %all-to-all-start.1 = ((f32[16,104,128]{2,1,0:T(8,128)}), f32[16,104,128]{2,1,0:T(8,128)S(1)}, u32[]{:S(2)}, u32[]{:S(2)}) async-start(f32[16,104,128]{2,1,0:T(8,128)} %get-tuple-element.98), calls=%async_computation.1 | async-start | bytes 1703936 | tf_op jit(solution)/shard_map/all_to_all | solution.py:528
  48.6 12.8 %all-to-all-done.1.recv_ref = f32[16,104,128]{2,1,0:T(8,128)S(1)} async-done(((f32[16,104,128]{2,1,0:T(8,128)}), f32[16,104,128]{2,1,0:T(8,128)S(1)}, u32[]{:S(2)}, u32[]{:S(2)}) %all-to-all-start.1) | async-done | bytes 852000 | tf_op jit(solution)/shard_map/all_to_all | solution.py:528
  61.4 2.1 %collect.2 = (f32[192,384]{1,0:T(8,128)S(1)}, s32[1]{0:T(128)}) custom-call(f32[1]{0:T(128)} %bitcast.15.step_ref, f32[16,104,128]{2,1,0:T(8,128)S(1)} %all-to-all-done.1.recv_ref, f32[192,384]{1,0:T(8,128)S(1)} %reshape.26.base_ref), custom_call_target="tpu_custom_call" | custom-call | tf_op jit(solution)/shard_map/collect/pallas_call | solution.py:531
  65.0 1.4 collective-permute-start.9
  66.4 1.5 collective-permute-start.10
  67.8 7.7 %collective-permute-done.8.refs_1_ = f32[192,384]{1,0:T(8,128)S(1)} collective-permute-done((f32[192,384]{1,0:T(8,128)S(1)}, f32[192,384]{1,0:T(8,128)S(1)}, u32[]{:S(2)}, u32[]{:S(2)}) %collective-permute-start.8) | collective-permute-done | bytes 294944 | tf_op jit(solution)/shard_map/ppermute | solution.py:566
  78.0 1.4 arrange.1
  79.4 2.2 %pair0.1 = (f32[32,24,128]{2,1,0:T(8,128)S(1)}, f32[24,128]{1,0:T(8,128)S(1)}) custom-call(bf16[2304,384]{1,0:T(8,128)(2,1)S(1)} %get-tuple-element.103.refs_0_.refs_1_.refs_4_, bf16[384,768]{1,0:T(8,128)(2,1)S(1)} %get-tuple-element.104.refs_1_.refs_2_.refs_5_, bf16[384,768]{1,0:T(8,128)(2,1)S(1)} %get-tuple-element.105.refs_2_.refs_3_.refs_6_, ...), custom_call_target="tpu_custom_call" | custom-call | tf_op jit(solution)/shard_map/pair0/pallas_call | solution.py:581
  81.6 16.5 %all_to_all.26.refs_0_ = f32[32,24,128]{2,1,0:T(8,128)S(1)} all-to-all(f32[32,24,128]{2,1,0:T(8,128)S(1)} %get-tuple-element.109), channel_id=1, replica_groups={{0,1,2,3,4,5,6,7,8,9,10,11,12,13,14,15,32,33,34,35,36,37,38,39,40,41,42..., dimensions={0} | all-to-all | bytes 786432 | tf_op jit(solution)/shard_map/all_to_all | solution.py:599
  98.1 2.7 %pair1.1 = (f32[32,24,128]{2,1,0:T(8,128)S(1)}, f32[24,128]{1,0:T(8,128)S(1)}, f32[24,128]{1,0:T(8,128)S(1)}) custom-call(f32[32,24,128]{2,1,0:T(8,128)S(1)} %all_to_all.26.refs_0_, bf16[2304,384]{1,0:T(8,128)(2,1)S(1)} %get-tuple-element.103.refs_0_.refs_1_.refs_4_, bf16[384,768]{1,0:T(8,128)(2,1)S(1)} %get-tuple-element.104.refs_1_.refs_2_.refs_5_, ...), custom_call_target="tpu_custom_call" | custom-call | tf_op jit(solution)/shard_map/pair1/pallas_call | solution.py:581
  100.8 14.0 %all_to_all.27.refs_0_ = f32[32,24,128]{2,1,0:T(8,128)S(1)} all-to-all(f32[32,24,128]{2,1,0:T(8,128)S(1)} %get-tuple-element.111), channel_id=1, replica_groups={{32,33,34,35,36,37,38,39,40,41,42,43,44,45,46,47,64,65,66,67,68,69,70,7..., dimensions={0} | all-to-all | bytes 786432 | tf_op jit(solution)/shard_map/all_to_all | solution.py:599
  114.8 2.7 %pair2.1 = (f32[32,24,128]{2,1,0:T(8,128)S(1)}, f32[24,128]{1,0:T(8,128)S(1)}, f32[24,128]{1,0:T(8,128)S(1)}) custom-call(f32[32,24,128]{2,1,0:T(8,128)S(1)} %all_to_all.27.refs_0_, bf16[2304,384]{1,0:T(8,128)(2,1)S(1)} %get-tuple-element.103.refs_0_.refs_1_.refs_4_, bf16[384,768]{1,0:T(8,128)(2,1)S(1)} %get-tuple-element.104.refs_1_.refs_2_.refs_5_, ...), custom_call_target="tpu_custom_call" | custom-call | tf_op jit(solution)/shard_map/pair2/pallas_call | solution.py:581
  117.5 15.6 %all_to_all.28.refs_0_ = f32[32,24,128]{2,1,0:T(8,128)S(1)} all-to-all(f32[32,24,128]{2,1,0:T(8,128)S(1)} %get-tuple-element.113), channel_id=1, replica_groups={{64,65,66,67,68,69,70,71,72,73,74,75,76,77,78,79,96,97,98,99,100,101,10..., dimensions={0} | all-to-all | bytes 786432 | tf_op jit(solution)/shard_map/all_to_all | solution.py:599
  133.2 1.4 pair3.1
  135.1 2.6 %collective-permute-start.16 = (f32[24,128]{1,0:T(8,128)S(1)}, f32[24,128]{1,0:T(8,128)S(1)}, u32[]{:S(2)}, u32[]{:S(2)}) collective-permute-start(f32[24,128]{1,0:T(8,128)S(1)} %get-tuple-element.118.refs_3_), channel_id=1, source_target_pairs={{0,8},{1,9},{2,10},{3,11},{4,12},{5,13},{6,14},{7,15},{8,0},{9,1},... | collective-permute-start | bytes 36872 | tf_op jit(solution)/shard_map/ppermute | solution.py:591
  137.7 1.1 collective-permute-start.17
  140.3 1.1 collective-permute-done.17.refs_6_
  141.4 3.3 %final.1 = f32[192,384]{1,0:T(8,128)S(1)} custom-call(f32[24,128]{1,0:T(8,128)S(1)} %get-tuple-element.110.refs_0_, f32[24,128]{1,0:T(8,128)S(1)} %get-tuple-element.112.refs_1_, f32[24,128]{1,0:T(8,128)S(1)} %get-tuple-element.117.refs_2_, f32[24,128]{1,0:T(8,128)S(1)} %get-tuple-element.118.refs_3_, f32[24,128]{1,0:T(8,128)S(1)} %collective-permute-done.15.refs_4_, ...), custom_call_target="tpu_custom_call" | custom-call | tf_op jit(solution)/shard_map/final/pallas_call | solution.py:603
  (36 shorter events, 14.2 us)
Async XLA Ops:
  0.0 8.1 %collective-permute-start = (f32[512,2304]{1,0:T(8,128)}, f32[512,2304]{1,0:T(8,128)S(1)}, u32[]{:S(2)}, u32[]{:S(2)}) collective-permute-start(f32[512,2304]{1,0:T(8,128)} %bitcast.17), channel_id=1, source_target_pairs={{0,16},{16,0},{32,48},{48,32},{64,80},{80,64},{96,112},{112,96},{1... | collective-permute-start | bytes 14155784 | tf_op jit(solution)/shard_map/ppermute | solution.py:455
  13.0 6.0 %collective-permute-start.2 = (f32[48,256]{1,0:T(8,128)S(1)}, f32[48,256]{1,0:T(8,128)S(1)}, u32[]{:S(2)}, u32[]{:S(2)}) collective-permute-start(f32[48,256]{1,0:T(8,128)S(1)} %get-tuple-element.83), channel_id=1, source_target_pairs={{0,32},{16,48},{96,64},{112,80},{1,33},{17,49},{97,65},{113,81},{2... | collective-permute-start | bytes 147464 | tf_op jit(solution)/shard_map/ppermute | solution.py:508
  15.0 7.1 %collective-permute-start.1 = (f32[48,256]{1,0:T(8,128)S(1)}, f32[48,256]{1,0:T(8,128)S(1)}, u32[]{:S(2)}, u32[]{:S(2)}) collective-permute-start(f32[48,256]{1,0:T(8,128)S(1)} %get-tuple-element.82), channel_id=1, source_target_pairs={{0,32},{16,48},{96,64},{112,80},{1,33},{17,49},{97,65},{113,81},{2... | collective-permute-start | bytes 147464 | tf_op jit(solution)/shard_map/ppermute | solution.py:508
  19.7 6.6 %collective-permute-start.4 = (f32[48,256]{1,0:T(8,128)S(1)}, f32[48,256]{1,0:T(8,128)S(1)}, u32[]{:S(2)}, u32[]{:S(2)}) collective-permute-start(f32[48,256]{1,0:T(8,128)S(1)} %get-tuple-element.85), channel_id=1, source_target_pairs={{32,64},{48,80},{64,32},{80,48},{33,65},{49,81},{65,33},{81,49},{3... | collective-permute-start | bytes 147464 | tf_op jit(solution)/shard_map/ppermute | solution.py:508
  22.9 6.0 %collective-permute-start.3 = (f32[48,256]{1,0:T(8,128)S(1)}, f32[48,256]{1,0:T(8,128)S(1)}, u32[]{:S(2)}, u32[]{:S(2)}) collective-permute-start(f32[48,256]{1,0:T(8,128)S(1)} %get-tuple-element.84), channel_id=1, source_target_pairs={{32,64},{48,80},{64,32},{80,48},{33,65},{49,81},{65,33},{81,49},{3... | collective-permute-start | bytes 147464 | tf_op jit(solution)/shard_map/ppermute | solution.py:508
  27.1 5.5 %copy-start = (f32[1024]{0:T(1024)S(1)}, f32[1024]{0:T(1024)}, u32[]{:S(2)}) copy-start(f32[1024]{0:T(1024)} %param.8) | copy-start | bytes 12292
  27.1 3.8 %collective-permute-start.6 = (f32[48,256]{1,0:T(8,128)S(1)}, f32[48,256]{1,0:T(8,128)S(1)}, u32[]{:S(2)}, u32[]{:S(2)}) collective-permute-start(f32[48,256]{1,0:T(8,128)S(1)} %get-tuple-element.87.refs_13_), channel_id=1, source_target_pairs={{64,96},{80,112},{32,0},{48,16},{65,97},{81,113},{33,1},{49,17},{6... | collective-permute-start | bytes 147464 | tf_op jit(solution)/shard_map/ppermute | solution.py:508
  29.6 3.0 %collective-permute-start.5 = (f32[48,256]{1,0:T(8,128)S(1)}, f32[48,256]{1,0:T(8,128)S(1)}, u32[]{:S(2)}, u32[]{:S(2)}) collective-permute-start(f32[48,256]{1,0:T(8,128)S(1)} %get-tuple-element.86.refs_12_), channel_id=1, source_target_pairs={{64,96},{80,112},{32,0},{48,16},{65,97},{81,113},{33,1},{49,17},{6... | collective-permute-start | bytes 147464 | tf_op jit(solution)/shard_map/ppermute | solution.py:508
  34.2 1.5 %collective-permute-start.7 = (f32[96,512]{1,0:T(8,128)S(1)}, f32[96,512]{1,0:T(8,128)S(1)}, u32[]{:S(2)}, u32[]{:S(2)}) collective-permute-start(f32[96,512]{1,0:T(8,128)S(1)} %get-tuple-element.95), channel_id=1, source_target_pairs={{0,16},{16,0},{32,48},{48,32},{64,80},{80,64},{96,112},{112,96},{1... | collective-permute-start | bytes 589832 | tf_op jit(solution)/shard_map/ppermute | solution.py:519
  38.1 23.3 %all-to-all-start.1 = ((f32[16,104,128]{2,1,0:T(8,128)}), f32[16,104,128]{2,1,0:T(8,128)S(1)}, u32[]{:S(2)}, u32[]{:S(2)}) async-start(f32[16,104,128]{2,1,0:T(8,128)} %get-tuple-element.98), calls=%async_computation.1 | async-start | bytes 1703936 | tf_op jit(solution)/shard_map/all_to_all | solution.py:528
  64.4 11.2 %collective-permute-start.8 = (f32[192,384]{1,0:T(8,128)S(1)}, f32[192,384]{1,0:T(8,128)S(1)}, u32[]{:S(2)}, u32[]{:S(2)}) collective-permute-start(f32[192,384]{1,0:T(8,128)S(1)} %get-tuple-element.102.refs_0_.refs_7_), channel_id=1, source_target_pairs={{0,1},{1,2},{2,3},{3,0},{4,5},{5,6},{6,7},{7,4},{8,9},{9,10},{10,1... | collective-permute-start | bytes 884744 | tf_op jit(solution)/shard_map/ppermute | solution.py:566
  65.0 10.5 %collective-permute-start.9 = (f32[192,384]{1,0:T(8,128)S(1)}, f32[192,384]{1,0:T(8,128)S(1)}, u32[]{:S(2)}, u32[]{:S(2)}) collective-permute-start(f32[192,384]{1,0:T(8,128)S(1)} %get-tuple-element.102.refs_0_.refs_7_), channel_id=1, source_target_pairs={{0,2},{1,3},{2,0},{3,1},{4,6},{5,7},{6,4},{7,5},{8,10},{9,11},{10,... | collective-permute-start | bytes 884744 | tf_op jit(solution)/shard_map/ppermute | solution.py:566
  66.4 10.1 %collective-permute-start.10 = (f32[192,384]{1,0:T(8,128)S(1)}, f32[192,384]{1,0:T(8,128)S(1)}, u32[]{:S(2)}, u32[]{:S(2)}) collective-permute-start(f32[192,384]{1,0:T(8,128)S(1)} %get-tuple-element.102.refs_0_.refs_7_), channel_id=1, source_target_pairs={{0,3},{1,0},{2,1},{3,2},{4,7},{5,4},{6,5},{7,6},{8,11},{9,8},{10,9... | collective-permute-start | bytes 884744 | tf_op jit(solution)/shard_map/ppermute | solution.py:566
  67.8 8.6 %collective-permute-start.11 = (f32[192,384]{1,0:T(8,128)S(1)}, f32[192,384]{1,0:T(8,128)S(1)}, u32[]{:S(2)}, u32[]{:S(2)}) collective-permute-start(f32[192,384]{1,0:T(8,128)S(1)} %get-tuple-element.102.refs_0_.refs_7_), channel_id=1, source_target_pairs={{0,16},{16,0},{32,48},{48,32},{64,80},{80,64},{96,112},{112,96},{1... | collective-permute-start | bytes 884744 | tf_op jit(solution)/shard_map/ppermute | solution.py:567
  75.5 1.6 %collective-permute-start.12 = (f32[192,384]{1,0:T(8,128)S(1)}, f32[192,384]{1,0:T(8,128)S(1)}, u32[]{:S(2)}, u32[]{:S(2)}) collective-permute-start(f32[192,384]{1,0:T(8,128)S(1)} %collective-permute-done.8.refs_1_), channel_id=1, source_target_pairs={{0,16},{16,0},{32,48},{48,32},{64,80},{80,64},{96,112},{112,96},{1... | collective-permute-start | bytes 884744 | tf_op jit(solution)/shard_map/ppermute | solution.py:567
  75.5 2.0 %collective-permute-start.13 = (f32[192,384]{1,0:T(8,128)S(1)}, f32[192,384]{1,0:T(8,128)S(1)}, u32[]{:S(2)}, u32[]{:S(2)}) collective-permute-start(f32[192,384]{1,0:T(8,128)S(1)} %collective-permute-done.9.refs_2_), channel_id=1, source_target_pairs={{0,16},{16,0},{32,48},{48,32},{64,80},{80,64},{96,112},{112,96},{1... | collective-permute-start | bytes 884744 | tf_op jit(solution)/shard_map/ppermute | solution.py:567
  76.4 1.6 %collective-permute-start.14 = (f32[192,384]{1,0:T(8,128)S(1)}, f32[192,384]{1,0:T(8,128)S(1)}, u32[]{:S(2)}, u32[]{:S(2)}) collective-permute-start(f32[192,384]{1,0:T(8,128)S(1)} %collective-permute-done.10.refs_3_), channel_id=1, source_target_pairs={{0,16},{16,0},{32,48},{48,32},{64,80},{80,64},{96,112},{112,96},{1... | collective-permute-start | bytes 884744 | tf_op jit(solution)/shard_map/ppermute | solution.py:567
  134.6 5.0 %collective-permute-start.15 = (f32[24,128]{1,0:T(8,128)S(1)}, f32[24,128]{1,0:T(8,128)S(1)}, u32[]{:S(2)}, u32[]{:S(2)}) collective-permute-start(f32[24,128]{1,0:T(8,128)S(1)} %get-tuple-element.118.refs_3_), channel_id=1, source_target_pairs={{0,4},{1,5},{2,6},{3,7},{4,8},{5,9},{6,10},{7,11},{8,12},{9,13},{1... | collective-permute-start | bytes 36872 | tf_op jit(solution)/shard_map/ppermute | solution.py:591
  135.1 5.2 %collective-permute-start.16 = (f32[24,128]{1,0:T(8,128)S(1)}, f32[24,128]{1,0:T(8,128)S(1)}, u32[]{:S(2)}, u32[]{:S(2)}) collective-permute-start(f32[24,128]{1,0:T(8,128)S(1)} %get-tuple-element.118.refs_3_), channel_id=1, source_target_pairs={{0,8},{1,9},{2,10},{3,11},{4,12},{5,13},{6,14},{7,15},{8,0},{9,1},... | collective-permute-start | bytes 36872 | tf_op jit(solution)/shard_map/ppermute | solution.py:591
  137.7 3.7 %collective-permute-start.17 = (f32[24,128]{1,0:T(8,128)S(1)}, f32[24,128]{1,0:T(8,128)S(1)}, u32[]{:S(2)}, u32[]{:S(2)}) collective-permute-start(f32[24,128]{1,0:T(8,128)S(1)} %get-tuple-element.118.refs_3_), channel_id=1, source_target_pairs={{0,12},{1,13},{2,14},{3,15},{4,0},{5,1},{6,2},{7,3},{8,4},{9,5},{1... | collective-permute-start | bytes 36872 | tf_op jit(solution)/shard_map/ppermute | solution.py:591

commit v9 on v7

--- a/solution.py
+++ b/solution.py
@@ -150,9 +150,19 @@
 
 def hop_kernel(mats_ref, *refs, turn):
     vec_ref, mid_ref, out_ref = refs if turn else (refs[2], refs[0], refs[1])
-    if turn == 0:
-        vec_ref[...] = unit_at_ends(vec_ref.shape)
-    both_modes(turn, mats_ref, vec_ref, mid_ref, out_ref)
+    chip = lax.axis_index("cores") // 2
+    live = jnp.logical_or(chip == turn, chip == MODES // 2 - 1 - turn)
+
+    @pl.when(live)
+    def _():
+        if turn == 0:
+            vec_ref[...] = unit_at_ends(vec_ref.shape)
+        both_modes(turn, mats_ref, vec_ref, mid_ref, out_ref)
+
+    @pl.when(jnp.logical_not(live))
+    def _():
+        mid_ref[...] = jnp.zeros(mid_ref.shape, F32)
+        out_ref[...] = jnp.zeros(out_ref.shape, F32)
 
 
 def finish_kernel(mats_ref, *refs):
@@ -237,15 +247,17 @@
     turns_ref[0] = (most + SLOTS - 1) // SLOTS
 
 
-def arrange_kernel(*refs):
-    own = refs[:WAYS]
-    other = refs[WAYS : 2 * WAYS]
-    outs = refs[2 * WAYS :]
+def arrange_kernel(*refs, last):
+    n = 2 if last else WAYS - 1
+    own, other = refs[:n], refs[n : 2 * n]
+    outs = refs[-6:]
+    if last:
+        slabs = [tuple(jnp.concatenate([r[...] for r in side], axis=0) for side in (own, other))]
+    else:
+        slabs = [(own[w][...], other[w][...]) for w in range(n)]
     even_first = jnp.where(lax.axis_index("cores") % 2 == 0, 1.0, 0.0)
-    for w in range(WAYS):
+    for w, (mine, theirs) in enumerate(slabs, WAYS - 1 if last else 0):
         rows = slice(w * ROWS, (w + 1) * ROWS)
-        mine = own[w][...]
-        theirs = other[w][...]
         for k in range(2):
             stack_ref, high_ref, low_ref = outs[3 * k : 3 * k + 3]
             flag = even_first if k == 0 else 1.0 - even_first
@@ -413,13 +425,14 @@
     return pl.BlockSpec(memory_space=pltpu.SMEM)
 
 
-def call(kernel, outs, ins, scratch=(), name=None):
+def call(kernel, outs, ins, scratch=(), name=None, aliases={}):
     return pl.pallas_call(
         kernel,
         out_shape=outs,
         in_specs=ins,
         out_specs=jax.tree.map(lambda o: smem() if o.dtype == jnp.int32 and o.size == 1 else vmem(), outs),
         scratch_shapes=list(scratch),
+        input_output_aliases=aliases,
         compiler_params=pltpu.CompilerParams(vmem_limit_bytes=BIG),
         name=name,
     )
@@ -546,11 +559,33 @@
         for by in range(1, side)
     ]
     level = [[(p, along(1, p, by)) for p in range(peers)] for by in range(1, side)]
-    own = [updated] + [lax.ppermute(updated, ("cores", "samp"), pairs) for pairs in ring]
-    other = [lax.ppermute(o, "cores", siblings) for o in own]
+    mid = ROWS // 2
+
+    def swapped(array):
+        return lax.ppermute(array, "cores", siblings)
+
+    ahead = lax.ppermute(updated, ("cores", "samp"), ring[0])
+    behind = lax.ppermute(updated, ("cores", "samp"), ring[2])
+    far = [
+        lax.ppermute(ahead[:mid], ("cores", "samp"), ring[0]),
+        lax.ppermute(behind[mid:], ("cores", "samp"), ring[2]),
+    ]
+    near = [updated, ahead, behind]
     stack = shape(3 * WAYS * ROWS, LANES, dtype=BF16)
     flat = shape(LANES, WAYS * ROWS, dtype=BF16)
-    arranged = call(arrange_kernel, [stack, flat, flat] * 2, [vmem()] * 8, name="arrange")(*own, *other)
+    arranged = call(
+        functools.partial(arrange_kernel, last=False),
+        [stack, flat, flat] * 2,
+        [vmem()] * 6,
+        name="arrange_near",
+    )(*near, *[swapped(a) for a in near])
+    arranged = call(
+        functools.partial(arrange_kernel, last=True),
+        [stack, flat, flat] * 2,
+        [vmem()] * 10,
+        name="arrange_far",
+        aliases={4 + i: i for i in range(6)},
+    )(*far, *[swapped(a) for a in far], *arranged)
     even, odd = list(arranged[:3]), list(arranged[3:])
 
     saved, sums = [], []

time: 145 us -> 149 us (1.028)
  starting transfers between devices: 20.7 us -> 23.6 us
  waiting for transfers between devices: 41 us -> 43.3 us
    ppermute x7 -> x9, starting transfers between devices: 3.49 us -> 6.69 us  [the longest x1 2.8 us: on_device(): lax.ppermute(behind[mid:], ('cores', 'samp'), ring[2])]
    ppermute x7 -> x9, waiting for transfers between devices: 9.72 us -> 11.4 us  [the longest x1 4.69 us: on_device(): ahead = lax.ppermute(updated, ('cores', 'samp'), ring[0])]
  transfers between devices with their start and end apart: 16 -> 18, of which waited for: 13 -> 13; matrix products, arithmetic and copies ran while one was open for 1% -> 1% of each run, Pallas kernels for 4% -> 4%
where the time goes in v9:
time: 149 us; the launch traced here: 148 us
  blocking collectives  43.8 us (29%)
  waiting for transfers between devices  43.3 us (29%)
  Pallas kernels  32.1 us (22%)
  starting transfers between devices  23.6 us (16%)
  local copies, waits for them, and re-layouts  3.47 us (2%)
    all_to_all x3, blocking collectives, on_device(): lax.all_to_all(res[0], ('cores', 'samp'), 0, 0, axis_index_groups=groups,...  43.8 us
    all_to_all x1, waiting for transfers between devices, exchanged(): return lax.all_to_all(block, 'samp', 0, 0, tiled=True)  12.8 us
    ppermute x3, waiting for transfers between devices, on_device(): recv.append(lax.ppermute(out, 'cores', pairs))  12.4 us
    pallas_call x4, Pallas kernels, on_device(): call(functools.partial(pair_kernel, pair=pair), outs, [vmem()] * len(ins)...  8.94 us
    all_to_all x1, starting transfers between devices, exchanged(): return lax.all_to_all(block, 'samp', 0, 0, tiled=True)  7.88 us
    pallas_call x1, Pallas kernels, on_device(): pl.pallas_call(functools.partial(gather_kernel, peers=peers), grid=(steps...  5.34 us
    ppermute x1, waiting for transfers between devices, on_device(): ahead = lax.ppermute(updated, ('cores', 'samp'), ring[0])  4.69 us
    ppermute x3, starting transfers between devices, on_device(): recv.append(lax.ppermute(out, 'cores', pairs))  4.62 us
  transfers between devices with their start and end apart: 18, of which 13 were waited for; matrix products, arithmetic and copies ran while one was open for 1% of the time, Pallas kernels for 4%

profile of v9, /device:TPU:16, one launch (start us, length us, event | category | flops | bytes accessed | tf_op | source)
XLA Modules:
  0.0 148.0 jit_solution(11160828877971748382)
XLA Ops:
  0.0 5.3 %gather.1 = (f32[4608,512]{1,0:T(8,128)S(1)}, s32[8,1024]{1,0:T(8,128)S(1)}, f32[8,128]{1,0:T(8,128)S(1)}) custom-call(s32[8,1024]{1,0:T(8,128)} %bitcast.21, f32[512,2304]{1,0:T(8,128)} %bitcast.18), custom_call_target="tpu_custom_call" | custom-call | tf_op jit(solution)/shard_map/gather/pallas_call | solution.py:464
  5.3 2.8 %collective-permute-done.table_ref = f32[512,2304]{1,0:T(8,128)S(1)} collective-permute-done((f32[512,2304]{1,0:T(8,128)}, f32[512,2304]{1,0:T(8,128)S(1)}, u32[]{:S(2)}, u32[]{:S(2)}) %collective-permute-start) | collective-permute-done | bytes 4718624 | tf_op jit(solution)/shard_map/ppermute | solution.py:455
  8.1 4.2 %gather_other.1.mats_ref = f32[4608,512]{1,0:T(8,128)S(1)} custom-call(s32[8,1024]{1,0:T(8,128)} %bitcast.22, f32[512,2304]{1,0:T(8,128)S(1)} %collective-permute-done.table_ref, f32[4608,512]{1,0:T(8,128)S(1)} %get-tuple-element.81.refs_0_), custom_call_target="tpu_custom_call", output_to_operand_aliasing={{}: (2, {})} | custom-call | tf_op jit(solution)/shard_map/gather_other/pallas_call | solution.py:478
  12.3 1.3 collective-permute-start.1
  13.6 5.8 %collective-permute-done.1.refs_0_ = f32[48,512]{1,0:T(8,128)S(1)} collective-permute-done((f32[48,512]{1,0:T(8,128)S(1)}, f32[48,512]{1,0:T(8,128)S(1)}, u32[]{:S(2)}, u32[]{:S(2)}) %collective-permute-start.1) | collective-permute-done | bytes 98336 | tf_op jit(solution)/shard_map/ppermute | solution.py:506
  19.4 1.4 hop1.1
  20.8 2.0 %collective-permute-start.2 = (f32[48,512]{1,0:T(8,128)S(1)}, f32[48,512]{1,0:T(8,128)S(1)}, u32[]{:S(2)}, u32[]{:S(2)}) collective-permute-start(f32[48,512]{1,0:T(8,128)S(1)} %get-tuple-element.83), channel_id=1, source_target_pairs={{32,64},{48,80},{64,32},{80,48},{33,65},{49,81},{65,33},{81,49},{3... | collective-permute-start | bytes 294920 | tf_op jit(solution)/shard_map/ppermute | solution.py:506
  22.9 4.5 %collective-permute-done.2.refs_0_.refs_1_ = f32[48,512]{1,0:T(8,128)S(1)} collective-permute-done((f32[48,512]{1,0:T(8,128)S(1)}, f32[48,512]{1,0:T(8,128)S(1)}, u32[]{:S(2)}, u32[]{:S(2)}) %collective-permute-start.2) | collective-permute-done | bytes 98336 | tf_op jit(solution)/shard_map/ppermute | solution.py:506
  27.3 1.4 hop2.1
  28.8 1.3 collective-permute-start.3
  30.1 2.2 %collective-permute-done.3.refs_2_ = f32[48,512]{1,0:T(8,128)S(1)} collective-permute-done((f32[48,512]{1,0:T(8,128)S(1)}, f32[48,512]{1,0:T(8,128)S(1)}, u32[]{:S(2)}, u32[]{:S(2)}) %collective-permute-start.3) | collective-permute-done | bytes 98336 | tf_op jit(solution)/shard_map/ppermute | solution.py:506
  32.3 1.5 %finish.1 = (f32[96,512]{1,0:T(8,128)S(1)}, f32[96,512]{1,0:T(8,128)S(1)}) custom-call(f32[4608,512]{1,0:T(8,128)S(1)} %gather_other.1.mats_ref, f32[48,512]{1,0:T(8,128)S(1)} %collective-permute-done.1.refs_0_, f32[48,512]{1,0:T(8,128)S(1)} %collective-permute-done.2.refs_0_.refs_1_, f32[48,512]{1,0:T(8,128)S(1)} %collective-permute-done.3.refs_2_, ...), custom_call_target="tpu_custom_call" | custom-call | tf_op jit(solution)/shard_map/finish/pallas_call | solution.py:508
  33.9 1.4 collective-permute-done.4.got_ref
  35.3 2.4 %route.1 = (f32[16,104,128]{2,1,0:T(8,128)}, f32[104,1024]{1,0:T(8,128)S(1)}) custom-call(f32[96,512]{1,0:T(8,128)S(1)} %get-tuple-element.88.own_ref, f32[96,512]{1,0:T(8,128)S(1)} %collective-permute-done.4.got_ref, s32[8,1024]{1,0:T(8,128)S(1)} %get-tuple-element.183.slot_ref, f32[8,128]{1,0:T(8,128)S(1)} %get-tuple-element.184.most_ref), custom_call_target="tpu_custom_call" | custom-call | tf_op jit(solution)/shard_map/route/pallas_call | solution.py:516
  37.7 7.9 %all-to-all-start.1 = ((f32[16,104,128]{2,1,0:T(8,128)}), f32[16,104,128]{2,1,0:T(8,128)S(1)}, u32[]{:S(2)}, u32[]{:S(2)}) async-start(f32[16,104,128]{2,1,0:T(8,128)} %get-tuple-element.92), calls=%async_computation.1 | async-start | bytes 1703936 | tf_op jit(solution)/shard_map/all_to_all | solution.py:524
  48.2 12.8 %all-to-all-done.1.recv_ref = f32[16,104,128]{2,1,0:T(8,128)S(1)} async-done(((f32[16,104,128]{2,1,0:T(8,128)}), f32[16,104,128]{2,1,0:T(8,128)S(1)}, u32[]{:S(2)}, u32[]{:S(2)}) %all-to-all-start.1) | async-done | bytes 852000 | tf_op jit(solution)/shard_map/all_to_all | solution.py:524
  61.0 2.1 %collect.2 = (f32[192,384]{1,0:T(8,128)S(1)}, s32[1]{0:T(128)}) custom-call(f32[1]{0:T(128)} %bitcast.15.step_ref, f32[16,104,128]{2,1,0:T(8,128)S(1)} %all-to-all-done.1.recv_ref, f32[192,384]{1,0:T(8,128)S(1)} %reshape.26.base_ref), custom_call_target="tpu_custom_call" | custom-call | tf_op jit(solution)/shard_map/collect/pallas_call | solution.py:527
  64.6 2.7 %collective-permute-start.7 = (f32[192,384]{1,0:T(8,128)S(1)}, f32[192,384]{1,0:T(8,128)S(1)}, u32[]{:S(2)}, u32[]{:S(2)}) collective-permute-start(f32[192,384]{1,0:T(8,128)S(1)} %get-tuple-element.96.refs_0_.refs_7_), channel_id=1, source_target_pairs={{0,3},{1,0},{2,1},{3,2},{4,7},{5,4},{6,5},{7,6},{8,11},{9,8},{10,9... | collective-permute-start | bytes 884744 | tf_op jit(solution)/shard_map/ppermute | solution.py:568
  67.3 4.7 %collective-permute-done.5.refs_1_ = f32[192,384]{1,0:T(8,128)S(1)} collective-permute-done((f32[192,384]{1,0:T(8,128)S(1)}, f32[192,384]{1,0:T(8,128)S(1)}, u32[]{:S(2)}, u32[]{:S(2)}) %collective-permute-start.5) | collective-permute-done | bytes 294944 | tf_op jit(solution)/shard_map/ppermute | solution.py:567
  72.5 2.8 %collective-permute-start.8 = (f32[96,384]{1,0:T(8,128)S(1)}, f32[96,384]{1,0:T(8,128)S(1)}, u32[]{:S(2)}, u32[]{:S(2)}) collective-permute-start(f32[96,384]{1,0:T(8,128)S(1)} %slice.9), channel_id=1, source_target_pairs={{0,3},{1,0},{2,1},{3,2},{4,7},{5,4},{6,5},{7,6},{8,11},{9,8},{10,9... | collective-permute-start | bytes 442376 | tf_op jit(solution)/shard_map/ppermute | solution.py:571
  75.4 2.6 %collective-permute-done.8.refs_1_ = f32[96,384]{1,0:T(8,128)S(1)} collective-permute-done((f32[96,384]{1,0:T(8,128)S(1)}, f32[96,384]{1,0:T(8,128)S(1)}, u32[]{:S(2)}, u32[]{:S(2)}) %collective-permute-start.8) | collective-permute-done | bytes 147488 | tf_op jit(solution)/shard_map/ppermute | solution.py:571
  78.0 3.8 %collective-permute-done.6.refs_0_ = f32[96,384]{1,0:T(8,128)S(1)} collective-permute-done((f32[96,384]{1,0:T(8,128)S(1)}, f32[96,384]{1,0:T(8,128)S(1)}, u32[]{:S(2)}, u32[]{:S(2)}) %collective-permute-start.6) | collective-permute-done | bytes 147488 | tf_op jit(solution)/shard_map/ppermute | solution.py:570
  83.6 2.2 %pair0.1 = (f32[32,24,128]{2,1,0:T(8,128)S(1)}, f32[24,128]{1,0:T(8,128)S(1)}) custom-call(bf16[2304,384]{1,0:T(8,128)(2,1)S(1)} %get-tuple-element.103.refs_0_.refs_1_.refs_4_, bf16[384,768]{1,0:T(8,128)(2,1)S(1)} %get-tuple-element.104.refs_1_.refs_2_.refs_5_, bf16[384,768]{1,0:T(8,128)(2,1)S(1)} %get-tuple-element.105.refs_2_.refs_3_.refs_6_, ...), custom_call_target="tpu_custom_call" | custom-call | tf_op jit(solution)/shard_map/pair0/pallas_call | solution.py:599
  85.8 14.5 %all_to_all.26.refs_0_ = f32[32,24,128]{2,1,0:T(8,128)S(1)} all-to-all(f32[32,24,128]{2,1,0:T(8,128)S(1)} %get-tuple-element.109), channel_id=1, replica_groups={{0,1,2,3,4,5,6,7,8,9,10,11,12,13,14,15,32,33,34,35,36,37,38,39,40,41,42..., dimensions={0} | all-to-all | bytes 786432 | tf_op jit(solution)/shard_map/all_to_all | solution.py:617
  100.4 2.7 %pair1.1 = (f32[32,24,128]{2,1,0:T(8,128)S(1)}, f32[24,128]{1,0:T(8,128)S(1)}, f32[24,128]{1,0:T(8,128)S(1)}) custom-call(f32[32,24,128]{2,1,0:T(8,128)S(1)} %all_to_all.26.refs_0_, bf16[2304,384]{1,0:T(8,128)(2,1)S(1)} %get-tuple-element.103.refs_0_.refs_1_.refs_4_, bf16[384,768]{1,0:T(8,128)(2,1)S(1)} %get-tuple-element.104.refs_1_.refs_2_.refs_5_, ...), custom_call_target="tpu_custom_call" | custom-call | tf_op jit(solution)/shard_map/pair1/pallas_call | solution.py:599
  103.0 14.0 %all_to_all.27.refs_0_ = f32[32,24,128]{2,1,0:T(8,128)S(1)} all-to-all(f32[32,24,128]{2,1,0:T(8,128)S(1)} %get-tuple-element.111), channel_id=1, replica_groups={{32,33,34,35,36,37,38,39,40,41,42,43,44,45,46,47,64,65,66,67,68,69,70,7..., dimensions={0} | all-to-all | bytes 786432 | tf_op jit(solution)/shard_map/all_to_all | solution.py:617
  117.0 2.7 %pair2.1 = (f32[32,24,128]{2,1,0:T(8,128)S(1)}, f32[24,128]{1,0:T(8,128)S(1)}, f32[24,128]{1,0:T(8,128)S(1)}) custom-call(f32[32,24,128]{2,1,0:T(8,128)S(1)} %all_to_all.27.refs_0_, bf16[2304,384]{1,0:T(8,128)(2,1)S(1)} %get-tuple-element.103.refs_0_.refs_1_.refs_4_, bf16[384,768]{1,0:T(8,128)(2,1)S(1)} %get-tuple-element.104.refs_1_.refs_2_.refs_5_, ...), custom_call_target="tpu_custom_call" | custom-call | tf_op jit(solution)/shard_map/pair2/pallas_call | solution.py:599
  119.7 15.3 %all_to_all.28.refs_0_ = f32[32,24,128]{2,1,0:T(8,128)S(1)} all-to-all(f32[32,24,128]{2,1,0:T(8,128)S(1)} %get-tuple-element.113), channel_id=1, replica_groups={{64,65,66,67,68,69,70,71,72,73,74,75,76,77,78,79,96,97,98,99,100,101,10..., dimensions={0} | all-to-all | bytes 786432 | tf_op jit(solution)/shard_map/all_to_all | solution.py:617
  135.0 1.4 pair3.1
  136.9 2.6 %collective-permute-start.15 = (f32[24,128]{1,0:T(8,128)S(1)}, f32[24,128]{1,0:T(8,128)S(1)}, u32[]{:S(2)}, u32[]{:S(2)}) collective-permute-start(f32[24,128]{1,0:T(8,128)S(1)} %get-tuple-element.118.refs_3_), channel_id=1, source_target_pairs={{0,8},{1,9},{2,10},{3,11},{4,12},{5,13},{6,14},{7,15},{8,0},{9,1},... | collective-permute-start | bytes 36872 | tf_op jit(solution)/shard_map/ppermute | solution.py:609
  142.1 1.1 collective-permute-done.16.refs_6_
  143.2 3.3 %final.1 = f32[192,384]{1,0:T(8,128)S(1)} custom-call(f32[24,128]{1,0:T(8,128)S(1)} %get-tuple-element.110.refs_0_, f32[24,128]{1,0:T(8,128)S(1)} %get-tuple-element.112.refs_1_, f32[24,128]{1,0:T(8,128)S(1)} %get-tuple-element.117.refs_2_, f32[24,128]{1,0:T(8,128)S(1)} %get-tuple-element.118.refs_3_, f32[24,128]{1,0:T(8,128)S(1)} %collective-permute-done.14.refs_4_, ...), custom_call_target="tpu_custom_call" | custom-call | tf_op jit(solution)/shard_map/final/pallas_call | solution.py:621
  (34 shorter events, 10.6 us)
Async XLA Ops:
  0.0 8.1 %collective-permute-start = (f32[512,2304]{1,0:T(8,128)}, f32[512,2304]{1,0:T(8,128)S(1)}, u32[]{:S(2)}, u32[]{:S(2)}) collective-permute-start(f32[512,2304]{1,0:T(8,128)} %bitcast.17), channel_id=1, source_target_pairs={{0,16},{16,0},{32,48},{48,32},{64,80},{80,64},{96,112},{112,96},{1... | collective-permute-start | bytes 14155784 | tf_op jit(solution)/shard_map/ppermute | solution.py:455
  12.3 7.1 %collective-permute-start.1 = (f32[48,512]{1,0:T(8,128)S(1)}, f32[48,512]{1,0:T(8,128)S(1)}, u32[]{:S(2)}, u32[]{:S(2)}) collective-permute-start(f32[48,512]{1,0:T(8,128)S(1)} %get-tuple-element.82), channel_id=1, source_target_pairs={{0,32},{16,48},{96,64},{112,80},{1,33},{17,49},{97,65},{113,81},{2... | collective-permute-start | bytes 294920 | tf_op jit(solution)/shard_map/ppermute | solution.py:506
  20.8 11.4 %copy-start = (f32[1024]{0:T(1024)S(1)}, f32[1024]{0:T(1024)}, u32[]{:S(2)}) copy-start(f32[1024]{0:T(1024)} %param.8) | copy-start | bytes 12292
  20.8 6.5 %collective-permute-start.2 = (f32[48,512]{1,0:T(8,128)S(1)}, f32[48,512]{1,0:T(8,128)S(1)}, u32[]{:S(2)}, u32[]{:S(2)}) collective-permute-start(f32[48,512]{1,0:T(8,128)S(1)} %get-tuple-element.83), channel_id=1, source_target_pairs={{32,64},{48,80},{64,32},{80,48},{33,65},{49,81},{65,33},{81,49},{3... | collective-permute-start | bytes 294920 | tf_op jit(solution)/shard_map/ppermute | solution.py:506
  28.8 3.5 %collective-permute-start.3 = (f32[48,512]{1,0:T(8,128)S(1)}, f32[48,512]{1,0:T(8,128)S(1)}, u32[]{:S(2)}, u32[]{:S(2)}) collective-permute-start(f32[48,512]{1,0:T(8,128)S(1)} %get-tuple-element.84.refs_6_), channel_id=1, source_target_pairs={{64,96},{80,112},{32,0},{48,16},{65,97},{81,113},{33,1},{49,17},{6... | collective-permute-start | bytes 294920 | tf_op jit(solution)/shard_map/ppermute | solution.py:506
  33.8 1.5 %collective-permute-start.4 = (f32[96,512]{1,0:T(8,128)S(1)}, f32[96,512]{1,0:T(8,128)S(1)}, u32[]{:S(2)}, u32[]{:S(2)}) collective-permute-start(f32[96,512]{1,0:T(8,128)S(1)} %get-tuple-element.89), channel_id=1, source_target_pairs={{0,16},{16,0},{32,48},{48,32},{64,80},{80,64},{96,112},{112,96},{1... | collective-permute-start | bytes 589832 | tf_op jit(solution)/shard_map/ppermute | solution.py:515
  37.7 23.3 %all-to-all-start.1 = ((f32[16,104,128]{2,1,0:T(8,128)}), f32[16,104,128]{2,1,0:T(8,128)S(1)}, u32[]{:S(2)}, u32[]{:S(2)}) async-start(f32[16,104,128]{2,1,0:T(8,128)} %get-tuple-element.92), calls=%async_computation.1 | async-start | bytes 1703936 | tf_op jit(solution)/shard_map/all_to_all | solution.py:524
  64.0 8.0 %collective-permute-start.5 = (f32[192,384]{1,0:T(8,128)S(1)}, f32[192,384]{1,0:T(8,128)S(1)}, u32[]{:S(2)}, u32[]{:S(2)}) collective-permute-start(f32[192,384]{1,0:T(8,128)S(1)} %get-tuple-element.96.refs_0_.refs_7_), channel_id=1, source_target_pairs={{0,1},{1,2},{2,3},{3,0},{4,5},{5,6},{6,7},{7,4},{8,9},{9,10},{10,1... | collective-permute-start | bytes 884744 | tf_op jit(solution)/shard_map/ppermute | solution.py:567
  64.6 7.4 %collective-permute-start.7 = (f32[192,384]{1,0:T(8,128)S(1)}, f32[192,384]{1,0:T(8,128)S(1)}, u32[]{:S(2)}, u32[]{:S(2)}) collective-permute-start(f32[192,384]{1,0:T(8,128)S(1)} %get-tuple-element.96.refs_0_.refs_7_), channel_id=1, source_target_pairs={{0,3},{1,0},{2,1},{3,2},{4,7},{5,4},{6,5},{7,6},{8,11},{9,8},{10,9... | collective-permute-start | bytes 884744 | tf_op jit(solution)/shard_map/ppermute | solution.py:568
  67.3 14.5 %collective-permute-start.11 = (f32[192,384]{1,0:T(8,128)S(1)}, f32[192,384]{1,0:T(8,128)S(1)}, u32[]{:S(2)}, u32[]{:S(2)}) collective-permute-start(f32[192,384]{1,0:T(8,128)S(1)} %get-tuple-element.96.refs_0_.refs_7_), channel_id=1, source_target_pairs={{0,16},{16,0},{32,48},{48,32},{64,80},{80,64},{96,112},{112,96},{1... | collective-permute-start | bytes 884744 | tf_op jit(solution)/shard_map/ppermute | solution.py:565
  72.0 9.8 %collective-permute-start.12 = (f32[192,384]{1,0:T(8,128)S(1)}, f32[192,384]{1,0:T(8,128)S(1)}, u32[]{:S(2)}, u32[]{:S(2)}) collective-permute-start(f32[192,384]{1,0:T(8,128)S(1)} %collective-permute-done.5.refs_1_), channel_id=1, source_target_pairs={{0,16},{16,0},{32,48},{48,32},{64,80},{80,64},{96,112},{112,96},{1... | collective-permute-start | bytes 884744 | tf_op jit(solution)/shard_map/ppermute | solution.py:565
  72.0 9.8 %collective-permute-start.13 = (f32[192,384]{1,0:T(8,128)S(1)}, f32[192,384]{1,0:T(8,128)S(1)}, u32[]{:S(2)}, u32[]{:S(2)}) collective-permute-start(f32[192,384]{1,0:T(8,128)S(1)} %collective-permute-done.7.refs_2_), channel_id=1, source_target_pairs={{0,16},{16,0},{32,48},{48,32},{64,80},{80,64},{96,112},{112,96},{1... | collective-permute-start | bytes 884744 | tf_op jit(solution)/shard_map/ppermute | solution.py:565
  72.5 5.5 %collective-permute-start.8 = (f32[96,384]{1,0:T(8,128)S(1)}, f32[96,384]{1,0:T(8,128)S(1)}, u32[]{:S(2)}, u32[]{:S(2)}) collective-permute-start(f32[96,384]{1,0:T(8,128)S(1)} %slice.9), channel_id=1, source_target_pairs={{0,3},{1,0},{2,1},{3,2},{4,7},{5,4},{6,5},{7,6},{8,11},{9,8},{10,9... | collective-permute-start | bytes 442376 | tf_op jit(solution)/shard_map/ppermute | solution.py:571
  75.3 6.4 %collective-permute-start.6 = (f32[96,384]{1,0:T(8,128)S(1)}, f32[96,384]{1,0:T(8,128)S(1)}, u32[]{:S(2)}, u32[]{:S(2)}) collective-permute-start(f32[96,384]{1,0:T(8,128)S(1)} %slice.8), channel_id=1, source_target_pairs={{0,1},{1,2},{2,3},{3,0},{4,5},{5,6},{6,7},{7,4},{8,9},{9,10},{10,1... | collective-permute-start | bytes 442376 | tf_op jit(solution)/shard_map/ppermute | solution.py:570
  78.0 4.8 %collective-permute-start.10 = (f32[96,384]{1,0:T(8,128)S(1)}, f32[96,384]{1,0:T(8,128)S(1)}, u32[]{:S(2)}, u32[]{:S(2)}) collective-permute-start(f32[96,384]{1,0:T(8,128)S(1)} %collective-permute-done.8.refs_1_), channel_id=1, source_target_pairs={{0,16},{16,0},{32,48},{48,32},{64,80},{80,64},{96,112},{112,96},{1... | collective-permute-start | bytes 442376 | tf_op jit(solution)/shard_map/ppermute | solution.py:565
  81.7 1.4 collective-permute-start.9
  136.4 5.0 %collective-permute-start.14 = (f32[24,128]{1,0:T(8,128)S(1)}, f32[24,128]{1,0:T(8,128)S(1)}, u32[]{:S(2)}, u32[]{:S(2)}) collective-permute-start(f32[24,128]{1,0:T(8,128)S(1)} %get-tuple-element.118.refs_3_), channel_id=1, source_target_pairs={{0,4},{1,5},{2,6},{3,7},{4,8},{5,9},{6,10},{7,11},{8,12},{9,13},{1... | collective-permute-start | bytes 36872 | tf_op jit(solution)/shard_map/ppermute | solution.py:609
  136.9 5.2 %collective-permute-start.15 = (f32[24,128]{1,0:T(8,128)S(1)}, f32[24,128]{1,0:T(8,128)S(1)}, u32[]{:S(2)}, u32[]{:S(2)}) collective-permute-start(f32[24,128]{1,0:T(8,128)S(1)} %get-tuple-element.118.refs_3_), channel_id=1, source_target_pairs={{0,8},{1,9},{2,10},{3,11},{4,12},{5,13},{6,14},{7,15},{8,0},{9,1},... | collective-permute-start | bytes 36872 | tf_op jit(solution)/shard_map/ppermute | solution.py:609
  139.5 3.7 %collective-permute-start.16 = (f32[24,128]{1,0:T(8,128)S(1)}, f32[24,128]{1,0:T(8,128)S(1)}, u32[]{:S(2)}, u32[]{:S(2)}) collective-permute-start(f32[24,128]{1,0:T(8,128)S(1)} %get-tuple-element.118.refs_3_), channel_id=1, source_target_pairs={{0,12},{1,13},{2,14},{3,15},{4,0},{5,1},{6,2},{7,3},{8,4},{9,5},{1... | collective-permute-start | bytes 36872 | tf_op jit(solution)/shard_map/ppermute | solution.py:609

commit v10 on v7

--- a/solution.py
+++ b/solution.py
@@ -150,9 +150,19 @@
 
 def hop_kernel(mats_ref, *refs, turn):
     vec_ref, mid_ref, out_ref = refs if turn else (refs[2], refs[0], refs[1])
-    if turn == 0:
-        vec_ref[...] = unit_at_ends(vec_ref.shape)
-    both_modes(turn, mats_ref, vec_ref, mid_ref, out_ref)
+    chip = lax.axis_index("cores") // 2
+    live = jnp.logical_or(chip == turn, chip == MODES // 2 - 1 - turn)
+
+    @pl.when(live)
+    def _():
+        if turn == 0:
+            vec_ref[...] = unit_at_ends(vec_ref.shape)
+        both_modes(turn, mats_ref, vec_ref, mid_ref, out_ref)
+
+    @pl.when(jnp.logical_not(live))
+    def _():
+        mid_ref[...] = jnp.zeros(mid_ref.shape, F32)
+        out_ref[...] = jnp.zeros(out_ref.shape, F32)
 
 
 def finish_kernel(mats_ref, *refs):
@@ -176,38 +186,57 @@
         other_ref[rows, :] = jnp.where(second, even[k], odd[k])
 
 
-def spread(values, slot_ref, most_ref, turn, pay_ref):
+def keys(slot_ref, turn):
     place = slot_ref[0:1, :] - turn * SLOTS
     fits = jnp.logical_and(place >= 0, place < SLOTS)
-    key = jnp.where(fits, slot_ref[1:2, :] * SLOTS + place, -1)
+    return jnp.where(fits, slot_ref[1:2, :] * SLOTS + place, -1)
+
+
+def spread(values, key, pay_ref, so_far_ref=None):
     hi, lo = halves(values)
     both = jnp.concatenate([hi, lo], axis=0)
-    peers = pay_ref.shape[0]
-    count = values.shape[1]
-    for pair in range(peers // 2):
+    for pair in range(pay_ref.shape[0] // 2):
         base = pair * 2 * SLOTS
-        hot = (iota((2 * SLOTS, count), 0) + base == key).astype(BF16)
+        hot = (iota((2 * SLOTS, values.shape[1]), 0) + base == key).astype(BF16)
         out = dot_lanes(both, hot)
         out = out[:FEATS] + out[FEATS:]
-        pay_ref[2 * pair] = out[:, :SLOTS]
-        pay_ref[2 * pair + 1] = out[:, SLOTS:]
-    for peer in range(peers):
+        for k in range(2):
+            part = out[:, k * SLOTS : (k + 1) * SLOTS]
+            peer = 2 * pair + k
+            pay_ref[peer] = part if so_far_ref is None else part + so_far_ref[peer]
+
+
+def mark(most_ref, pay_ref):
+    for peer in range(pay_ref.shape[0]):
         pay_ref[peer, 97:98, :] = most_ref[0:1, :]
 
 
-def route_kernel(own_ref, got_ref, slot_ref, most_ref, pay_ref, val_ref):
-    second = jnp.where(lax.axis_index("cores") % 2 == 1, 1.0, 0.0) > 0.5
+def with_place(vecs, loc):
+    pad = jnp.zeros((FEATS - 97, vecs.shape[1]), F32)
+    return jnp.concatenate([vecs, loc.astype(F32), pad], axis=0)
+
+
+def route_own_kernel(vecs_ref, slot_ref, pay_ref):
+    second = lax.axis_index("cores") % 2 == 1
+    values = with_place(vecs_ref[...], half_of(slot_ref[2:3, :], second))
+    spread(values, half_of(keys(slot_ref, 0), second), pay_ref)
+
+
+def route_kernel(own_ref, got_ref, slot_ref, most_ref, part_ref, pay_ref, val_ref):
+    first = lax.axis_index("cores") % 2 == 0
     own = own_ref[...]
     got = got_ref[...]
-    vecs = jnp.concatenate([jnp.where(second, got, own), jnp.where(second, own, got)], axis=1)
-    loc = slot_ref[2:3, :].astype(F32)
-    values = jnp.concatenate([vecs, loc, jnp.zeros((FEATS - 97, vecs.shape[1]), F32)], axis=0)
-    val_ref[...] = values
-    spread(values, slot_ref, most_ref, 0, pay_ref)
+    values = with_place(got, half_of(slot_ref[2:3, :], first))
+    spread(values, half_of(keys(slot_ref, 0), first), pay_ref, part_ref)
+    mark(most_ref, pay_ref)
+    flag = jnp.where(first, 1.0, 0.0) > 0.5
+    vecs = jnp.concatenate([jnp.where(flag, own, got), jnp.where(flag, got, own)], axis=1)
+    val_ref[...] = with_place(vecs, slot_ref[2:3, :])
 
 
 def again_kernel(turn_ref, val_ref, slot_ref, most_ref, pay_ref):
-    spread(val_ref[...], slot_ref, most_ref, turn_ref[0], pay_ref)
+    spread(val_ref[...], keys(slot_ref, turn_ref[0]), pay_ref)
+    mark(most_ref, pay_ref)
 
 
 def collect_kernel(step_ref, recv_ref, base_ref, out_ref, turns_ref):
@@ -243,11 +272,10 @@
     outs = refs[2 * WAYS :]
     even_first = jnp.where(lax.axis_index("cores") % 2 == 0, 1.0, 0.0)
     for w in range(WAYS):
-        rows = slice(w * ROWS, (w + 1) * ROWS)
         mine = own[w][...]
         theirs = other[w][...]
         for k in range(2):
-            stack_ref, high_ref, low_ref = outs[3 * k : 3 * k + 3]
+            stack_ref, turned_ref = outs[2 * k : 2 * k + 2]
             flag = even_first if k == 0 else 1.0 - even_first
             core = jnp.where(flag > 0.5, mine, theirs)
             hi, lo = halves(core)
@@ -257,7 +285,9 @@
                 stack_ref[at : at + R, :] = hi[here]
                 stack_ref[at + R : at + 2 * R, :] = hi[here]
                 stack_ref[at + 2 * R : at + 3 * R, :] = lo[here]
-            high_ref[:, rows], low_ref[:, rows] = halves(core.T)
+            hi, lo = halves(core.T)
+            for k3, piece in enumerate((hi, hi, lo)):
+                turned_ref[:, (k3 * WAYS + w) * ROWS : (k3 * WAYS + w + 1) * ROWS] = piece
 
 
 def stacked(square):
@@ -267,12 +297,6 @@
     return (hi + (pltpu.roll(lo, R, 1) + pltpu.roll(hi, 2 * R, 1)))[:, : 3 * R].astype(BF16)
 
 
-def three(a, b):
-    (ah, al), (bh, bl) = a, b
-    mul = functools.partial(jnp.dot, preferred_element_type=F32)
-    return mul(ah, bh) + (mul(ah, bl) + mul(al, bh))
-
-
 def packed_of(full):
     lane = iota((24, 128), 1)
     return jnp.where(lane < 64, full[0:24], pltpu.roll(full[24:48], 64, 1))
@@ -284,22 +308,23 @@
 
 
 def pulled(before, core, prod_ref):
-    stack, high_t, low_t = core
-    if before is None:
-        first = [stack[3 * g * R : 3 * g * R + R, :] for g in range(WAYS * GROUPS)]
-        second = [stack[3 * g * R + 2 * R : 3 * g * R + 3 * R, :] for g in range(WAYS * GROUPS)]
-        prod = (jnp.concatenate(first, axis=0), jnp.concatenate(second, axis=0))
-    else:
-        weights = stacked(before)
-        for g in range(WAYS * GROUPS):
-            prod_ref[g * R : (g + 1) * R, :] = jnp.dot(
-                weights, stack[3 * g * R : 3 * (g + 1) * R, :], preferred_element_type=F32
+    stack, turned = core
+    all_rows = WAYS * ROWS
+    weights = None if before is None else stacked(before)
+    for g in range(WAYS * GROUPS):
+        at = 3 * g * R
+        if before is None:
+            hi, lo = stack[at : at + R, :], stack[at + 2 * R : at + 3 * R, :]
+        else:
+            hi, lo = halves(
+                jnp.dot(weights, stack[at : at + 3 * R, :], preferred_element_type=F32)
             )
-        prod = halves(prod_ref[...])
+        for k3, piece in enumerate((hi, lo, hi)):
+            prod_ref[k3 * all_rows + g * R : k3 * all_rows + (g + 1) * R, :] = piece
     total = jnp.zeros((R, 256), F32)
     for part, slices in ((0, range(5)), (128, range(5, WIDE))):
         cols = slice(part, part + 256)
-        z = three((high_t[cols, :], low_t[cols, :]), (prod[0][:, cols], prod[1][:, cols]))
+        z = jnp.dot(turned[cols, :], prod_ref[:, cols], preferred_element_type=F32)
         for h in slices:
             at = h * R - part
             block = z[at : at + R]
@@ -312,12 +337,12 @@
     refs = list(refs)
     recv_ref = refs.pop(0) if pair else None
     saved = [refs.pop(0) for _ in range(pair)] if last else []
-    even = [refs.pop(0) for _ in range(3)]
-    odd = None if last else [refs.pop(0) for _ in range(3)]
+    even = [refs.pop(0) for _ in range(2)]
+    odd = None if last else [refs.pop(0) for _ in range(2)]
     prod_ref = refs.pop()
     if pair:
         sum_ref = refs.pop()
-        arrived = jnp.sum(recv_ref[...], axis=0)
+        arrived = jnp.sum(recv_ref[0 : recv_ref.shape[0] // 2], axis=0)
         sum_ref[...] = arrived
         before = whole(arrived)
     else:
@@ -500,12 +525,13 @@
         name="finish",
     )(mats, *recv, *mids, out, observed.reshape(1, count))
     got_vecs = lax.ppermute(other_vecs, "cores", siblings)
+    part = call(route_own_kernel, shape(peers, FEATS, SLOTS), [vmem()] * 2, name="route_own")(own_vecs, slot)
     pay, values = call(
         route_kernel,
         (shape(peers, FEATS, SLOTS), shape(FEATS, count)),
-        [vmem()] * 4,
+        [vmem()] * 5,
         name="route",
-    )(own_vecs, got_vecs, slot, most)
+    )(own_vecs, got_vecs, slot, most, part)
 
     def exchanged(block):
         return lax.all_to_all(block, "samp", 0, 0, tiled=True)
@@ -537,21 +563,25 @@
 
     side = int(peers**0.5)
 
-    def along(mode, peer, by):
+    def partner(mode, peer, which):
         z, x = peer // side, peer % side
-        return z * side + (x + by) % side if mode % 2 == 0 else (z + by) % side * side + x
+        if which & 1:
+            x = side - 1 - x if mode % 2 else x ^ 1
+        if which & 2:
+            z = side - 1 - z if mode % 2 else z ^ 1
+        return z * side + x
 
     ring = [
-        [(m * peers + p, m * peers + along(m, p, by)) for m in range(MODES) for p in range(peers)]
-        for by in range(1, side)
+        [(m * peers + p, m * peers + partner(m, p, w)) for m in range(MODES) for p in range(peers)]
+        for w in range(1, WAYS)
     ]
-    level = [[(p, along(1, p, by)) for p in range(peers)] for by in range(1, side)]
+    level = [[(p, partner(1, p, w)) for p in range(peers)] for w in range(1, WAYS)]
     own = [updated] + [lax.ppermute(updated, ("cores", "samp"), pairs) for pairs in ring]
     other = [lax.ppermute(o, "cores", siblings) for o in own]
     stack = shape(3 * WAYS * ROWS, LANES, dtype=BF16)
-    flat = shape(LANES, WAYS * ROWS, dtype=BF16)
-    arranged = call(arrange_kernel, [stack, flat, flat] * 2, [vmem()] * 8, name="arrange")(*own, *other)
-    even, odd = list(arranged[:3]), list(arranged[3:])
+    flat = shape(LANES, 3 * WAYS * ROWS, dtype=BF16)
+    arranged = call(arrange_kernel, [stack, flat] * 2, [vmem()] * 8, name="arrange")(*own, *other)
+    even, odd = list(arranged[:2]), list(arranged[2:])
 
     saved, sums = [], []
     recv = None
@@ -565,7 +595,7 @@
             functools.partial(pair_kernel, pair=pair),
             outs,
             [vmem()] * len(ins),
-            [pltpu.VMEM((WAYS * ROWS, LANES), F32)],
+            [pltpu.VMEM((3 * WAYS * ROWS, LANES), BF16)],
             name=f"pair{pair}",
         )(*ins)
         if pair:

time: 145 us -> 147 us (1.014)
  starting transfers between devices: 20.7 us -> 22.9 us
    ppermute x3, waiting for transfers between devices: 2.58 us -> 4.33 us  [on_device(): parts = [res[0]] + [lax.ppermute(res[0], 'samp', pairs) for pairs in level]]
    ppermute x3, starting transfers between devices: 4.27 us -> 5.97 us  [on_device(): parts = [res[0]] + [lax.ppermute(res[0], 'samp', pairs) for pairs in level]]
where the time goes in v10:
time: 147 us; the launch traced here: 146 us
  blocking collectives  43.7 us (30%)
  waiting for transfers between devices  41.6 us (28%)
  Pallas kernels  32.5 us (22%)
  starting transfers between devices  22.9 us (16%)
  local copies, waits for them, and re-layouts  3.45 us (2%)
    all_to_all x3, blocking collectives, on_device(): lax.all_to_all(res[0], ('cores', 'samp'), 0, 0, axis_index_groups=groups,...  43.7 us
    all_to_all x1, waiting for transfers between devices, exchanged(): return lax.all_to_all(block, 'samp', 0, 0, tiled=True)  12.8 us
    ppermute x3, waiting for transfers between devices, on_device(): recv.append(lax.ppermute(out, 'cores', pairs))  12.4 us
    pallas_call x4, Pallas kernels, on_device(): call(functools.partial(pair_kernel, pair=pair), outs, [vmem()] * len(ins)...  9.1 us
    all_to_all x1, starting transfers between devices, exchanged(): return lax.all_to_all(block, 'samp', 0, 0, tiled=True)  7.87 us
    ppermute x3, waiting for transfers between devices, on_device(): lax.ppermute(updated, ('cores', 'samp'), pairs)  7.14 us
    ppermute x3, starting transfers between devices, on_device(): parts = [res[0]] + [lax.ppermute(res[0], 'samp', pairs) for pairs in level]  5.97 us
    pallas_call x1, Pallas kernels, on_device(): pl.pallas_call(functools.partial(gather_kernel, peers=peers), grid=(steps...  5.34 us
  transfers between devices with their start and end apart: 16, of which 13 were waited for; matrix products, arithmetic and copies ran while one was open for 1% of the time, Pallas kernels for 4%

profile of v10, /device:TPU:16, one launch (start us, length us, event | category | flops | bytes accessed | tf_op | source)
XLA Modules:
  0.0 145.7 jit_solution(18434470558206018364)
XLA Ops:
  0.0 5.3 %gather.1 = (f32[4608,512]{1,0:T(8,128)S(1)}, s32[8,1024]{1,0:T(8,128)S(1)}, f32[8,128]{1,0:T(8,128)S(1)}) custom-call(s32[8,1024]{1,0:T(8,128)} %bitcast.21, f32[512,2304]{1,0:T(8,128)} %bitcast.18), custom_call_target="tpu_custom_call" | custom-call | tf_op jit(solution)/shard_map/gather/pallas_call | solution.py:476
  5.3 2.8 %collective-permute-done.table_ref = f32[512,2304]{1,0:T(8,128)S(1)} collective-permute-done((f32[512,2304]{1,0:T(8,128)}, f32[512,2304]{1,0:T(8,128)S(1)}, u32[]{:S(2)}, u32[]{:S(2)}) %collective-permute-start) | collective-permute-done | bytes 4718624 | tf_op jit(solution)/shard_map/ppermute | solution.py:467
  8.1 4.2 %gather_other.1.mats_ref = f32[4608,512]{1,0:T(8,128)S(1)} custom-call(s32[8,1024]{1,0:T(8,128)} %bitcast.22, f32[512,2304]{1,0:T(8,128)S(1)} %collective-permute-done.table_ref, f32[4608,512]{1,0:T(8,128)S(1)} %get-tuple-element.73.refs_0_), custom_call_target="tpu_custom_call", output_to_operand_aliasing={{}: (2, {})} | custom-call | tf_op jit(solution)/shard_map/gather_other/pallas_call | solution.py:490
  12.3 1.3 collective-permute-start.1
  13.6 5.8 %collective-permute-done.1.refs_0_ = f32[48,512]{1,0:T(8,128)S(1)} collective-permute-done((f32[48,512]{1,0:T(8,128)S(1)}, f32[48,512]{1,0:T(8,128)S(1)}, u32[]{:S(2)}, u32[]{:S(2)}) %collective-permute-start.1) | collective-permute-done | bytes 98336 | tf_op jit(solution)/shard_map/ppermute | solution.py:518
  19.4 1.4 hop1.1
  20.8 2.0 %collective-permute-start.2 = (f32[48,512]{1,0:T(8,128)S(1)}, f32[48,512]{1,0:T(8,128)S(1)}, u32[]{:S(2)}, u32[]{:S(2)}) collective-permute-start(f32[48,512]{1,0:T(8,128)S(1)} %get-tuple-element.75), channel_id=1, source_target_pairs={{32,64},{48,80},{64,32},{80,48},{33,65},{49,81},{65,33},{81,49},{3... | collective-permute-start | bytes 294920 | tf_op jit(solution)/shard_map/ppermute | solution.py:518
  22.9 4.5 %collective-permute-done.2.refs_0_.refs_1_ = f32[48,512]{1,0:T(8,128)S(1)} collective-permute-done((f32[48,512]{1,0:T(8,128)S(1)}, f32[48,512]{1,0:T(8,128)S(1)}, u32[]{:S(2)}, u32[]{:S(2)}) %collective-permute-start.2) | collective-permute-done | bytes 98336 | tf_op jit(solution)/shard_map/ppermute | solution.py:518
  27.3 1.4 hop2.1
  28.8 1.3 collective-permute-start.3
  30.1 2.2 %collective-permute-done.3.refs_2_ = f32[48,512]{1,0:T(8,128)S(1)} collective-permute-done((f32[48,512]{1,0:T(8,128)S(1)}, f32[48,512]{1,0:T(8,128)S(1)}, u32[]{:S(2)}, u32[]{:S(2)}) %collective-permute-start.3) | collective-permute-done | bytes 98336 | tf_op jit(solution)/shard_map/ppermute | solution.py:518
  32.3 1.5 %finish.1 = (f32[96,512]{1,0:T(8,128)S(1)}, f32[96,512]{1,0:T(8,128)S(1)}) custom-call(f32[4608,512]{1,0:T(8,128)S(1)} %gather_other.1.mats_ref, f32[48,512]{1,0:T(8,128)S(1)} %collective-permute-done.1.refs_0_, f32[48,512]{1,0:T(8,128)S(1)} %collective-permute-done.2.refs_0_.refs_1_, f32[48,512]{1,0:T(8,128)S(1)} %collective-permute-done.3.refs_2_, ...), custom_call_target="tpu_custom_call" | custom-call | tf_op jit(solution)/shard_map/finish/pallas_call | solution.py:520
  35.3 1.8 %route.1 = (f32[16,104,128]{2,1,0:T(8,128)}, f32[104,1024]{1,0:T(8,128)S(1)}) custom-call(f32[96,512]{1,0:T(8,128)S(1)} %get-tuple-element.80.vecs_ref.own_ref, f32[96,512]{1,0:T(8,128)S(1)} %collective-permute-done.4.got_ref, s32[8,1024]{1,0:T(8,128)S(1)} %get-tuple-element.167.slot_ref, f32[8,128]{1,0:T(8,128)S(1)} %get-tuple-element.168.most_ref, ...), custom_call_target="tpu_custom_call" | custom-call | tf_op jit(solution)/shard_map/route/pallas_call | solution.py:529
  37.1 7.9 %all-to-all-start.1 = ((f32[16,104,128]{2,1,0:T(8,128)}), f32[16,104,128]{2,1,0:T(8,128)S(1)}, u32[]{:S(2)}, u32[]{:S(2)}) async-start(f32[16,104,128]{2,1,0:T(8,128)} %get-tuple-element.84), calls=%async_computation.1 | async-start | bytes 1703936 | tf_op jit(solution)/shard_map/all_to_all | solution.py:537
  47.6 12.8 %all-to-all-done.1.recv_ref = f32[16,104,128]{2,1,0:T(8,128)S(1)} async-done(((f32[16,104,128]{2,1,0:T(8,128)}), f32[16,104,128]{2,1,0:T(8,128)S(1)}, u32[]{:S(2)}, u32[]{:S(2)}) %all-to-all-start.1) | async-done | bytes 852000 | tf_op jit(solution)/shard_map/all_to_all | solution.py:537
  60.4 2.1 %collect.2 = (f32[192,384]{1,0:T(8,128)S(1)}, s32[1]{0:T(128)}) custom-call(f32[1]{0:T(128)} %bitcast.15.step_ref, f32[16,104,128]{2,1,0:T(8,128)S(1)} %all-to-all-done.1.recv_ref, f32[192,384]{1,0:T(8,128)S(1)} %reshape.26.base_ref), custom_call_target="tpu_custom_call" | custom-call | tf_op jit(solution)/shard_map/collect/pallas_call | solution.py:540
  63.4 2.0 %collective-permute-start.7 = (f32[192,384]{1,0:T(8,128)S(1)}, f32[192,384]{1,0:T(8,128)S(1)}, u32[]{:S(2)}, u32[]{:S(2)}) collective-permute-start(f32[192,384]{1,0:T(8,128)S(1)} %get-tuple-element.88.refs_0_.refs_7_), channel_id=1, source_target_pairs={{0,5},{1,4},{2,7},{3,6},{4,1},{5,0},{6,3},{7,2},{8,13},{9,12},{10,... | collective-permute-start | bytes 884744 | tf_op jit(solution)/shard_map/ppermute | solution.py:579
  65.3 1.5 %collective-permute-start.5 = (f32[192,384]{1,0:T(8,128)S(1)}, f32[192,384]{1,0:T(8,128)S(1)}, u32[]{:S(2)}, u32[]{:S(2)}) collective-permute-start(f32[192,384]{1,0:T(8,128)S(1)} %get-tuple-element.88.refs_0_.refs_7_), channel_id=1, source_target_pairs={{0,1},{1,0},{2,3},{3,2},{4,5},{5,4},{6,7},{7,6},{8,9},{9,8},{10,11... | collective-permute-start | bytes 884744 | tf_op jit(solution)/shard_map/ppermute | solution.py:579
  67.1 6.1 %collective-permute-done.6.refs_2_ = f32[192,384]{1,0:T(8,128)S(1)} collective-permute-done((f32[192,384]{1,0:T(8,128)S(1)}, f32[192,384]{1,0:T(8,128)S(1)}, u32[]{:S(2)}, u32[]{:S(2)}) %collective-permute-start.6) | collective-permute-done | bytes 294944 | tf_op jit(solution)/shard_map/ppermute | solution.py:579
  76.3 1.4 arrange.1
  77.7 2.3 %pair0.1 = (f32[32,24,128]{2,1,0:T(8,128)S(1)}, f32[24,128]{1,0:T(8,128)S(1)}) custom-call(bf16[2304,384]{1,0:T(8,128)(2,1)S(1)} %get-tuple-element.89.refs_0_.refs_1_.refs_4_, bf16[384,2304]{1,0:T(8,128)(2,1)S(1)} %get-tuple-element.90.refs_1_.refs_2_.refs_5_, bf16[2304,384]{1,0:T(8,128)(2,1)S(1)} %get-tuple-element.91.refs_2_.refs_3_, ...), custom_call_target="tpu_custom_call" | custom-call | tf_op jit(solution)/shard_map/pair0/pallas_call | solution.py:594
  80.0 15.3 %all_to_all.26.refs_0_ = f32[32,24,128]{2,1,0:T(8,128)S(1)} all-to-all(f32[32,24,128]{2,1,0:T(8,128)S(1)} %get-tuple-element.93), channel_id=1, replica_groups={{0,1,2,3,4,5,6,7,8,9,10,11,12,13,14,15,32,33,34,35,36,37,38,39,40,41,42..., dimensions={0} | all-to-all | bytes 786432 | tf_op jit(solution)/shard_map/all_to_all | solution.py:612
  95.3 2.7 %pair1.1 = (f32[32,24,128]{2,1,0:T(8,128)S(1)}, f32[24,128]{1,0:T(8,128)S(1)}, f32[24,128]{1,0:T(8,128)S(1)}) custom-call(f32[32,24,128]{2,1,0:T(8,128)S(1)} %all_to_all.26.refs_0_, bf16[2304,384]{1,0:T(8,128)(2,1)S(1)} %get-tuple-element.89.refs_0_.refs_1_.refs_4_, bf16[384,2304]{1,0:T(8,128)(2,1)S(1)} %get-tuple-element.90.refs_1_.refs_2_.refs_5_, ...), custom_call_target="tpu_custom_call" | custom-call | tf_op jit(solution)/shard_map/pair1/pallas_call | solution.py:594
  98.0 14.0 %all_to_all.27.refs_0_ = f32[32,24,128]{2,1,0:T(8,128)S(1)} all-to-all(f32[32,24,128]{2,1,0:T(8,128)S(1)} %get-tuple-element.95), channel_id=1, replica_groups={{32,33,34,35,36,37,38,39,40,41,42,43,44,45,46,47,64,65,66,67,68,69,70,7..., dimensions={0} | all-to-all | bytes 786432 | tf_op jit(solution)/shard_map/all_to_all | solution.py:612
  112.0 2.7 %pair2.1 = (f32[32,24,128]{2,1,0:T(8,128)S(1)}, f32[24,128]{1,0:T(8,128)S(1)}, f32[24,128]{1,0:T(8,128)S(1)}) custom-call(f32[32,24,128]{2,1,0:T(8,128)S(1)} %all_to_all.27.refs_0_, bf16[2304,384]{1,0:T(8,128)(2,1)S(1)} %get-tuple-element.89.refs_0_.refs_1_.refs_4_, bf16[384,2304]{1,0:T(8,128)(2,1)S(1)} %get-tuple-element.90.refs_1_.refs_2_.refs_5_, ...), custom_call_target="tpu_custom_call" | custom-call | tf_op jit(solution)/shard_map/pair2/pallas_call | solution.py:594
  114.8 14.4 %all_to_all.28.refs_0_ = f32[32,24,128]{2,1,0:T(8,128)S(1)} all-to-all(f32[32,24,128]{2,1,0:T(8,128)S(1)} %get-tuple-element.97), channel_id=1, replica_groups={{64,65,66,67,68,69,70,71,72,73,74,75,76,77,78,79,96,97,98,99,100,101,10..., dimensions={0} | all-to-all | bytes 786432 | tf_op jit(solution)/shard_map/all_to_all | solution.py:612
  129.2 1.4 pair3.1
  130.6 1.7 %collective-permute-start.12 = (f32[24,128]{1,0:T(8,128)S(1)}, f32[24,128]{1,0:T(8,128)S(1)}, u32[]{:S(2)}, u32[]{:S(2)}) collective-permute-start(f32[24,128]{1,0:T(8,128)S(1)} %get-tuple-element.102.refs_3_), channel_id=1, source_target_pairs={{0,3},{1,2},{2,1},{3,0},{4,7},{5,6},{6,5},{7,4},{8,11},{9,10},{10,... | collective-permute-start | bytes 36872 | tf_op jit(solution)/shard_map/ppermute | solution.py:604
  132.3 1.6 %collective-permute-start.13 = (f32[24,128]{1,0:T(8,128)S(1)}, f32[24,128]{1,0:T(8,128)S(1)}, u32[]{:S(2)}, u32[]{:S(2)}) collective-permute-start(f32[24,128]{1,0:T(8,128)S(1)} %get-tuple-element.102.refs_3_), channel_id=1, source_target_pairs={{0,12},{1,13},{2,14},{3,15},{4,8},{5,9},{6,10},{7,11},{8,4},{9,5},... | collective-permute-start | bytes 36872 | tf_op jit(solution)/shard_map/ppermute | solution.py:604
  133.9 2.7 %collective-permute-start.14 = (f32[24,128]{1,0:T(8,128)S(1)}, f32[24,128]{1,0:T(8,128)S(1)}, u32[]{:S(2)}, u32[]{:S(2)}) collective-permute-start(f32[24,128]{1,0:T(8,128)S(1)} %get-tuple-element.102.refs_3_), channel_id=1, source_target_pairs={{0,15},{1,14},{2,13},{3,12},{4,11},{5,10},{6,9},{7,8},{8,7},{9,6},... | collective-permute-start | bytes 36872 | tf_op jit(solution)/shard_map/ppermute | solution.py:604
  137.2 3.7 %collective-permute-done.14.refs_6_ = f32[24,128]{1,0:T(8,128)S(1)} collective-permute-done((f32[24,128]{1,0:T(8,128)S(1)}, f32[24,128]{1,0:T(8,128)S(1)}, u32[]{:S(2)}, u32[]{:S(2)}) %collective-permute-start.14) | collective-permute-done | bytes 12320 | tf_op jit(solution)/shard_map/ppermute | solution.py:604
  140.9 3.3 %final.1 = f32[192,384]{1,0:T(8,128)S(1)} custom-call(f32[24,128]{1,0:T(8,128)S(1)} %get-tuple-element.94.refs_0_, f32[24,128]{1,0:T(8,128)S(1)} %get-tuple-element.96.refs_1_, f32[24,128]{1,0:T(8,128)S(1)} %get-tuple-element.101.refs_2_, f32[24,128]{1,0:T(8,128)S(1)} %get-tuple-element.102.refs_3_, f32[24,128]{1,0:T(8,128)S(1)} %collective-permute-done.12.refs_4_, ...), custom_call_target="tpu_custom_call" | custom-call | tf_op jit(solution)/shard_map/final/pallas_call | solution.py:616
  (28 shorter events, 9.8 us)
Async XLA Ops:
  0.0 8.1 %collective-permute-start = (f32[512,2304]{1,0:T(8,128)}, f32[512,2304]{1,0:T(8,128)S(1)}, u32[]{:S(2)}, u32[]{:S(2)}) collective-permute-start(f32[512,2304]{1,0:T(8,128)} %bitcast.17), channel_id=1, source_target_pairs={{0,16},{16,0},{32,48},{48,32},{64,80},{80,64},{96,112},{112,96},{1... | collective-permute-start | bytes 14155784 | tf_op jit(solution)/shard_map/ppermute | solution.py:467
  12.3 7.1 %collective-permute-start.1 = (f32[48,512]{1,0:T(8,128)S(1)}, f32[48,512]{1,0:T(8,128)S(1)}, u32[]{:S(2)}, u32[]{:S(2)}) collective-permute-start(f32[48,512]{1,0:T(8,128)S(1)} %get-tuple-element.74), channel_id=1, source_target_pairs={{0,32},{16,48},{96,64},{112,80},{1,33},{17,49},{97,65},{113,81},{2... | collective-permute-start | bytes 294920 | tf_op jit(solution)/shard_map/ppermute | solution.py:518
  20.8 11.4 %copy-start = (f32[1024]{0:T(1024)S(1)}, f32[1024]{0:T(1024)}, u32[]{:S(2)}) copy-start(f32[1024]{0:T(1024)} %param.8) | copy-start | bytes 12292
  20.8 6.5 %collective-permute-start.2 = (f32[48,512]{1,0:T(8,128)S(1)}, f32[48,512]{1,0:T(8,128)S(1)}, u32[]{:S(2)}, u32[]{:S(2)}) collective-permute-start(f32[48,512]{1,0:T(8,128)S(1)} %get-tuple-element.75), channel_id=1, source_target_pairs={{32,64},{48,80},{64,32},{80,48},{33,65},{49,81},{65,33},{81,49},{3... | collective-permute-start | bytes 294920 | tf_op jit(solution)/shard_map/ppermute | solution.py:518
  28.8 3.5 %collective-permute-start.3 = (f32[48,512]{1,0:T(8,128)S(1)}, f32[48,512]{1,0:T(8,128)S(1)}, u32[]{:S(2)}, u32[]{:S(2)}) collective-permute-start(f32[48,512]{1,0:T(8,128)S(1)} %get-tuple-element.76.refs_6_), channel_id=1, source_target_pairs={{64,96},{80,112},{32,0},{48,16},{65,97},{81,113},{33,1},{49,17},{6... | collective-permute-start | bytes 294920 | tf_op jit(solution)/shard_map/ppermute | solution.py:518
  33.8 1.5 %collective-permute-start.4 = (f32[96,512]{1,0:T(8,128)S(1)}, f32[96,512]{1,0:T(8,128)S(1)}, u32[]{:S(2)}, u32[]{:S(2)}) collective-permute-start(f32[96,512]{1,0:T(8,128)S(1)} %get-tuple-element.81), channel_id=1, source_target_pairs={{0,16},{16,0},{32,48},{48,32},{64,80},{80,64},{96,112},{112,96},{1... | collective-permute-start | bytes 589832 | tf_op jit(solution)/shard_map/ppermute | solution.py:527
  37.1 23.3 %all-to-all-start.1 = ((f32[16,104,128]{2,1,0:T(8,128)}), f32[16,104,128]{2,1,0:T(8,128)S(1)}, u32[]{:S(2)}, u32[]{:S(2)}) async-start(f32[16,104,128]{2,1,0:T(8,128)} %get-tuple-element.84), calls=%async_computation.1 | async-start | bytes 1703936 | tf_op jit(solution)/shard_map/all_to_all | solution.py:537
  63.3 10.0 %collective-permute-start.6 = (f32[192,384]{1,0:T(8,128)S(1)}, f32[192,384]{1,0:T(8,128)S(1)}, u32[]{:S(2)}, u32[]{:S(2)}) collective-permute-start(f32[192,384]{1,0:T(8,128)S(1)} %get-tuple-element.88.refs_0_.refs_7_), channel_id=1, source_target_pairs={{0,4},{1,5},{2,6},{3,7},{4,0},{5,1},{6,2},{7,3},{8,12},{9,13},{10,... | collective-permute-start | bytes 884744 | tf_op jit(solution)/shard_map/ppermute | solution.py:579
  63.4 9.9 %collective-permute-start.7 = (f32[192,384]{1,0:T(8,128)S(1)}, f32[192,384]{1,0:T(8,128)S(1)}, u32[]{:S(2)}, u32[]{:S(2)}) collective-permute-start(f32[192,384]{1,0:T(8,128)S(1)} %get-tuple-element.88.refs_0_.refs_7_), channel_id=1, source_target_pairs={{0,5},{1,4},{2,7},{3,6},{4,1},{5,0},{6,3},{7,2},{8,13},{9,12},{10,... | collective-permute-start | bytes 884744 | tf_op jit(solution)/shard_map/ppermute | solution.py:579
  65.3 9.4 %collective-permute-start.5 = (f32[192,384]{1,0:T(8,128)S(1)}, f32[192,384]{1,0:T(8,128)S(1)}, u32[]{:S(2)}, u32[]{:S(2)}) collective-permute-start(f32[192,384]{1,0:T(8,128)S(1)} %get-tuple-element.88.refs_0_.refs_7_), channel_id=1, source_target_pairs={{0,1},{1,0},{2,3},{3,2},{4,5},{5,4},{6,7},{7,6},{8,9},{9,8},{10,11... | collective-permute-start | bytes 884744 | tf_op jit(solution)/shard_map/ppermute | solution.py:579
  66.8 7.9 %collective-permute-start.8 = (f32[192,384]{1,0:T(8,128)S(1)}, f32[192,384]{1,0:T(8,128)S(1)}, u32[]{:S(2)}, u32[]{:S(2)}) collective-permute-start(f32[192,384]{1,0:T(8,128)S(1)} %get-tuple-element.88.refs_0_.refs_7_), channel_id=1, source_target_pairs={{0,16},{16,0},{32,48},{48,32},{64,80},{80,64},{96,112},{112,96},{1... | collective-permute-start | bytes 884744 | tf_op jit(solution)/shard_map/ppermute | solution.py:580
  73.2 1.6 %collective-permute-start.10 = (f32[192,384]{1,0:T(8,128)S(1)}, f32[192,384]{1,0:T(8,128)S(1)}, u32[]{:S(2)}, u32[]{:S(2)}) collective-permute-start(f32[192,384]{1,0:T(8,128)S(1)} %collective-permute-done.6.refs_2_), channel_id=1, source_target_pairs={{0,16},{16,0},{32,48},{48,32},{64,80},{80,64},{96,112},{112,96},{1... | collective-permute-start | bytes 884744 | tf_op jit(solution)/shard_map/ppermute | solution.py:580
  73.2 2.0 %collective-permute-start.11 = (f32[192,384]{1,0:T(8,128)S(1)}, f32[192,384]{1,0:T(8,128)S(1)}, u32[]{:S(2)}, u32[]{:S(2)}) collective-permute-start(f32[192,384]{1,0:T(8,128)S(1)} %collective-permute-done.7.refs_3_), channel_id=1, source_target_pairs={{0,16},{16,0},{32,48},{48,32},{64,80},{80,64},{96,112},{112,96},{1... | collective-permute-start | bytes 884744 | tf_op jit(solution)/shard_map/ppermute | solution.py:580
  74.7 1.6 %collective-permute-start.9 = (f32[192,384]{1,0:T(8,128)S(1)}, f32[192,384]{1,0:T(8,128)S(1)}, u32[]{:S(2)}, u32[]{:S(2)}) collective-permute-start(f32[192,384]{1,0:T(8,128)S(1)} %collective-permute-done.5.refs_1_), channel_id=1, source_target_pairs={{0,16},{16,0},{32,48},{48,32},{64,80},{80,64},{96,112},{112,96},{1... | collective-permute-start | bytes 884744 | tf_op jit(solution)/shard_map/ppermute | solution.py:580
  130.6 6.0 %collective-permute-start.12 = (f32[24,128]{1,0:T(8,128)S(1)}, f32[24,128]{1,0:T(8,128)S(1)}, u32[]{:S(2)}, u32[]{:S(2)}) collective-permute-start(f32[24,128]{1,0:T(8,128)S(1)} %get-tuple-element.102.refs_3_), channel_id=1, source_target_pairs={{0,3},{1,2},{2,1},{3,0},{4,7},{5,6},{6,5},{7,4},{8,11},{9,10},{10,... | collective-permute-start | bytes 36872 | tf_op jit(solution)/shard_map/ppermute | solution.py:604
  132.3 4.9 %collective-permute-start.13 = (f32[24,128]{1,0:T(8,128)S(1)}, f32[24,128]{1,0:T(8,128)S(1)}, u32[]{:S(2)}, u32[]{:S(2)}) collective-permute-start(f32[24,128]{1,0:T(8,128)S(1)} %get-tuple-element.102.refs_3_), channel_id=1, source_target_pairs={{0,12},{1,13},{2,14},{3,15},{4,8},{5,9},{6,10},{7,11},{8,4},{9,5},... | collective-permute-start | bytes 36872 | tf_op jit(solution)/shard_map/ppermute | solution.py:604
  133.9 7.0 %collective-permute-start.14 = (f32[24,128]{1,0:T(8,128)S(1)}, f32[24,128]{1,0:T(8,128)S(1)}, u32[]{:S(2)}, u32[]{:S(2)}) collective-permute-start(f32[24,128]{1,0:T(8,128)S(1)} %get-tuple-element.102.refs_3_), channel_id=1, source_target_pairs={{0,15},{1,14},{2,13},{3,12},{4,11},{5,10},{6,9},{7,8},{8,7},{9,6},... | collective-permute-start | bytes 36872 | tf_op jit(solution)/shard_map/ppermute | solution.py:604

commit v11 on v10

--- a/solution.py
+++ b/solution.py
@@ -342,25 +342,27 @@
     prod_ref = refs.pop()
     if pair:
         sum_ref = refs.pop()
-        arrived = jnp.sum(recv_ref[0 : recv_ref.shape[0] // 2], axis=0)
-        sum_ref[...] = arrived
-        before = whole(arrived)
-    else:
-        before = None
-    chip = lax.axis_index("cores") // 2
-    live = jnp.where(chip == pair, 1.0, 0.0)
-    middle = pulled(before, even, prod_ref) * live
-    kept = packed_of(middle)
-    if last:
+        sum_ref[...] = jnp.sum(recv_ref[0 : recv_ref.shape[0] // 2], axis=0)
+    kept_ref = refs.pop()
+    live = lax.axis_index("cores") // 2 == pair
+
+    @pl.when(live)
+    def _():
+        middle = pulled(whole(sum_ref[...]) if pair else None, even, prod_ref)
+        kept_ref[...] = packed_of(middle)
+        if not last:
+            packed = packed_of(pulled(middle, odd, prod_ref))
+            for peer in range(refs[0].shape[0]):
+                refs[0][peer] = packed
+
+    @pl.when(jnp.logical_not(live))
+    def _():
+        kept = jnp.zeros((24, 128), F32)
         for s in saved:
             kept = kept + s[...]
-        refs[0][...] = kept
-        return
-    out_ref, save_ref = refs
-    save_ref[...] = kept
-    packed = packed_of(pulled(middle, odd, prod_ref))
-    for peer in range(out_ref.shape[0]):
-        out_ref[peer] = packed
+        kept_ref[...] = kept
+        if not last:
+            refs[0][...] = jnp.zeros(refs[0].shape, F32)
 
 
 def final_kernel(*refs):
@@ -563,13 +565,9 @@
 
     side = int(peers**0.5)
 
-    def partner(mode, peer, which):
+    def partner(mode, peer, by):
         z, x = peer // side, peer % side
-        if which & 1:
-            x = side - 1 - x if mode % 2 else x ^ 1
-        if which & 2:
-            z = side - 1 - z if mode % 2 else z ^ 1
-        return z * side + x
+        return (z + by) % side * side + x if mode % 2 else z * side + (x + by) % side
 
     ring = [
         [(m * peers + p, m * peers + partner(m, p, w)) for m in range(MODES) for p in range(peers)]

time: 147 us -> 139 us (0.946)
  Pallas kernels: 32.5 us -> 26.4 us
  starting transfers between devices: 22.9 us -> 20.2 us
    pallas_call x4, Pallas kernels: 9.1 us -> 3.05 us  [on_device(): call(functools.partial(pair_kernel, pair=pair), outs, [vmem()] * len(ins)...]
    ppermute x3, waiting for transfers between devices: 4.33 us -> 2.57 us  [on_device(): parts = [res[0]] + [lax.ppermute(res[0], 'samp', pairs) for pairs in level]]
    ppermute x3, starting transfers between devices: 5.97 us -> 4.29 us  [on_device(): parts = [res[0]] + [lax.ppermute(res[0], 'samp', pairs) for pairs in level]]
where the time goes in v11:
time: 139 us; the launch traced here: 138 us
  blocking collectives  45.1 us (32%)
  waiting for transfers between devices  40.8 us (29%)
  Pallas kernels  26.4 us (19%)
  starting transfers between devices  20.2 us (15%)
  local copies, waits for them, and re-layouts  3.45 us (2%)
    all_to_all x3, blocking collectives, on_device(): lax.all_to_all(res[0], ('cores', 'samp'), 0, 0, axis_index_groups=groups,...  45.1 us
    all_to_all x1, waiting for transfers between devices, exchanged(): return lax.all_to_all(block, 'samp', 0, 0, tiled=True)  12.8 us
    ppermute x3, waiting for transfers between devices, on_device(): recv.append(lax.ppermute(out, 'cores', pairs))  12.4 us
    ppermute x3, waiting for transfers between devices, on_device(): lax.ppermute(updated, ('cores', 'samp'), pairs)  8.15 us
    all_to_all x1, starting transfers between devices, exchanged(): return lax.all_to_all(block, 'samp', 0, 0, tiled=True)  7.87 us
    pallas_call x1, Pallas kernels, on_device(): pl.pallas_call(functools.partial(gather_kernel, peers=peers), grid=(steps...  5.34 us
    ppermute x3, starting transfers between devices, on_device(): recv.append(lax.ppermute(out, 'cores', pairs))  4.62 us
    ppermute x3, starting transfers between devices, on_device(): parts = [res[0]] + [lax.ppermute(res[0], 'samp', pairs) for pairs in level]  4.29 us
  transfers between devices with their start and end apart: 16, of which 13 were waited for; matrix products, arithmetic and copies ran while one was open for 1% of the time, Pallas kernels for 4%

profile of v11, /device:TPU:16, one launch (start us, length us, event | category | flops | bytes accessed | tf_op | source)
XLA Modules:
  0.0 137.6 jit_solution(6992490880406133160)
XLA Ops:
  0.0 5.3 %gather.1 = (f32[4608,512]{1,0:T(8,128)S(1)}, s32[8,1024]{1,0:T(8,128)S(1)}, f32[8,128]{1,0:T(8,128)S(1)}) custom-call(s32[8,1024]{1,0:T(8,128)} %bitcast.21, f32[512,2304]{1,0:T(8,128)} %bitcast.18), custom_call_target="tpu_custom_call" | custom-call | tf_op jit(solution)/shard_map/gather/pallas_call | solution.py:478
  5.3 2.8 %collective-permute-done.table_ref = f32[512,2304]{1,0:T(8,128)S(1)} collective-permute-done((f32[512,2304]{1,0:T(8,128)}, f32[512,2304]{1,0:T(8,128)S(1)}, u32[]{:S(2)}, u32[]{:S(2)}) %collective-permute-start) | collective-permute-done | bytes 4718624 | tf_op jit(solution)/shard_map/ppermute | solution.py:469
  8.1 4.2 %gather_other.1.mats_ref = f32[4608,512]{1,0:T(8,128)S(1)} custom-call(s32[8,1024]{1,0:T(8,128)} %bitcast.22, f32[512,2304]{1,0:T(8,128)S(1)} %collective-permute-done.table_ref, f32[4608,512]{1,0:T(8,128)S(1)} %get-tuple-element.73.refs_0_), custom_call_target="tpu_custom_call", output_to_operand_aliasing={{}: (2, {})} | custom-call | tf_op jit(solution)/shard_map/gather_other/pallas_call | solution.py:492
  12.3 1.3 collective-permute-start.1
  13.6 5.8 %collective-permute-done.1.refs_0_ = f32[48,512]{1,0:T(8,128)S(1)} collective-permute-done((f32[48,512]{1,0:T(8,128)S(1)}, f32[48,512]{1,0:T(8,128)S(1)}, u32[]{:S(2)}, u32[]{:S(2)}) %collective-permute-start.1) | collective-permute-done | bytes 98336 | tf_op jit(solution)/shard_map/ppermute | solution.py:520
  19.4 1.4 %hop1.1 = (f32[48,512]{1,0:T(8,128)S(1)}, f32[48,512]{1,0:T(8,128)S(1)}) custom-call(f32[4608,512]{1,0:T(8,128)S(1)} %gather_other.1.mats_ref, f32[48,512]{1,0:T(8,128)S(1)} %collective-permute-done.1.refs_0_), custom_call_target="tpu_custom_call" | custom-call | tf_op jit(solution)/shard_map/hop1/pallas_call | solution.py:512
  20.8 2.0 %collective-permute-start.2 = (f32[48,512]{1,0:T(8,128)S(1)}, f32[48,512]{1,0:T(8,128)S(1)}, u32[]{:S(2)}, u32[]{:S(2)}) collective-permute-start(f32[48,512]{1,0:T(8,128)S(1)} %get-tuple-element.75), channel_id=1, source_target_pairs={{32,64},{48,80},{64,32},{80,48},{33,65},{49,81},{65,33},{81,49},{3... | collective-permute-start | bytes 294920 | tf_op jit(solution)/shard_map/ppermute | solution.py:520
  22.9 4.5 %collective-permute-done.2.refs_0_.refs_1_ = f32[48,512]{1,0:T(8,128)S(1)} collective-permute-done((f32[48,512]{1,0:T(8,128)S(1)}, f32[48,512]{1,0:T(8,128)S(1)}, u32[]{:S(2)}, u32[]{:S(2)}) %collective-permute-start.2) | collective-permute-done | bytes 98336 | tf_op jit(solution)/shard_map/ppermute | solution.py:520
  27.3 1.4 %hop2.1 = (f32[48,512]{1,0:T(8,128)S(1)}, f32[48,512]{1,0:T(8,128)S(1)}) custom-call(f32[4608,512]{1,0:T(8,128)S(1)} %gather_other.1.mats_ref, f32[48,512]{1,0:T(8,128)S(1)} %collective-permute-done.2.refs_0_.refs_1_), custom_call_target="tpu_custom_call" | custom-call | tf_op jit(solution)/shard_map/hop2/pallas_call | solution.py:512
  28.8 1.3 collective-permute-start.3
  30.1 2.2 %collective-permute-done.3.refs_2_ = f32[48,512]{1,0:T(8,128)S(1)} collective-permute-done((f32[48,512]{1,0:T(8,128)S(1)}, f32[48,512]{1,0:T(8,128)S(1)}, u32[]{:S(2)}, u32[]{:S(2)}) %collective-permute-start.3) | collective-permute-done | bytes 98336 | tf_op jit(solution)/shard_map/ppermute | solution.py:520
  32.3 1.5 %finish.1 = (f32[96,512]{1,0:T(8,128)S(1)}, f32[96,512]{1,0:T(8,128)S(1)}) custom-call(f32[4608,512]{1,0:T(8,128)S(1)} %gather_other.1.mats_ref, f32[48,512]{1,0:T(8,128)S(1)} %collective-permute-done.1.refs_0_, f32[48,512]{1,0:T(8,128)S(1)} %collective-permute-done.2.refs_0_.refs_1_, f32[48,512]{1,0:T(8,128)S(1)} %collective-permute-done.3.refs_2_, ...), custom_call_target="tpu_custom_call" | custom-call | tf_op jit(solution)/shard_map/finish/pallas_call | solution.py:522
  35.3 1.8 %route.1 = (f32[16,104,128]{2,1,0:T(8,128)}, f32[104,1024]{1,0:T(8,128)S(1)}) custom-call(f32[96,512]{1,0:T(8,128)S(1)} %get-tuple-element.80.vecs_ref.own_ref, f32[96,512]{1,0:T(8,128)S(1)} %collective-permute-done.4.got_ref, s32[8,1024]{1,0:T(8,128)S(1)} %get-tuple-element.167.slot_ref, f32[8,128]{1,0:T(8,128)S(1)} %get-tuple-element.168.most_ref, ...), custom_call_target="tpu_custom_call" | custom-call | tf_op jit(solution)/shard_map/route/pallas_call | solution.py:531
  37.1 7.9 %all-to-all-start.1 = ((f32[16,104,128]{2,1,0:T(8,128)}), f32[16,104,128]{2,1,0:T(8,128)S(1)}, u32[]{:S(2)}, u32[]{:S(2)}) async-start(f32[16,104,128]{2,1,0:T(8,128)} %get-tuple-element.84), calls=%async_computation.1 | async-start | bytes 1703936 | tf_op jit(solution)/shard_map/all_to_all | solution.py:539
  45.0 1.0 constant_dynamic-slice_fusion
  47.6 12.8 %all-to-all-done.1.recv_ref = f32[16,104,128]{2,1,0:T(8,128)S(1)} async-done(((f32[16,104,128]{2,1,0:T(8,128)}), f32[16,104,128]{2,1,0:T(8,128)S(1)}, u32[]{:S(2)}, u32[]{:S(2)}) %all-to-all-start.1) | async-done | bytes 852000 | tf_op jit(solution)/shard_map/all_to_all | solution.py:539
  60.4 2.1 %collect.2 = (f32[192,384]{1,0:T(8,128)S(1)}, s32[1]{0:T(128)}) custom-call(f32[1]{0:T(128)} %bitcast.15.step_ref, f32[16,104,128]{2,1,0:T(8,128)S(1)} %all-to-all-done.1.recv_ref, f32[192,384]{1,0:T(8,128)S(1)} %reshape.26.base_ref), custom_call_target="tpu_custom_call" | custom-call | tf_op jit(solution)/shard_map/collect/pallas_call | solution.py:542
  64.1 2.5 %collective-permute-start.7 = (f32[192,384]{1,0:T(8,128)S(1)}, f32[192,384]{1,0:T(8,128)S(1)}, u32[]{:S(2)}, u32[]{:S(2)}) collective-permute-start(f32[192,384]{1,0:T(8,128)S(1)} %get-tuple-element.88.refs_0_.refs_7_), channel_id=1, source_target_pairs={{0,3},{1,0},{2,1},{3,2},{4,7},{5,4},{6,5},{7,6},{8,11},{9,8},{10,9... | collective-permute-start | bytes 884744 | tf_op jit(solution)/shard_map/ppermute | solution.py:577
  66.6 5.0 %collective-permute-done.6.refs_2_ = f32[192,384]{1,0:T(8,128)S(1)} collective-permute-done((f32[192,384]{1,0:T(8,128)S(1)}, f32[192,384]{1,0:T(8,128)S(1)}, u32[]{:S(2)}, u32[]{:S(2)}) %collective-permute-start.6) | collective-permute-done | bytes 294944 | tf_op jit(solution)/shard_map/ppermute | solution.py:577
  71.6 0.9 collective-permute-done.7.refs_3_
  72.5 2.2 %collective-permute-done.5.refs_1_ = f32[192,384]{1,0:T(8,128)S(1)} collective-permute-done((f32[192,384]{1,0:T(8,128)S(1)}, f32[192,384]{1,0:T(8,128)S(1)}, u32[]{:S(2)}, u32[]{:S(2)}) %collective-permute-start.5) | collective-permute-done | bytes 294944 | tf_op jit(solution)/shard_map/ppermute | solution.py:577
  74.8 1.6 %collective-permute-done.9.refs_5_ = f32[192,384]{1,0:T(8,128)S(1)} collective-permute-done((f32[192,384]{1,0:T(8,128)S(1)}, f32[192,384]{1,0:T(8,128)S(1)}, u32[]{:S(2)}, u32[]{:S(2)}) %collective-permute-start.9) | collective-permute-done | bytes 294944 | tf_op jit(solution)/shard_map/ppermute | solution.py:578
  76.3 1.4 %arrange.1 = (bf16[2304,384]{1,0:T(8,128)(2,1)S(1)}, bf16[384,2304]{1,0:T(8,128)(2,1)S(1)}, bf16[2304,384]{1,0:T(8,128)(2,1)S(1)}, bf16[384,2304]{1,0:T(8,128)(2,1)S(1)}) custom-call(f32[192,384]{1,0:T(8,128)S(1)} %get-tuple-element.88.refs_0_.refs_7_, f32[192,384]{1,0:T(8,128)S(1)} %collective-permute-done.5.refs_1_, ...), custom_call_target="tpu_custom_call" | custom-call | tf_op jit(solution)/shard_map/arrange/pallas_call | solution.py:581
  77.8 15.6 %all_to_all.26.refs_0_ = f32[32,24,128]{2,1,0:T(8,128)S(1)} all-to-all(f32[32,24,128]{2,1,0:T(8,128)S(1)} %get-tuple-element.93), channel_id=1, replica_groups={{0,1,2,3,4,5,6,7,8,9,10,11,12,13,14,15,32,33,34,35,36,37,38,39,40,41,42..., dimensions={0} | all-to-all | bytes 786432 | tf_op jit(solution)/shard_map/all_to_all | solution.py:610
  93.4 16.6 %all_to_all.27.refs_0_ = f32[32,24,128]{2,1,0:T(8,128)S(1)} all-to-all(f32[32,24,128]{2,1,0:T(8,128)S(1)} %get-tuple-element.95), channel_id=1, replica_groups={{32,33,34,35,36,37,38,39,40,41,42,43,44,45,46,47,64,65,66,67,68,69,70,7..., dimensions={0} | all-to-all | bytes 786432 | tf_op jit(solution)/shard_map/all_to_all | solution.py:610
  110.0 2.9 %pair2.1 = (f32[32,24,128]{2,1,0:T(8,128)S(1)}, f32[24,128]{1,0:T(8,128)S(1)}, f32[24,128]{1,0:T(8,128)S(1)}) custom-call(f32[32,24,128]{2,1,0:T(8,128)S(1)} %all_to_all.27.refs_0_, bf16[2304,384]{1,0:T(8,128)(2,1)S(1)} %get-tuple-element.89.refs_0_.refs_1_.refs_4_, bf16[384,2304]{1,0:T(8,128)(2,1)S(1)} %get-tuple-element.90.refs_1_.refs_2_.refs_5_, ...), custom_call_target="tpu_custom_call" | custom-call | tf_op jit(solution)/shard_map/pair2/pallas_call | solution.py:592
  112.9 12.9 %all_to_all.28.refs_0_ = f32[32,24,128]{2,1,0:T(8,128)S(1)} all-to-all(f32[32,24,128]{2,1,0:T(8,128)S(1)} %get-tuple-element.97), channel_id=1, replica_groups={{64,65,66,67,68,69,70,71,72,73,74,75,76,77,78,79,96,97,98,99,100,101,10..., dimensions={0} | all-to-all | bytes 786432 | tf_op jit(solution)/shard_map/all_to_all | solution.py:610
  126.4 2.6 %collective-permute-start.13 = (f32[24,128]{1,0:T(8,128)S(1)}, f32[24,128]{1,0:T(8,128)S(1)}, u32[]{:S(2)}, u32[]{:S(2)}) collective-permute-start(f32[24,128]{1,0:T(8,128)S(1)} %get-tuple-element.102.refs_3_), channel_id=1, source_target_pairs={{0,8},{1,9},{2,10},{3,11},{4,12},{5,13},{6,14},{7,15},{8,0},{9,1},... | collective-permute-start | bytes 36872 | tf_op jit(solution)/shard_map/ppermute | solution.py:602
  129.1 1.1 collective-permute-start.14
  131.6 1.1 collective-permute-done.14.refs_6_
  132.8 3.3 %final.1 = f32[192,384]{1,0:T(8,128)S(1)} custom-call(f32[24,128]{1,0:T(8,128)S(1)} %get-tuple-element.94.refs_0_, f32[24,128]{1,0:T(8,128)S(1)} %get-tuple-element.96.refs_1_, f32[24,128]{1,0:T(8,128)S(1)} %get-tuple-element.101.refs_2_, f32[24,128]{1,0:T(8,128)S(1)} %get-tuple-element.102.refs_3_, f32[24,128]{1,0:T(8,128)S(1)} %collective-permute-done.12.refs_4_, ...), custom_call_target="tpu_custom_call" | custom-call | tf_op jit(solution)/shard_map/final/pallas_call | solution.py:614
  136.5 1.0 reshape.28
  (28 shorter events, 6.7 us)
Async XLA Ops:
  0.0 8.1 %collective-permute-start = (f32[512,2304]{1,0:T(8,128)}, f32[512,2304]{1,0:T(8,128)S(1)}, u32[]{:S(2)}, u32[]{:S(2)}) collective-permute-start(f32[512,2304]{1,0:T(8,128)} %bitcast.17), channel_id=1, source_target_pairs={{0,16},{16,0},{32,48},{48,32},{64,80},{80,64},{96,112},{112,96},{1... | collective-permute-start | bytes 14155784 | tf_op jit(solution)/shard_map/ppermute | solution.py:469
  12.3 7.1 %collective-permute-start.1 = (f32[48,512]{1,0:T(8,128)S(1)}, f32[48,512]{1,0:T(8,128)S(1)}, u32[]{:S(2)}, u32[]{:S(2)}) collective-permute-start(f32[48,512]{1,0:T(8,128)S(1)} %get-tuple-element.74), channel_id=1, source_target_pairs={{0,32},{16,48},{96,64},{112,80},{1,33},{17,49},{97,65},{113,81},{2... | collective-permute-start | bytes 294920 | tf_op jit(solution)/shard_map/ppermute | solution.py:520
  20.8 11.4 %copy-start = (f32[1024]{0:T(1024)S(1)}, f32[1024]{0:T(1024)}, u32[]{:S(2)}) copy-start(f32[1024]{0:T(1024)} %param.8) | copy-start | bytes 12292
  20.8 6.5 %collective-permute-start.2 = (f32[48,512]{1,0:T(8,128)S(1)}, f32[48,512]{1,0:T(8,128)S(1)}, u32[]{:S(2)}, u32[]{:S(2)}) collective-permute-start(f32[48,512]{1,0:T(8,128)S(1)} %get-tuple-element.75), channel_id=1, source_target_pairs={{32,64},{48,80},{64,32},{80,48},{33,65},{49,81},{65,33},{81,49},{3... | collective-permute-start | bytes 294920 | tf_op jit(solution)/shard_map/ppermute | solution.py:520
  28.8 3.5 %collective-permute-start.3 = (f32[48,512]{1,0:T(8,128)S(1)}, f32[48,512]{1,0:T(8,128)S(1)}, u32[]{:S(2)}, u32[]{:S(2)}) collective-permute-start(f32[48,512]{1,0:T(8,128)S(1)} %get-tuple-element.76.refs_6_), channel_id=1, source_target_pairs={{64,96},{80,112},{32,0},{48,16},{65,97},{81,113},{33,1},{49,17},{6... | collective-permute-start | bytes 294920 | tf_op jit(solution)/shard_map/ppermute | solution.py:520
  33.8 1.5 %collective-permute-start.4 = (f32[96,512]{1,0:T(8,128)S(1)}, f32[96,512]{1,0:T(8,128)S(1)}, u32[]{:S(2)}, u32[]{:S(2)}) collective-permute-start(f32[96,512]{1,0:T(8,128)S(1)} %get-tuple-element.81), channel_id=1, source_target_pairs={{0,16},{16,0},{32,48},{48,32},{64,80},{80,64},{96,112},{112,96},{1... | collective-permute-start | bytes 589832 | tf_op jit(solution)/shard_map/ppermute | solution.py:529
  37.1 23.3 %all-to-all-start.1 = ((f32[16,104,128]{2,1,0:T(8,128)}), f32[16,104,128]{2,1,0:T(8,128)S(1)}, u32[]{:S(2)}, u32[]{:S(2)}) async-start(f32[16,104,128]{2,1,0:T(8,128)} %get-tuple-element.84), calls=%async_computation.1 | async-start | bytes 1703936 | tf_op jit(solution)/shard_map/all_to_all | solution.py:539
  63.3 8.3 %collective-permute-start.6 = (f32[192,384]{1,0:T(8,128)S(1)}, f32[192,384]{1,0:T(8,128)S(1)}, u32[]{:S(2)}, u32[]{:S(2)}) collective-permute-start(f32[192,384]{1,0:T(8,128)S(1)} %get-tuple-element.88.refs_0_.refs_7_), channel_id=1, source_target_pairs={{0,2},{1,3},{2,0},{3,1},{4,6},{5,7},{6,4},{7,5},{8,10},{9,11},{10,... | collective-permute-start | bytes 884744 | tf_op jit(solution)/shard_map/ppermute | solution.py:577
  64.1 8.4 %collective-permute-start.7 = (f32[192,384]{1,0:T(8,128)S(1)}, f32[192,384]{1,0:T(8,128)S(1)}, u32[]{:S(2)}, u32[]{:S(2)}) collective-permute-start(f32[192,384]{1,0:T(8,128)S(1)} %get-tuple-element.88.refs_0_.refs_7_), channel_id=1, source_target_pairs={{0,3},{1,0},{2,1},{3,2},{4,7},{5,4},{6,5},{7,6},{8,11},{9,8},{10,9... | collective-permute-start | bytes 884744 | tf_op jit(solution)/shard_map/ppermute | solution.py:577
  66.6 8.2 %collective-permute-start.5 = (f32[192,384]{1,0:T(8,128)S(1)}, f32[192,384]{1,0:T(8,128)S(1)}, u32[]{:S(2)}, u32[]{:S(2)}) collective-permute-start(f32[192,384]{1,0:T(8,128)S(1)} %get-tuple-element.88.refs_0_.refs_7_), channel_id=1, source_target_pairs={{0,1},{1,2},{2,3},{3,0},{4,5},{5,6},{6,7},{7,4},{8,9},{9,10},{10,1... | collective-permute-start | bytes 884744 | tf_op jit(solution)/shard_map/ppermute | solution.py:577
  66.6 8.2 %collective-permute-start.8 = (f32[192,384]{1,0:T(8,128)S(1)}, f32[192,384]{1,0:T(8,128)S(1)}, u32[]{:S(2)}, u32[]{:S(2)}) collective-permute-start(f32[192,384]{1,0:T(8,128)S(1)} %get-tuple-element.88.refs_0_.refs_7_), channel_id=1, source_target_pairs={{0,16},{16,0},{32,48},{48,32},{64,80},{80,64},{96,112},{112,96},{1... | collective-permute-start | bytes 884744 | tf_op jit(solution)/shard_map/ppermute | solution.py:578
  71.6 3.1 %collective-permute-start.10 = (f32[192,384]{1,0:T(8,128)S(1)}, f32[192,384]{1,0:T(8,128)S(1)}, u32[]{:S(2)}, u32[]{:S(2)}) collective-permute-start(f32[192,384]{1,0:T(8,128)S(1)} %collective-permute-done.6.refs_2_), channel_id=1, source_target_pairs={{0,16},{16,0},{32,48},{48,32},{64,80},{80,64},{96,112},{112,96},{1... | collective-permute-start | bytes 884744 | tf_op jit(solution)/shard_map/ppermute | solution.py:578
  72.5 2.2 %collective-permute-start.11 = (f32[192,384]{1,0:T(8,128)S(1)}, f32[192,384]{1,0:T(8,128)S(1)}, u32[]{:S(2)}, u32[]{:S(2)}) collective-permute-start(f32[192,384]{1,0:T(8,128)S(1)} %collective-permute-done.7.refs_3_), channel_id=1, source_target_pairs={{0,16},{16,0},{32,48},{48,32},{64,80},{80,64},{96,112},{112,96},{1... | collective-permute-start | bytes 884744 | tf_op jit(solution)/shard_map/ppermute | solution.py:578
  74.7 1.6 %collective-permute-start.9 = (f32[192,384]{1,0:T(8,128)S(1)}, f32[192,384]{1,0:T(8,128)S(1)}, u32[]{:S(2)}, u32[]{:S(2)}) collective-permute-start(f32[192,384]{1,0:T(8,128)S(1)} %collective-permute-done.5.refs_1_), channel_id=1, source_target_pairs={{0,16},{16,0},{32,48},{48,32},{64,80},{80,64},{96,112},{112,96},{1... | collective-permute-start | bytes 884744 | tf_op jit(solution)/shard_map/ppermute | solution.py:578
  125.9 5.0 %collective-permute-start.12 = (f32[24,128]{1,0:T(8,128)S(1)}, f32[24,128]{1,0:T(8,128)S(1)}, u32[]{:S(2)}, u32[]{:S(2)}) collective-permute-start(f32[24,128]{1,0:T(8,128)S(1)} %get-tuple-element.102.refs_3_), channel_id=1, source_target_pairs={{0,4},{1,5},{2,6},{3,7},{4,8},{5,9},{6,10},{7,11},{8,12},{9,13},{1... | collective-permute-start | bytes 36872 | tf_op jit(solution)/shard_map/ppermute | solution.py:602
  126.4 5.2 %collective-permute-start.13 = (f32[24,128]{1,0:T(8,128)S(1)}, f32[24,128]{1,0:T(8,128)S(1)}, u32[]{:S(2)}, u32[]{:S(2)}) collective-permute-start(f32[24,128]{1,0:T(8,128)S(1)} %get-tuple-element.102.refs_3_), channel_id=1, source_target_pairs={{0,8},{1,9},{2,10},{3,11},{4,12},{5,13},{6,14},{7,15},{8,0},{9,1},... | collective-permute-start | bytes 36872 | tf_op jit(solution)/shard_map/ppermute | solution.py:602
  129.1 3.7 %collective-permute-start.14 = (f32[24,128]{1,0:T(8,128)S(1)}, f32[24,128]{1,0:T(8,128)S(1)}, u32[]{:S(2)}, u32[]{:S(2)}) collective-permute-start(f32[24,128]{1,0:T(8,128)S(1)} %get-tuple-element.102.refs_3_), channel_id=1, source_target_pairs={{0,12},{1,13},{2,14},{3,15},{4,0},{5,1},{6,2},{7,3},{8,4},{9,5},{1... | collective-permute-start | bytes 36872 | tf_op jit(solution)/shard_map/ppermute | solution.py:602

commit v12 on v11

--- a/solution.py
+++ b/solution.py
@@ -266,7 +266,7 @@
     turns_ref[0] = (most + SLOTS - 1) // SLOTS
 
 
-def arrange_kernel(*refs):
+def arrange(refs):
     own = refs[:WAYS]
     other = refs[WAYS : 2 * WAYS]
     outs = refs[2 * WAYS :]
@@ -337,12 +337,17 @@
     refs = list(refs)
     recv_ref = refs.pop(0) if pair else None
     saved = [refs.pop(0) for _ in range(pair)] if last else []
-    even = [refs.pop(0) for _ in range(2)]
-    odd = None if last else [refs.pop(0) for _ in range(2)]
     prod_ref = refs.pop()
     if pair:
+        even = [refs.pop(0) for _ in range(2)]
+        odd = None if last else [refs.pop(0) for _ in range(2)]
         sum_ref = refs.pop()
         sum_ref[...] = jnp.sum(recv_ref[0 : recv_ref.shape[0] // 2], axis=0)
+    else:
+        cores = refs[2 * WAYS : 2 * WAYS + 4]
+        arrange(refs[: 2 * WAYS + 4])
+        even, odd = cores[:2], cores[2:]
+        refs = refs[2 * WAYS + 4 :]
     kept_ref = refs.pop()
     live = lax.axis_index("cores") // 2 == pair
 
@@ -365,71 +370,78 @@
             refs[0][...] = jnp.zeros(refs[0].shape, F32)
 
 
-def final_kernel(*refs):
-    pairs = MODES // 2 - 1
-    sums = refs[:pairs]
-    parts = refs[pairs : pairs + WAYS]
-    own_ref, out_ref, prod_ref, block_ref = refs[pairs + WAYS :]
+def factored(packed, absent):
+    row = iota((R, 128), 0)
+    lane = iota((R, 128), 1)
+    eye = jnp.where(lane == row, 1.0, 0.0)
+    full = whole(packed) + eye * absent + jnp.where(lane == row + 64, 1.0, 0.0)
+    m = [full[8 * t : 8 * t + 8] for t in range(R // 8)]
+    for begin in range(0, R, 4):
+        top = begin // 8
+        below = range(top, R // 8)
+        col = [
+            {t: jnp.broadcast_to(m[t][:, begin + k : begin + k + 1], (8, 128)) for t in below} for k in range(4)
+        ]
+        for k in range(4):
+            at = begin + k - 8 * top
+            scale = 1.0 / col[k][top][at : at + 1]
+            fact = {t: col[k][t] * scale for t in below}
+            fact[top] = jnp.where(iota((8, 128), 0) > at, fact[top], 0.0)
+            pivot = m[top][at : at + 1]
+            for q in range(k + 1, 4):
+                lead = col[q][top][at : at + 1]
+                for t in below:
+                    col[q][t] = col[q][t] - fact[t] * lead
+            for t in below:
+                m[t] = m[t] - fact[t] * pivot
+    m = jnp.concatenate(m, axis=0)
+    diag = jnp.sum(jnp.where(lane == row, m, 0.0), axis=1, keepdims=True)
+    return m * (1.0 / jnp.sqrt(diag))
+
+
+def from_left(tri, in_ref, out_ref):
+    for g in range(GROUPS):
+        rows = slice(g * R, (g + 1) * R)
+        out_ref[rows, :] = jnp.dot(
+            tri[:, :R], in_ref[rows, :], preferred_element_type=F32, precision=HIGH
+        )
+
+
+def from_right(tri, in_ref, out_ref, block_ref):
+    inv = jnp.where(iota((R, 128), 1) < R, pltpu.roll(tri, 64, 1), 0.0)
+    wide = jnp.concatenate([inv, jnp.zeros((R, LANES - 128), F32)], axis=1)
+    for h in range(WIDE):
+        block_ref[h * R : (h + 1) * R, :] = pltpu.roll(wide, h * R, 1) if h else wide
+    out_ref[...] = dot_lanes(in_ref[...], block_ref[...], HIGH)
+
+
+def applied(tri, left, in_ref, out_ref, block_ref):
+    @pl.when(left)
+    def _():
+        from_left(tri, in_ref, out_ref)
+
+    @pl.when(jnp.logical_not(left))
+    def _():
+        from_right(tri, in_ref, out_ref, block_ref)
+
+
+def known_kernel(*refs):
+    *sums, core_ref, out_ref, block_ref = refs
     mode = lax.axis_index("cores")
     chip = mode // 2
     first = jnp.where(mode % 2 == 0, 1.0, 0.0)
-    second = 1.0 - first
-    level = (parts[0][...] + parts[1][...]) + (parts[2][...] + parts[3][...])
-    own = level * first
-    prev = level * second
-    for p in range(pairs):
-        own = own + sums[p][...] * jnp.where(chip == p, second, 0.0)
-        prev = prev + sums[p][...] * jnp.where(chip == p + 1, first, 0.0)
-    row = iota((R, 128), 0)
-    lane = iota((R, 128), 1)
-    eye = jnp.where(lane == row, 1.0, 0.0)
-    side = jnp.where(lane == row + 64, 1.0, 0.0)
-
-    def start(packed, absent):
-        return whole(packed) + eye * absent + side
-
-    mats = [
-        start(own, jnp.where(mode == MODES - 1, 1.0, 0.0)),
-        start(prev, jnp.where(mode == 0, 1.0, 0.0)),
-    ]
-    mats = [[m[8 * t : 8 * t + 8] for t in range(R // 8)] for m in mats]
-    for start_ in range(0, R, 4):
-        top = start_ // 8
-        below = range(top, R // 8)
-        cols = [
-            [{t: jnp.broadcast_to(m[t][:, start_ + k : start_ + k + 1], (8, 128)) for t in below} for k in range(4)]
-            for m in mats
-        ]
-        for k in range(4):
-            at = start_ + k - 8 * top
-            for w in range(2):
-                m, col = mats[w], cols[w]
-                scale = 1.0 / col[k][top][at : at + 1]
-                fact = {t: col[k][t] * scale for t in below}
-                fact[top] = jnp.where(iota((8, 128), 0) > at, fact[top], 0.0)
-                pivot = m[top][at : at + 1]
-                for q in range(k + 1, 4):
-                    lead = col[q][top][at : at + 1]
-                    for t in below:
-                        col[q][t] = col[q][t] - fact[t] * lead
-                for t in below:
-                    m[t] = m[t] - fact[t] * pivot
-    mats = [jnp.concatenate(m, axis=0) for m in mats]
-    tri = []
-    for w in range(2):
-        diag = jnp.sum(jnp.where(lane == row, mats[w], 0.0), axis=1, keepdims=True)
-        tri.append(mats[w] * (1.0 / jnp.sqrt(diag)))
-    carry = tri[1][:, :R]
-    inv = jnp.where(lane >= 64, tri[0], 0.0)
-    turned = pltpu.roll(inv, 64, 1)
-    wide = jnp.concatenate([jnp.where(lane < R, turned, 0.0), jnp.zeros((R, LANES - 128), F32)], axis=1)
-    for h in range(WIDE):
-        block_ref[h * R : (h + 1) * R, :] = pltpu.roll(wide, h * R, 1) if h else wide
-    for g in range(GROUPS):
-        prod_ref[g * R : (g + 1) * R, :] = jnp.dot(
-            carry, own_ref[g * R : (g + 1) * R, :], preferred_element_type=F32, precision=HIGH
-        )
-    out_ref[...] = dot_lanes(prod_ref[...], block_ref[...], HIGH)
+    known = jnp.zeros((24, 128), F32)
+    for p, s in enumerate(sums):
+        known = known + s[...] * jnp.where(chip == p, 1.0 - first, 0.0)
+        known = known + s[...] * jnp.where(chip == p + 1, first, 0.0)
+    absent = jnp.where(jnp.logical_or(mode == 0, mode == MODES - 1), 1.0, 0.0)
+    applied(factored(known, absent), mode % 2 == 0, core_ref, out_ref, block_ref)
+
+
+def final_kernel(a_ref, b_ref, c_ref, d_ref, core_ref, out_ref, block_ref):
+    level = (a_ref[...] + b_ref[...]) + (c_ref[...] + d_ref[...])
+    odd = lax.axis_index("cores") % 2 == 1
+    applied(factored(level, 0.0), odd, core_ref, out_ref, block_ref)
 
 
 def vmem():
@@ -578,17 +590,18 @@
     other = [lax.ppermute(o, "cores", siblings) for o in own]
     stack = shape(3 * WAYS * ROWS, LANES, dtype=BF16)
     flat = shape(LANES, 3 * WAYS * ROWS, dtype=BF16)
-    arranged = call(arrange_kernel, [stack, flat] * 2, [vmem()] * 8, name="arrange")(*own, *other)
-    even, odd = list(arranged[:2]), list(arranged[2:])
 
     saved, sums = [], []
     recv = None
     for pair in range(MODES // 2):
         last = pair == MODES // 2 - 1
-        ins = ([recv] if pair else []) + (saved if last else []) + even + ([] if last else odd)
         outs = [shape(24, 128)] if last else [shape(2 * peers, 24, 128), shape(24, 128)]
         if pair:
+            ins = [recv] + (saved + even if last else even + odd)
             outs.append(shape(24, 128))
+        else:
+            ins = own + other
+            outs = [stack, flat] * 2 + outs
         res = call(
             functools.partial(pair_kernel, pair=pair),
             outs,
@@ -598,6 +611,8 @@
         )(*ins)
         if pair:
             sums.append(res[-1])
+        else:
+            even, odd, res = list(res[:2]), list(res[2:4]), res[4:]
         if last:
             parts = [res[0]] + [lax.ppermute(res[0], "samp", pairs) for pairs in level]
         else:
@@ -611,13 +626,9 @@
                 res[0], ("cores", "samp"), 0, 0, axis_index_groups=groups, tiled=True
             )
 
-    out = call(
-        final_kernel,
-        shape(ROWS, LANES),
-        [vmem()] * (MODES // 2 - 1 + WAYS + 1),
-        [pltpu.VMEM((ROWS, LANES), F32), pltpu.VMEM((LANES, LANES), F32)],
-        name="final",
-    )(*sums, *parts, updated)
+    block = [pltpu.VMEM((LANES, LANES), F32)]
+    ahead = call(known_kernel, shape(ROWS, LANES), [vmem()] * (MODES // 2), block, name="known")(*sums, updated)
+    out = call(final_kernel, shape(ROWS, LANES), [vmem()] * (WAYS + 1), block, name="final")(*parts, ahead)
     out = out.reshape(GROUPS, R, WIDE, R).transpose(0, 2, 1, 3)
     return out.reshape(1, slab, RR)
 

time: 139 us -> 139 us (level)
  waiting for transfers between devices: 40.8 us -> 38.3 us
  Pallas kernels: 26.4 us -> 28.5 us
    ppermute x3, waiting for transfers between devices: 2.57 us -> 0.11 us  [on_device(): parts = [res[0]] + [lax.ppermute(res[0], 'samp', pairs) for pairs in level]]
    pallas_call x4, Pallas kernels: 3.05 us -> 4.45 us  [on_device(): call(functools.partial(pair_kernel, pair=pair), outs, [vmem()] * len(ins)...]
  transfers between devices with their start and end apart: 16 -> 16, of which waited for: 13 -> 11; matrix products, arithmetic and copies ran while one was open for 1% -> 1% of each run, Pallas kernels for 4% -> 6%
where the time goes in v12:
time: 139 us; the launch traced here: 137 us
  blocking collectives  45.2 us (33%)
  waiting for transfers between devices  38.3 us (28%)
  Pallas kernels  28.5 us (21%)
  starting transfers between devices  20.2 us (15%)
  local copies, waits for them, and re-layouts  3.45 us (2%)
    all_to_all x3, blocking collectives, on_device(): lax.all_to_all(res[0], ('cores', 'samp'), 0, 0, axis_index_groups=groups,...  45.2 us
    all_to_all x1, waiting for transfers between devices, exchanged(): return lax.all_to_all(block, 'samp', 0, 0, tiled=True)  12.8 us
    ppermute x3, waiting for transfers between devices, on_device(): recv.append(lax.ppermute(out, 'cores', pairs))  12.4 us
    ppermute x3, waiting for transfers between devices, on_device(): lax.ppermute(updated, ('cores', 'samp'), pairs)  8.15 us
    all_to_all x1, starting transfers between devices, exchanged(): return lax.all_to_all(block, 'samp', 0, 0, tiled=True)  7.87 us
    pallas_call x1, Pallas kernels, on_device(): pl.pallas_call(functools.partial(gather_kernel, peers=peers), grid=(steps...  5.34 us
    ppermute x3, starting transfers between devices, on_device(): recv.append(lax.ppermute(out, 'cores', pairs))  4.62 us
    pallas_call x4, Pallas kernels, on_device(): call(functools.partial(pair_kernel, pair=pair), outs, [vmem()] * len(ins)...  4.45 us
  transfers between devices with their start and end apart: 16, of which 11 were waited for; matrix products, arithmetic and copies ran while one was open for 1% of the time, Pallas kernels for 6%

profile of v12, /device:TPU:16, one launch (start us, length us, event | category | flops | bytes accessed | tf_op | source)
XLA Modules:
  0.0 137.4 jit_solution(2274905782423706590)
XLA Ops:
  0.0 5.3 %gather.1 = (f32[4608,512]{1,0:T(8,128)S(1)}, s32[8,1024]{1,0:T(8,128)S(1)}, f32[8,128]{1,0:T(8,128)S(1)}) custom-call(s32[8,1024]{1,0:T(8,128)} %bitcast.21, f32[512,2304]{1,0:T(8,128)} %bitcast.18), custom_call_target="tpu_custom_call" | custom-call | tf_op jit(solution)/shard_map/gather/pallas_call | solution.py:490
  5.3 2.8 %collective-permute-done.table_ref = f32[512,2304]{1,0:T(8,128)S(1)} collective-permute-done((f32[512,2304]{1,0:T(8,128)}, f32[512,2304]{1,0:T(8,128)S(1)}, u32[]{:S(2)}, u32[]{:S(2)}) %collective-permute-start) | collective-permute-done | bytes 4718624 | tf_op jit(solution)/shard_map/ppermute | solution.py:481
  8.1 4.2 %gather_other.1.mats_ref = f32[4608,512]{1,0:T(8,128)S(1)} custom-call(s32[8,1024]{1,0:T(8,128)} %bitcast.22, f32[512,2304]{1,0:T(8,128)S(1)} %collective-permute-done.table_ref, f32[4608,512]{1,0:T(8,128)S(1)} %get-tuple-element.73.refs_0_), custom_call_target="tpu_custom_call", output_to_operand_aliasing={{}: (2, {})} | custom-call | tf_op jit(solution)/shard_map/gather_other/pallas_call | solution.py:504
  12.3 1.3 collective-permute-start.1
  13.6 5.8 %collective-permute-done.1.refs_0_ = f32[48,512]{1,0:T(8,128)S(1)} collective-permute-done((f32[48,512]{1,0:T(8,128)S(1)}, f32[48,512]{1,0:T(8,128)S(1)}, u32[]{:S(2)}, u32[]{:S(2)}) %collective-permute-start.1) | collective-permute-done | bytes 98336 | tf_op jit(solution)/shard_map/ppermute | solution.py:532
  19.4 1.4 %hop1.1 = (f32[48,512]{1,0:T(8,128)S(1)}, f32[48,512]{1,0:T(8,128)S(1)}) custom-call(f32[4608,512]{1,0:T(8,128)S(1)} %gather_other.1.mats_ref, f32[48,512]{1,0:T(8,128)S(1)} %collective-permute-done.1.refs_0_), custom_call_target="tpu_custom_call" | custom-call | tf_op jit(solution)/shard_map/hop1/pallas_call | solution.py:524
  20.8 2.0 %collective-permute-start.2 = (f32[48,512]{1,0:T(8,128)S(1)}, f32[48,512]{1,0:T(8,128)S(1)}, u32[]{:S(2)}, u32[]{:S(2)}) collective-permute-start(f32[48,512]{1,0:T(8,128)S(1)} %get-tuple-element.75), channel_id=1, source_target_pairs={{32,64},{48,80},{64,32},{80,48},{33,65},{49,81},{65,33},{81,49},{3... | collective-permute-start | bytes 294920 | tf_op jit(solution)/shard_map/ppermute | solution.py:532
  22.9 4.5 %collective-permute-done.2.refs_0_.refs_1_ = f32[48,512]{1,0:T(8,128)S(1)} collective-permute-done((f32[48,512]{1,0:T(8,128)S(1)}, f32[48,512]{1,0:T(8,128)S(1)}, u32[]{:S(2)}, u32[]{:S(2)}) %collective-permute-start.2) | collective-permute-done | bytes 98336 | tf_op jit(solution)/shard_map/ppermute | solution.py:532
  27.3 1.4 %hop2.1 = (f32[48,512]{1,0:T(8,128)S(1)}, f32[48,512]{1,0:T(8,128)S(1)}) custom-call(f32[4608,512]{1,0:T(8,128)S(1)} %gather_other.1.mats_ref, f32[48,512]{1,0:T(8,128)S(1)} %collective-permute-done.2.refs_0_.refs_1_), custom_call_target="tpu_custom_call" | custom-call | tf_op jit(solution)/shard_map/hop2/pallas_call | solution.py:524
  28.8 1.3 collective-permute-start.3
  30.1 2.2 %collective-permute-done.3.refs_2_ = f32[48,512]{1,0:T(8,128)S(1)} collective-permute-done((f32[48,512]{1,0:T(8,128)S(1)}, f32[48,512]{1,0:T(8,128)S(1)}, u32[]{:S(2)}, u32[]{:S(2)}) %collective-permute-start.3) | collective-permute-done | bytes 98336 | tf_op jit(solution)/shard_map/ppermute | solution.py:532
  32.3 1.5 %finish.1 = (f32[96,512]{1,0:T(8,128)S(1)}, f32[96,512]{1,0:T(8,128)S(1)}) custom-call(f32[4608,512]{1,0:T(8,128)S(1)} %gather_other.1.mats_ref, f32[48,512]{1,0:T(8,128)S(1)} %collective-permute-done.1.refs_0_, f32[48,512]{1,0:T(8,128)S(1)} %collective-permute-done.2.refs_0_.refs_1_, f32[48,512]{1,0:T(8,128)S(1)} %collective-permute-done.3.refs_2_, ...), custom_call_target="tpu_custom_call" | custom-call | tf_op jit(solution)/shard_map/finish/pallas_call | solution.py:534
  35.3 1.8 %route.1 = (f32[16,104,128]{2,1,0:T(8,128)}, f32[104,1024]{1,0:T(8,128)S(1)}) custom-call(f32[96,512]{1,0:T(8,128)S(1)} %get-tuple-element.80.vecs_ref.own_ref, f32[96,512]{1,0:T(8,128)S(1)} %collective-permute-done.4.got_ref, s32[8,1024]{1,0:T(8,128)S(1)} %get-tuple-element.167.slot_ref, f32[8,128]{1,0:T(8,128)S(1)} %get-tuple-element.168.most_ref, ...), custom_call_target="tpu_custom_call" | custom-call | tf_op jit(solution)/shard_map/route/pallas_call | solution.py:543
  37.1 7.9 %all-to-all-start.1 = ((f32[16,104,128]{2,1,0:T(8,128)}), f32[16,104,128]{2,1,0:T(8,128)S(1)}, u32[]{:S(2)}, u32[]{:S(2)}) async-start(f32[16,104,128]{2,1,0:T(8,128)} %get-tuple-element.84), calls=%async_computation.1 | async-start | bytes 1703936 | tf_op jit(solution)/shard_map/all_to_all | solution.py:551
  45.0 1.0 constant_dynamic-slice_fusion
  47.6 12.8 %all-to-all-done.1.recv_ref = f32[16,104,128]{2,1,0:T(8,128)S(1)} async-done(((f32[16,104,128]{2,1,0:T(8,128)}), f32[16,104,128]{2,1,0:T(8,128)S(1)}, u32[]{:S(2)}, u32[]{:S(2)}) %all-to-all-start.1) | async-done | bytes 852000 | tf_op jit(solution)/shard_map/all_to_all | solution.py:551
  60.4 2.1 %collect.2 = (f32[192,384]{1,0:T(8,128)S(1)}, s32[1]{0:T(128)}) custom-call(f32[1]{0:T(128)} %bitcast.15.step_ref, f32[16,104,128]{2,1,0:T(8,128)S(1)} %all-to-all-done.1.recv_ref, f32[192,384]{1,0:T(8,128)S(1)} %reshape.26.base_ref), custom_call_target="tpu_custom_call" | custom-call | tf_op jit(solution)/shard_map/collect/pallas_call | solution.py:554
  64.2 2.5 %collective-permute-start.7 = (f32[192,384]{1,0:T(8,128)S(1)}, f32[192,384]{1,0:T(8,128)S(1)}, u32[]{:S(2)}, u32[]{:S(2)}) collective-permute-start(f32[192,384]{1,0:T(8,128)S(1)} %get-tuple-element.88.refs_0_.refs_3_), channel_id=1, source_target_pairs={{0,3},{1,0},{2,1},{3,2},{4,7},{5,4},{6,5},{7,6},{8,11},{9,8},{10,9... | collective-permute-start | bytes 884744 | tf_op jit(solution)/shard_map/ppermute | solution.py:589
  66.7 5.0 %collective-permute-done.6.refs_2_ = f32[192,384]{1,0:T(8,128)S(1)} collective-permute-done((f32[192,384]{1,0:T(8,128)S(1)}, f32[192,384]{1,0:T(8,128)S(1)}, u32[]{:S(2)}, u32[]{:S(2)}) %collective-permute-start.6) | collective-permute-done | bytes 294944 | tf_op jit(solution)/shard_map/ppermute | solution.py:589
  71.7 0.9 collective-permute-done.7.refs_3_
  72.6 2.2 %collective-permute-done.5.refs_1_ = f32[192,384]{1,0:T(8,128)S(1)} collective-permute-done((f32[192,384]{1,0:T(8,128)S(1)}, f32[192,384]{1,0:T(8,128)S(1)}, u32[]{:S(2)}, u32[]{:S(2)}) %collective-permute-start.5) | collective-permute-done | bytes 294944 | tf_op jit(solution)/shard_map/ppermute | solution.py:589
  74.8 1.6 %collective-permute-done.9.refs_5_ = f32[192,384]{1,0:T(8,128)S(1)} collective-permute-done((f32[192,384]{1,0:T(8,128)S(1)}, f32[192,384]{1,0:T(8,128)S(1)}, u32[]{:S(2)}, u32[]{:S(2)}) %collective-permute-start.9) | collective-permute-done | bytes 294944 | tf_op jit(solution)/shard_map/ppermute | solution.py:590
  76.4 1.4 %pair0.1 = (bf16[2304,384]{1,0:T(8,128)(2,1)S(1)}, bf16[384,2304]{1,0:T(8,128)(2,1)S(1)}, bf16[2304,384]{1,0:T(8,128)(2,1)S(1)}, bf16[384,2304]{1,0:T(8,128)(2,1...) custom-call(f32[192,384]{1,0:T(8,128)S(1)} %get-tuple-element.88.refs_0_.refs_3_, ...), custom_call_target="tpu_custom_call" | custom-call | tf_op jit(solution)/shard_map/pair0/pallas_call | solution.py:605
  77.9 15.6 %all_to_all.26.refs_0_ = f32[32,24,128]{2,1,0:T(8,128)S(1)} all-to-all(f32[32,24,128]{2,1,0:T(8,128)S(1)} %get-tuple-element.89), channel_id=1, replica_groups={{0,1,2,3,4,5,6,7,8,9,10,11,12,13,14,15,32,33,34,35,36,37,38,39,40,41,42..., dimensions={0} | all-to-all | bytes 786432 | tf_op jit(solution)/shard_map/all_to_all | solution.py:625
  93.5 16.7 %all_to_all.27.refs_0_ = f32[32,24,128]{2,1,0:T(8,128)S(1)} all-to-all(f32[32,24,128]{2,1,0:T(8,128)S(1)} %get-tuple-element.94), channel_id=1, replica_groups={{32,33,34,35,36,37,38,39,40,41,42,43,44,45,46,47,64,65,66,67,68,69,70,7..., dimensions={0} | all-to-all | bytes 786432 | tf_op jit(solution)/shard_map/all_to_all | solution.py:625
  110.1 2.9 %pair2.1 = (f32[32,24,128]{2,1,0:T(8,128)S(1)}, f32[24,128]{1,0:T(8,128)S(1)}, f32[24,128]{1,0:T(8,128)S(1)}) custom-call(f32[32,24,128]{2,1,0:T(8,128)S(1)} %all_to_all.27.refs_0_, bf16[2304,384]{1,0:T(8,128)(2,1)S(1)} %get-tuple-element.90.refs_1_.refs_4_, bf16[384,2304]{1,0:T(8,128)(2,1)S(1)} %get-tuple-element.91.refs_2_.refs_5_, ...), custom_call_target="tpu_custom_call" | custom-call | tf_op jit(solution)/shard_map/pair2/pallas_call | solution.py:605
  113.1 12.9 %all_to_all.28.refs_0_ = f32[32,24,128]{2,1,0:T(8,128)S(1)} all-to-all(f32[32,24,128]{2,1,0:T(8,128)S(1)} %get-tuple-element.95), channel_id=1, replica_groups={{64,65,66,67,68,69,70,71,72,73,74,75,76,77,78,79,96,97,98,99,100,101,10..., dimensions={0} | all-to-all | bytes 786432 | tf_op jit(solution)/shard_map/all_to_all | solution.py:625
  126.6 2.6 %collective-permute-start.13 = (f32[24,128]{1,0:T(8,128)S(1)}, f32[24,128]{1,0:T(8,128)S(1)}, u32[]{:S(2)}, u32[]{:S(2)}) collective-permute-start(f32[24,128]{1,0:T(8,128)S(1)} %get-tuple-element.99.a_ref), channel_id=1, source_target_pairs={{0,8},{1,9},{2,10},{3,11},{4,12},{5,13},{6,14},{7,15},{8,0},{9,1},... | collective-permute-start | bytes 36872 | tf_op jit(solution)/shard_map/ppermute | solution.py:617
  129.2 1.1 collective-permute-start.14
  130.3 2.4 %known.1.core_ref = f32[192,384]{1,0:T(8,128)S(1)} custom-call(f32[24,128]{1,0:T(8,128)S(1)} %get-tuple-element.100.refs_0_, f32[24,128]{1,0:T(8,128)S(1)} %get-tuple-element.101.refs_1_, f32[24,128]{1,0:T(8,128)S(1)} %get-tuple-element.102.refs_2_, f32[192,384]{1,0:T(8,128)S(1)} %get-tuple-element.88.refs_0_.refs_3_), custom_call_target="tpu_custom_call" | custom-call | tf_op jit(solution)/shard_map/known/pallas_call | solution.py:630
  132.9 3.0 %final.1 = f32[192,384]{1,0:T(8,128)S(1)} custom-call(f32[24,128]{1,0:T(8,128)S(1)} %get-tuple-element.99.a_ref, f32[24,128]{1,0:T(8,128)S(1)} %collective-permute-done.12.b_ref, f32[24,128]{1,0:T(8,128)S(1)} %collective-permute-done.13.c_ref, f32[24,128]{1,0:T(8,128)S(1)} %collective-permute-done.14.d_ref, f32[192,384]{1,0:T(8,128)S(1)} %known.1.core_ref), custom_call_target="tpu_custom_call" | custom-call | tf_op jit(solution)/shard_map/final/pallas_call | solution.py:631
  136.3 1.0 reshape.28
  (28 shorter events, 5.4 us)
Async XLA Ops:
  0.0 8.1 %collective-permute-start = (f32[512,2304]{1,0:T(8,128)}, f32[512,2304]{1,0:T(8,128)S(1)}, u32[]{:S(2)}, u32[]{:S(2)}) collective-permute-start(f32[512,2304]{1,0:T(8,128)} %bitcast.17), channel_id=1, source_target_pairs={{0,16},{16,0},{32,48},{48,32},{64,80},{80,64},{96,112},{112,96},{1... | collective-permute-start | bytes 14155784 | tf_op jit(solution)/shard_map/ppermute | solution.py:481
  12.3 7.1 %collective-permute-start.1 = (f32[48,512]{1,0:T(8,128)S(1)}, f32[48,512]{1,0:T(8,128)S(1)}, u32[]{:S(2)}, u32[]{:S(2)}) collective-permute-start(f32[48,512]{1,0:T(8,128)S(1)} %get-tuple-element.74), channel_id=1, source_target_pairs={{0,32},{16,48},{96,64},{112,80},{1,33},{17,49},{97,65},{113,81},{2... | collective-permute-start | bytes 294920 | tf_op jit(solution)/shard_map/ppermute | solution.py:532
  20.8 11.4 %copy-start = (f32[1024]{0:T(1024)S(1)}, f32[1024]{0:T(1024)}, u32[]{:S(2)}) copy-start(f32[1024]{0:T(1024)} %param.8) | copy-start | bytes 12292
  20.8 6.5 %collective-permute-start.2 = (f32[48,512]{1,0:T(8,128)S(1)}, f32[48,512]{1,0:T(8,128)S(1)}, u32[]{:S(2)}, u32[]{:S(2)}) collective-permute-start(f32[48,512]{1,0:T(8,128)S(1)} %get-tuple-element.75), channel_id=1, source_target_pairs={{32,64},{48,80},{64,32},{80,48},{33,65},{49,81},{65,33},{81,49},{3... | collective-permute-start | bytes 294920 | tf_op jit(solution)/shard_map/ppermute | solution.py:532
  28.8 3.5 %collective-permute-start.3 = (f32[48,512]{1,0:T(8,128)S(1)}, f32[48,512]{1,0:T(8,128)S(1)}, u32[]{:S(2)}, u32[]{:S(2)}) collective-permute-start(f32[48,512]{1,0:T(8,128)S(1)} %get-tuple-element.76.refs_6_), channel_id=1, source_target_pairs={{64,96},{80,112},{32,0},{48,16},{65,97},{81,113},{33,1},{49,17},{6... | collective-permute-start | bytes 294920 | tf_op jit(solution)/shard_map/ppermute | solution.py:532
  33.8 1.5 %collective-permute-start.4 = (f32[96,512]{1,0:T(8,128)S(1)}, f32[96,512]{1,0:T(8,128)S(1)}, u32[]{:S(2)}, u32[]{:S(2)}) collective-permute-start(f32[96,512]{1,0:T(8,128)S(1)} %get-tuple-element.81), channel_id=1, source_target_pairs={{0,16},{16,0},{32,48},{48,32},{64,80},{80,64},{96,112},{112,96},{1... | collective-permute-start | bytes 589832 | tf_op jit(solution)/shard_map/ppermute | solution.py:541
  37.1 23.3 %all-to-all-start.1 = ((f32[16,104,128]{2,1,0:T(8,128)}), f32[16,104,128]{2,1,0:T(8,128)S(1)}, u32[]{:S(2)}, u32[]{:S(2)}) async-start(f32[16,104,128]{2,1,0:T(8,128)} %get-tuple-element.84), calls=%async_computation.1 | async-start | bytes 1703936 | tf_op jit(solution)/shard_map/all_to_all | solution.py:551
  63.4 8.3 %collective-permute-start.6 = (f32[192,384]{1,0:T(8,128)S(1)}, f32[192,384]{1,0:T(8,128)S(1)}, u32[]{:S(2)}, u32[]{:S(2)}) collective-permute-start(f32[192,384]{1,0:T(8,128)S(1)} %get-tuple-element.88.refs_0_.refs_3_), channel_id=1, source_target_pairs={{0,2},{1,3},{2,0},{3,1},{4,6},{5,7},{6,4},{7,5},{8,10},{9,11},{10,... | collective-permute-start | bytes 884744 | tf_op jit(solution)/shard_map/ppermute | solution.py:589
  64.2 8.4 %collective-permute-start.7 = (f32[192,384]{1,0:T(8,128)S(1)}, f32[192,384]{1,0:T(8,128)S(1)}, u32[]{:S(2)}, u32[]{:S(2)}) collective-permute-start(f32[192,384]{1,0:T(8,128)S(1)} %get-tuple-element.88.refs_0_.refs_3_), channel_id=1, source_target_pairs={{0,3},{1,0},{2,1},{3,2},{4,7},{5,4},{6,5},{7,6},{8,11},{9,8},{10,9... | collective-permute-start | bytes 884744 | tf_op jit(solution)/shard_map/ppermute | solution.py:589
  66.7 8.2 %collective-permute-start.5 = (f32[192,384]{1,0:T(8,128)S(1)}, f32[192,384]{1,0:T(8,128)S(1)}, u32[]{:S(2)}, u32[]{:S(2)}) collective-permute-start(f32[192,384]{1,0:T(8,128)S(1)} %get-tuple-element.88.refs_0_.refs_3_), channel_id=1, source_target_pairs={{0,1},{1,2},{2,3},{3,0},{4,5},{5,6},{6,7},{7,4},{8,9},{9,10},{10,1... | collective-permute-start | bytes 884744 | tf_op jit(solution)/shard_map/ppermute | solution.py:589
  66.7 8.2 %collective-permute-start.8 = (f32[192,384]{1,0:T(8,128)S(1)}, f32[192,384]{1,0:T(8,128)S(1)}, u32[]{:S(2)}, u32[]{:S(2)}) collective-permute-start(f32[192,384]{1,0:T(8,128)S(1)} %get-tuple-element.88.refs_0_.refs_3_), channel_id=1, source_target_pairs={{0,16},{16,0},{32,48},{48,32},{64,80},{80,64},{96,112},{112,96},{1... | collective-permute-start | bytes 884744 | tf_op jit(solution)/shard_map/ppermute | solution.py:590
  71.7 3.1 %collective-permute-start.10 = (f32[192,384]{1,0:T(8,128)S(1)}, f32[192,384]{1,0:T(8,128)S(1)}, u32[]{:S(2)}, u32[]{:S(2)}) collective-permute-start(f32[192,384]{1,0:T(8,128)S(1)} %collective-permute-done.6.refs_2_), channel_id=1, source_target_pairs={{0,16},{16,0},{32,48},{48,32},{64,80},{80,64},{96,112},{112,96},{1... | collective-permute-start | bytes 884744 | tf_op jit(solution)/shard_map/ppermute | solution.py:590
  72.6 2.2 %collective-permute-start.11 = (f32[192,384]{1,0:T(8,128)S(1)}, f32[192,384]{1,0:T(8,128)S(1)}, u32[]{:S(2)}, u32[]{:S(2)}) collective-permute-start(f32[192,384]{1,0:T(8,128)S(1)} %collective-permute-done.7.refs_3_), channel_id=1, source_target_pairs={{0,16},{16,0},{32,48},{48,32},{64,80},{80,64},{96,112},{112,96},{1... | collective-permute-start | bytes 884744 | tf_op jit(solution)/shard_map/ppermute | solution.py:590
  74.8 1.6 %collective-permute-start.9 = (f32[192,384]{1,0:T(8,128)S(1)}, f32[192,384]{1,0:T(8,128)S(1)}, u32[]{:S(2)}, u32[]{:S(2)}) collective-permute-start(f32[192,384]{1,0:T(8,128)S(1)} %collective-permute-done.5.refs_1_), channel_id=1, source_target_pairs={{0,16},{16,0},{32,48},{48,32},{64,80},{80,64},{96,112},{112,96},{1... | collective-permute-start | bytes 884744 | tf_op jit(solution)/shard_map/ppermute | solution.py:590
  126.0 6.7 %collective-permute-start.12 = (f32[24,128]{1,0:T(8,128)S(1)}, f32[24,128]{1,0:T(8,128)S(1)}, u32[]{:S(2)}, u32[]{:S(2)}) collective-permute-start(f32[24,128]{1,0:T(8,128)S(1)} %get-tuple-element.99.a_ref), channel_id=1, source_target_pairs={{0,4},{1,5},{2,6},{3,7},{4,8},{5,9},{6,10},{7,11},{8,12},{9,13},{1... | collective-permute-start | bytes 36872 | tf_op jit(solution)/shard_map/ppermute | solution.py:617
  126.6 6.2 %collective-permute-start.13 = (f32[24,128]{1,0:T(8,128)S(1)}, f32[24,128]{1,0:T(8,128)S(1)}, u32[]{:S(2)}, u32[]{:S(2)}) collective-permute-start(f32[24,128]{1,0:T(8,128)S(1)} %get-tuple-element.99.a_ref), channel_id=1, source_target_pairs={{0,8},{1,9},{2,10},{3,11},{4,12},{5,13},{6,14},{7,15},{8,0},{9,1},... | collective-permute-start | bytes 36872 | tf_op jit(solution)/shard_map/ppermute | solution.py:617
  129.2 3.7 %collective-permute-start.14 = (f32[24,128]{1,0:T(8,128)S(1)}, f32[24,128]{1,0:T(8,128)S(1)}, u32[]{:S(2)}, u32[]{:S(2)}) collective-permute-start(f32[24,128]{1,0:T(8,128)S(1)} %get-tuple-element.99.a_ref), channel_id=1, source_target_pairs={{0,12},{1,13},{2,14},{3,15},{4,0},{5,1},{6,2},{7,3},{8,4},{9,5},{1... | collective-permute-start | bytes 36872 | tf_op jit(solution)/shard_map/ppermute | solution.py:617

commit v13 on v12

--- a/solution.py
+++ b/solution.py
@@ -68,35 +68,45 @@
     return jnp.where(flag > 0.5, row[:, half:], row[:, :half])
 
 
-def gather_kernel(idx_ref, table_ref, *refs, peers):
-    own = peers is not None
-    mats_ref, *outs, hot_ref = refs if own else refs[1:]
+def one_hot(row, second, hot_ref):
+    hot_ref[...] = (iota(hot_ref.shape, 0) == half_of(row, second)).astype(BF16)
+
+
+def gathered(table, hot):
+    hi, lo = halves(table)
+    return dot_rows(hi, hot) + dot_rows(lo, hot)
+
+
+def gather_kernel(idx_ref, table_ref, mats_ref, slot_ref, most_ref, hot_ref, *, peers):
     step = pl.program_id(0)
     mode = lax.axis_index("cores")
 
     @pl.when(step == 0)
     def _():
-        which = mode if own else mode + 1 - 2 * (mode % 2)
-        row = idx_ref[pl.ds(which, 1), :]
-        half = half_of(row, mode % 2 == 1)
-        hot_ref[...] = (iota(hot_ref.shape, 0) == half).astype(BF16)
-        if own:
-            slot_ref, most_ref = outs
-            slab = N // peers
-            place, dest = ranks(row, peers, slab)
-            slot_ref[0:1, :] = place
-            slot_ref[1:2, :] = dest
-            slot_ref[2:3, :] = row - dest * slab
-            slot_ref[3:8, :] = jnp.zeros((5, row.shape[1]), jnp.int32)
-            every = idx_ref[...] // slab
-            most = jnp.zeros((MODES, 1), F32)
-            for j in range(peers):
-                most = jnp.maximum(most, jnp.sum((every == j).astype(F32), axis=1, keepdims=True))
-            most_ref[...] = jnp.broadcast_to(jnp.max(most, axis=0, keepdims=True), (8, 128))
-
-    hot = hot_ref[...]
-    hi, lo = halves(table_ref[...])
-    mats_ref[...] = dot_rows(hi, hot) + dot_rows(lo, hot)
+        row = idx_ref[pl.ds(mode, 1), :]
+        one_hot(row, mode % 2 == 1, hot_ref)
+        slab = N // peers
+        place, dest = ranks(row, peers, slab)
+        slot_ref[0:1, :] = place
+        slot_ref[1:2, :] = dest
+        slot_ref[2:3, :] = row - dest * slab
+        slot_ref[3:8, :] = jnp.zeros((5, row.shape[1]), jnp.int32)
+        every = idx_ref[...] // slab
+        most = jnp.zeros((MODES, 1), F32)
+        for j in range(peers):
+            most = jnp.maximum(most, jnp.sum((every == j).astype(F32), axis=1, keepdims=True))
+        most_ref[...] = jnp.broadcast_to(jnp.max(most, axis=0, keepdims=True), (8, 128))
+
+    rows = pl.ds(pl.multiple_of(step * COLS, COLS), COLS)
+    mats_ref[rows, :] = gathered(table_ref[...], hot_ref[...])
+
+
+def gather_other_kernel(idx_ref, table_ref, _, mats_ref, hot_ref):
+    mode = lax.axis_index("cores")
+    second = mode % 2
+    one_hot(idx_ref[pl.ds(mode + 1 - 2 * second, 1), :], second == 1, hot_ref)
+    for at in range(0, RR, COLS):
+        mats_ref[RR + at : RR + at + COLS, :] = gathered(table_ref[:, at : at + COLS], hot_ref[...])
 
 
 def times(left, mats_ref, base, vec_ref, out_ref):
@@ -452,13 +462,14 @@
     return pl.BlockSpec(memory_space=pltpu.SMEM)
 
 
-def call(kernel, outs, ins, scratch=(), name=None):
+def call(kernel, outs, ins, scratch=(), name=None, aliases={}):
     return pl.pallas_call(
         kernel,
         out_shape=outs,
         in_specs=ins,
         out_specs=jax.tree.map(lambda o: smem() if o.dtype == jnp.int32 and o.size == 1 else vmem(), outs),
         scratch_shapes=list(scratch),
+        input_output_aliases=aliases,
         compiler_params=pltpu.CompilerParams(vmem_limit_bytes=BIG),
         name=name,
     )
@@ -479,38 +490,22 @@
     half = count // 2
     siblings = [(m, m ^ 1) for m in range(MODES)]
     other_table = lax.ppermute(table, "cores", siblings)
-    steps = RR // COLS
-    params = pltpu.CompilerParams(vmem_limit_bytes=BIG)
-    in_specs = [
-        pl.BlockSpec((MODES, count), lambda i: (0, 0)),
-        pl.BlockSpec((N, COLS), lambda i: (0, i)),
-    ]
     hot = [pltpu.VMEM((N, half), BF16)]
-    idx, table_in = [pltpu.with_memory_space_constraint(a, pltpu.HBM) for a in (idx, table)]
     mats, slot, most = pl.pallas_call(
         functools.partial(gather_kernel, peers=peers),
-        grid=(steps,),
-        in_specs=in_specs,
-        out_specs=[
-            pl.BlockSpec((COLS, half), lambda i: (i, 0)),
-            pl.BlockSpec((8, count), lambda i: (0, 0)),
-            pl.BlockSpec((8, 128), lambda i: (0, 0)),
+        grid=(RR // COLS,),
+        in_specs=[
+            pl.BlockSpec((MODES, count), lambda i: (0, 0)),
+            pl.BlockSpec((N, COLS), lambda i: (0, i)),
         ],
+        out_specs=[vmem(), vmem(), vmem()],
         out_shape=[shape(2 * RR, half), shape(8, count, dtype=jnp.int32), shape(8, 128)],
         scratch_shapes=hot,
-        compiler_params=params,
+        compiler_params=pltpu.CompilerParams(vmem_limit_bytes=BIG),
         name="gather",
-    )(idx, table_in)
-    mats = pl.pallas_call(
-        functools.partial(gather_kernel, peers=None),
-        grid=(steps,),
-        in_specs=in_specs + [pl.BlockSpec(memory_space=pl.ANY)],
-        out_specs=pl.BlockSpec((COLS, half), lambda i: (i + steps, 0)),
-        out_shape=shape(2 * RR, half),
-        scratch_shapes=hot,
-        input_output_aliases={2: 0},
-        compiler_params=params,
-        name="gather_other",
+    )(*[pltpu.with_memory_space_constraint(a, pltpu.HBM) for a in (idx, table)])
+    mats = call(
+        gather_other_kernel, shape(2 * RR, half), [vmem()] * 3, hot, name="gather_other", aliases={2: 0}
     )(idx, other_table, mats)
 
     first = lax.axis_index("samp") * slab

time: 139 us -> 137 us (0.986)
  transfers between devices with their start and end apart: 16 -> 16, of which waited for: 11 -> 11; matrix products, arithmetic and copies ran while one was open for 1% -> 1% of each run, Pallas kernels for 6% -> 7%
where the time goes in v13:
time: 137 us; the launch traced here: 136 us
  blocking collectives  45.1 us (33%)
  waiting for transfers between devices  38.1 us (28%)
  Pallas kernels  27.3 us (20%)
  starting transfers between devices  20.2 us (15%)
  local copies, waits for them, and re-layouts  3.46 us (3%)
    all_to_all x3, blocking collectives, on_device(): lax.all_to_all(res[0], ('cores', 'samp'), 0, 0, axis_index_groups=groups,...  45.1 us
    all_to_all x1, waiting for transfers between devices, exchanged(): return lax.all_to_all(block, 'samp', 0, 0, tiled=True)  12.8 us
    ppermute x3, waiting for transfers between devices, on_device(): recv.append(lax.ppermute(out, 'cores', pairs))  12.4 us
    ppermute x3, waiting for transfers between devices, on_device(): lax.ppermute(updated, ('cores', 'samp'), pairs)  8.16 us
    all_to_all x1, starting transfers between devices, exchanged(): return lax.all_to_all(block, 'samp', 0, 0, tiled=True)  7.87 us
    pallas_call x1, Pallas kernels, on_device(): pl.pallas_call(functools.partial(gather_kernel, peers=peers), grid=(RR //...  5.61 us
    ppermute x3, starting transfers between devices, on_device(): recv.append(lax.ppermute(out, 'cores', pairs))  4.62 us
    pallas_call x4, Pallas kernels, on_device(): call(functools.partial(pair_kernel, pair=pair), outs, [vmem()] * len(ins)...  4.45 us
  transfers between devices with their start and end apart: 16, of which 11 were waited for; matrix products, arithmetic and copies ran while one was open for 1% of the time, Pallas kernels for 7%

profile of v13, /device:TPU:16, one launch (start us, length us, event | category | flops | bytes accessed | tf_op | source)
XLA Modules:
  0.0 135.8 jit_solution(4249147635179130980)
XLA Ops:
  0.0 5.6 %gather.1 = (f32[4608,512]{1,0:T(8,128)S(1)}, s32[8,1024]{1,0:T(8,128)S(1)}, f32[8,128]{1,0:T(8,128)S(1)}) custom-call(s32[8,1024]{1,0:T(8,128)} %bitcast.16, f32[512,2304]{1,0:T(8,128)} %bitcast.20), custom_call_target="tpu_custom_call" | custom-call | tf_op jit(solution)/shard_map/gather/pallas_call | solution.py:494
  5.6 2.5 %collective-permute-done.table_ref = f32[512,2304]{1,0:T(8,128)S(1)} collective-permute-done((f32[512,2304]{1,0:T(8,128)}, f32[512,2304]{1,0:T(8,128)S(1)}, u32[]{:S(2)}, u32[]{:S(2)}) %collective-permute-start) | collective-permute-done | bytes 4718624 | tf_op jit(solution)/shard_map/ppermute | solution.py:492
  8.1 2.7 %gather_other.1.mats_ref = f32[4608,512]{1,0:T(8,128)S(1)} custom-call(s32[8,1024]{1,0:T(8,128)S(1)} %bitcast.17, f32[512,2304]{1,0:T(8,128)S(1)} %collective-permute-done.table_ref, f32[4608,512]{1,0:T(8,128)S(1)} %get-tuple-element.73._), custom_call_target="tpu_custom_call", output_to_operand_aliasing={{}: (2, {})} | custom-call | tf_op jit(solution)/shard_map/gather_other/pallas_call | solution.py:507
  10.9 1.3 collective-permute-start.1
  12.2 5.8 %collective-permute-done.1.refs_0_ = f32[48,512]{1,0:T(8,128)S(1)} collective-permute-done((f32[48,512]{1,0:T(8,128)S(1)}, f32[48,512]{1,0:T(8,128)S(1)}, u32[]{:S(2)}, u32[]{:S(2)}) %collective-permute-start.1) | collective-permute-done | bytes 98336 | tf_op jit(solution)/shard_map/ppermute | solution.py:527
  17.9 1.4 %hop1.1 = (f32[48,512]{1,0:T(8,128)S(1)}, f32[48,512]{1,0:T(8,128)S(1)}) custom-call(f32[4608,512]{1,0:T(8,128)S(1)} %gather_other.1.mats_ref, f32[48,512]{1,0:T(8,128)S(1)} %collective-permute-done.1.refs_0_), custom_call_target="tpu_custom_call" | custom-call | tf_op jit(solution)/shard_map/hop1/pallas_call | solution.py:519
  19.4 2.0 %collective-permute-start.2 = (f32[48,512]{1,0:T(8,128)S(1)}, f32[48,512]{1,0:T(8,128)S(1)}, u32[]{:S(2)}, u32[]{:S(2)}) collective-permute-start(f32[48,512]{1,0:T(8,128)S(1)} %get-tuple-element.75), channel_id=1, source_target_pairs={{32,64},{48,80},{64,32},{80,48},{33,65},{49,81},{65,33},{81,49},{3... | collective-permute-start | bytes 294920 | tf_op jit(solution)/shard_map/ppermute | solution.py:527
  21.4 4.5 %collective-permute-done.2.refs_0_.refs_1_ = f32[48,512]{1,0:T(8,128)S(1)} collective-permute-done((f32[48,512]{1,0:T(8,128)S(1)}, f32[48,512]{1,0:T(8,128)S(1)}, u32[]{:S(2)}, u32[]{:S(2)}) %collective-permute-start.2) | collective-permute-done | bytes 98336 | tf_op jit(solution)/shard_map/ppermute | solution.py:527
  25.9 1.4 %hop2.1 = (f32[48,512]{1,0:T(8,128)S(1)}, f32[48,512]{1,0:T(8,128)S(1)}) custom-call(f32[4608,512]{1,0:T(8,128)S(1)} %gather_other.1.mats_ref, f32[48,512]{1,0:T(8,128)S(1)} %collective-permute-done.2.refs_0_.refs_1_), custom_call_target="tpu_custom_call" | custom-call | tf_op jit(solution)/shard_map/hop2/pallas_call | solution.py:519
  27.3 1.3 collective-permute-start.3
  28.6 2.2 %collective-permute-done.3.refs_2_ = f32[48,512]{1,0:T(8,128)S(1)} collective-permute-done((f32[48,512]{1,0:T(8,128)S(1)}, f32[48,512]{1,0:T(8,128)S(1)}, u32[]{:S(2)}, u32[]{:S(2)}) %collective-permute-start.3) | collective-permute-done | bytes 98336 | tf_op jit(solution)/shard_map/ppermute | solution.py:527
  30.8 1.5 %finish.1 = (f32[96,512]{1,0:T(8,128)S(1)}, f32[96,512]{1,0:T(8,128)S(1)}) custom-call(f32[4608,512]{1,0:T(8,128)S(1)} %gather_other.1.mats_ref, f32[48,512]{1,0:T(8,128)S(1)} %collective-permute-done.1.refs_0_, f32[48,512]{1,0:T(8,128)S(1)} %collective-permute-done.2.refs_0_.refs_1_, f32[48,512]{1,0:T(8,128)S(1)} %collective-permute-done.3.refs_2_, ...), custom_call_target="tpu_custom_call" | custom-call | tf_op jit(solution)/shard_map/finish/pallas_call | solution.py:529
  33.8 1.8 %route.1 = (f32[16,104,128]{2,1,0:T(8,128)}, f32[104,1024]{1,0:T(8,128)S(1)}) custom-call(f32[96,512]{1,0:T(8,128)S(1)} %get-tuple-element.80.vecs_ref.own_ref, f32[96,512]{1,0:T(8,128)S(1)} %collective-permute-done.4.got_ref, s32[8,1024]{1,0:T(8,128)S(1)} %get-tuple-element.167.slot_ref, f32[8,128]{1,0:T(8,128)S(1)} %get-tuple-element.168.most_ref, ...), custom_call_target="tpu_custom_call" | custom-call | tf_op jit(solution)/shard_map/route/pallas_call | solution.py:538
  35.6 7.9 %all-to-all-start.1 = ((f32[16,104,128]{2,1,0:T(8,128)}), f32[16,104,128]{2,1,0:T(8,128)S(1)}, u32[]{:S(2)}, u32[]{:S(2)}) async-start(f32[16,104,128]{2,1,0:T(8,128)} %get-tuple-element.84), calls=%async_computation.1 | async-start | bytes 1703936 | tf_op jit(solution)/shard_map/all_to_all | solution.py:546
  43.5 1.0 constant_dynamic-slice_fusion
  46.1 12.8 %all-to-all-done.1.recv_ref = f32[16,104,128]{2,1,0:T(8,128)S(1)} async-done(((f32[16,104,128]{2,1,0:T(8,128)}), f32[16,104,128]{2,1,0:T(8,128)S(1)}, u32[]{:S(2)}, u32[]{:S(2)}) %all-to-all-start.1) | async-done | bytes 852000 | tf_op jit(solution)/shard_map/all_to_all | solution.py:546
  58.9 2.1 %collect.2 = (f32[192,384]{1,0:T(8,128)S(1)}, s32[1]{0:T(128)}) custom-call(f32[1]{0:T(128)} %bitcast.15.step_ref, f32[16,104,128]{2,1,0:T(8,128)S(1)} %all-to-all-done.1.recv_ref, f32[192,384]{1,0:T(8,128)S(1)} %reshape.26.base_ref), custom_call_target="tpu_custom_call" | custom-call | tf_op jit(solution)/shard_map/collect/pallas_call | solution.py:549
  62.6 2.5 %collective-permute-start.7 = (f32[192,384]{1,0:T(8,128)S(1)}, f32[192,384]{1,0:T(8,128)S(1)}, u32[]{:S(2)}, u32[]{:S(2)}) collective-permute-start(f32[192,384]{1,0:T(8,128)S(1)} %get-tuple-element.88.refs_0_.refs_3_), channel_id=1, source_target_pairs={{0,3},{1,0},{2,1},{3,2},{4,7},{5,4},{6,5},{7,6},{8,11},{9,8},{10,9... | collective-permute-start | bytes 884744 | tf_op jit(solution)/shard_map/ppermute | solution.py:584
  65.1 5.0 %collective-permute-done.6.refs_2_ = f32[192,384]{1,0:T(8,128)S(1)} collective-permute-done((f32[192,384]{1,0:T(8,128)S(1)}, f32[192,384]{1,0:T(8,128)S(1)}, u32[]{:S(2)}, u32[]{:S(2)}) %collective-permute-start.6) | collective-permute-done | bytes 294944 | tf_op jit(solution)/shard_map/ppermute | solution.py:584
  70.1 0.9 collective-permute-done.7.refs_3_
  71.0 2.2 %collective-permute-done.5.refs_1_ = f32[192,384]{1,0:T(8,128)S(1)} collective-permute-done((f32[192,384]{1,0:T(8,128)S(1)}, f32[192,384]{1,0:T(8,128)S(1)}, u32[]{:S(2)}, u32[]{:S(2)}) %collective-permute-start.5) | collective-permute-done | bytes 294944 | tf_op jit(solution)/shard_map/ppermute | solution.py:584
  73.3 1.6 %collective-permute-done.9.refs_5_ = f32[192,384]{1,0:T(8,128)S(1)} collective-permute-done((f32[192,384]{1,0:T(8,128)S(1)}, f32[192,384]{1,0:T(8,128)S(1)}, u32[]{:S(2)}, u32[]{:S(2)}) %collective-permute-start.9) | collective-permute-done | bytes 294944 | tf_op jit(solution)/shard_map/ppermute | solution.py:585
  74.8 1.4 %pair0.1 = (bf16[2304,384]{1,0:T(8,128)(2,1)S(1)}, bf16[384,2304]{1,0:T(8,128)(2,1)S(1)}, bf16[2304,384]{1,0:T(8,128)(2,1)S(1)}, bf16[384,2304]{1,0:T(8,128)(2,1...) custom-call(f32[192,384]{1,0:T(8,128)S(1)} %get-tuple-element.88.refs_0_.refs_3_, ...), custom_call_target="tpu_custom_call" | custom-call | tf_op jit(solution)/shard_map/pair0/pallas_call | solution.py:600
  76.3 15.5 %all_to_all.26.refs_0_ = f32[32,24,128]{2,1,0:T(8,128)S(1)} all-to-all(f32[32,24,128]{2,1,0:T(8,128)S(1)} %get-tuple-element.89), channel_id=1, replica_groups={{0,1,2,3,4,5,6,7,8,9,10,11,12,13,14,15,32,33,34,35,36,37,38,39,40,41,42..., dimensions={0} | all-to-all | bytes 786432 | tf_op jit(solution)/shard_map/all_to_all | solution.py:620
  91.9 16.7 %all_to_all.27.refs_0_ = f32[32,24,128]{2,1,0:T(8,128)S(1)} all-to-all(f32[32,24,128]{2,1,0:T(8,128)S(1)} %get-tuple-element.94), channel_id=1, replica_groups={{32,33,34,35,36,37,38,39,40,41,42,43,44,45,46,47,64,65,66,67,68,69,70,7..., dimensions={0} | all-to-all | bytes 786432 | tf_op jit(solution)/shard_map/all_to_all | solution.py:620
  108.6 2.9 %pair2.1 = (f32[32,24,128]{2,1,0:T(8,128)S(1)}, f32[24,128]{1,0:T(8,128)S(1)}, f32[24,128]{1,0:T(8,128)S(1)}) custom-call(f32[32,24,128]{2,1,0:T(8,128)S(1)} %all_to_all.27.refs_0_, bf16[2304,384]{1,0:T(8,128)(2,1)S(1)} %get-tuple-element.90.refs_1_.refs_4_, bf16[384,2304]{1,0:T(8,128)(2,1)S(1)} %get-tuple-element.91.refs_2_.refs_5_, ...), custom_call_target="tpu_custom_call" | custom-call | tf_op jit(solution)/shard_map/pair2/pallas_call | solution.py:600
  111.5 12.9 %all_to_all.28.refs_0_ = f32[32,24,128]{2,1,0:T(8,128)S(1)} all-to-all(f32[32,24,128]{2,1,0:T(8,128)S(1)} %get-tuple-element.95), channel_id=1, replica_groups={{64,65,66,67,68,69,70,71,72,73,74,75,76,77,78,79,96,97,98,99,100,101,10..., dimensions={0} | all-to-all | bytes 786432 | tf_op jit(solution)/shard_map/all_to_all | solution.py:620
  125.0 2.6 %collective-permute-start.13 = (f32[24,128]{1,0:T(8,128)S(1)}, f32[24,128]{1,0:T(8,128)S(1)}, u32[]{:S(2)}, u32[]{:S(2)}) collective-permute-start(f32[24,128]{1,0:T(8,128)S(1)} %get-tuple-element.99.a_ref), channel_id=1, source_target_pairs={{0,8},{1,9},{2,10},{3,11},{4,12},{5,13},{6,14},{7,15},{8,0},{9,1},... | collective-permute-start | bytes 36872 | tf_op jit(solution)/shard_map/ppermute | solution.py:612
  127.6 1.1 collective-permute-start.14
  128.8 2.4 %known.1.core_ref = f32[192,384]{1,0:T(8,128)S(1)} custom-call(f32[24,128]{1,0:T(8,128)S(1)} %get-tuple-element.100.refs_0_, f32[24,128]{1,0:T(8,128)S(1)} %get-tuple-element.101.refs_1_, f32[24,128]{1,0:T(8,128)S(1)} %get-tuple-element.102.refs_2_, f32[192,384]{1,0:T(8,128)S(1)} %get-tuple-element.88.refs_0_.refs_3_), custom_call_target="tpu_custom_call" | custom-call | tf_op jit(solution)/shard_map/known/pallas_call | solution.py:625
  131.3 3.0 %final.1 = f32[192,384]{1,0:T(8,128)S(1)} custom-call(f32[24,128]{1,0:T(8,128)S(1)} %get-tuple-element.99.a_ref, f32[24,128]{1,0:T(8,128)S(1)} %collective-permute-done.12.b_ref, f32[24,128]{1,0:T(8,128)S(1)} %collective-permute-done.13.c_ref, f32[24,128]{1,0:T(8,128)S(1)} %collective-permute-done.14.d_ref, f32[192,384]{1,0:T(8,128)S(1)} %known.1.core_ref), custom_call_target="tpu_custom_call" | custom-call | tf_op jit(solution)/shard_map/final/pallas_call | solution.py:626
  134.8 1.0 reshape.28
  (30 shorter events, 5.3 us)
Async XLA Ops:
  0.0 8.1 %copy-start = (s32[1024,8]{0,1:T(8,128)S(1)}, s32[1024,8]{0,1:T(8,128)}, u32[]{:S(2)}) copy-start(s32[1024,8]{0,1:T(8,128)} %param.7) | copy-start | bytes 98308
  0.0 8.1 %collective-permute-start = (f32[512,2304]{1,0:T(8,128)}, f32[512,2304]{1,0:T(8,128)S(1)}, u32[]{:S(2)}, u32[]{:S(2)}) collective-permute-start(f32[512,2304]{1,0:T(8,128)} %bitcast.19), channel_id=1, source_target_pairs={{0,16},{16,0},{32,48},{48,32},{64,80},{80,64},{96,112},{112,96},{1... | collective-permute-start | bytes 14155784 | tf_op jit(solution)/shard_map/ppermute | solution.py:492
  10.9 7.1 %collective-permute-start.1 = (f32[48,512]{1,0:T(8,128)S(1)}, f32[48,512]{1,0:T(8,128)S(1)}, u32[]{:S(2)}, u32[]{:S(2)}) collective-permute-start(f32[48,512]{1,0:T(8,128)S(1)} %get-tuple-element.74), channel_id=1, source_target_pairs={{0,32},{16,48},{96,64},{112,80},{1,33},{17,49},{97,65},{113,81},{2... | collective-permute-start | bytes 294920 | tf_op jit(solution)/shard_map/ppermute | solution.py:527
  19.4 11.4 %copy-start.1 = (f32[1024]{0:T(1024)S(1)}, f32[1024]{0:T(1024)}, u32[]{:S(2)}) copy-start(f32[1024]{0:T(1024)} %param.8) | copy-start | bytes 12292
  19.4 6.5 %collective-permute-start.2 = (f32[48,512]{1,0:T(8,128)S(1)}, f32[48,512]{1,0:T(8,128)S(1)}, u32[]{:S(2)}, u32[]{:S(2)}) collective-permute-start(f32[48,512]{1,0:T(8,128)S(1)} %get-tuple-element.75), channel_id=1, source_target_pairs={{32,64},{48,80},{64,32},{80,48},{33,65},{49,81},{65,33},{81,49},{3... | collective-permute-start | bytes 294920 | tf_op jit(solution)/shard_map/ppermute | solution.py:527
  27.3 3.5 %collective-permute-start.3 = (f32[48,512]{1,0:T(8,128)S(1)}, f32[48,512]{1,0:T(8,128)S(1)}, u32[]{:S(2)}, u32[]{:S(2)}) collective-permute-start(f32[48,512]{1,0:T(8,128)S(1)} %get-tuple-element.76.refs_6_), channel_id=1, source_target_pairs={{64,96},{80,112},{32,0},{48,16},{65,97},{81,113},{33,1},{49,17},{6... | collective-permute-start | bytes 294920 | tf_op jit(solution)/shard_map/ppermute | solution.py:527
  32.3 1.5 %collective-permute-start.4 = (f32[96,512]{1,0:T(8,128)S(1)}, f32[96,512]{1,0:T(8,128)S(1)}, u32[]{:S(2)}, u32[]{:S(2)}) collective-permute-start(f32[96,512]{1,0:T(8,128)S(1)} %get-tuple-element.81), channel_id=1, source_target_pairs={{0,16},{16,0},{32,48},{48,32},{64,80},{80,64},{96,112},{112,96},{1... | collective-permute-start | bytes 589832 | tf_op jit(solution)/shard_map/ppermute | solution.py:536
  35.6 23.3 %all-to-all-start.1 = ((f32[16,104,128]{2,1,0:T(8,128)}), f32[16,104,128]{2,1,0:T(8,128)S(1)}, u32[]{:S(2)}, u32[]{:S(2)}) async-start(f32[16,104,128]{2,1,0:T(8,128)} %get-tuple-element.84), calls=%async_computation.1 | async-start | bytes 1703936 | tf_op jit(solution)/shard_map/all_to_all | solution.py:546
  61.8 8.3 %collective-permute-start.6 = (f32[192,384]{1,0:T(8,128)S(1)}, f32[192,384]{1,0:T(8,128)S(1)}, u32[]{:S(2)}, u32[]{:S(2)}) collective-permute-start(f32[192,384]{1,0:T(8,128)S(1)} %get-tuple-element.88.refs_0_.refs_3_), channel_id=1, source_target_pairs={{0,2},{1,3},{2,0},{3,1},{4,6},{5,7},{6,4},{7,5},{8,10},{9,11},{10,... | collective-permute-start | bytes 884744 | tf_op jit(solution)/shard_map/ppermute | solution.py:584
  62.6 8.4 %collective-permute-start.7 = (f32[192,384]{1,0:T(8,128)S(1)}, f32[192,384]{1,0:T(8,128)S(1)}, u32[]{:S(2)}, u32[]{:S(2)}) collective-permute-start(f32[192,384]{1,0:T(8,128)S(1)} %get-tuple-element.88.refs_0_.refs_3_), channel_id=1, source_target_pairs={{0,3},{1,0},{2,1},{3,2},{4,7},{5,4},{6,5},{7,6},{8,11},{9,8},{10,9... | collective-permute-start | bytes 884744 | tf_op jit(solution)/shard_map/ppermute | solution.py:584
  65.1 8.2 %collective-permute-start.5 = (f32[192,384]{1,0:T(8,128)S(1)}, f32[192,384]{1,0:T(8,128)S(1)}, u32[]{:S(2)}, u32[]{:S(2)}) collective-permute-start(f32[192,384]{1,0:T(8,128)S(1)} %get-tuple-element.88.refs_0_.refs_3_), channel_id=1, source_target_pairs={{0,1},{1,2},{2,3},{3,0},{4,5},{5,6},{6,7},{7,4},{8,9},{9,10},{10,1... | collective-permute-start | bytes 884744 | tf_op jit(solution)/shard_map/ppermute | solution.py:584
  65.1 8.2 %collective-permute-start.8 = (f32[192,384]{1,0:T(8,128)S(1)}, f32[192,384]{1,0:T(8,128)S(1)}, u32[]{:S(2)}, u32[]{:S(2)}) collective-permute-start(f32[192,384]{1,0:T(8,128)S(1)} %get-tuple-element.88.refs_0_.refs_3_), channel_id=1, source_target_pairs={{0,16},{16,0},{32,48},{48,32},{64,80},{80,64},{96,112},{112,96},{1... | collective-permute-start | bytes 884744 | tf_op jit(solution)/shard_map/ppermute | solution.py:585
  70.1 3.1 %collective-permute-start.10 = (f32[192,384]{1,0:T(8,128)S(1)}, f32[192,384]{1,0:T(8,128)S(1)}, u32[]{:S(2)}, u32[]{:S(2)}) collective-permute-start(f32[192,384]{1,0:T(8,128)S(1)} %collective-permute-done.6.refs_2_), channel_id=1, source_target_pairs={{0,16},{16,0},{32,48},{48,32},{64,80},{80,64},{96,112},{112,96},{1... | collective-permute-start | bytes 884744 | tf_op jit(solution)/shard_map/ppermute | solution.py:585
  71.0 2.2 %collective-permute-start.11 = (f32[192,384]{1,0:T(8,128)S(1)}, f32[192,384]{1,0:T(8,128)S(1)}, u32[]{:S(2)}, u32[]{:S(2)}) collective-permute-start(f32[192,384]{1,0:T(8,128)S(1)} %collective-permute-done.7.refs_3_), channel_id=1, source_target_pairs={{0,16},{16,0},{32,48},{48,32},{64,80},{80,64},{96,112},{112,96},{1... | collective-permute-start | bytes 884744 | tf_op jit(solution)/shard_map/ppermute | solution.py:585
  73.3 1.6 %collective-permute-start.9 = (f32[192,384]{1,0:T(8,128)S(1)}, f32[192,384]{1,0:T(8,128)S(1)}, u32[]{:S(2)}, u32[]{:S(2)}) collective-permute-start(f32[192,384]{1,0:T(8,128)S(1)} %collective-permute-done.5.refs_1_), channel_id=1, source_target_pairs={{0,16},{16,0},{32,48},{48,32},{64,80},{80,64},{96,112},{112,96},{1... | collective-permute-start | bytes 884744 | tf_op jit(solution)/shard_map/ppermute | solution.py:585
  124.5 6.7 %collective-permute-start.12 = (f32[24,128]{1,0:T(8,128)S(1)}, f32[24,128]{1,0:T(8,128)S(1)}, u32[]{:S(2)}, u32[]{:S(2)}) collective-permute-start(f32[24,128]{1,0:T(8,128)S(1)} %get-tuple-element.99.a_ref), channel_id=1, source_target_pairs={{0,4},{1,5},{2,6},{3,7},{4,8},{5,9},{6,10},{7,11},{8,12},{9,13},{1... | collective-permute-start | bytes 36872 | tf_op jit(solution)/shard_map/ppermute | solution.py:612
  125.0 6.2 %collective-permute-start.13 = (f32[24,128]{1,0:T(8,128)S(1)}, f32[24,128]{1,0:T(8,128)S(1)}, u32[]{:S(2)}, u32[]{:S(2)}) collective-permute-start(f32[24,128]{1,0:T(8,128)S(1)} %get-tuple-element.99.a_ref), channel_id=1, source_target_pairs={{0,8},{1,9},{2,10},{3,11},{4,12},{5,13},{6,14},{7,15},{8,0},{9,1},... | collective-permute-start | bytes 36872 | tf_op jit(solution)/shard_map/ppermute | solution.py:612
  127.6 3.7 %collective-permute-start.14 = (f32[24,128]{1,0:T(8,128)S(1)}, f32[24,128]{1,0:T(8,128)S(1)}, u32[]{:S(2)}, u32[]{:S(2)}) collective-permute-start(f32[24,128]{1,0:T(8,128)S(1)} %get-tuple-element.99.a_ref), channel_id=1, source_target_pairs={{0,12},{1,13},{2,14},{3,15},{4,0},{5,1},{6,2},{7,3},{8,4},{9,5},{1... | collective-permute-start | bytes 36872 | tf_op jit(solution)/shard_map/ppermute | solution.py:612

commit v14 on v13

--- a/solution.py
+++ b/solution.py
@@ -142,14 +142,21 @@
         lax.fori_loop(0, count // 128, chunk, 0)
 
 
-def both_modes(turn, mats_ref, vec_ref, mid_ref, out_ref):
+def heading(turn):
     mode = lax.axis_index("cores")
     chips = MODES // 2
     left = (mode // 2 < chips // 2) if turn < chips // 2 else (mode // 2 >= chips // 2)
     even = (mode % 2) * RR
-    base = jnp.where(left, even, RR - even)
-    times(left, mats_ref, base, vec_ref, mid_ref)
-    times(left, mats_ref, RR - base, mid_ref, out_ref)
+    return left, jnp.where(left, even, RR - even)
+
+
+def column(mats_ref, base):
+    rows = [mats_ref[pl.ds(pl.multiple_of(base + a * R, 8), 1), :] for a in range(R)]
+    return jnp.concatenate(rows, axis=0)
+
+
+def row(mats_ref, base):
+    return mats_ref[pl.ds(pl.multiple_of(base, 8), R), :]
 
 
 def unit_at_ends(shape_):
@@ -159,15 +166,25 @@
 
 
 def hop_kernel(mats_ref, *refs, turn):
-    vec_ref, mid_ref, out_ref = refs if turn else (refs[2], refs[0], refs[1])
+    mid_ref, out_ref = refs[-2:]
     chip = lax.axis_index("cores") // 2
     live = jnp.logical_or(chip == turn, chip == MODES // 2 - 1 - turn)
+    left, base = heading(turn)
 
     @pl.when(live)
     def _():
         if turn == 0:
-            vec_ref[...] = unit_at_ends(vec_ref.shape)
-        both_modes(turn, mats_ref, vec_ref, mid_ref, out_ref)
+
+            @pl.when(left)
+            def _():
+                mid_ref[...] = row(mats_ref, base)
+
+            @pl.when(jnp.logical_not(left))
+            def _():
+                mid_ref[...] = column(mats_ref, base)
+        else:
+            times(left, mats_ref, base, refs[0], mid_ref)
+        times(left, mats_ref, RR - base, mid_ref, out_ref)
 
     @pl.when(jnp.logical_not(live))
     def _():
@@ -177,14 +194,24 @@
 
 def finish_kernel(mats_ref, *refs):
     recv, mids = refs[0:3], refs[3:6]
-    out2_ref, obs_ref, own_ref, other_ref, mid_ref, out_ref = refs[6:]
+    out2_ref, obs_ref, own_ref, other_ref, mid_ref, part_ref = refs[6:]
     mode = lax.axis_index("cores")
-    both_modes(3, mats_ref, recv[2], mid_ref, out_ref)
+    left, base = heading(3)
+    times(left, mats_ref, base, recv[2], mid_ref)
+
+    @pl.when(left)
+    def _():
+        part_ref[...] = column(mats_ref, RR - base)
+
+    @pl.when(jnp.logical_not(left))
+    def _():
+        part_ref[...] = row(mats_ref, RR - base)
+
     end1 = unit_at_ends(mid_ref.shape) + recv[0][...]
     mid1 = mids[0][...] + mids[1][...]
     end2 = recv[1][...] + recv[2][...]
     mid2 = mids[2][...] + mid_ref[...]
-    predicted = jnp.sum((out2_ref[...] + out_ref[...]) * end1, axis=0, keepdims=True)
+    predicted = jnp.sum(out2_ref[...] * end1 + part_ref[...] * mid_ref[...], axis=0, keepdims=True)
     residual = predicted - half_of(obs_ref[...], mode % 2 == 1)
     early = jnp.where(mode // 2 < MODES // 4, 1.0, 0.0) > 0.5
     even = (jnp.where(early, end1, end2), jnp.where(early, mid2, mid1) * residual)
@@ -520,7 +547,6 @@
             functools.partial(hop_kernel, turn=turn),
             [vec, vec],
             [vmem()] * (2 if turn else 1),
-            [] if turn else [pltpu.VMEM((R, half), F32)],
             name=f"hop{turn}",
         )(mats, *recv[-1:])
         pairs = [(2 * a + h, 2 * b + h) for a, b in ((turn, turn + 1), (3 - turn, 2 - turn)) for h in range(2)]

time: 137 us -> 137 us (level)
  no operation moved by 1% of the time
where the time goes in v14:
time: 137 us; the launch traced here: 135 us
  blocking collectives  45.4 us (33%)
  waiting for transfers between devices  37.4 us (27%)
  Pallas kernels  26.7 us (19%)
  starting transfers between devices  20.5 us (15%)
  local copies, waits for them, and re-layouts  3.46 us (3%)
    all_to_all x3, blocking collectives, on_device(): lax.all_to_all(res[0], ('cores', 'samp'), 0, 0, axis_index_groups=groups,...  45.4 us
    all_to_all x1, waiting for transfers between devices, exchanged(): return lax.all_to_all(block, 'samp', 0, 0, tiled=True)  12.8 us
    ppermute x3, waiting for transfers between devices, on_device(): recv.append(lax.ppermute(out, 'cores', pairs))  11.8 us
    ppermute x3, waiting for transfers between devices, on_device(): lax.ppermute(updated, ('cores', 'samp'), pairs)  8.15 us
    all_to_all x1, starting transfers between devices, exchanged(): return lax.all_to_all(block, 'samp', 0, 0, tiled=True)  7.88 us
    pallas_call x1, Pallas kernels, on_device(): pl.pallas_call(functools.partial(gather_kernel, peers=peers), grid=(RR //...  5.61 us
    ppermute x3, starting transfers between devices, on_device(): recv.append(lax.ppermute(out, 'cores', pairs))  4.94 us
    pallas_call x4, Pallas kernels, on_device(): call(functools.partial(pair_kernel, pair=pair), outs, [vmem()] * len(ins)...  4.46 us
  transfers between devices with their start and end apart: 16, of which 11 were waited for; matrix products, arithmetic and copies ran while one was open for 1% of the time, Pallas kernels for 7%

profile of v14, /device:TPU:16, one launch (start us, length us, event | category | flops | bytes accessed | tf_op | source)
XLA Modules:
  0.0 135.1 jit_solution(1272070797260745380)
XLA Ops:
  0.0 5.6 %gather.1 = (f32[4608,512]{1,0:T(8,128)S(1)}, s32[8,1024]{1,0:T(8,128)S(1)}, f32[8,128]{1,0:T(8,128)S(1)}) custom-call(s32[8,1024]{1,0:T(8,128)} %bitcast.16, f32[512,2304]{1,0:T(8,128)} %bitcast.20), custom_call_target="tpu_custom_call" | custom-call | tf_op jit(solution)/shard_map/gather/pallas_call | solution.py:521
  5.6 2.5 %collective-permute-done.table_ref = f32[512,2304]{1,0:T(8,128)S(1)} collective-permute-done((f32[512,2304]{1,0:T(8,128)}, f32[512,2304]{1,0:T(8,128)S(1)}, u32[]{:S(2)}, u32[]{:S(2)}) %collective-permute-start) | collective-permute-done | bytes 4718624 | tf_op jit(solution)/shard_map/ppermute | solution.py:519
  8.1 2.7 %gather_other.1.mats_ref = f32[4608,512]{1,0:T(8,128)S(1)} custom-call(s32[8,1024]{1,0:T(8,128)S(1)} %bitcast.17, f32[512,2304]{1,0:T(8,128)S(1)} %collective-permute-done.table_ref, f32[4608,512]{1,0:T(8,128)S(1)} %get-tuple-element.73._), custom_call_target="tpu_custom_call", output_to_operand_aliasing={{}: (2, {})} | custom-call | tf_op jit(solution)/shard_map/gather_other/pallas_call | solution.py:534
  10.9 1.3 collective-permute-start.1
  12.2 5.4 %collective-permute-done.1.refs_0_ = f32[48,512]{1,0:T(8,128)S(1)} collective-permute-done((f32[48,512]{1,0:T(8,128)S(1)}, f32[48,512]{1,0:T(8,128)S(1)}, u32[]{:S(2)}, u32[]{:S(2)}) %collective-permute-start.1) | collective-permute-done | bytes 98336 | tf_op jit(solution)/shard_map/ppermute | solution.py:553
  17.6 1.4 %hop1.1 = (f32[48,512]{1,0:T(8,128)S(1)}, f32[48,512]{1,0:T(8,128)S(1)}) custom-call(f32[4608,512]{1,0:T(8,128)S(1)} %gather_other.1.mats_ref, f32[48,512]{1,0:T(8,128)S(1)} %collective-permute-done.1.refs_0_), custom_call_target="tpu_custom_call" | custom-call | tf_op jit(solution)/shard_map/hop1/pallas_call | solution.py:546
  19.0 2.4 %collective-permute-start.2 = (f32[48,512]{1,0:T(8,128)S(1)}, f32[48,512]{1,0:T(8,128)S(1)}, u32[]{:S(2)}, u32[]{:S(2)}) collective-permute-start(f32[48,512]{1,0:T(8,128)S(1)} %get-tuple-element.75), channel_id=1, source_target_pairs={{32,64},{48,80},{64,32},{80,48},{33,65},{49,81},{65,33},{81,49},{3... | collective-permute-start | bytes 294920 | tf_op jit(solution)/shard_map/ppermute | solution.py:553
  21.4 4.1 %collective-permute-done.2.refs_0_.refs_1_ = f32[48,512]{1,0:T(8,128)S(1)} collective-permute-done((f32[48,512]{1,0:T(8,128)S(1)}, f32[48,512]{1,0:T(8,128)S(1)}, u32[]{:S(2)}, u32[]{:S(2)}) %collective-permute-start.2) | collective-permute-done | bytes 98336 | tf_op jit(solution)/shard_map/ppermute | solution.py:553
  25.6 1.4 %hop2.1 = (f32[48,512]{1,0:T(8,128)S(1)}, f32[48,512]{1,0:T(8,128)S(1)}) custom-call(f32[4608,512]{1,0:T(8,128)S(1)} %gather_other.1.mats_ref, f32[48,512]{1,0:T(8,128)S(1)} %collective-permute-done.2.refs_0_.refs_1_), custom_call_target="tpu_custom_call" | custom-call | tf_op jit(solution)/shard_map/hop2/pallas_call | solution.py:546
  27.0 1.3 collective-permute-start.3
  28.3 2.2 %collective-permute-done.3.refs_2_ = f32[48,512]{1,0:T(8,128)S(1)} collective-permute-done((f32[48,512]{1,0:T(8,128)S(1)}, f32[48,512]{1,0:T(8,128)S(1)}, u32[]{:S(2)}, u32[]{:S(2)}) %collective-permute-start.3) | collective-permute-done | bytes 98336 | tf_op jit(solution)/shard_map/ppermute | solution.py:553
  30.5 0.9 finish.1
  32.9 1.8 %route.1 = (f32[16,104,128]{2,1,0:T(8,128)}, f32[104,1024]{1,0:T(8,128)S(1)}) custom-call(f32[96,512]{1,0:T(8,128)S(1)} %get-tuple-element.80.vecs_ref.own_ref, f32[96,512]{1,0:T(8,128)S(1)} %collective-permute-done.4.got_ref, s32[8,1024]{1,0:T(8,128)S(1)} %get-tuple-element.167.slot_ref, f32[8,128]{1,0:T(8,128)S(1)} %get-tuple-element.168.most_ref, ...), custom_call_target="tpu_custom_call" | custom-call | tf_op jit(solution)/shard_map/route/pallas_call | solution.py:564
  34.6 7.9 %all-to-all-start.1 = ((f32[16,104,128]{2,1,0:T(8,128)}), f32[16,104,128]{2,1,0:T(8,128)S(1)}, u32[]{:S(2)}, u32[]{:S(2)}) async-start(f32[16,104,128]{2,1,0:T(8,128)} %get-tuple-element.84), calls=%async_computation.1 | async-start | bytes 1703936 | tf_op jit(solution)/shard_map/all_to_all | solution.py:572
  42.5 1.0 constant_dynamic-slice_fusion
  45.2 12.8 %all-to-all-done.1.recv_ref = f32[16,104,128]{2,1,0:T(8,128)S(1)} async-done(((f32[16,104,128]{2,1,0:T(8,128)}), f32[16,104,128]{2,1,0:T(8,128)S(1)}, u32[]{:S(2)}, u32[]{:S(2)}) %all-to-all-start.1) | async-done | bytes 852000 | tf_op jit(solution)/shard_map/all_to_all | solution.py:572
  57.9 2.1 %collect.2 = (f32[192,384]{1,0:T(8,128)S(1)}, s32[1]{0:T(128)}) custom-call(f32[1]{0:T(128)} %bitcast.15.step_ref, f32[16,104,128]{2,1,0:T(8,128)S(1)} %all-to-all-done.1.recv_ref, f32[192,384]{1,0:T(8,128)S(1)} %reshape.26.base_ref), custom_call_target="tpu_custom_call" | custom-call | tf_op jit(solution)/shard_map/collect/pallas_call | solution.py:575
  61.7 2.5 %collective-permute-start.7 = (f32[192,384]{1,0:T(8,128)S(1)}, f32[192,384]{1,0:T(8,128)S(1)}, u32[]{:S(2)}, u32[]{:S(2)}) collective-permute-start(f32[192,384]{1,0:T(8,128)S(1)} %get-tuple-element.88.refs_0_.refs_3_), channel_id=1, source_target_pairs={{0,3},{1,0},{2,1},{3,2},{4,7},{5,4},{6,5},{7,6},{8,11},{9,8},{10,9... | collective-permute-start | bytes 884744 | tf_op jit(solution)/shard_map/ppermute | solution.py:610
  64.1 5.0 %collective-permute-done.6.refs_2_ = f32[192,384]{1,0:T(8,128)S(1)} collective-permute-done((f32[192,384]{1,0:T(8,128)S(1)}, f32[192,384]{1,0:T(8,128)S(1)}, u32[]{:S(2)}, u32[]{:S(2)}) %collective-permute-start.6) | collective-permute-done | bytes 294944 | tf_op jit(solution)/shard_map/ppermute | solution.py:610
  69.2 0.9 collective-permute-done.7.refs_3_
  70.1 2.2 %collective-permute-done.5.refs_1_ = f32[192,384]{1,0:T(8,128)S(1)} collective-permute-done((f32[192,384]{1,0:T(8,128)S(1)}, f32[192,384]{1,0:T(8,128)S(1)}, u32[]{:S(2)}, u32[]{:S(2)}) %collective-permute-start.5) | collective-permute-done | bytes 294944 | tf_op jit(solution)/shard_map/ppermute | solution.py:610
  72.3 1.6 %collective-permute-done.9.refs_5_ = f32[192,384]{1,0:T(8,128)S(1)} collective-permute-done((f32[192,384]{1,0:T(8,128)S(1)}, f32[192,384]{1,0:T(8,128)S(1)}, u32[]{:S(2)}, u32[]{:S(2)}) %collective-permute-start.9) | collective-permute-done | bytes 294944 | tf_op jit(solution)/shard_map/ppermute | solution.py:611
  73.9 1.4 %pair0.1 = (bf16[2304,384]{1,0:T(8,128)(2,1)S(1)}, bf16[384,2304]{1,0:T(8,128)(2,1)S(1)}, bf16[2304,384]{1,0:T(8,128)(2,1)S(1)}, bf16[384,2304]{1,0:T(8,128)(2,1...) custom-call(f32[192,384]{1,0:T(8,128)S(1)} %get-tuple-element.88.refs_0_.refs_3_, ...), custom_call_target="tpu_custom_call" | custom-call | tf_op jit(solution)/shard_map/pair0/pallas_call | solution.py:626
  75.3 15.6 %all_to_all.26.refs_0_ = f32[32,24,128]{2,1,0:T(8,128)S(1)} all-to-all(f32[32,24,128]{2,1,0:T(8,128)S(1)} %get-tuple-element.89), channel_id=1, replica_groups={{0,1,2,3,4,5,6,7,8,9,10,11,12,13,14,15,32,33,34,35,36,37,38,39,40,41,42..., dimensions={0} | all-to-all | bytes 786432 | tf_op jit(solution)/shard_map/all_to_all | solution.py:646
  90.9 16.9 %all_to_all.27.refs_0_ = f32[32,24,128]{2,1,0:T(8,128)S(1)} all-to-all(f32[32,24,128]{2,1,0:T(8,128)S(1)} %get-tuple-element.94), channel_id=1, replica_groups={{32,33,34,35,36,37,38,39,40,41,42,43,44,45,46,47,64,65,66,67,68,69,70,7..., dimensions={0} | all-to-all | bytes 786432 | tf_op jit(solution)/shard_map/all_to_all | solution.py:646
  107.9 3.0 %pair2.1 = (f32[32,24,128]{2,1,0:T(8,128)S(1)}, f32[24,128]{1,0:T(8,128)S(1)}, f32[24,128]{1,0:T(8,128)S(1)}) custom-call(f32[32,24,128]{2,1,0:T(8,128)S(1)} %all_to_all.27.refs_0_, bf16[2304,384]{1,0:T(8,128)(2,1)S(1)} %get-tuple-element.90.refs_1_.refs_4_, bf16[384,2304]{1,0:T(8,128)(2,1)S(1)} %get-tuple-element.91.refs_2_.refs_5_, ...), custom_call_target="tpu_custom_call" | custom-call | tf_op jit(solution)/shard_map/pair2/pallas_call | solution.py:626
  110.8 12.9 %all_to_all.28.refs_0_ = f32[32,24,128]{2,1,0:T(8,128)S(1)} all-to-all(f32[32,24,128]{2,1,0:T(8,128)S(1)} %get-tuple-element.95), channel_id=1, replica_groups={{64,65,66,67,68,69,70,71,72,73,74,75,76,77,78,79,96,97,98,99,100,101,10..., dimensions={0} | all-to-all | bytes 786432 | tf_op jit(solution)/shard_map/all_to_all | solution.py:646
  124.3 2.6 %collective-permute-start.13 = (f32[24,128]{1,0:T(8,128)S(1)}, f32[24,128]{1,0:T(8,128)S(1)}, u32[]{:S(2)}, u32[]{:S(2)}) collective-permute-start(f32[24,128]{1,0:T(8,128)S(1)} %get-tuple-element.99.a_ref), channel_id=1, source_target_pairs={{0,8},{1,9},{2,10},{3,11},{4,12},{5,13},{6,14},{7,15},{8,0},{9,1},... | collective-permute-start | bytes 36872 | tf_op jit(solution)/shard_map/ppermute | solution.py:638
  126.9 1.1 collective-permute-start.14
  128.1 2.4 %known.1.core_ref = f32[192,384]{1,0:T(8,128)S(1)} custom-call(f32[24,128]{1,0:T(8,128)S(1)} %get-tuple-element.100.refs_0_, f32[24,128]{1,0:T(8,128)S(1)} %get-tuple-element.101.refs_1_, f32[24,128]{1,0:T(8,128)S(1)} %get-tuple-element.102.refs_2_, f32[192,384]{1,0:T(8,128)S(1)} %get-tuple-element.88.refs_0_.refs_3_), custom_call_target="tpu_custom_call" | custom-call | tf_op jit(solution)/shard_map/known/pallas_call | solution.py:651
  130.6 3.0 %final.1 = f32[192,384]{1,0:T(8,128)S(1)} custom-call(f32[24,128]{1,0:T(8,128)S(1)} %get-tuple-element.99.a_ref, f32[24,128]{1,0:T(8,128)S(1)} %collective-permute-done.12.b_ref, f32[24,128]{1,0:T(8,128)S(1)} %collective-permute-done.13.c_ref, f32[24,128]{1,0:T(8,128)S(1)} %collective-permute-done.14.d_ref, f32[192,384]{1,0:T(8,128)S(1)} %known.1.core_ref), custom_call_target="tpu_custom_call" | custom-call | tf_op jit(solution)/shard_map/final/pallas_call | solution.py:652
  134.1 1.0 reshape.28
  (30 shorter events, 5.3 us)
Async XLA Ops:
  0.0 8.1 %copy-start = (s32[1024,8]{0,1:T(8,128)S(1)}, s32[1024,8]{0,1:T(8,128)}, u32[]{:S(2)}) copy-start(s32[1024,8]{0,1:T(8,128)} %param.7) | copy-start | bytes 98308
  0.0 8.1 %collective-permute-start = (f32[512,2304]{1,0:T(8,128)}, f32[512,2304]{1,0:T(8,128)S(1)}, u32[]{:S(2)}, u32[]{:S(2)}) collective-permute-start(f32[512,2304]{1,0:T(8,128)} %bitcast.19), channel_id=1, source_target_pairs={{0,16},{16,0},{32,48},{48,32},{64,80},{80,64},{96,112},{112,96},{1... | collective-permute-start | bytes 14155784 | tf_op jit(solution)/shard_map/ppermute | solution.py:519
  10.9 6.7 %collective-permute-start.1 = (f32[48,512]{1,0:T(8,128)S(1)}, f32[48,512]{1,0:T(8,128)S(1)}, u32[]{:S(2)}, u32[]{:S(2)}) collective-permute-start(f32[48,512]{1,0:T(8,128)S(1)} %get-tuple-element.74), channel_id=1, source_target_pairs={{0,32},{16,48},{96,64},{112,80},{1,33},{17,49},{97,65},{113,81},{2... | collective-permute-start | bytes 294920 | tf_op jit(solution)/shard_map/ppermute | solution.py:553
  19.0 11.4 %copy-start.1 = (f32[1024]{0:T(1024)S(1)}, f32[1024]{0:T(1024)}, u32[]{:S(2)}) copy-start(f32[1024]{0:T(1024)} %param.8) | copy-start | bytes 12292
  19.0 6.5 %collective-permute-start.2 = (f32[48,512]{1,0:T(8,128)S(1)}, f32[48,512]{1,0:T(8,128)S(1)}, u32[]{:S(2)}, u32[]{:S(2)}) collective-permute-start(f32[48,512]{1,0:T(8,128)S(1)} %get-tuple-element.75), channel_id=1, source_target_pairs={{32,64},{48,80},{64,32},{80,48},{33,65},{49,81},{65,33},{81,49},{3... | collective-permute-start | bytes 294920 | tf_op jit(solution)/shard_map/ppermute | solution.py:553
  27.0 3.5 %collective-permute-start.3 = (f32[48,512]{1,0:T(8,128)S(1)}, f32[48,512]{1,0:T(8,128)S(1)}, u32[]{:S(2)}, u32[]{:S(2)}) collective-permute-start(f32[48,512]{1,0:T(8,128)S(1)} %get-tuple-element.76.refs_6_), channel_id=1, source_target_pairs={{64,96},{80,112},{32,0},{48,16},{65,97},{81,113},{33,1},{49,17},{6... | collective-permute-start | bytes 294920 | tf_op jit(solution)/shard_map/ppermute | solution.py:553
  31.3 1.5 %collective-permute-start.4 = (f32[96,512]{1,0:T(8,128)S(1)}, f32[96,512]{1,0:T(8,128)S(1)}, u32[]{:S(2)}, u32[]{:S(2)}) collective-permute-start(f32[96,512]{1,0:T(8,128)S(1)} %get-tuple-element.81), channel_id=1, source_target_pairs={{0,16},{16,0},{32,48},{48,32},{64,80},{80,64},{96,112},{112,96},{1... | collective-permute-start | bytes 589832 | tf_op jit(solution)/shard_map/ppermute | solution.py:562
  34.6 23.3 %all-to-all-start.1 = ((f32[16,104,128]{2,1,0:T(8,128)}), f32[16,104,128]{2,1,0:T(8,128)S(1)}, u32[]{:S(2)}, u32[]{:S(2)}) async-start(f32[16,104,128]{2,1,0:T(8,128)} %get-tuple-element.84), calls=%async_computation.1 | async-start | bytes 1703936 | tf_op jit(solution)/shard_map/all_to_all | solution.py:572
  60.8 8.3 %collective-permute-start.6 = (f32[192,384]{1,0:T(8,128)S(1)}, f32[192,384]{1,0:T(8,128)S(1)}, u32[]{:S(2)}, u32[]{:S(2)}) collective-permute-start(f32[192,384]{1,0:T(8,128)S(1)} %get-tuple-element.88.refs_0_.refs_3_), channel_id=1, source_target_pairs={{0,2},{1,3},{2,0},{3,1},{4,6},{5,7},{6,4},{7,5},{8,10},{9,11},{10,... | collective-permute-start | bytes 884744 | tf_op jit(solution)/shard_map/ppermute | solution.py:610
  61.7 8.4 %collective-permute-start.7 = (f32[192,384]{1,0:T(8,128)S(1)}, f32[192,384]{1,0:T(8,128)S(1)}, u32[]{:S(2)}, u32[]{:S(2)}) collective-permute-start(f32[192,384]{1,0:T(8,128)S(1)} %get-tuple-element.88.refs_0_.refs_3_), channel_id=1, source_target_pairs={{0,3},{1,0},{2,1},{3,2},{4,7},{5,4},{6,5},{7,6},{8,11},{9,8},{10,9... | collective-permute-start | bytes 884744 | tf_op jit(solution)/shard_map/ppermute | solution.py:610
  64.1 8.2 %collective-permute-start.5 = (f32[192,384]{1,0:T(8,128)S(1)}, f32[192,384]{1,0:T(8,128)S(1)}, u32[]{:S(2)}, u32[]{:S(2)}) collective-permute-start(f32[192,384]{1,0:T(8,128)S(1)} %get-tuple-element.88.refs_0_.refs_3_), channel_id=1, source_target_pairs={{0,1},{1,2},{2,3},{3,0},{4,5},{5,6},{6,7},{7,4},{8,9},{9,10},{10,1... | collective-permute-start | bytes 884744 | tf_op jit(solution)/shard_map/ppermute | solution.py:610
  64.1 8.2 %collective-permute-start.8 = (f32[192,384]{1,0:T(8,128)S(1)}, f32[192,384]{1,0:T(8,128)S(1)}, u32[]{:S(2)}, u32[]{:S(2)}) collective-permute-start(f32[192,384]{1,0:T(8,128)S(1)} %get-tuple-element.88.refs_0_.refs_3_), channel_id=1, source_target_pairs={{0,16},{16,0},{32,48},{48,32},{64,80},{80,64},{96,112},{112,96},{1... | collective-permute-start | bytes 884744 | tf_op jit(solution)/shard_map/ppermute | solution.py:611
  69.2 3.1 %collective-permute-start.10 = (f32[192,384]{1,0:T(8,128)S(1)}, f32[192,384]{1,0:T(8,128)S(1)}, u32[]{:S(2)}, u32[]{:S(2)}) collective-permute-start(f32[192,384]{1,0:T(8,128)S(1)} %collective-permute-done.6.refs_2_), channel_id=1, source_target_pairs={{0,16},{16,0},{32,48},{48,32},{64,80},{80,64},{96,112},{112,96},{1... | collective-permute-start | bytes 884744 | tf_op jit(solution)/shard_map/ppermute | solution.py:611
  70.1 2.2 %collective-permute-start.11 = (f32[192,384]{1,0:T(8,128)S(1)}, f32[192,384]{1,0:T(8,128)S(1)}, u32[]{:S(2)}, u32[]{:S(2)}) collective-permute-start(f32[192,384]{1,0:T(8,128)S(1)} %collective-permute-done.7.refs_3_), channel_id=1, source_target_pairs={{0,16},{16,0},{32,48},{48,32},{64,80},{80,64},{96,112},{112,96},{1... | collective-permute-start | bytes 884744 | tf_op jit(solution)/shard_map/ppermute | solution.py:611
  72.3 1.6 %collective-permute-start.9 = (f32[192,384]{1,0:T(8,128)S(1)}, f32[192,384]{1,0:T(8,128)S(1)}, u32[]{:S(2)}, u32[]{:S(2)}) collective-permute-start(f32[192,384]{1,0:T(8,128)S(1)} %collective-permute-done.5.refs_1_), channel_id=1, source_target_pairs={{0,16},{16,0},{32,48},{48,32},{64,80},{80,64},{96,112},{112,96},{1... | collective-permute-start | bytes 884744 | tf_op jit(solution)/shard_map/ppermute | solution.py:611
  123.8 6.7 %collective-permute-start.12 = (f32[24,128]{1,0:T(8,128)S(1)}, f32[24,128]{1,0:T(8,128)S(1)}, u32[]{:S(2)}, u32[]{:S(2)}) collective-permute-start(f32[24,128]{1,0:T(8,128)S(1)} %get-tuple-element.99.a_ref), channel_id=1, source_target_pairs={{0,4},{1,5},{2,6},{3,7},{4,8},{5,9},{6,10},{7,11},{8,12},{9,13},{1... | collective-permute-start | bytes 36872 | tf_op jit(solution)/shard_map/ppermute | solution.py:638
  124.3 6.2 %collective-permute-start.13 = (f32[24,128]{1,0:T(8,128)S(1)}, f32[24,128]{1,0:T(8,128)S(1)}, u32[]{:S(2)}, u32[]{:S(2)}) collective-permute-start(f32[24,128]{1,0:T(8,128)S(1)} %get-tuple-element.99.a_ref), channel_id=1, source_target_pairs={{0,8},{1,9},{2,10},{3,11},{4,12},{5,13},{6,14},{7,15},{8,0},{9,1},... | collective-permute-start | bytes 36872 | tf_op jit(solution)/shard_map/ppermute | solution.py:638
  126.9 3.7 %collective-permute-start.14 = (f32[24,128]{1,0:T(8,128)S(1)}, f32[24,128]{1,0:T(8,128)S(1)}, u32[]{:S(2)}, u32[]{:S(2)}) collective-permute-start(f32[24,128]{1,0:T(8,128)S(1)} %get-tuple-element.99.a_ref), channel_id=1, source_target_pairs={{0,12},{1,13},{2,14},{3,15},{4,0},{5,1},{6,2},{7,3},{8,4},{9,5},{1... | collective-permute-start | bytes 36872 | tf_op jit(solution)/shard_map/ppermute | solution.py:638

commit v15 on v14

--- a/solution.py
+++ b/solution.py
@@ -475,10 +475,13 @@
     applied(factored(known, absent), mode % 2 == 0, core_ref, out_ref, block_ref)
 
 
-def final_kernel(a_ref, b_ref, c_ref, d_ref, core_ref, out_ref, block_ref):
+def final_kernel(a_ref, b_ref, c_ref, d_ref, core_ref, out_ref, block_ref, flat_ref):
     level = (a_ref[...] + b_ref[...]) + (c_ref[...] + d_ref[...])
     odd = lax.axis_index("cores") % 2 == 1
-    applied(factored(level, 0.0), odd, core_ref, out_ref, block_ref)
+    applied(factored(level, 0.0), odd, core_ref, flat_ref, block_ref)
+    for g in range(GROUPS):
+        for h in range(WIDE):
+            out_ref[g * WIDE + h] = flat_ref[g * R : (g + 1) * R, h * R : (h + 1) * R]
 
 
 def vmem():
@@ -649,8 +652,8 @@
 
     block = [pltpu.VMEM((LANES, LANES), F32)]
     ahead = call(known_kernel, shape(ROWS, LANES), [vmem()] * (MODES // 2), block, name="known")(*sums, updated)
-    out = call(final_kernel, shape(ROWS, LANES), [vmem()] * (WAYS + 1), block, name="final")(*parts, ahead)
-    out = out.reshape(GROUPS, R, WIDE, R).transpose(0, 2, 1, 3)
+    block.append(pltpu.VMEM((ROWS, LANES), F32))
+    out = call(final_kernel, shape(slab, R, R), [vmem()] * (WAYS + 1), block, name="final")(*parts, ahead)
     return out.reshape(1, slab, RR)
 
 

time: 137 us -> 136 us (level)
  no operation moved by 1% of the time
where the time goes in v15:
time: 136 us; the launch traced here: 135 us
  blocking collectives  45.4 us (33%)
  waiting for transfers between devices  37.4 us (28%)
  Pallas kernels  27 us (20%)
  starting transfers between devices  20.5 us (15%)
  local copies, waits for them, and re-layouts  3.02 us (2%)
    all_to_all x3, blocking collectives, on_device(): lax.all_to_all(res[0], ('cores', 'samp'), 0, 0, axis_index_groups=groups,...  45.4 us
    all_to_all x1, waiting for transfers between devices, exchanged(): return lax.all_to_all(block, 'samp', 0, 0, tiled=True)  12.8 us
    ppermute x3, waiting for transfers between devices, on_device(): recv.append(lax.ppermute(out, 'cores', pairs))  11.8 us
    ppermute x3, waiting for transfers between devices, on_device(): lax.ppermute(updated, ('cores', 'samp'), pairs)  8.15 us
    all_to_all x1, starting transfers between devices, exchanged(): return lax.all_to_all(block, 'samp', 0, 0, tiled=True)  7.88 us
    pallas_call x1, Pallas kernels, on_device(): pl.pallas_call(functools.partial(gather_kernel, peers=peers), grid=(RR //...  5.61 us
    ppermute x3, starting transfers between devices, on_device(): recv.append(lax.ppermute(out, 'cores', pairs))  4.94 us
    pallas_call x4, Pallas kernels, on_device(): call(functools.partial(pair_kernel, pair=pair), outs, [vmem()] * len(ins)...  4.46 us
  transfers between devices with their start and end apart: 16, of which 11 were waited for; matrix products, arithmetic and copies ran while one was open for 1% of the time, Pallas kernels for 7%

profile of v15, /device:TPU:16, one launch (start us, length us, event | category | flops | bytes accessed | tf_op | source)
XLA Modules:
  0.0 134.9 jit_solution(6467011868134177423)
XLA Ops:
  0.0 5.6 %gather.1 = (f32[4608,512]{1,0:T(8,128)S(1)}, s32[8,1024]{1,0:T(8,128)S(1)}, f32[8,128]{1,0:T(8,128)S(1)}) custom-call(s32[8,1024]{1,0:T(8,128)} %bitcast.13, f32[512,2304]{1,0:T(8,128)} %bitcast.17), custom_call_target="tpu_custom_call" | custom-call | tf_op jit(solution)/shard_map/gather/pallas_call | solution.py:524
  5.6 2.5 %collective-permute-done.table_ref = f32[512,2304]{1,0:T(8,128)S(1)} collective-permute-done((f32[512,2304]{1,0:T(8,128)}, f32[512,2304]{1,0:T(8,128)S(1)}, u32[]{:S(2)}, u32[]{:S(2)}) %collective-permute-start) | collective-permute-done | bytes 4718624 | tf_op jit(solution)/shard_map/ppermute | solution.py:522
  8.1 2.7 %gather_other.1.mats_ref = f32[4608,512]{1,0:T(8,128)S(1)} custom-call(s32[8,1024]{1,0:T(8,128)S(1)} %bitcast.14, f32[512,2304]{1,0:T(8,128)S(1)} %collective-permute-done.table_ref, f32[4608,512]{1,0:T(8,128)S(1)} %get-tuple-element.73._), custom_call_target="tpu_custom_call", output_to_operand_aliasing={{}: (2, {})} | custom-call | tf_op jit(solution)/shard_map/gather_other/pallas_call | solution.py:537
  10.9 1.3 collective-permute-start.1
  12.2 5.4 %collective-permute-done.1.refs_0_ = f32[48,512]{1,0:T(8,128)S(1)} collective-permute-done((f32[48,512]{1,0:T(8,128)S(1)}, f32[48,512]{1,0:T(8,128)S(1)}, u32[]{:S(2)}, u32[]{:S(2)}) %collective-permute-start.1) | collective-permute-done | bytes 98336 | tf_op jit(solution)/shard_map/ppermute | solution.py:556
  17.6 1.4 %hop1.1 = (f32[48,512]{1,0:T(8,128)S(1)}, f32[48,512]{1,0:T(8,128)S(1)}) custom-call(f32[4608,512]{1,0:T(8,128)S(1)} %gather_other.1.mats_ref, f32[48,512]{1,0:T(8,128)S(1)} %collective-permute-done.1.refs_0_), custom_call_target="tpu_custom_call" | custom-call | tf_op jit(solution)/shard_map/hop1/pallas_call | solution.py:549
  19.0 2.4 %collective-permute-start.2 = (f32[48,512]{1,0:T(8,128)S(1)}, f32[48,512]{1,0:T(8,128)S(1)}, u32[]{:S(2)}, u32[]{:S(2)}) collective-permute-start(f32[48,512]{1,0:T(8,128)S(1)} %get-tuple-element.75), channel_id=1, source_target_pairs={{32,64},{48,80},{64,32},{80,48},{33,65},{49,81},{65,33},{81,49},{3... | collective-permute-start | bytes 294920 | tf_op jit(solution)/shard_map/ppermute | solution.py:556
  21.4 4.1 %collective-permute-done.2.refs_0_.refs_1_ = f32[48,512]{1,0:T(8,128)S(1)} collective-permute-done((f32[48,512]{1,0:T(8,128)S(1)}, f32[48,512]{1,0:T(8,128)S(1)}, u32[]{:S(2)}, u32[]{:S(2)}) %collective-permute-start.2) | collective-permute-done | bytes 98336 | tf_op jit(solution)/shard_map/ppermute | solution.py:556
  25.6 1.4 %hop2.1 = (f32[48,512]{1,0:T(8,128)S(1)}, f32[48,512]{1,0:T(8,128)S(1)}) custom-call(f32[4608,512]{1,0:T(8,128)S(1)} %gather_other.1.mats_ref, f32[48,512]{1,0:T(8,128)S(1)} %collective-permute-done.2.refs_0_.refs_1_), custom_call_target="tpu_custom_call" | custom-call | tf_op jit(solution)/shard_map/hop2/pallas_call | solution.py:549
  27.0 1.3 collective-permute-start.3
  28.3 2.2 %collective-permute-done.3.refs_2_ = f32[48,512]{1,0:T(8,128)S(1)} collective-permute-done((f32[48,512]{1,0:T(8,128)S(1)}, f32[48,512]{1,0:T(8,128)S(1)}, u32[]{:S(2)}, u32[]{:S(2)}) %collective-permute-start.3) | collective-permute-done | bytes 98336 | tf_op jit(solution)/shard_map/ppermute | solution.py:556
  30.5 0.9 finish.1
  32.9 1.8 %route.1 = (f32[16,104,128]{2,1,0:T(8,128)}, f32[104,1024]{1,0:T(8,128)S(1)}) custom-call(f32[96,512]{1,0:T(8,128)S(1)} %get-tuple-element.80.vecs_ref.own_ref, f32[96,512]{1,0:T(8,128)S(1)} %collective-permute-done.4.got_ref, s32[8,1024]{1,0:T(8,128)S(1)} %get-tuple-element.167.slot_ref, f32[8,128]{1,0:T(8,128)S(1)} %get-tuple-element.168.most_ref, ...), custom_call_target="tpu_custom_call" | custom-call | tf_op jit(solution)/shard_map/route/pallas_call | solution.py:567
  34.6 7.9 %all-to-all-start.1 = ((f32[16,104,128]{2,1,0:T(8,128)}), f32[16,104,128]{2,1,0:T(8,128)S(1)}, u32[]{:S(2)}, u32[]{:S(2)}) async-start(f32[16,104,128]{2,1,0:T(8,128)} %get-tuple-element.84), calls=%async_computation.1 | async-start | bytes 1703936 | tf_op jit(solution)/shard_map/all_to_all | solution.py:575
  42.5 1.0 constant_dynamic-slice_fusion
  45.2 12.8 %all-to-all-done.1.recv_ref = f32[16,104,128]{2,1,0:T(8,128)S(1)} async-done(((f32[16,104,128]{2,1,0:T(8,128)}), f32[16,104,128]{2,1,0:T(8,128)S(1)}, u32[]{:S(2)}, u32[]{:S(2)}) %all-to-all-start.1) | async-done | bytes 852000 | tf_op jit(solution)/shard_map/all_to_all | solution.py:575
  57.9 2.1 %collect.2 = (f32[192,384]{1,0:T(8,128)S(1)}, s32[1]{0:T(128)}) custom-call(f32[1]{0:T(128)} %bitcast.12.step_ref, f32[16,104,128]{2,1,0:T(8,128)S(1)} %all-to-all-done.1.recv_ref, f32[192,384]{1,0:T(8,128)S(1)} %reshape.23.base_ref), custom_call_target="tpu_custom_call" | custom-call | tf_op jit(solution)/shard_map/collect/pallas_call | solution.py:578
  61.7 2.5 %collective-permute-start.7 = (f32[192,384]{1,0:T(8,128)S(1)}, f32[192,384]{1,0:T(8,128)S(1)}, u32[]{:S(2)}, u32[]{:S(2)}) collective-permute-start(f32[192,384]{1,0:T(8,128)S(1)} %get-tuple-element.88.refs_0_.refs_3_), channel_id=1, source_target_pairs={{0,3},{1,0},{2,1},{3,2},{4,7},{5,4},{6,5},{7,6},{8,11},{9,8},{10,9... | collective-permute-start | bytes 884744 | tf_op jit(solution)/shard_map/ppermute | solution.py:613
  64.1 5.0 %collective-permute-done.6.refs_2_ = f32[192,384]{1,0:T(8,128)S(1)} collective-permute-done((f32[192,384]{1,0:T(8,128)S(1)}, f32[192,384]{1,0:T(8,128)S(1)}, u32[]{:S(2)}, u32[]{:S(2)}) %collective-permute-start.6) | collective-permute-done | bytes 294944 | tf_op jit(solution)/shard_map/ppermute | solution.py:613
  69.2 0.9 collective-permute-done.7.refs_3_
  70.1 2.2 %collective-permute-done.5.refs_1_ = f32[192,384]{1,0:T(8,128)S(1)} collective-permute-done((f32[192,384]{1,0:T(8,128)S(1)}, f32[192,384]{1,0:T(8,128)S(1)}, u32[]{:S(2)}, u32[]{:S(2)}) %collective-permute-start.5) | collective-permute-done | bytes 294944 | tf_op jit(solution)/shard_map/ppermute | solution.py:613
  72.3 1.6 %collective-permute-done.9.refs_5_ = f32[192,384]{1,0:T(8,128)S(1)} collective-permute-done((f32[192,384]{1,0:T(8,128)S(1)}, f32[192,384]{1,0:T(8,128)S(1)}, u32[]{:S(2)}, u32[]{:S(2)}) %collective-permute-start.9) | collective-permute-done | bytes 294944 | tf_op jit(solution)/shard_map/ppermute | solution.py:614
  73.9 1.4 %pair0.1 = (bf16[2304,384]{1,0:T(8,128)(2,1)S(1)}, bf16[384,2304]{1,0:T(8,128)(2,1)S(1)}, bf16[2304,384]{1,0:T(8,128)(2,1)S(1)}, bf16[384,2304]{1,0:T(8,128)(2,1...) custom-call(f32[192,384]{1,0:T(8,128)S(1)} %get-tuple-element.88.refs_0_.refs_3_, ...), custom_call_target="tpu_custom_call" | custom-call | tf_op jit(solution)/shard_map/pair0/pallas_call | solution.py:629
  75.3 15.6 %all_to_all.26.refs_0_ = f32[32,24,128]{2,1,0:T(8,128)S(1)} all-to-all(f32[32,24,128]{2,1,0:T(8,128)S(1)} %get-tuple-element.89), channel_id=1, replica_groups={{0,1,2,3,4,5,6,7,8,9,10,11,12,13,14,15,32,33,34,35,36,37,38,39,40,41,42..., dimensions={0} | all-to-all | bytes 786432 | tf_op jit(solution)/shard_map/all_to_all | solution.py:649
  90.9 16.9 %all_to_all.27.refs_0_ = f32[32,24,128]{2,1,0:T(8,128)S(1)} all-to-all(f32[32,24,128]{2,1,0:T(8,128)S(1)} %get-tuple-element.94), channel_id=1, replica_groups={{32,33,34,35,36,37,38,39,40,41,42,43,44,45,46,47,64,65,66,67,68,69,70,7..., dimensions={0} | all-to-all | bytes 786432 | tf_op jit(solution)/shard_map/all_to_all | solution.py:649
  107.9 3.0 %pair2.1 = (f32[32,24,128]{2,1,0:T(8,128)S(1)}, f32[24,128]{1,0:T(8,128)S(1)}, f32[24,128]{1,0:T(8,128)S(1)}) custom-call(f32[32,24,128]{2,1,0:T(8,128)S(1)} %all_to_all.27.refs_0_, bf16[2304,384]{1,0:T(8,128)(2,1)S(1)} %get-tuple-element.90.refs_1_.refs_4_, bf16[384,2304]{1,0:T(8,128)(2,1)S(1)} %get-tuple-element.91.refs_2_.refs_5_, ...), custom_call_target="tpu_custom_call" | custom-call | tf_op jit(solution)/shard_map/pair2/pallas_call | solution.py:629
  110.8 12.9 %all_to_all.28.refs_0_ = f32[32,24,128]{2,1,0:T(8,128)S(1)} all-to-all(f32[32,24,128]{2,1,0:T(8,128)S(1)} %get-tuple-element.95), channel_id=1, replica_groups={{64,65,66,67,68,69,70,71,72,73,74,75,76,77,78,79,96,97,98,99,100,101,10..., dimensions={0} | all-to-all | bytes 786432 | tf_op jit(solution)/shard_map/all_to_all | solution.py:649
  124.3 2.6 %collective-permute-start.13 = (f32[24,128]{1,0:T(8,128)S(1)}, f32[24,128]{1,0:T(8,128)S(1)}, u32[]{:S(2)}, u32[]{:S(2)}) collective-permute-start(f32[24,128]{1,0:T(8,128)S(1)} %get-tuple-element.99.a_ref), channel_id=1, source_target_pairs={{0,8},{1,9},{2,10},{3,11},{4,12},{5,13},{6,14},{7,15},{8,0},{9,1},... | collective-permute-start | bytes 36872 | tf_op jit(solution)/shard_map/ppermute | solution.py:641
  126.9 1.1 collective-permute-start.14
  128.1 2.4 %known.1.core_ref = f32[192,384]{1,0:T(8,128)S(1)} custom-call(f32[24,128]{1,0:T(8,128)S(1)} %get-tuple-element.100.refs_0_, f32[24,128]{1,0:T(8,128)S(1)} %get-tuple-element.101.refs_1_, f32[24,128]{1,0:T(8,128)S(1)} %get-tuple-element.102.refs_2_, f32[192,384]{1,0:T(8,128)S(1)} %get-tuple-element.88.refs_0_.refs_3_), custom_call_target="tpu_custom_call" | custom-call | tf_op jit(solution)/shard_map/known/pallas_call | solution.py:654
  130.6 3.3 %final.1 = f32[32,48,48]{2,1,0:T(8,128)S(1)} custom-call(f32[24,128]{1,0:T(8,128)S(1)} %get-tuple-element.99.a_ref, f32[24,128]{1,0:T(8,128)S(1)} %collective-permute-done.12.b_ref, f32[24,128]{1,0:T(8,128)S(1)} %collective-permute-done.13.c_ref, f32[24,128]{1,0:T(8,128)S(1)} %collective-permute-done.14.d_ref, f32[192,384]{1,0:T(8,128)S(1)} %known.1.core_ref), custom_call_target="tpu_custom_call" | custom-call | tf_op jit(solution)/shard_map/final/pallas_call | solution.py:656
  133.9 1.0 reshape.24
  (28 shorter events, 4.9 us)
Async XLA Ops:
  0.0 8.1 %copy-start = (s32[1024,8]{0,1:T(8,128)S(1)}, s32[1024,8]{0,1:T(8,128)}, u32[]{:S(2)}) copy-start(s32[1024,8]{0,1:T(8,128)} %param.7) | copy-start | bytes 98308
  0.0 8.1 %collective-permute-start = (f32[512,2304]{1,0:T(8,128)}, f32[512,2304]{1,0:T(8,128)S(1)}, u32[]{:S(2)}, u32[]{:S(2)}) collective-permute-start(f32[512,2304]{1,0:T(8,128)} %bitcast.16), channel_id=1, source_target_pairs={{0,16},{16,0},{32,48},{48,32},{64,80},{80,64},{96,112},{112,96},{1... | collective-permute-start | bytes 14155784 | tf_op jit(solution)/shard_map/ppermute | solution.py:522
  10.9 6.7 %collective-permute-start.1 = (f32[48,512]{1,0:T(8,128)S(1)}, f32[48,512]{1,0:T(8,128)S(1)}, u32[]{:S(2)}, u32[]{:S(2)}) collective-permute-start(f32[48,512]{1,0:T(8,128)S(1)} %get-tuple-element.74), channel_id=1, source_target_pairs={{0,32},{16,48},{96,64},{112,80},{1,33},{17,49},{97,65},{113,81},{2... | collective-permute-start | bytes 294920 | tf_op jit(solution)/shard_map/ppermute | solution.py:556
  19.0 11.4 %copy-start.1 = (f32[1024]{0:T(1024)S(1)}, f32[1024]{0:T(1024)}, u32[]{:S(2)}) copy-start(f32[1024]{0:T(1024)} %param.8) | copy-start | bytes 12292
  19.0 6.5 %collective-permute-start.2 = (f32[48,512]{1,0:T(8,128)S(1)}, f32[48,512]{1,0:T(8,128)S(1)}, u32[]{:S(2)}, u32[]{:S(2)}) collective-permute-start(f32[48,512]{1,0:T(8,128)S(1)} %get-tuple-element.75), channel_id=1, source_target_pairs={{32,64},{48,80},{64,32},{80,48},{33,65},{49,81},{65,33},{81,49},{3... | collective-permute-start | bytes 294920 | tf_op jit(solution)/shard_map/ppermute | solution.py:556
  27.0 3.5 %collective-permute-start.3 = (f32[48,512]{1,0:T(8,128)S(1)}, f32[48,512]{1,0:T(8,128)S(1)}, u32[]{:S(2)}, u32[]{:S(2)}) collective-permute-start(f32[48,512]{1,0:T(8,128)S(1)} %get-tuple-element.76.refs_6_), channel_id=1, source_target_pairs={{64,96},{80,112},{32,0},{48,16},{65,97},{81,113},{33,1},{49,17},{6... | collective-permute-start | bytes 294920 | tf_op jit(solution)/shard_map/ppermute | solution.py:556
  31.3 1.5 %collective-permute-start.4 = (f32[96,512]{1,0:T(8,128)S(1)}, f32[96,512]{1,0:T(8,128)S(1)}, u32[]{:S(2)}, u32[]{:S(2)}) collective-permute-start(f32[96,512]{1,0:T(8,128)S(1)} %get-tuple-element.81), channel_id=1, source_target_pairs={{0,16},{16,0},{32,48},{48,32},{64,80},{80,64},{96,112},{112,96},{1... | collective-permute-start | bytes 589832 | tf_op jit(solution)/shard_map/ppermute | solution.py:565
  34.6 23.3 %all-to-all-start.1 = ((f32[16,104,128]{2,1,0:T(8,128)}), f32[16,104,128]{2,1,0:T(8,128)S(1)}, u32[]{:S(2)}, u32[]{:S(2)}) async-start(f32[16,104,128]{2,1,0:T(8,128)} %get-tuple-element.84), calls=%async_computation.1 | async-start | bytes 1703936 | tf_op jit(solution)/shard_map/all_to_all | solution.py:575
  60.8 8.3 %collective-permute-start.6 = (f32[192,384]{1,0:T(8,128)S(1)}, f32[192,384]{1,0:T(8,128)S(1)}, u32[]{:S(2)}, u32[]{:S(2)}) collective-permute-start(f32[192,384]{1,0:T(8,128)S(1)} %get-tuple-element.88.refs_0_.refs_3_), channel_id=1, source_target_pairs={{0,2},{1,3},{2,0},{3,1},{4,6},{5,7},{6,4},{7,5},{8,10},{9,11},{10,... | collective-permute-start | bytes 884744 | tf_op jit(solution)/shard_map/ppermute | solution.py:613
  61.7 8.4 %collective-permute-start.7 = (f32[192,384]{1,0:T(8,128)S(1)}, f32[192,384]{1,0:T(8,128)S(1)}, u32[]{:S(2)}, u32[]{:S(2)}) collective-permute-start(f32[192,384]{1,0:T(8,128)S(1)} %get-tuple-element.88.refs_0_.refs_3_), channel_id=1, source_target_pairs={{0,3},{1,0},{2,1},{3,2},{4,7},{5,4},{6,5},{7,6},{8,11},{9,8},{10,9... | collective-permute-start | bytes 884744 | tf_op jit(solution)/shard_map/ppermute | solution.py:613
  64.1 8.2 %collective-permute-start.5 = (f32[192,384]{1,0:T(8,128)S(1)}, f32[192,384]{1,0:T(8,128)S(1)}, u32[]{:S(2)}, u32[]{:S(2)}) collective-permute-start(f32[192,384]{1,0:T(8,128)S(1)} %get-tuple-element.88.refs_0_.refs_3_), channel_id=1, source_target_pairs={{0,1},{1,2},{2,3},{3,0},{4,5},{5,6},{6,7},{7,4},{8,9},{9,10},{10,1... | collective-permute-start | bytes 884744 | tf_op jit(solution)/shard_map/ppermute | solution.py:613
  64.1 8.2 %collective-permute-start.8 = (f32[192,384]{1,0:T(8,128)S(1)}, f32[192,384]{1,0:T(8,128)S(1)}, u32[]{:S(2)}, u32[]{:S(2)}) collective-permute-start(f32[192,384]{1,0:T(8,128)S(1)} %get-tuple-element.88.refs_0_.refs_3_), channel_id=1, source_target_pairs={{0,16},{16,0},{32,48},{48,32},{64,80},{80,64},{96,112},{112,96},{1... | collective-permute-start | bytes 884744 | tf_op jit(solution)/shard_map/ppermute | solution.py:614
  69.2 3.1 %collective-permute-start.10 = (f32[192,384]{1,0:T(8,128)S(1)}, f32[192,384]{1,0:T(8,128)S(1)}, u32[]{:S(2)}, u32[]{:S(2)}) collective-permute-start(f32[192,384]{1,0:T(8,128)S(1)} %collective-permute-done.6.refs_2_), channel_id=1, source_target_pairs={{0,16},{16,0},{32,48},{48,32},{64,80},{80,64},{96,112},{112,96},{1... | collective-permute-start | bytes 884744 | tf_op jit(solution)/shard_map/ppermute | solution.py:614
  70.1 2.2 %collective-permute-start.11 = (f32[192,384]{1,0:T(8,128)S(1)}, f32[192,384]{1,0:T(8,128)S(1)}, u32[]{:S(2)}, u32[]{:S(2)}) collective-permute-start(f32[192,384]{1,0:T(8,128)S(1)} %collective-permute-done.7.refs_3_), channel_id=1, source_target_pairs={{0,16},{16,0},{32,48},{48,32},{64,80},{80,64},{96,112},{112,96},{1... | collective-permute-start | bytes 884744 | tf_op jit(solution)/shard_map/ppermute | solution.py:614
  72.3 1.6 %collective-permute-start.9 = (f32[192,384]{1,0:T(8,128)S(1)}, f32[192,384]{1,0:T(8,128)S(1)}, u32[]{:S(2)}, u32[]{:S(2)}) collective-permute-start(f32[192,384]{1,0:T(8,128)S(1)} %collective-permute-done.5.refs_1_), channel_id=1, source_target_pairs={{0,16},{16,0},{32,48},{48,32},{64,80},{80,64},{96,112},{112,96},{1... | collective-permute-start | bytes 884744 | tf_op jit(solution)/shard_map/ppermute | solution.py:614
  123.8 6.7 %collective-permute-start.12 = (f32[24,128]{1,0:T(8,128)S(1)}, f32[24,128]{1,0:T(8,128)S(1)}, u32[]{:S(2)}, u32[]{:S(2)}) collective-permute-start(f32[24,128]{1,0:T(8,128)S(1)} %get-tuple-element.99.a_ref), channel_id=1, source_target_pairs={{0,4},{1,5},{2,6},{3,7},{4,8},{5,9},{6,10},{7,11},{8,12},{9,13},{1... | collective-permute-start | bytes 36872 | tf_op jit(solution)/shard_map/ppermute | solution.py:641
  124.3 6.2 %collective-permute-start.13 = (f32[24,128]{1,0:T(8,128)S(1)}, f32[24,128]{1,0:T(8,128)S(1)}, u32[]{:S(2)}, u32[]{:S(2)}) collective-permute-start(f32[24,128]{1,0:T(8,128)S(1)} %get-tuple-element.99.a_ref), channel_id=1, source_target_pairs={{0,8},{1,9},{2,10},{3,11},{4,12},{5,13},{6,14},{7,15},{8,0},{9,1},... | collective-permute-start | bytes 36872 | tf_op jit(solution)/shard_map/ppermute | solution.py:641
  126.9 3.7 %collective-permute-start.14 = (f32[24,128]{1,0:T(8,128)S(1)}, f32[24,128]{1,0:T(8,128)S(1)}, u32[]{:S(2)}, u32[]{:S(2)}) collective-permute-start(f32[24,128]{1,0:T(8,128)S(1)} %get-tuple-element.99.a_ref), channel_id=1, source_target_pairs={{0,12},{1,13},{2,14},{3,15},{4,0},{5,1},{6,2},{7,3},{8,4},{9,5},{1... | collective-permute-start | bytes 36872 | tf_op jit(solution)/shard_map/ppermute | solution.py:641

commit v16 on v15

--- a/solution.py
+++ b/solution.py
@@ -382,7 +382,7 @@
         sum_ref[...] = jnp.sum(recv_ref[0 : recv_ref.shape[0] // 2], axis=0)
     else:
         cores = refs[2 * WAYS : 2 * WAYS + 4]
-        arrange(refs[: 2 * WAYS + 4])
+        slabs = refs[: 2 * WAYS + 4]
         even, odd = cores[:2], cores[2:]
         refs = refs[2 * WAYS + 4 :]
     kept_ref = refs.pop()
@@ -390,6 +390,8 @@
 
     @pl.when(live)
     def _():
+        if not pair:
+            arrange(slabs)
         middle = pulled(whole(sum_ref[...]) if pair else None, even, prod_ref)
         kept_ref[...] = packed_of(middle)
         if not last:
@@ -399,6 +401,8 @@
 
     @pl.when(jnp.logical_not(live))
     def _():
+        if not pair:
+            arrange(slabs)
         kept = jnp.zeros((24, 128), F32)
         for s in saved:
             kept = kept + s[...]

time: 136 us -> 136 us (level)
  no operation moved by 1% of the time
where the time goes in v16:
time: 136 us; the launch traced here: 135 us
  blocking collectives  45.1 us (33%)
  waiting for transfers between devices  37.4 us (28%)
  Pallas kernels  26.9 us (20%)
  starting transfers between devices  20.5 us (15%)
  local copies, waits for them, and re-layouts  3.02 us (2%)
    all_to_all x3, blocking collectives, on_device(): lax.all_to_all(res[0], ('cores', 'samp'), 0, 0, axis_index_groups=groups,...  45.1 us
    all_to_all x1, waiting for transfers between devices, exchanged(): return lax.all_to_all(block, 'samp', 0, 0, tiled=True)  12.8 us
    ppermute x3, waiting for transfers between devices, on_device(): recv.append(lax.ppermute(out, 'cores', pairs))  11.8 us
    ppermute x3, waiting for transfers between devices, on_device(): lax.ppermute(updated, ('cores', 'samp'), pairs)  8.15 us
    all_to_all x1, starting transfers between devices, exchanged(): return lax.all_to_all(block, 'samp', 0, 0, tiled=True)  7.88 us
    pallas_call x1, Pallas kernels, on_device(): pl.pallas_call(functools.partial(gather_kernel, peers=peers), grid=(RR //...  5.61 us
    ppermute x3, starting transfers between devices, on_device(): recv.append(lax.ppermute(out, 'cores', pairs))  4.94 us
    pallas_call x4, Pallas kernels, on_device(): call(functools.partial(pair_kernel, pair=pair), outs, [vmem()] * len(ins)...  4.43 us
  transfers between devices with their start and end apart: 16, of which 11 were waited for; matrix products, arithmetic and copies ran while one was open for 1% of the time, Pallas kernels for 7%

profile of v16, /device:TPU:16, one launch (start us, length us, event | category | flops | bytes accessed | tf_op | source)
XLA Modules:
  0.0 134.6 jit_solution(7342638760226867231)
XLA Ops:
  0.0 5.6 %gather.1 = (f32[4608,512]{1,0:T(8,128)S(1)}, s32[8,1024]{1,0:T(8,128)S(1)}, f32[8,128]{1,0:T(8,128)S(1)}) custom-call(s32[8,1024]{1,0:T(8,128)} %bitcast.13, f32[512,2304]{1,0:T(8,128)} %bitcast.17), custom_call_target="tpu_custom_call" | custom-call | tf_op jit(solution)/shard_map/gather/pallas_call | solution.py:528
  5.6 2.5 %collective-permute-done.table_ref = f32[512,2304]{1,0:T(8,128)S(1)} collective-permute-done((f32[512,2304]{1,0:T(8,128)}, f32[512,2304]{1,0:T(8,128)S(1)}, u32[]{:S(2)}, u32[]{:S(2)}) %collective-permute-start) | collective-permute-done | bytes 4718624 | tf_op jit(solution)/shard_map/ppermute | solution.py:526
  8.1 2.7 %gather_other.1.mats_ref = f32[4608,512]{1,0:T(8,128)S(1)} custom-call(s32[8,1024]{1,0:T(8,128)S(1)} %bitcast.14, f32[512,2304]{1,0:T(8,128)S(1)} %collective-permute-done.table_ref, f32[4608,512]{1,0:T(8,128)S(1)} %get-tuple-element.73._), custom_call_target="tpu_custom_call", output_to_operand_aliasing={{}: (2, {})} | custom-call | tf_op jit(solution)/shard_map/gather_other/pallas_call | solution.py:541
  10.9 1.3 collective-permute-start.1
  12.2 5.4 %collective-permute-done.1.refs_0_ = f32[48,512]{1,0:T(8,128)S(1)} collective-permute-done((f32[48,512]{1,0:T(8,128)S(1)}, f32[48,512]{1,0:T(8,128)S(1)}, u32[]{:S(2)}, u32[]{:S(2)}) %collective-permute-start.1) | collective-permute-done | bytes 98336 | tf_op jit(solution)/shard_map/ppermute | solution.py:560
  17.6 1.4 %hop1.1 = (f32[48,512]{1,0:T(8,128)S(1)}, f32[48,512]{1,0:T(8,128)S(1)}) custom-call(f32[4608,512]{1,0:T(8,128)S(1)} %gather_other.1.mats_ref, f32[48,512]{1,0:T(8,128)S(1)} %collective-permute-done.1.refs_0_), custom_call_target="tpu_custom_call" | custom-call | tf_op jit(solution)/shard_map/hop1/pallas_call | solution.py:553
  19.0 2.4 %collective-permute-start.2 = (f32[48,512]{1,0:T(8,128)S(1)}, f32[48,512]{1,0:T(8,128)S(1)}, u32[]{:S(2)}, u32[]{:S(2)}) collective-permute-start(f32[48,512]{1,0:T(8,128)S(1)} %get-tuple-element.75), channel_id=1, source_target_pairs={{32,64},{48,80},{64,32},{80,48},{33,65},{49,81},{65,33},{81,49},{3... | collective-permute-start | bytes 294920 | tf_op jit(solution)/shard_map/ppermute | solution.py:560
  21.4 4.1 %collective-permute-done.2.refs_0_.refs_1_ = f32[48,512]{1,0:T(8,128)S(1)} collective-permute-done((f32[48,512]{1,0:T(8,128)S(1)}, f32[48,512]{1,0:T(8,128)S(1)}, u32[]{:S(2)}, u32[]{:S(2)}) %collective-permute-start.2) | collective-permute-done | bytes 98336 | tf_op jit(solution)/shard_map/ppermute | solution.py:560
  25.6 1.4 %hop2.1 = (f32[48,512]{1,0:T(8,128)S(1)}, f32[48,512]{1,0:T(8,128)S(1)}) custom-call(f32[4608,512]{1,0:T(8,128)S(1)} %gather_other.1.mats_ref, f32[48,512]{1,0:T(8,128)S(1)} %collective-permute-done.2.refs_0_.refs_1_), custom_call_target="tpu_custom_call" | custom-call | tf_op jit(solution)/shard_map/hop2/pallas_call | solution.py:553
  27.0 1.3 collective-permute-start.3
  28.3 2.2 %collective-permute-done.3.refs_2_ = f32[48,512]{1,0:T(8,128)S(1)} collective-permute-done((f32[48,512]{1,0:T(8,128)S(1)}, f32[48,512]{1,0:T(8,128)S(1)}, u32[]{:S(2)}, u32[]{:S(2)}) %collective-permute-start.3) | collective-permute-done | bytes 98336 | tf_op jit(solution)/shard_map/ppermute | solution.py:560
  30.5 0.9 finish.1
  32.9 1.8 %route.1 = (f32[16,104,128]{2,1,0:T(8,128)}, f32[104,1024]{1,0:T(8,128)S(1)}) custom-call(f32[96,512]{1,0:T(8,128)S(1)} %get-tuple-element.80.vecs_ref.own_ref, f32[96,512]{1,0:T(8,128)S(1)} %collective-permute-done.4.got_ref, s32[8,1024]{1,0:T(8,128)S(1)} %get-tuple-element.167.slot_ref, f32[8,128]{1,0:T(8,128)S(1)} %get-tuple-element.168.most_ref, ...), custom_call_target="tpu_custom_call" | custom-call | tf_op jit(solution)/shard_map/route/pallas_call | solution.py:571
  34.6 7.9 %all-to-all-start.1 = ((f32[16,104,128]{2,1,0:T(8,128)}), f32[16,104,128]{2,1,0:T(8,128)S(1)}, u32[]{:S(2)}, u32[]{:S(2)}) async-start(f32[16,104,128]{2,1,0:T(8,128)} %get-tuple-element.84), calls=%async_computation.1 | async-start | bytes 1703936 | tf_op jit(solution)/shard_map/all_to_all | solution.py:579
  42.5 1.0 constant_dynamic-slice_fusion
  45.2 12.8 %all-to-all-done.1.recv_ref = f32[16,104,128]{2,1,0:T(8,128)S(1)} async-done(((f32[16,104,128]{2,1,0:T(8,128)}), f32[16,104,128]{2,1,0:T(8,128)S(1)}, u32[]{:S(2)}, u32[]{:S(2)}) %all-to-all-start.1) | async-done | bytes 852000 | tf_op jit(solution)/shard_map/all_to_all | solution.py:579
  57.9 2.1 %collect.2 = (f32[192,384]{1,0:T(8,128)S(1)}, s32[1]{0:T(128)}) custom-call(f32[1]{0:T(128)} %bitcast.12.step_ref, f32[16,104,128]{2,1,0:T(8,128)S(1)} %all-to-all-done.1.recv_ref, f32[192,384]{1,0:T(8,128)S(1)} %reshape.23.base_ref), custom_call_target="tpu_custom_call" | custom-call | tf_op jit(solution)/shard_map/collect/pallas_call | solution.py:582
  61.7 2.5 %collective-permute-start.7 = (f32[192,384]{1,0:T(8,128)S(1)}, f32[192,384]{1,0:T(8,128)S(1)}, u32[]{:S(2)}, u32[]{:S(2)}) collective-permute-start(f32[192,384]{1,0:T(8,128)S(1)} %get-tuple-element.88.refs_0_.refs_3_), channel_id=1, source_target_pairs={{0,3},{1,0},{2,1},{3,2},{4,7},{5,4},{6,5},{7,6},{8,11},{9,8},{10,9... | collective-permute-start | bytes 884744 | tf_op jit(solution)/shard_map/ppermute | solution.py:617
  64.1 5.0 %collective-permute-done.6.refs_2_ = f32[192,384]{1,0:T(8,128)S(1)} collective-permute-done((f32[192,384]{1,0:T(8,128)S(1)}, f32[192,384]{1,0:T(8,128)S(1)}, u32[]{:S(2)}, u32[]{:S(2)}) %collective-permute-start.6) | collective-permute-done | bytes 294944 | tf_op jit(solution)/shard_map/ppermute | solution.py:617
  69.2 0.9 collective-permute-done.7.refs_3_
  70.1 2.2 %collective-permute-done.5.refs_1_ = f32[192,384]{1,0:T(8,128)S(1)} collective-permute-done((f32[192,384]{1,0:T(8,128)S(1)}, f32[192,384]{1,0:T(8,128)S(1)}, u32[]{:S(2)}, u32[]{:S(2)}) %collective-permute-start.5) | collective-permute-done | bytes 294944 | tf_op jit(solution)/shard_map/ppermute | solution.py:617
  72.3 1.6 %collective-permute-done.9.refs_5_ = f32[192,384]{1,0:T(8,128)S(1)} collective-permute-done((f32[192,384]{1,0:T(8,128)S(1)}, f32[192,384]{1,0:T(8,128)S(1)}, u32[]{:S(2)}, u32[]{:S(2)}) %collective-permute-start.9) | collective-permute-done | bytes 294944 | tf_op jit(solution)/shard_map/ppermute | solution.py:618
  73.9 1.4 %pair0.1 = (bf16[2304,384]{1,0:T(8,128)(2,1)S(1)}, bf16[384,2304]{1,0:T(8,128)(2,1)S(1)}, bf16[2304,384]{1,0:T(8,128)(2,1)S(1)}, bf16[384,2304]{1,0:T(8,128)(2,1...) custom-call(f32[192,384]{1,0:T(8,128)S(1)} %get-tuple-element.88.refs_0_.refs_3_, ...), custom_call_target="tpu_custom_call" | custom-call | tf_op jit(solution)/shard_map/pair0/pallas_call | solution.py:633
  75.3 15.6 %all_to_all.26.refs_0_ = f32[32,24,128]{2,1,0:T(8,128)S(1)} all-to-all(f32[32,24,128]{2,1,0:T(8,128)S(1)} %get-tuple-element.89), channel_id=1, replica_groups={{0,1,2,3,4,5,6,7,8,9,10,11,12,13,14,15,32,33,34,35,36,37,38,39,40,41,42..., dimensions={0} | all-to-all | bytes 786432 | tf_op jit(solution)/shard_map/all_to_all | solution.py:653
  90.9 16.6 %all_to_all.27.refs_0_ = f32[32,24,128]{2,1,0:T(8,128)S(1)} all-to-all(f32[32,24,128]{2,1,0:T(8,128)S(1)} %get-tuple-element.94), channel_id=1, replica_groups={{32,33,34,35,36,37,38,39,40,41,42,43,44,45,46,47,64,65,66,67,68,69,70,7..., dimensions={0} | all-to-all | bytes 786432 | tf_op jit(solution)/shard_map/all_to_all | solution.py:653
  107.6 2.9 %pair2.1 = (f32[32,24,128]{2,1,0:T(8,128)S(1)}, f32[24,128]{1,0:T(8,128)S(1)}, f32[24,128]{1,0:T(8,128)S(1)}) custom-call(f32[32,24,128]{2,1,0:T(8,128)S(1)} %all_to_all.27.refs_0_, bf16[2304,384]{1,0:T(8,128)(2,1)S(1)} %get-tuple-element.90.refs_1_.refs_4_, bf16[384,2304]{1,0:T(8,128)(2,1)S(1)} %get-tuple-element.91.refs_2_.refs_5_, ...), custom_call_target="tpu_custom_call" | custom-call | tf_op jit(solution)/shard_map/pair2/pallas_call | solution.py:633
  110.5 12.9 %all_to_all.28.refs_0_ = f32[32,24,128]{2,1,0:T(8,128)S(1)} all-to-all(f32[32,24,128]{2,1,0:T(8,128)S(1)} %get-tuple-element.95), channel_id=1, replica_groups={{64,65,66,67,68,69,70,71,72,73,74,75,76,77,78,79,96,97,98,99,100,101,10..., dimensions={0} | all-to-all | bytes 786432 | tf_op jit(solution)/shard_map/all_to_all | solution.py:653
  124.0 2.6 %collective-permute-start.13 = (f32[24,128]{1,0:T(8,128)S(1)}, f32[24,128]{1,0:T(8,128)S(1)}, u32[]{:S(2)}, u32[]{:S(2)}) collective-permute-start(f32[24,128]{1,0:T(8,128)S(1)} %get-tuple-element.99.a_ref), channel_id=1, source_target_pairs={{0,8},{1,9},{2,10},{3,11},{4,12},{5,13},{6,14},{7,15},{8,0},{9,1},... | collective-permute-start | bytes 36872 | tf_op jit(solution)/shard_map/ppermute | solution.py:645
  126.6 1.1 collective-permute-start.14
  127.7 2.4 %known.1.core_ref = f32[192,384]{1,0:T(8,128)S(1)} custom-call(f32[24,128]{1,0:T(8,128)S(1)} %get-tuple-element.100.refs_0_, f32[24,128]{1,0:T(8,128)S(1)} %get-tuple-element.101.refs_1_, f32[24,128]{1,0:T(8,128)S(1)} %get-tuple-element.102.refs_2_, f32[192,384]{1,0:T(8,128)S(1)} %get-tuple-element.88.refs_0_.refs_3_), custom_call_target="tpu_custom_call" | custom-call | tf_op jit(solution)/shard_map/known/pallas_call | solution.py:658
  130.3 3.3 %final.1 = f32[32,48,48]{2,1,0:T(8,128)S(1)} custom-call(f32[24,128]{1,0:T(8,128)S(1)} %get-tuple-element.99.a_ref, f32[24,128]{1,0:T(8,128)S(1)} %collective-permute-done.12.b_ref, f32[24,128]{1,0:T(8,128)S(1)} %collective-permute-done.13.c_ref, f32[24,128]{1,0:T(8,128)S(1)} %collective-permute-done.14.d_ref, f32[192,384]{1,0:T(8,128)S(1)} %known.1.core_ref), custom_call_target="tpu_custom_call" | custom-call | tf_op jit(solution)/shard_map/final/pallas_call | solution.py:660
  133.6 1.0 reshape.24
  (28 shorter events, 4.9 us)
Async XLA Ops:
  0.0 8.1 %copy-start = (s32[1024,8]{0,1:T(8,128)S(1)}, s32[1024,8]{0,1:T(8,128)}, u32[]{:S(2)}) copy-start(s32[1024,8]{0,1:T(8,128)} %param.7) | copy-start | bytes 98308
  0.0 8.1 %collective-permute-start = (f32[512,2304]{1,0:T(8,128)}, f32[512,2304]{1,0:T(8,128)S(1)}, u32[]{:S(2)}, u32[]{:S(2)}) collective-permute-start(f32[512,2304]{1,0:T(8,128)} %bitcast.16), channel_id=1, source_target_pairs={{0,16},{16,0},{32,48},{48,32},{64,80},{80,64},{96,112},{112,96},{1... | collective-permute-start | bytes 14155784 | tf_op jit(solution)/shard_map/ppermute | solution.py:526
  10.9 6.7 %collective-permute-start.1 = (f32[48,512]{1,0:T(8,128)S(1)}, f32[48,512]{1,0:T(8,128)S(1)}, u32[]{:S(2)}, u32[]{:S(2)}) collective-permute-start(f32[48,512]{1,0:T(8,128)S(1)} %get-tuple-element.74), channel_id=1, source_target_pairs={{0,32},{16,48},{96,64},{112,80},{1,33},{17,49},{97,65},{113,81},{2... | collective-permute-start | bytes 294920 | tf_op jit(solution)/shard_map/ppermute | solution.py:560
  19.0 11.4 %copy-start.1 = (f32[1024]{0:T(1024)S(1)}, f32[1024]{0:T(1024)}, u32[]{:S(2)}) copy-start(f32[1024]{0:T(1024)} %param.8) | copy-start | bytes 12292
  19.0 6.5 %collective-permute-start.2 = (f32[48,512]{1,0:T(8,128)S(1)}, f32[48,512]{1,0:T(8,128)S(1)}, u32[]{:S(2)}, u32[]{:S(2)}) collective-permute-start(f32[48,512]{1,0:T(8,128)S(1)} %get-tuple-element.75), channel_id=1, source_target_pairs={{32,64},{48,80},{64,32},{80,48},{33,65},{49,81},{65,33},{81,49},{3... | collective-permute-start | bytes 294920 | tf_op jit(solution)/shard_map/ppermute | solution.py:560
  27.0 3.5 %collective-permute-start.3 = (f32[48,512]{1,0:T(8,128)S(1)}, f32[48,512]{1,0:T(8,128)S(1)}, u32[]{:S(2)}, u32[]{:S(2)}) collective-permute-start(f32[48,512]{1,0:T(8,128)S(1)} %get-tuple-element.76.refs_6_), channel_id=1, source_target_pairs={{64,96},{80,112},{32,0},{48,16},{65,97},{81,113},{33,1},{49,17},{6... | collective-permute-start | bytes 294920 | tf_op jit(solution)/shard_map/ppermute | solution.py:560
  31.3 1.5 %collective-permute-start.4 = (f32[96,512]{1,0:T(8,128)S(1)}, f32[96,512]{1,0:T(8,128)S(1)}, u32[]{:S(2)}, u32[]{:S(2)}) collective-permute-start(f32[96,512]{1,0:T(8,128)S(1)} %get-tuple-element.81), channel_id=1, source_target_pairs={{0,16},{16,0},{32,48},{48,32},{64,80},{80,64},{96,112},{112,96},{1... | collective-permute-start | bytes 589832 | tf_op jit(solution)/shard_map/ppermute | solution.py:569
  34.6 23.3 %all-to-all-start.1 = ((f32[16,104,128]{2,1,0:T(8,128)}), f32[16,104,128]{2,1,0:T(8,128)S(1)}, u32[]{:S(2)}, u32[]{:S(2)}) async-start(f32[16,104,128]{2,1,0:T(8,128)} %get-tuple-element.84), calls=%async_computation.1 | async-start | bytes 1703936 | tf_op jit(solution)/shard_map/all_to_all | solution.py:579
  60.8 8.3 %collective-permute-start.6 = (f32[192,384]{1,0:T(8,128)S(1)}, f32[192,384]{1,0:T(8,128)S(1)}, u32[]{:S(2)}, u32[]{:S(2)}) collective-permute-start(f32[192,384]{1,0:T(8,128)S(1)} %get-tuple-element.88.refs_0_.refs_3_), channel_id=1, source_target_pairs={{0,2},{1,3},{2,0},{3,1},{4,6},{5,7},{6,4},{7,5},{8,10},{9,11},{10,... | collective-permute-start | bytes 884744 | tf_op jit(solution)/shard_map/ppermute | solution.py:617
  61.7 8.4 %collective-permute-start.7 = (f32[192,384]{1,0:T(8,128)S(1)}, f32[192,384]{1,0:T(8,128)S(1)}, u32[]{:S(2)}, u32[]{:S(2)}) collective-permute-start(f32[192,384]{1,0:T(8,128)S(1)} %get-tuple-element.88.refs_0_.refs_3_), channel_id=1, source_target_pairs={{0,3},{1,0},{2,1},{3,2},{4,7},{5,4},{6,5},{7,6},{8,11},{9,8},{10,9... | collective-permute-start | bytes 884744 | tf_op jit(solution)/shard_map/ppermute | solution.py:617
  64.1 8.2 %collective-permute-start.5 = (f32[192,384]{1,0:T(8,128)S(1)}, f32[192,384]{1,0:T(8,128)S(1)}, u32[]{:S(2)}, u32[]{:S(2)}) collective-permute-start(f32[192,384]{1,0:T(8,128)S(1)} %get-tuple-element.88.refs_0_.refs_3_), channel_id=1, source_target_pairs={{0,1},{1,2},{2,3},{3,0},{4,5},{5,6},{6,7},{7,4},{8,9},{9,10},{10,1... | collective-permute-start | bytes 884744 | tf_op jit(solution)/shard_map/ppermute | solution.py:617
  64.1 8.2 %collective-permute-start.8 = (f32[192,384]{1,0:T(8,128)S(1)}, f32[192,384]{1,0:T(8,128)S(1)}, u32[]{:S(2)}, u32[]{:S(2)}) collective-permute-start(f32[192,384]{1,0:T(8,128)S(1)} %get-tuple-element.88.refs_0_.refs_3_), channel_id=1, source_target_pairs={{0,16},{16,0},{32,48},{48,32},{64,80},{80,64},{96,112},{112,96},{1... | collective-permute-start | bytes 884744 | tf_op jit(solution)/shard_map/ppermute | solution.py:618
  69.2 3.1 %collective-permute-start.10 = (f32[192,384]{1,0:T(8,128)S(1)}, f32[192,384]{1,0:T(8,128)S(1)}, u32[]{:S(2)}, u32[]{:S(2)}) collective-permute-start(f32[192,384]{1,0:T(8,128)S(1)} %collective-permute-done.6.refs_2_), channel_id=1, source_target_pairs={{0,16},{16,0},{32,48},{48,32},{64,80},{80,64},{96,112},{112,96},{1... | collective-permute-start | bytes 884744 | tf_op jit(solution)/shard_map/ppermute | solution.py:618
  70.1 2.2 %collective-permute-start.11 = (f32[192,384]{1,0:T(8,128)S(1)}, f32[192,384]{1,0:T(8,128)S(1)}, u32[]{:S(2)}, u32[]{:S(2)}) collective-permute-start(f32[192,384]{1,0:T(8,128)S(1)} %collective-permute-done.7.refs_3_), channel_id=1, source_target_pairs={{0,16},{16,0},{32,48},{48,32},{64,80},{80,64},{96,112},{112,96},{1... | collective-permute-start | bytes 884744 | tf_op jit(solution)/shard_map/ppermute | solution.py:618
  72.3 1.6 %collective-permute-start.9 = (f32[192,384]{1,0:T(8,128)S(1)}, f32[192,384]{1,0:T(8,128)S(1)}, u32[]{:S(2)}, u32[]{:S(2)}) collective-permute-start(f32[192,384]{1,0:T(8,128)S(1)} %collective-permute-done.5.refs_1_), channel_id=1, source_target_pairs={{0,16},{16,0},{32,48},{48,32},{64,80},{80,64},{96,112},{112,96},{1... | collective-permute-start | bytes 884744 | tf_op jit(solution)/shard_map/ppermute | solution.py:618
  123.4 6.7 %collective-permute-start.12 = (f32[24,128]{1,0:T(8,128)S(1)}, f32[24,128]{1,0:T(8,128)S(1)}, u32[]{:S(2)}, u32[]{:S(2)}) collective-permute-start(f32[24,128]{1,0:T(8,128)S(1)} %get-tuple-element.99.a_ref), channel_id=1, source_target_pairs={{0,4},{1,5},{2,6},{3,7},{4,8},{5,9},{6,10},{7,11},{8,12},{9,13},{1... | collective-permute-start | bytes 36872 | tf_op jit(solution)/shard_map/ppermute | solution.py:645
  124.0 6.2 %collective-permute-start.13 = (f32[24,128]{1,0:T(8,128)S(1)}, f32[24,128]{1,0:T(8,128)S(1)}, u32[]{:S(2)}, u32[]{:S(2)}) collective-permute-start(f32[24,128]{1,0:T(8,128)S(1)} %get-tuple-element.99.a_ref), channel_id=1, source_target_pairs={{0,8},{1,9},{2,10},{3,11},{4,12},{5,13},{6,14},{7,15},{8,0},{9,1},... | collective-permute-start | bytes 36872 | tf_op jit(solution)/shard_map/ppermute | solution.py:645
  126.6 3.7 %collective-permute-start.14 = (f32[24,128]{1,0:T(8,128)S(1)}, f32[24,128]{1,0:T(8,128)S(1)}, u32[]{:S(2)}, u32[]{:S(2)}) collective-permute-start(f32[24,128]{1,0:T(8,128)S(1)} %get-tuple-element.99.a_ref), channel_id=1, source_target_pairs={{0,12},{1,13},{2,14},{3,15},{4,0},{5,1},{6,2},{7,3},{8,4},{9,5},{1... | collective-permute-start | bytes 36872 | tf_op jit(solution)/shard_map/ppermute | solution.py:645
